TPU v7x, 32 devices: a whole 2x2x4 slice. The times are simulated.
32 devices in a mesh: dp: 8 (over y, x, core), mp: 4 (over z).
Axes of the slice: x: 2, y: 2, z: 4, core: 2. Of those that a mesh axis runs over, the one named last changes fastest.
Arguments:
- tokens: bfloat16 [12288, 1792], P(('dp', 'mp')), may hold values from -6 to 6
- cotangent: bfloat16 [12288, 1792], P(('dp', 'mp')), may hold values from -6 to 6
- route: int32 [12288], P(('dp', 'mp')), may hold values from 0 to 12287, as said below
- lengths: int32 [8, 3], P('dp'), may hold values from 1 to 1024, 1536 in all within a row
- key_mask: int32 [12288], P('dp'), may hold values 0 or 1
- norm1_gain: float32 [1792], replicated, may hold values from 0.1 to 1.9
- norm2_gain: float32 [1792], replicated, may hold values from 0.1 to 1.9
- w_query: bfloat16 [1792, 1792], P(None, 'mp'), may hold values from -0.1875 to 0.1875
- w_key: bfloat16 [1792, 1792], P(None, 'mp'), may hold values from -0.1875 to 0.1875
- w_value: bfloat16 [1792, 1792], P(None, 'mp'), may hold values from -0.125 to 0.125
- w_out: bfloat16 [1792, 1792], P('mp'), may hold values from -0.375 to 0.375
- w_gate: bfloat16 [1792, 4096], P(None, 'mp'), may hold values from -0.125 to 0.125
- w_up: bfloat16 [1792, 4096], P(None, 'mp'), may hold values from -0.125 to 0.125
- w_down: bfloat16 [4096, 1792], P('mp'), may hold values from -0.125 to 0.125
Outputs:
- output: bfloat16 [12288, 1792], P(('dp', 'mp'))
- input_grad: bfloat16 [12288, 1792], P(('dp', 'mp'))
- norm1_gain_grad: float32 [1792], replicated
- norm2_gain_grad: float32 [1792], replicated
- w_query_grad: float32 [1792, 1792], P(None, 'mp')
- w_key_grad: float32 [1792, 1792], P(None, 'mp')
- w_value_grad: float32 [1792, 1792], P(None, 'mp')
- w_out_grad: float32 [1792, 1792], P('mp')
- w_gate_grad: float32 [1792, 4096], P(None, 'mp')
- w_up_grad: float32 [1792, 4096], P(None, 'mp')
- w_down_grad: float32 [4096, 1792], P('mp')
Inputs may be any that keep to these rules, and one draw needn't show every extreme that they name: route is a permutation of the 12288 slots. For every row r, slot s = route[r] lies on index s // 1536 of dp and on index (s // 384) % (number of mp indices) of mp, and that mp index equals the mp index of the device that holds row r in given order; every device holds exactly 48 rows bound for each index of dp. Each row of lengths sums to 1536; its largest entry is exactly 1024.
All inputs are finite; a program needn't handle non-finite values. No bound on the sum of `key_mask` on one device may be relied on, other than what follows from the above.
Results may differ from a plain program's by a relative error of at most 0.019.
Values may be sent and summed in bfloat16 or wider, within the bound.
A program may use at most 192 MiB of HBM per device.

v0:
```python
import jax
import jax.numpy as jnp
from jax import lax
from jax.sharding import PartitionSpec as P

HEAD_DIM = 112
WINDOW = 64
TOK_DEV = 1536


EPSILON = 1e-05
MASKED = 1e30


def norm_rows(values):
    inverse = lax.rsqrt(jnp.mean(values * values, axis=-1, keepdims=True) + EPSILON)
    return (values * inverse, inverse)


def norm_back(gradient, normed, inverse, norm_gain):
    scaled = gradient * norm_gain
    result = inverse * (scaled - normed * jnp.mean(scaled * normed, axis=-1, keepdims=True))
    return (result, jnp.sum(gradient * normed, axis=0))


def padded(values, filler):
    front = jnp.full((WINDOW,) + values.shape[1:], filler, values.dtype)
    return jnp.concatenate([front, values], axis=0)


def block_scores(query_block, key_block, query_seg, key_seg, key_flag, first_row, score_scale):
    query_pos = first_row + jnp.arange(query_block.shape[0], dtype=jnp.int32)
    key_pos = first_row - WINDOW + jnp.arange(key_block.shape[0], dtype=jnp.int32)
    distance = query_pos[:, None] - key_pos[None, :]
    allowed = (distance >= 0) & (distance < WINDOW) & (query_seg[:, None] == key_seg[None, :])
    allowed = allowed & ((key_flag[None, :] == 1) | (distance == 0))
    raw_scores = (
        jnp.einsum("qhd,khd->hqk", query_block, key_block, preferred_element_type=jnp.float32)
        * score_scale
    )
    return jnp.where(allowed[None], raw_scores, -MASKED)


def block_inputs(query, key_pad, value_pad, segment, seg_pad, live_pad, first_row, block_rows):
    key_span = block_rows + WINDOW
    return (
        lax.dynamic_slice_in_dim(query, first_row, block_rows, 0),
        lax.dynamic_slice_in_dim(key_pad, first_row, key_span, 0),
        lax.dynamic_slice_in_dim(value_pad, first_row, key_span, 0),
        lax.dynamic_slice_in_dim(segment, first_row, block_rows, 0),
        lax.dynamic_slice_in_dim(seg_pad, first_row, key_span, 0),
        lax.dynamic_slice_in_dim(live_pad, first_row, key_span, 0),
    )


def attend_forward(query, key_all, value_all, segment, key_live):
    token_count, head_count, head_width = query.shape
    block_rows = min(512, token_count)
    score_scale = head_width ** (-0.5)
    key_pad = padded(key_all, 0.0)
    value_pad = padded(value_all, 0.0)
    seg_pad = padded(segment, -1)
    live_pad = padded(key_live, 0)

    def one_block(running, block_index):
        first_row = block_index * block_rows
        query_block, key_block, value_block, query_seg, key_seg, key_flag = block_inputs(
            query, key_pad, value_pad, segment, seg_pad, live_pad, first_row, block_rows
        )
        scores = block_scores(
            query_block, key_block, query_seg, key_seg, key_flag, first_row, score_scale
        )
        row_max = jnp.max(scores, axis=-1, keepdims=True)
        weights = jnp.exp(scores - row_max)
        denominator = jnp.sum(weights, axis=-1, keepdims=True)
        chances = (weights / denominator).astype(jnp.bfloat16)
        mixed = jnp.einsum("hqk,khd->qhd", chances, value_block, preferred_element_type=jnp.float32)
        return (
            running,
            (mixed.astype(jnp.bfloat16), row_max[..., 0] + jnp.log(denominator[..., 0])),
        )

    _, (mixed, logsum) = lax.scan(
        one_block, jnp.zeros((), jnp.int32), jnp.arange(token_count // block_rows, dtype=jnp.int32)
    )
    return (mixed.reshape(token_count, head_count * head_width), logsum)


def attend_backward(query, key_all, value_all, segment, key_live, logsum, mixed_grad):
    token_count, head_count, head_width = query.shape
    block_rows = min(512, token_count)
    key_span = block_rows + WINDOW
    score_scale = head_width ** (-0.5)
    key_pad = padded(key_all, 0.0)
    value_pad = padded(value_all, 0.0)
    seg_pad = padded(segment, -1)
    live_pad = padded(key_live, 0)

    def one_block(running, inputs):
        key_grad, value_grad = running
        block_index, block_logsum = inputs
        first_row = block_index * block_rows
        query_block, key_block, value_block, query_seg, key_seg, key_flag = block_inputs(
            query, key_pad, value_pad, segment, seg_pad, live_pad, first_row, block_rows
        )
        grad_block = lax.dynamic_slice_in_dim(mixed_grad, first_row, block_rows, 0)
        scores = block_scores(
            query_block, key_block, query_seg, key_seg, key_flag, first_row, score_scale
        )
        chances = jnp.exp(scores - block_logsum[..., None])
        chance_grad = jnp.einsum(
            "qhd,khd->hqk", grad_block, value_block, preferred_element_type=jnp.float32
        )
        row_dot = jnp.sum(chances * chance_grad, axis=-1, keepdims=True)
        score_grad = (chances * (chance_grad - row_dot)).astype(jnp.bfloat16)
        query_grad = (
            jnp.einsum("hqk,khd->qhd", score_grad, key_block, preferred_element_type=jnp.float32)
            * score_scale
        )
        key_part = (
            jnp.einsum("hqk,qhd->khd", score_grad, query_block, preferred_element_type=jnp.float32)
            * score_scale
        )
        value_part = jnp.einsum(
            "hqk,qhd->khd",
            chances.astype(jnp.bfloat16),
            grad_block,
            preferred_element_type=jnp.float32,
        )
        key_grad = lax.dynamic_update_slice_in_dim(
            key_grad,
            lax.dynamic_slice_in_dim(key_grad, first_row, key_span, 0) + key_part,
            first_row,
            0,
        )
        value_grad = lax.dynamic_update_slice_in_dim(
            value_grad,
            lax.dynamic_slice_in_dim(value_grad, first_row, key_span, 0) + value_part,
            first_row,
            0,
        )
        return ((key_grad, value_grad), query_grad)

    empty_grad = jnp.zeros((token_count + WINDOW, head_count, head_width), jnp.float32)
    (key_grad, value_grad), query_grad = lax.scan(
        one_block,
        (empty_grad, empty_grad),
        (jnp.arange(token_count // block_rows, dtype=jnp.int32), logsum),
    )
    flat_width = head_count * head_width
    return (
        query_grad.reshape(token_count, flat_width).astype(jnp.bfloat16),
        key_grad[WINDOW:].reshape(token_count, flat_width).astype(jnp.bfloat16),
        value_grad[WINDOW:].reshape(token_count, flat_width).astype(jnp.bfloat16),
    )


def local(
    tokens,
    cotangent,
    route,
    lengths,
    key_mask,
    norm1_gain,
    norm2_gain,
    w_query,
    w_key,
    w_value,
    w_out,
    w_gate,
    w_up,
    w_down,
):
    groups = lax.axis_size("dp")
    members = lax.axis_size("mp")
    member = lax.axis_index("mp")
    local_rows = tokens.shape[0]
    group_rows = local_rows * members
    bucket = local_rows // groups
    target = route // TOK_DEV
    chosen = (target[:, None] == jnp.arange(groups, dtype=jnp.int32)[None, :]).astype(jnp.int32)
    ranking = jnp.sum((jnp.cumsum(chosen, axis=0) - chosen) * chosen, axis=1)
    send_at = target * bucket + ranking
    arrival, arrival_grad, arrival_slot = (
        lax.all_to_all(
            jnp.zeros_like(tokens).at[send_at].set(tokens),
            "dp",
            split_axis=0,
            concat_axis=0,
            tiled=True,
        ),
        lax.all_to_all(
            jnp.zeros_like(cotangent).at[send_at].set(cotangent),
            "dp",
            split_axis=0,
            concat_axis=0,
            tiled=True,
        ),
        lax.all_to_all(
            jnp.zeros_like(route).at[send_at].set(route % local_rows),
            "dp",
            split_axis=0,
            concat_axis=0,
            tiled=True,
        ),
    )
    token_rows = jnp.zeros_like(arrival).at[arrival_slot].set(arrival)
    grad_rows = jnp.zeros_like(arrival_grad).at[arrival_slot].set(arrival_grad)
    seq_ends = jnp.cumsum(lengths[0])
    positions = jnp.arange(group_rows, dtype=jnp.int32)
    segment = jnp.sum((positions[:, None] >= seq_ends[None, :]).astype(jnp.int32), axis=1)
    input_rows = token_rows.astype(jnp.float32)
    normed_one, inverse_one = norm_rows(input_rows)
    leading_all, grad_all = (
        lax.all_gather(token_rows, "mp", axis=0, tiled=True),
        lax.all_gather(grad_rows, "mp", axis=0, tiled=True),
    )
    input_all = leading_all.astype(jnp.float32)
    normed_all, _ = norm_rows(input_all)
    hidden_one = (normed_all * norm1_gain).astype(jnp.bfloat16)
    head_count = w_query.shape[1] // HEAD_DIM
    query = jnp.dot(hidden_one, w_query, preferred_element_type=jnp.float32).astype(jnp.bfloat16)
    keys = jnp.dot(hidden_one, w_key, preferred_element_type=jnp.float32).astype(jnp.bfloat16)
    values = jnp.dot(hidden_one, w_value, preferred_element_type=jnp.float32).astype(jnp.bfloat16)
    query_heads = query.reshape(group_rows, head_count, HEAD_DIM)
    key_heads = keys.reshape(group_rows, head_count, HEAD_DIM)
    value_heads = values.reshape(group_rows, head_count, HEAD_DIM)
    mixed_flat, logsum = attend_forward(query_heads, key_heads, value_heads, segment, key_mask)
    attention_all = lax.psum(jnp.dot(mixed_flat, w_out, preferred_element_type=jnp.float32), "mp")
    middle_all = input_all + attention_all
    middle_rows = lax.dynamic_slice_in_dim(middle_all, member * local_rows, local_rows, 0)
    normed_mid, _ = norm_rows(middle_all)
    hidden_two = (normed_mid * norm2_gain).astype(jnp.bfloat16)
    normed_two, inverse_two = norm_rows(middle_rows)
    gate_value = jnp.dot(hidden_two, w_gate, preferred_element_type=jnp.float32)
    upward = jnp.dot(hidden_two, w_up, preferred_element_type=jnp.float32)
    sigmoid = jax.nn.sigmoid(gate_value)
    activated = (gate_value * sigmoid * upward).astype(jnp.bfloat16)
    out_rows = middle_rows + lax.psum_scatter(
        jnp.dot(activated, w_down, preferred_element_type=jnp.float32).astype(jnp.bfloat16),
        "mp",
        scatter_dimension=0,
        tiled=True,
    ).astype(jnp.float32)
    activated_grad = jnp.einsum("td,fd->tf", grad_all, w_down, preferred_element_type=jnp.float32)
    gate_grad = (activated_grad * upward * sigmoid * (1.0 + gate_value * (1.0 - sigmoid))).astype(
        jnp.bfloat16
    )
    upward_grad = (activated_grad * gate_value * sigmoid).astype(jnp.bfloat16)
    down_sum = jnp.einsum("tf,td->fd", activated, grad_all, preferred_element_type=jnp.float32)
    gate_sum = jnp.einsum("td,tf->df", hidden_two, gate_grad, preferred_element_type=jnp.float32)
    upward_sum = jnp.einsum(
        "td,tf->df", hidden_two, upward_grad, preferred_element_type=jnp.float32
    )
    hidden_two_grad = lax.psum_scatter(
        jnp.einsum("tf,df->td", gate_grad, w_gate, preferred_element_type=jnp.float32)
        + jnp.einsum("tf,df->td", upward_grad, w_up, preferred_element_type=jnp.float32),
        "mp",
        scatter_dimension=0,
        tiled=True,
    )
    norm_part_two, gain_two_grad = norm_back(hidden_two_grad, normed_two, inverse_two, norm2_gain)
    middle_grad = grad_rows.astype(jnp.float32) + norm_part_two
    branch_all = lax.all_gather(middle_grad.astype(jnp.bfloat16), "mp", axis=0, tiled=True)
    output_sum = jnp.einsum("tc,td->cd", mixed_flat, branch_all, preferred_element_type=jnp.float32)
    mixed_grad = jnp.einsum(
        "td,cd->tc", branch_all, w_out, preferred_element_type=jnp.float32
    ).astype(jnp.bfloat16)
    query_grad, key_grad, value_grad = attend_backward(
        query_heads,
        key_heads,
        value_heads,
        segment,
        key_mask,
        logsum,
        mixed_grad.reshape(group_rows, head_count, HEAD_DIM),
    )
    query_sum = jnp.einsum("td,tc->dc", hidden_one, query_grad, preferred_element_type=jnp.float32)
    key_sum = jnp.einsum("td,tc->dc", hidden_one, key_grad, preferred_element_type=jnp.float32)
    value_sum = jnp.einsum("td,tc->dc", hidden_one, value_grad, preferred_element_type=jnp.float32)
    hidden_one_grad = lax.psum_scatter(
        (
            jnp.einsum("tc,dc->td", query_grad, w_query, preferred_element_type=jnp.float32)
            + jnp.einsum("tc,dc->td", key_grad, w_key, preferred_element_type=jnp.float32)
            + jnp.einsum("tc,dc->td", value_grad, w_value, preferred_element_type=jnp.float32)
        ).astype(jnp.bfloat16),
        "mp",
        scatter_dimension=0,
        tiled=True,
    ).astype(jnp.float32)
    norm_part_one, gain_one_grad = norm_back(hidden_one_grad, normed_one, inverse_one, norm1_gain)
    input_grad = middle_grad + norm_part_one
    gain_one_sum, gain_two_sum = lax.psum((gain_one_grad, gain_two_grad), ("dp", "mp"))
    weight_sums = (
        lax.psum(query_sum.astype(jnp.bfloat16), "dp").astype(jnp.float32),
        lax.psum(key_sum.astype(jnp.bfloat16), "dp").astype(jnp.float32),
        lax.psum(value_sum.astype(jnp.bfloat16), "dp").astype(jnp.float32),
        lax.psum(output_sum.astype(jnp.bfloat16), "dp").astype(jnp.float32),
        lax.psum(gate_sum.astype(jnp.bfloat16), "dp").astype(jnp.float32),
        lax.psum(upward_sum.astype(jnp.bfloat16), "dp").astype(jnp.float32),
        lax.psum(down_sum.astype(jnp.bfloat16), "dp").astype(jnp.float32),
    )
    back_out, back_grad = (
        lax.all_to_all(
            out_rows.astype(jnp.bfloat16)[arrival_slot],
            "dp",
            split_axis=0,
            concat_axis=0,
            tiled=True,
        ),
        lax.all_to_all(
            input_grad.astype(jnp.bfloat16)[arrival_slot],
            "dp",
            split_axis=0,
            concat_axis=0,
            tiled=True,
        ),
    )
    return (
        back_out[send_at],
        back_grad[send_at],
        gain_one_sum,
        gain_two_sum,
        weight_sums[0],
        weight_sums[1],
        weight_sums[2],
        weight_sums[3],
        weight_sums[4],
        weight_sums[5],
        weight_sums[6],
    )


def solution(mesh):
    in_specs = (
        P(("dp", "mp"), None),
        P(("dp", "mp"), None),
        P(("dp", "mp")),
        P("dp", None),
        P("dp"),
        P(),
        P(),
        P(None, "mp"),
        P(None, "mp"),
        P(None, "mp"),
        P("mp", None),
        P(None, "mp"),
        P(None, "mp"),
        P("mp", None),
    )
    out_specs = (
        P(("dp", "mp"), None),
        P(("dp", "mp"), None),
        P(),
        P(),
        P(None, "mp"),
        P(None, "mp"),
        P(None, "mp"),
        P("mp", None),
        P(None, "mp"),
        P(None, "mp"),
        P("mp", None),
    )
    return jax.shard_map(local, mesh=mesh, in_specs=in_specs, out_specs=out_specs, check_vma=False)
```

profile of v0, /device:TPU:0, one launch (start us, length us, event | category | flops | bytes accessed | tf_op | source)
XLA Modules:
  0.0 1727.3 jit_solution(16116755077285871703)
XLA Ops:
  28.3 17.6 %all-to-all-done.1 = bf16[8,48,1792]{2,1,0:T(8,128)(2,1)S(1)} async-done(((bf16[8,48,1792]{2,1,0:T(8,128)(2,1)}), bf16[8,48,1792]{2,1,0:T(8,128)(2,1)S(1)}, u32[]{:S(2)}, u32[]{:S(2)}) %all-to-all-start.1) | async-done | bytes 1376288 | tf_op jit(solution)/shard_map/all_to_all | solution.py:185
  50.2 101.4 %all-gather.4.cloned.1.call-done = bf16[1536,1792]{1,0:T(8,128)(2,1)} async-done(((bf16[384,1792]{1,0:T(8,128)(2,1)}), bf16[1536,1792]{1,0:T(8,128)(2,1)}) %all-gather.4.cloned.1.call-update) | async-done | bytes 5505040 | tf_op jit(solution)/shard_map/all_gather | solution.py:215
  169.8 26.9 %while.30 = (s32[]{:T(128)}, bf16[3,512,4,112]{1,3,2,0:T(8,128)(2,1)}, f32[3,4,512]{2,1,0:T(4,128)S(1)}, s32[3]{0:T(128)S(1)}, bf16[1600,4,112]{0,2,1:T(8,128)(2...) while((s32[]{:T(128)}, ...), condition=%wide.region_12.13_spmd, body=%wide.region_9.12_spmd.sunk | while | flops 545521280 | bytes 17490852 | solution.py:83
  204.2 7.9 fusion.83
  216.8 23.1 %all_to_all.60 = bf16[8,48,1792]{2,1,0:T(8,128)(2,1)} all-to-all(bf16[8,48,1792]{2,1,0:T(8,128)(2,1)} %bitcast.130), channel_id=1, replica_groups=mesh['dp'=8,'mp'=4] {'dp'}, dimensions={0} | all-to-all | bytes 2752512 | tf_op jit(solution)/shard_map/all_to_all | solution.py:192
  244.6 341.4 %all-reduce.9.cloned.1.call-done = f32[1536,1792]{1,0:T(8,128)} async-done(((f32[1536,1792]{1,0:T(8,128)}), f32[1536,1792]{1,0:T(8,128)}) %all-reduce.9.cloned.1.call-update) | async-done | bytes 11010064 | tf_op jit(solution)/shard_map/psum | solution.py:229
  586.1 11.9 multiply_reduce_fusion.1
  603.1 11.5 fusion.84
  614.6 7.7 fusion.85
  622.3 66.7 %all-gather.6.cloned.1.call-done = bf16[1536,1792]{1,0:T(8,128)(2,1)} async-done(((bf16[384,1792]{1,0:T(8,128)(2,1)}), bf16[1536,1792]{1,0:T(8,128)(2,1)}) %all-gather.6.cloned.1.call-update) | async-done | bytes 5505040 | tf_op jit(solution)/shard_map/all_gather | solution.py:216
  689.0 16.0 multiply_convert_fusion.2
  705.1 8.5 fusion.86
  713.6 11.2 convolution_add_fusion
  726.9 182.8 %reduce-scatter.6.cloned.1.call-done = f32[384,1792]{1,0:T(8,128)} async-done(((f32[1536,1792]{1,0:T(8,128)}), f32[384,1792]{1,0:T(8,128)}) %reduce-scatter.6.cloned.1.call-update) | async-done | bytes 2752528 | tf_op jit(solution)/shard_map/reduce_scatter | solution.py:255
  918.2 103.5 %all-gather.8.cloned.1.call-done = bf16[1536,1792]{1,0:T(8,128)(2,1)} async-done(((bf16[384,1792]{1,0:T(8,128)(2,1)}), bf16[1536,1792]{1,0:T(8,128)(2,1)}) %all-gather.8.cloned.1.call-update) | async-done | bytes 5505040 | tf_op jit(solution)/shard_map/all_gather | solution.py:264
  1032.5 127.1 %while.31 = (s32[]{:T(128)}, f32[1600,4,112]{0,2,1:T(8,128)}, f32[1600,4,112]{0,2,1:T(8,128)}, bf16[3,512,4,112]{1,3,2,0:T(8,128)(2,1)}, s32[3]{0:T(128)S(1)}, /...) while((s32[]{:T(128)}, f32[1600,4,112]{0,2,1:T(8,128)}, ...), condition=%wide.region_24.25_spmd, body=%wide.region_22.24_spmd.sunk | while | flops 1342557824 | bytes 73204776 | solution.py:145
  1049.1 9.8 dynamic_update_slice.44
  1063.3 9.8 dynamic_update_slice.45
  1092.8 9.7 dynamic_update_slice.44
  1106.8 9.7 dynamic_update_slice.45
  1136.0 8.1 dynamic_update_slice.44
  1148.5 8.1 dynamic_update_slice.45
  1180.5 7.5 add_convert_fusion
  1188.0 10.1 convolution_convert_fusion
  1198.2 10.7 convolution_convert_fusion.1
  1209.0 10.3 convolution_convert_fusion.3
  1219.3 7.4 convolution_convert_fusion.2
  1243.9 40.6 %reduce-scatter.8.cloned.1.call-done = bf16[384,1792]{1,0:T(8,128)(2,1)} async-done(((bf16[1536,1792]{1,0:T(8,128)(2,1)}), bf16[384,1792]{1,0:T(8,128)(2,1)}) %reduce-scatter.8.cloned.1.call-update) | async-done | bytes 1376272 | tf_op jit(solution)/shard_map/reduce_scatter | solution.py:281
  1286.8 99.1 %reduce-scatter.4.cloned.1.call-done = bf16[384,1792]{1,0:T(8,128)(2,1)} async-done(((bf16[1536,1792]{1,0:T(8,128)(2,1)}), bf16[384,1792]{1,0:T(8,128)(2,1)}) %reduce-scatter.4.cloned.1.call-update) | async-done | bytes 1376272 | tf_op jit(solution)/shard_map/reduce_scatter | solution.py:239
  1400.7 30.8 %all-to-all-done.2 = bf16[8,48,1792]{2,1,0:T(8,128)(2,1)S(1)} async-done(((bf16[8,48,1792]{2,1,0:T(8,128)(2,1)}), bf16[8,48,1792]{2,1,0:T(8,128)(2,1)S(1)}, u32[]{:S(2)}, u32[]{:S(2)}) %all-to-all-start.2) | async-done | bytes 1376288 | tf_op jit(solution)/shard_map/all_to_all | solution.py:304
  1436.1 213.3 %all-reduce.11.cloned.1.call-done = (bf16[1792,448]{0,1:T(8,128)(2,1)}, bf16[1792,448]{0,1:T(8,128)(2,1)}, bf16[1792,448]{0,1:T(8,128)(2,1)}, bf16[448,1792]{1,0...) async-done(((bf16[1792,448]{0,1:T(8,128)(2,1)}, bf16[1792,448]{0,1:T(8,128)(2,1)}, bf16[1792,448]{0,1:T(8,128)(2,1)}, ...) | async-done | bytes 17432592 | tf_op jit(solution)/shard_map/psum | solution.py:295
  1671.4 39.4 %all-reduce.4 = (f32[1792]{0:T(1024)}, f32[1792]{0:T(1024)}) all-reduce(f32[1792]{0:T(1024)S(1)} %get-tuple-element.307, f32[1792]{0:T(1024)S(1)} %copy-done.27), channel_id=1, replica_groups=mesh['dp'=8,'mp'=4] {'dp','mp'}, use_global_device_ids=true, to_apply=%region_28.29 | all-reduce | flops 3584 | bytes 28672 | tf_op jit(solution)/shard_map/psum | solution.py:293
  (297 shorter events, 272.0 us)
Async XLA Ops:
  7.2 197.1 %copy-start = (bf16[448,1792]{1,0:T(8,128)(2,1)S(1)}, bf16[448,1792]{1,0:T(8,128)(2,1)}, u32[]{:S(2)}) copy-start(bf16[448,1792]{1,0:T(8,128)(2,1)} %param.28) | copy-start | bytes 4816900
  9.3 203.0 %copy-start.30 = (s32[384]{0:T(512)}, s32[384]{0:T(512)S(1)}, u32[]{:S(2)}) copy-start(s32[384]{0:T(512)S(1)} %compare_select_fusion.1) | copy-start | bytes 4612
  12.9 9.8 all-to-all-start
  22.6 27.1 %copy-start.41 = (s32[1,3]{1,0:T(1,128)S(1)}, s32[1,3]{1,0:T(1,128)}, u32[]{:S(2)}) copy-start(s32[1,3]{1,0:T(1,128)} %param.21) | copy-start | bytes 40
  22.6 27.3 %copy-start.34 = (s32[1536]{0:T(1024)S(1)}, s32[1536]{0:T(1024)}, u32[]{:S(2)}) copy-start(s32[1536]{0:T(1024)} %param.22) | copy-start | bytes 18436
  22.6 23.2 %all-to-all-start.1 = ((bf16[8,48,1792]{2,1,0:T(8,128)(2,1)}), bf16[8,48,1792]{2,1,0:T(8,128)(2,1)S(1)}, u32[]{:S(2)}, u32[]{:S(2)}) async-start(bf16[8,48,1792]{2,1,0:T(8,128)(2,1)} %bitcast.14), calls=%async_computation.1 | async-start | bytes 2752512 | tf_op jit(solution)/shard_map/all_to_all | solution.py:185
  26.9 124.7 %all-gather.4.cloned.1.call-start = ((), (), s32[]{:S(2)}) async-start(), calls=%async_computation.8 | async-start | bytes 6881280 | tf_op jit(solution)/shard_map/all_gather | solution.py:215
  28.3 211.7 %copy-start.32 = (s32[384]{0:T(512)}, s32[384]{0:T(512)S(1)}, u32[]{:S(2)}) copy-start(s32[384]{0:T(512)S(1)} %fusion.79) | copy-start | bytes 4612
  49.7 536.4 %all-reduce.9.cloned.1.call-start = ((), (), s32[]{:S(2)}) async-start(), calls=%async_computation.9 | async-start | bytes 22020096 | tf_op jit(solution)/shard_map/psum | solution.py:229
  50.2 105.3 %copy-start.23 = (f32[1792]{0:T(1024)S(1)}, f32[1792]{0:T(1024)}, u32[]{:S(2)}) copy-start(f32[1792]{0:T(1024)} %param.23) | copy-start | bytes 21508
  212.2 476.8 %all-gather.6.cloned.1.call-start = ((), (), s32[]{:S(2)}) async-start(), calls=%async_computation.11 | async-start | bytes 6881280 | tf_op jit(solution)/shard_map/all_gather | solution.py:216
  244.6 353.4 %copy-start.21 = (f32[1792]{0:T(1024)S(1)}, f32[1792]{0:T(1024)}, u32[]{:S(2)}) copy-start(f32[1792]{0:T(1024)} %param.24) | copy-start | bytes 21508
  244.6 665.2 %reduce-scatter.6.cloned.1.call-start = ((), (), s32[]{:S(2)}) async-start(), calls=%async_computation.12 | async-start | bytes 13762560 | tf_op jit(solution)/shard_map/reduce_scatter | solution.py:255
  603.1 11.6 copy-start.7
  603.1 11.6 copy-start.36
  689.0 16.0 copy-start.35
  724.8 297.0 %all-gather.8.cloned.1.call-start = ((), (), s32[]{:S(2)}) async-start(), calls=%async_computation.13 | async-start | bytes 6881280 | tf_op jit(solution)/shard_map/all_gather | solution.py:264
  726.9 186.9 %copy-start.25 = (f32[384]{0:T(512)}, f32[384]{0:T(512)S(1)}, u32[]{:S(2)}) copy-start(f32[384]{0:T(512)S(1)} %add_rsqrt_fusion.3) | copy-start | bytes 4612
  918.2 366.3 %reduce-scatter.8.cloned.1.call-start = ((), (), s32[]{:S(2)}) async-start(), calls=%async_computation.14 | async-start | bytes 6881280 | tf_op jit(solution)/shard_map/reduce_scatter | solution.py:281
  1188.0 197.9 %reduce-scatter.4.cloned.1.call-start = ((), (), s32[]{:S(2)}) async-start(), calls=%async_computation.10 | async-start | bytes 6881280 | tf_op jit(solution)/shard_map/reduce_scatter | solution.py:239
  1198.1 451.2 %all-reduce.11.cloned.1.call-start = ((), (), s32[]{:S(2)}) async-start(), calls=%async_computation.15 | async-start | bytes 34865152 | tf_op jit(solution)/shard_map/psum | solution.py:295
  1198.2 10.8 copy-start.45
  1198.2 21.1 %slice-start.2 = ((s8[5505024]{0:T(1024)(128)(4,1)}), s8[4194304]{0:T(1024)(128)(4,1)S(1)}, s32[]{:S(2)}) async-start(s8[5505024]{0:T(1024)(128)(4,1)} %bitcast.124), calls=%async_computation.18 | async-start | bytes 8388608
  1208.9 17.8 %slice-start.4 = ((s8[5505024]{0:T(1024)(128)(4,1)}), s8[4194304]{0:T(1024)(128)(4,1)S(1)}, s32[]{:S(2)}) async-start(s8[5505024]{0:T(1024)(128)(4,1)} %bitcast.128), calls=%async_computation.20 | async-start | bytes 8388608
  1226.7 11.6 slice-start.6
  1242.2 42.3 %copy-start.24 = (f32[1792]{0:T(1024)S(1)}, f32[1792]{0:T(1024)}, u32[]{:S(2)}) copy-start(f32[1792]{0:T(1024)} %param.23) | copy-start | bytes 21508
  1242.8 143.1 %copy-start.22 = (f32[1792]{0:T(1024)S(1)}, f32[1792]{0:T(1024)}, u32[]{:S(2)}) copy-start(f32[1792]{0:T(1024)} %param.24) | copy-start | bytes 21508
  1242.8 143.1 %copy-start.26 = (f32[384]{0:T(512)S(1)}, f32[384]{0:T(512)}, u32[]{:S(2)}) copy-start(f32[384]{0:T(512)} %copy-done.25) | copy-start | bytes 4612
  1242.8 143.1 %copy-start.29 = (f32[384]{0:T(512)S(1)}, f32[384]{0:T(512)}, u32[]{:S(2)}) copy-start(f32[384]{0:T(512)} %copy-done.28) | copy-start | bytes 4612
  1394.1 37.5 %all-to-all-start.2 = ((bf16[8,48,1792]{2,1,0:T(8,128)(2,1)}), bf16[8,48,1792]{2,1,0:T(8,128)(2,1)S(1)}, u32[]{:S(2)}, u32[]{:S(2)}) async-start(bf16[8,48,1792]{2,1,0:T(8,128)(2,1)} %bitcast.127), calls=%async_computation.3 | async-start | bytes 2752512 | tf_op jit(solution)/shard_map/all_to_all | solution.py:304
  1400.7 35.4 %copy-start.31 = (s32[384]{0:T(512)S(1)}, s32[384]{0:T(512)}, u32[]{:S(2)}) copy-start(s32[384]{0:T(512)} %copy-done.30) | copy-start | bytes 4612
  1431.5 282.3 %all-to-all-start.4 = ((bf16[8,48,1792]{2,1,0:T(8,128)(2,1)}), bf16[8,48,1792]{2,1,0:T(8,128)(2,1)}, u32[]{:S(2)}, u32[]{:S(2)}) async-start(bf16[8,48,1792]{2,1,0:T(8,128)(2,1)} %bitcast.126), calls=%async_computation.7 | async-start | bytes 2752512 | tf_op jit(solution)/shard_map/all_to_all | solution.py:311
  (40 other events, 178.6 us)
Sparse Core Ops, SparseCore 0:
  49.8 101.7 all-gather.3
  212.3 373.7 all-reduce.8
  587.6 101.3 all-gather.5
  724.9 184.7 reduce-scatter.5
  918.3 103.4 all-gather.7
  1188.1 96.3 reduce-scatter.7
  1287.3 98.5 reduce-scatter.3
  1391.7 257.6 all-reduce.10
where the time goes:
time: 1740 us; the launch traced here: 1730 us
  waiting for transfers between devices  1200 us (69%)
  matrix products  226 us (13%)
  local copies, waits for them, and re-layouts  130 us (7%)
  other arithmetic  74.3 us (4%)
  blocking collectives  62.6 us (4%)
  starting transfers between devices  18 us (1%)
    psum x1, waiting for transfers between devices, local(): lax.psum(jnp.dot(mixed_flat, w_out, preferred_element_type=jnp.float32),...  341 us
    psum x1, waiting for transfers between devices, local(): lax.psum(query_sum.astype(jnp.bfloat16), 'dp').astype(jnp.float32)  213 us
    reduce_scatter x1, waiting for transfers between devices, local(): lax.psum_scatter(jnp.einsum('tf,df->td', gate_grad, w_gate, preferred_ele...  183 us
    all_gather x1, waiting for transfers between devices, local(): lax.all_gather(middle_grad.astype(jnp.bfloat16), 'mp', axis=0, tiled=True)  104 us
    all_gather x1, waiting for transfers between devices, local(): lax.all_gather(token_rows, 'mp', axis=0, tiled=True)  101 us
    reduce_scatter x1, waiting for transfers between devices, local(): lax.psum_scatter(jnp.dot(activated, w_down, preferred_element_type=jnp.fl...  99.1 us
    all_gather x1, waiting for transfers between devices, local(): lax.all_gather(grad_rows, 'mp', axis=0, tiled=True)  66.7 us
    reduce_scatter x1, waiting for transfers between devices, local(): lax.psum_scatter((jnp.einsum('tc,dc->td', query_grad, w_query, preferred_...  40.6 us
  transfers between devices with their start and end apart: 12, of which 10 were waited for; matrix products, arithmetic and copies ran while one was open for 8% of the time, Pallas kernels for 0%

commit v1 on v0

--- a/solution.py
+++ b/solution.py
@@ -1,6 +1,10 @@
+import functools
+
 import jax
 import jax.numpy as jnp
 from jax import lax
+from jax.experimental import pallas as pl
+from jax.experimental.pallas import tpu as pltpu
 from jax.sharding import PartitionSpec as P
 
 HEAD_DIM = 112
@@ -331,6 +335,930 @@
     )
 
 
+MESH = pl.DeviceIdType.MESH
+LANES = 128
+F32 = jnp.float32
+BF16 = jnp.bfloat16
+VMEM_LIMIT = 56 * 1024 * 1024
+
+
+def plane():
+    me = lax.axis_index("dp")
+    side = me + 1 - 2 * lax.rem(me, 2)
+    over_x = me + 2 - 4 * lax.rem(lax.div(me, 2), 2)
+    over_y = me + 4 - 8 * lax.rem(lax.div(me, 4), 2)
+    corner = over_x + 4 - 8 * lax.rem(lax.div(over_x, 4), 2)
+    return (me, side, over_x, over_y, corner)
+
+
+def to_dp(source, target, send_sem, recv_sem, index):
+    return pltpu.make_async_remote_copy(
+        src_ref=source,
+        dst_ref=target,
+        send_sem=send_sem,
+        recv_sem=recv_sem,
+        device_id={"dp": index},
+        device_id_type=MESH,
+    )
+
+
+def to_mp(source, target, send_sem, recv_sem, index):
+    return pltpu.make_async_remote_copy(
+        src_ref=source,
+        dst_ref=target,
+        send_sem=send_sem,
+        recv_sem=recv_sem,
+        device_id={"mp": index},
+        device_id_type=MESH,
+    )
+
+
+def greet_plane():
+    _, side, over_x, over_y, _ = plane()
+    barrier = pltpu.get_barrier_semaphore()
+    for other in (side, over_x, over_y):
+        pl.semaphore_signal(barrier, inc=1, device_id={"dp": other}, device_id_type=MESH)
+    return barrier
+
+
+class Gather:
+    COUNT = 13
+
+    def __init__(self, own, out, send, recv, local):
+        me, side, over_x, over_y, corner = plane()
+        half = own.shape[0] // 2
+        low, high = pl.ds(0, half), pl.ds(half, half)
+
+        def hop(number, source, target, index):
+            return to_dp(source, target, send.at[number], recv.at[number], index)
+
+        self.keep = pltpu.make_async_copy(own, out.at[me], local)
+        self.first = [
+            hop(0, own.at[low], out.at[me, low], over_x),
+            hop(1, own.at[high], out.at[me, high], over_y),
+            hop(2, own.at[high], out.at[me, high], over_x),
+            hop(3, own.at[low], out.at[me, low], over_y),
+            hop(4, own, out.at[me], side),
+        ]
+        self.onward = [
+            (0, hop(5, out.at[over_x, low], out.at[over_x, low], over_y)),
+            (0, hop(6, out.at[over_x, low], out.at[over_x, low], side)),
+            (1, hop(7, out.at[over_y, high], out.at[over_y, high], over_x)),
+            (1, hop(8, out.at[over_y, high], out.at[over_y, high], side)),
+            (2, hop(9, out.at[over_x, high], out.at[over_x, high], side)),
+            (3, hop(10, out.at[over_y, low], out.at[over_y, low], side)),
+        ]
+        self.last = [
+            (5, hop(11, out.at[corner, low], out.at[corner, low], side)),
+            (7, hop(12, out.at[corner, high], out.at[corner, high], side)),
+        ]
+        self.by_number = dict(enumerate(self.first))
+        for number, copy in zip((5, 6, 7, 8, 9, 10), [c for _, c in self.onward]):
+            self.by_number[number] = copy
+        for number, copy in zip((11, 12), [c for _, c in self.last]):
+            self.by_number[number] = copy
+
+    def start(self):
+        for copy in self.first:
+            copy.start()
+        self.keep.start()
+
+    def pass_on(self):
+        seen = set()
+        for after, copy in self.onward:
+            if after not in seen:
+                self.by_number[after].wait_recv()
+                seen.add(after)
+            copy.start()
+
+    def finish(self):
+        for after, copy in self.last:
+            self.by_number[after].wait_recv()
+            copy.start()
+        for number in (4, 6, 8, 9, 10, 11, 12):
+            self.by_number[number].wait_recv()
+        for number in range(self.COUNT):
+            self.by_number[number].wait_send()
+        self.keep.wait()
+
+
+def first_kernel(
+    hidden, cotangent, qkv_share, out_share,
+    hidden_all, cotangent_all, w_qkv, w_out,
+    send_a, recv_a, send_b, recv_b, send_w, recv_w, local,
+):
+    me, _, _, _, _ = plane()
+    z = lax.axis_index("mp")
+    core = lax.rem(me, 2)
+    barrier = greet_plane()
+    for step in (1, 2, 3):
+        pl.semaphore_signal(
+            barrier, inc=1, device_id={"mp": lax.rem(z + step, 4)}, device_id_type=MESH
+        )
+    pl.semaphore_wait(barrier, 6)
+    first = Gather(hidden, hidden_all, send_a, recv_a, local.at[0])
+    second = Gather(cotangent, cotangent_all, send_b, recv_b, local.at[1])
+    first.start()
+    place = lax.rem(z, 2)
+    owner = lax.div(z, 2) == core
+
+    def pieces(slot):
+        found = []
+        for part in range(3):
+            columns = pl.ds(pl.multiple_of((2 * part + slot) * LANES, LANES), LANES)
+            found.append((qkv_share.at[part], w_qkv.at[:, columns]))
+        rows = pl.ds(pl.multiple_of(slot * LANES, LANES), LANES)
+        found.append((out_share, w_out.at[rows]))
+        return found
+
+    @pl.when(owner)
+    def _():
+        for number, (source, target) in enumerate(pieces(place)):
+            pltpu.make_async_copy(source, target, local.at[2 + number]).start()
+        for step in (1, 2, 3):
+            other = lax.rem(z + step, 4)
+            for number, (source, target) in enumerate(pieces(place)):
+                index = (step - 1) * 4 + number
+                to_mp(source, target, send_w.at[index], recv_w.at[index], other).start()
+
+    second.start()
+    first.pass_on()
+    second.pass_on()
+    first.finish()
+    second.finish()
+
+    for step in (1, 2, 3):
+        source_z = lax.rem(z + 4 - step, 4)
+
+        @pl.when(lax.div(source_z, 2) == core)
+        def _():
+            for number, (source, target) in enumerate(pieces(lax.rem(source_z, 2))):
+                index = (step - 1) * 4 + number
+                to_mp(source, target, send_w.at[index], recv_w.at[index], source_z).wait_recv()
+
+    @pl.when(owner)
+    def _():
+        for step in (1, 2, 3):
+            other = lax.rem(z + step, 4)
+            for number, (source, target) in enumerate(pieces(place)):
+                index = (step - 1) * 4 + number
+                to_mp(source, target, send_w.at[index], recv_w.at[index], other).wait_send()
+        for number, (source, target) in enumerate(pieces(place)):
+            pltpu.make_async_copy(source, target, local.at[2 + number]).wait()
+
+
+def anywhere():
+    return pl.BlockSpec(memory_space=pl.ANY)
+
+
+def on_chip():
+    return pl.BlockSpec(memory_space=pltpu.VMEM)
+
+
+def in_scalar():
+    return pl.BlockSpec(memory_space=pltpu.SMEM)
+
+
+def remote_params(number, limit=VMEM_LIMIT):
+    return pltpu.CompilerParams(
+        collective_id=number, has_side_effects=True, vmem_limit_bytes=limit
+    )
+
+
+def gather_first(hidden, cotangent, qkv_share, out_share):
+    rows, width = hidden.shape
+    groups = lax.axis_size("dp")
+    dma = pltpu.SemaphoreType.DMA
+    return pl.pallas_call(
+        first_kernel,
+        out_shape=(
+            jax.ShapeDtypeStruct((groups, rows, width), BF16),
+            jax.ShapeDtypeStruct((groups, rows, width), BF16),
+            jax.ShapeDtypeStruct((width, 6 * LANES), BF16),
+            jax.ShapeDtypeStruct((2 * LANES, width), BF16),
+        ),
+        in_specs=[anywhere()] * 4,
+        out_specs=(anywhere(),) * 4,
+        scratch_shapes=[
+            dma((13,)), dma((13,)), dma((13,)), dma((13,)), dma((12,)), dma((12,)), dma((6,)),
+        ],
+        compiler_params=remote_params(1),
+        cost_estimate=pl.CostEstimate(flops=0, bytes_accessed=300_000_000, transcendentals=0),
+        name="gather_first",
+    )(hidden, cotangent, qkv_share, out_share)
+
+
+def one_hot(slots, k, size):
+    row = slots[pl.ds(k, 1), :]
+    place = lax.broadcasted_iota(jnp.int32, (size, size), 0)
+    return (place == row).astype(BF16)
+
+
+def block_mask(lengths, flags, k, block, z, rows):
+    position = rows * z + block * 128 + lax.broadcasted_iota(jnp.int32, (128, 1), 0)
+    first_end = lengths[k, 0]
+    second_end = first_end + lengths[k, 1]
+    begin = jnp.where(position >= first_end, first_end, 0)
+    begin = jnp.where(position >= second_end, second_end, begin)
+    column = lax.broadcasted_iota(jnp.int32, (128, 192), 1)
+    distance = 64 + lax.broadcasted_iota(jnp.int32, (128, 192), 0) - column
+    key_position = rows * z + block * 128 - 64 + column
+    live = flags[pl.ds(k, 1), block * 128 : block * 128 + 192]
+    allowed = (distance >= 0) & (distance < WINDOW) & (key_position >= begin)
+    return allowed & ((live == 1) | (distance == 0))
+
+
+NT = (((1,), (1,)), ((), ()))
+TN = (((0,), (0,)), ((), ()))
+
+
+def forward_kernel(
+    lengths, qkv, slots, flags, mixed, kept, send, recv, *, scale, groups, rows
+):
+    z = lax.axis_index("mp")
+    members = lax.axis_size("mp")
+    barrier = pltpu.get_barrier_semaphore()
+
+    @pl.when(z > 0)
+    def _():
+        pl.semaphore_signal(barrier, inc=1, device_id={"mp": z - 1}, device_id_type=MESH)
+
+    @pl.when(z < members - 1)
+    def _():
+        pl.semaphore_wait(barrier, 1)
+
+    def halo(k, other):
+        return to_mp(
+            kept.at[k, pl.ds(rows, 64), pl.ds(256, 512)],
+            kept.at[k, pl.ds(0, 64), pl.ds(256, 512)],
+            send.at[k],
+            recv.at[k],
+            other,
+        )
+
+    def order(k, carry):
+        hot = one_hot(slots, k, rows)
+        given = qkv[:, pl.ds(k, 1)].reshape(rows, 768)
+        kept[k, pl.ds(64, rows), :] = jnp.dot(hot, given, preferred_element_type=F32).astype(BF16)
+        kept[k, pl.ds(0, 64), pl.ds(0, 256)] = jnp.zeros((64, 256), BF16)
+
+        @pl.when(z < members - 1)
+        def _():
+            halo(k, z + 1).start()
+
+        @pl.when(z == 0)
+        def _():
+            kept[k, pl.ds(0, 64), pl.ds(256, 512)] = jnp.zeros((64, 512), BF16)
+
+        return carry
+
+    lax.fori_loop(0, groups, order, 0)
+
+    def attend(k, carry):
+        @pl.when(z > 0)
+        def _():
+            halo(k, z).wait_recv()
+
+        hot = one_hot(slots, k, rows)
+        found = []
+        for block in range(rows // 128):
+            allowed = block_mask(lengths, flags, k, block, z, rows)
+            heads = []
+            for head in range(2):
+                query = kept[k, pl.ds(64 + block * 128, 128), pl.ds(head * 128, 128)]
+                keys = kept[k, pl.ds(block * 128, 192), pl.ds(256 + head * 128, 128)]
+                values = kept[k, pl.ds(block * 128, 192), pl.ds(512 + head * 128, 128)]
+                scores = lax.dot_general(query, keys, NT, preferred_element_type=F32) * scale
+                scores = jnp.where(allowed, scores, -MASKED)
+                weights = jnp.exp(scores - jnp.max(scores, axis=-1, keepdims=True))
+                total = jnp.sum(weights, axis=-1, keepdims=True)
+                chances = (weights / total).astype(BF16)
+                heads.append(jnp.dot(chances, values, preferred_element_type=F32).astype(BF16))
+            found.append(jnp.concatenate(heads, axis=1))
+        ordered = jnp.concatenate(found, axis=0)
+        back = lax.dot_general(hot, ordered, TN, preferred_element_type=F32).astype(BF16)
+        mixed[:, pl.ds(k, 1)] = back.reshape(groups, 1, rows // groups, 256)
+        return carry
+
+    lax.fori_loop(0, groups, attend, 0)
+
+    @pl.when(z < members - 1)
+    def _():
+        def done(k, carry):
+            halo(k, z + 1).wait_send()
+            return carry
+
+        lax.fori_loop(0, groups, done, 0)
+
+
+def attend_ahead(lengths, qkv, slots, flags, scale):
+    groups = qkv.shape[0]
+    rows = slots.shape[1]
+    dma = pltpu.SemaphoreType.DMA
+    return pl.pallas_call(
+        functools.partial(forward_kernel, scale=scale, groups=groups, rows=rows),
+        out_shape=(
+            jax.ShapeDtypeStruct((groups, groups, rows // groups, 256), BF16),
+            jax.ShapeDtypeStruct((groups, rows + 64, 768), BF16),
+        ),
+        in_specs=[in_scalar(), on_chip(), on_chip(), on_chip()],
+        out_specs=(on_chip(), on_chip()),
+        scratch_shapes=[dma((groups,)), dma((groups,))],
+        compiler_params=remote_params(2),
+        cost_estimate=pl.CostEstimate(flops=0, bytes_accessed=70_000_000, transcendentals=0),
+        name="attend_ahead",
+    )(lengths, qkv, slots, flags)
+
+
+def backward_kernel(
+    lengths, kept, mixed_grad, slots, flags, out,
+    totals, query_part, key_value, leaving, arriving, send, recv,
+    *, scale, groups, rows,
+):
+    z = lax.axis_index("mp")
+    members = lax.axis_size("mp")
+    barrier = pltpu.get_barrier_semaphore()
+
+    @pl.when(z < members - 1)
+    def _():
+        pl.semaphore_signal(barrier, inc=1, device_id={"mp": z + 1}, device_id_type=MESH)
+
+    @pl.when(z > 0)
+    def _():
+        pl.semaphore_wait(barrier, 1)
+
+    def halo(k, other):
+        return to_mp(leaving.at[k], arriving.at[k], send.at[k], recv.at[k], other)
+
+    def attend(k, carry):
+        hot = one_hot(slots, k, rows)
+        given = mixed_grad[:, pl.ds(k, 1)].reshape(rows, 256)
+        grad_ordered = jnp.dot(hot, given, preferred_element_type=F32).astype(BF16)
+        totals[...] = jnp.zeros_like(totals)
+        for block in range(rows // 128):
+            allowed = block_mask(lengths, flags, k, block, z, rows)
+            for head in range(2):
+                query = kept[k, pl.ds(64 + block * 128, 128), pl.ds(head * 128, 128)]
+                keys = kept[k, pl.ds(block * 128, 192), pl.ds(256 + head * 128, 128)]
+                values = kept[k, pl.ds(block * 128, 192), pl.ds(512 + head * 128, 128)]
+                grad = grad_ordered[block * 128 : block * 128 + 128, head * 128 : head * 128 + 128]
+                scores = lax.dot_general(query, keys, NT, preferred_element_type=F32) * scale
+                scores = jnp.where(allowed, scores, -MASKED)
+                weights = jnp.exp(scores - jnp.max(scores, axis=-1, keepdims=True))
+                again = weights / jnp.sum(weights, axis=-1, keepdims=True)
+                chance_grad = lax.dot_general(grad, values, NT, preferred_element_type=F32)
+                row_dot = jnp.sum(again * chance_grad, axis=-1, keepdims=True)
+                score_grad = (again * (chance_grad - row_dot)).astype(BF16)
+                query_part[k, pl.ds(block * 128, 128), pl.ds(head * 128, 128)] = (
+                    jnp.dot(score_grad, keys, preferred_element_type=F32) * scale
+                ).astype(BF16)
+                totals[pl.ds(block * 128, 192), pl.ds(head * 128, 128)] += (
+                    lax.dot_general(score_grad, query, TN, preferred_element_type=F32) * scale
+                )
+                totals[pl.ds(block * 128, 192), pl.ds(256 + head * 128, 128)] += lax.dot_general(
+                    again.astype(BF16), grad, TN, preferred_element_type=F32
+                )
+        key_value[k] = totals[pl.ds(64, rows), :]
+
+        @pl.when(z > 0)
+        def _():
+            leaving[k] = totals[pl.ds(0, 64), :].astype(BF16)
+            halo(k, z - 1).start()
+
+        return carry
+
+    lax.fori_loop(0, groups, attend, 0)
+
+    def restore(k, carry):
+        @pl.when(z < members - 1)
+        def _():
+            halo(k, z).wait_recv()
+            key_value[k, pl.ds(rows - 64, 64), :] += arriving[k].astype(F32)
+
+        hot = one_hot(slots, k, rows)
+        ordered = jnp.concatenate([query_part[k], key_value[k].astype(BF16)], axis=1)
+        back = lax.dot_general(hot, ordered, TN, preferred_element_type=F32).astype(BF16)
+        out[:, pl.ds(k, 1)] = back.reshape(groups, 1, rows // groups, 768)
+        return carry
+
+    lax.fori_loop(0, groups, restore, 0)
+
+    @pl.when(z > 0)
+    def _():
+        def done(k, carry):
+            halo(k, z - 1).wait_send()
+            return carry
+
+        lax.fori_loop(0, groups, done, 0)
+
+
+def attend_back(lengths, kept, mixed_grad, slots, flags, scale):
+    groups = kept.shape[0]
+    rows = slots.shape[1]
+    dma = pltpu.SemaphoreType.DMA
+    return pl.pallas_call(
+        functools.partial(backward_kernel, scale=scale, groups=groups, rows=rows),
+        out_shape=jax.ShapeDtypeStruct((groups, groups, rows // groups, 768), BF16),
+        in_specs=[in_scalar()] + [on_chip()] * 4,
+        out_specs=on_chip(),
+        scratch_shapes=[
+            pltpu.VMEM((rows + 64, 512), F32),
+            pltpu.VMEM((groups, rows, 256), BF16),
+            pltpu.VMEM((groups, rows, 512), F32),
+            pltpu.VMEM((groups, 64, 512), BF16),
+            pltpu.VMEM((groups, 64, 512), BF16),
+            dma((groups,)),
+            dma((groups,)),
+        ],
+        compiler_params=remote_params(3),
+        cost_estimate=pl.CostEstimate(flops=0, bytes_accessed=120_000_000, transcendentals=0),
+        name="attend_back",
+    )(lengths, kept, mixed_grad, slots, flags)
+
+
+def feed_kernel(hidden, cotangent, w_both, w_down, both_grad, activated, *, members):
+    rows = hidden[...]
+    raw = jnp.dot(rows, w_both[...], preferred_element_type=F32)
+    grad = lax.dot_general(cotangent[...], w_down[...], NT, preferred_element_type=F32)
+    for part in range(members):
+        gate = raw[:, part * 256 : part * 256 + 128]
+        upward = raw[:, part * 256 + 128 : part * 256 + 256]
+        active_grad = grad[:, part * 128 : part * 128 + 128]
+        sigmoid = jax.nn.sigmoid(gate)
+        activated[:, part * 128 : part * 128 + 128] = (gate * sigmoid * upward).astype(BF16)
+        both_grad[:, part * 256 : part * 256 + 128] = (
+            active_grad * upward * sigmoid * (1.0 + gate * (1.0 - sigmoid))
+        ).astype(BF16)
+        both_grad[:, part * 256 + 128 : part * 256 + 256] = (
+            active_grad * gate * sigmoid
+        ).astype(BF16)
+
+
+def feed(hidden, cotangent, w_both, w_down):
+    count, width = hidden.shape
+    wide = w_both.shape[1]
+    units = w_down.shape[0]
+    tile = 256
+    return pl.pallas_call(
+        functools.partial(feed_kernel, members=wide // 256),
+        grid=(count // tile,),
+        out_shape=(
+            jax.ShapeDtypeStruct((count, wide), BF16),
+            jax.ShapeDtypeStruct((count, units), BF16),
+        ),
+        in_specs=[
+            pl.BlockSpec((tile, width), lambda i: (i, 0)),
+            pl.BlockSpec((tile, width), lambda i: (i, 0)),
+            pl.BlockSpec((width, wide), lambda i: (0, 0)),
+            pl.BlockSpec((units, width), lambda i: (0, 0)),
+        ],
+        out_specs=(
+            pl.BlockSpec((tile, wide), lambda i: (i, 0)),
+            pl.BlockSpec((tile, units), lambda i: (i, 0)),
+        ),
+        compiler_params=pltpu.CompilerParams(vmem_limit_bytes=VMEM_LIMIT),
+        cost_estimate=pl.CostEstimate(
+            flops=2 * count * width * (wide + units), bytes_accessed=50_000_000, transcendentals=0
+        ),
+        name="feed",
+    )(hidden, cotangent, w_both, w_down)
+
+
+CHUNK = 32
+
+
+def each_chunk(rows, body):
+    def step(i, carry):
+        body(pl.ds(pl.multiple_of(i * CHUNK, CHUNK), CHUNK))
+        return carry
+
+    lax.fori_loop(0, rows // CHUNK, step, 0)
+
+
+class Reduce:
+    COUNT = 10
+
+    def __init__(self, left, right, across, part, from_side, from_corner, from_near, send, recv):
+        self.left, self.right, self.across, self.part = left, right, across, part
+        self.from_side, self.from_corner, self.from_near = from_side, from_corner, from_near
+        self.send, self.recv = send, recv
+        self.rows = part.shape[1]
+
+    def product(self, owner, slot):
+        rows, width = self.rows, self.part.shape[2]
+        picked = pl.ds(pl.multiple_of(owner * rows, rows), rows)
+
+        def tile(t, carry):
+            columns = pl.ds(pl.multiple_of(t * 256, 256), 256)
+            if self.across:
+                value = lax.dot_general(
+                    self.left[picked, :], self.right[columns, :], NT, preferred_element_type=F32
+                )
+            else:
+                value = jnp.dot(
+                    self.left[picked, :], self.right[:, columns], preferred_element_type=F32
+                )
+            self.part[slot, :, columns] = value.astype(BF16)
+            return carry
+
+        lax.fori_loop(0, width // 256, tile, 0)
+
+    def run(self):
+        me, side, over_x, over_y, corner = plane()
+        part, near, rows = self.part, self.from_near, self.rows
+        half = rows // 2
+        low, high = pl.ds(0, half), pl.ds(half, half)
+
+        def hop(number, source, target, index):
+            return to_dp(source, target, self.send.at[number], self.recv.at[number], index)
+
+        shares = [hop(i, part.at[4 + i], self.from_side.at[i], side) for i in range(4)]
+        corners = [
+            hop(4, part.at[0, low], self.from_corner.at[0], over_x),
+            hop(5, part.at[0, high], self.from_corner.at[1], over_y),
+        ]
+        nears = [
+            hop(6, part.at[1, low], near.at[0, low], over_x),
+            hop(7, part.at[1, high], near.at[0, high], over_x),
+            hop(8, part.at[2, high], near.at[1, high], over_y),
+            hop(9, part.at[2, low], near.at[1, low], over_y),
+        ]
+        owners = [corner, over_x, over_y, me]
+        for slot in range(4):
+            other = owners[slot] + 1 - 2 * lax.rem(me, 2)
+            self.product(other, 4 + slot)
+            shares[slot].start()
+
+        def add_side(slot):
+            shares[slot].wait_recv()
+
+            def body(span):
+                part[slot, span, :] = (
+                    part[slot, span, :].astype(F32) + self.from_side[slot, span, :].astype(F32)
+                ).astype(BF16)
+
+            each_chunk(rows, body)
+
+        self.product(corner, 0)
+        add_side(0)
+        corners[0].start()
+        corners[1].start()
+        self.product(over_x, 1)
+        add_side(1)
+        nears[0].start()
+        self.product(over_y, 2)
+        add_side(2)
+        nears[2].start()
+        self.product(me, 3)
+
+        def add_corner(slot, offset, which):
+            def body(span):
+                target = pl.ds(pl.multiple_of(offset + span.start, CHUNK), CHUNK)
+                part[slot, target, :] = (
+                    part[slot, target, :].astype(F32)
+                    + self.from_corner[which, span, :].astype(F32)
+                ).astype(BF16)
+
+            each_chunk(half, body)
+
+        corners[0].wait_recv()
+        add_corner(2, 0, 0)
+        nears[3].start()
+        corners[1].wait_recv()
+        add_corner(1, half, 1)
+        nears[1].start()
+        shares[3].wait_recv()
+        for copy in nears:
+            copy.wait_recv()
+        self.pending = shares + corners + nears
+
+    def rows_of(self, span):
+        return (
+            self.part[3, span, :].astype(F32)
+            + self.from_side[3, span, :].astype(F32)
+            + self.from_near[0, span, :].astype(F32)
+            + self.from_near[1, span, :].astype(F32)
+        )
+
+    def finish(self):
+        for copy in self.pending:
+            copy.wait_send()
+
+
+def reduce_scratch(rows, width):
+    dma = pltpu.SemaphoreType.DMA
+    return [
+        pltpu.VMEM((8, rows, width), BF16),
+        pltpu.VMEM((4, rows, width), BF16),
+        pltpu.VMEM((2, rows // 2, width), BF16),
+        pltpu.VMEM((2, rows, width), BF16),
+        dma((10,)),
+        dma((10,)),
+    ]
+
+
+def gather_scratch(rows, width):
+    dma = pltpu.SemaphoreType.DMA
+    return [pltpu.VMEM((rows, width), BF16), dma((13,)), dma((13,)), dma(())]
+
+
+def mean_rows(values):
+    return jnp.mean(values, axis=-1, keepdims=True)
+
+
+def middle_kernel(
+    mixed, w_out, tokens, gain, middle, hidden_all,
+    part, from_side, from_corner, from_near, send, recv, own, send_g, recv_g, local,
+):
+    pl.semaphore_wait(greet_plane(), 3)
+    reduce = Reduce(mixed, w_out, False, part, from_side, from_corner, from_near, send, recv)
+    reduce.run()
+
+    def body(span):
+        values = tokens[span, :].astype(F32) + reduce.rows_of(span)
+        middle[span, :] = values
+        inverse = lax.rsqrt(mean_rows(values * values) + EPSILON)
+        own[span, :] = (values * inverse * gain[...]).astype(BF16)
+
+    each_chunk(own.shape[0], body)
+    gather = Gather(own, hidden_all, send_g, recv_g, local)
+    gather.start()
+    gather.pass_on()
+    gather.finish()
+    reduce.finish()
+
+
+def project_middle(mixed, w_out, tokens, gain):
+    rows, width = tokens.shape
+    groups = lax.axis_size("dp")
+    return pl.pallas_call(
+        middle_kernel,
+        out_shape=(
+            jax.ShapeDtypeStruct((rows, width), F32),
+            jax.ShapeDtypeStruct((groups, rows, width), BF16),
+        ),
+        in_specs=[on_chip()] * 4,
+        out_specs=(on_chip(), anywhere()),
+        scratch_shapes=reduce_scratch(rows, width) + gather_scratch(rows, width),
+        compiler_params=remote_params(4),
+        cost_estimate=pl.CostEstimate(flops=0, bytes_accessed=300_000_000, transcendentals=0),
+        name="project_middle",
+    )(mixed, w_out, tokens, gain)
+
+
+def norm_back_rows(gradient, values, gain, sums, span):
+    inverse = lax.rsqrt(mean_rows(values * values) + EPSILON)
+    normed = values * inverse
+    product = gradient * normed
+    folded = product[0:8]
+    for step in range(1, CHUNK // 8):
+        folded = folded + product[step * 8 : step * 8 + 8]
+    sums[...] += folded
+    scaled = gradient * gain
+    return inverse * (scaled - normed * mean_rows(scaled * normed))
+
+
+def branch_kernel(
+    both_grad, w_both, middle, cotangent, gain, middle_grad, branch_all, sums,
+    part, from_side, from_corner, from_near, send, recv, own, send_g, recv_g, local,
+):
+    pl.semaphore_wait(greet_plane(), 3)
+    reduce = Reduce(both_grad, w_both, True, part, from_side, from_corner, from_near, send, recv)
+    reduce.run()
+    sums[...] = jnp.zeros_like(sums)
+
+    def body(span):
+        change = norm_back_rows(reduce.rows_of(span), middle[span, :], gain[...], sums, span)
+        total = cotangent[span, :].astype(F32) + change
+        middle_grad[span, :] = total
+        own[span, :] = total.astype(BF16)
+
+    each_chunk(own.shape[0], body)
+    gather = Gather(own, branch_all, send_g, recv_g, local)
+    gather.start()
+    gather.pass_on()
+    gather.finish()
+    reduce.finish()
+
+
+def project_branch(both_grad, w_both, middle, cotangent, gain):
+    rows, width = middle.shape
+    groups = lax.axis_size("dp")
+    return pl.pallas_call(
+        branch_kernel,
+        out_shape=(
+            jax.ShapeDtypeStruct((rows, width), F32),
+            jax.ShapeDtypeStruct((groups, rows, width), BF16),
+            jax.ShapeDtypeStruct((8, width), F32),
+        ),
+        in_specs=[on_chip()] * 5,
+        out_specs=(on_chip(), anywhere(), on_chip()),
+        scratch_shapes=reduce_scratch(rows, width) + gather_scratch(rows, width),
+        compiler_params=remote_params(5),
+        cost_estimate=pl.CostEstimate(flops=0, bytes_accessed=300_000_000, transcendentals=0),
+        name="project_branch",
+    )(both_grad, w_both, middle, cotangent, gain)
+
+
+def input_kernel(
+    qkv_grad, w_qkv, tokens, middle_grad, gain, result, sums,
+    part, from_side, from_corner, from_near, send, recv,
+):
+    pl.semaphore_wait(greet_plane(), 3)
+    reduce = Reduce(qkv_grad, w_qkv, True, part, from_side, from_corner, from_near, send, recv)
+    reduce.run()
+    sums[...] = jnp.zeros_like(sums)
+
+    def body(span):
+        values = tokens[span, :].astype(F32)
+        change = norm_back_rows(reduce.rows_of(span), values, gain[...], sums, span)
+        result[span, :] = (middle_grad[span, :] + change).astype(BF16)
+
+    each_chunk(result.shape[0], body)
+    reduce.finish()
+
+
+def project_input(qkv_grad, w_qkv, tokens, middle_grad, gain):
+    rows, width = tokens.shape
+    return pl.pallas_call(
+        input_kernel,
+        out_shape=(
+            jax.ShapeDtypeStruct((rows, width), BF16),
+            jax.ShapeDtypeStruct((8, width), F32),
+        ),
+        in_specs=[on_chip()] * 5,
+        out_specs=(on_chip(), on_chip()),
+        scratch_shapes=reduce_scratch(rows, width),
+        compiler_params=remote_params(6),
+        cost_estimate=pl.CostEstimate(flops=0, bytes_accessed=150_000_000, transcendentals=0),
+        name="project_input",
+    )(qkv_grad, w_qkv, tokens, middle_grad, gain)
+
+
+def output_kernel(
+    activated, w_down, middle, result, part, from_side, from_corner, from_near, send, recv
+):
+    pl.semaphore_wait(greet_plane(), 3)
+    reduce = Reduce(activated, w_down, False, part, from_side, from_corner, from_near, send, recv)
+    reduce.run()
+
+    def body(span):
+        result[span, :] = (middle[span, :] + reduce.rows_of(span)).astype(BF16)
+
+    each_chunk(result.shape[0], body)
+    reduce.finish()
+
+
+def project_output(activated, w_down, middle):
+    rows, width = middle.shape
+    return pl.pallas_call(
+        output_kernel,
+        out_shape=jax.ShapeDtypeStruct((rows, width), BF16),
+        in_specs=[on_chip()] * 3,
+        out_specs=on_chip(),
+        scratch_shapes=reduce_scratch(rows, width),
+        compiler_params=remote_params(7),
+        cost_estimate=pl.CostEstimate(flops=0, bytes_accessed=150_000_000, transcendentals=0),
+        name="project_output",
+    )(activated, w_down, middle)
+
+
+def swapped(
+    tokens, cotangent, route, lengths, key_mask, norm1_gain, norm2_gain,
+    w_query, w_key, w_value, w_out, w_gate, w_up, w_down,
+):
+    groups = lax.axis_size("dp")
+    members = lax.axis_size("mp")
+    me = lax.axis_index("dp")
+    z = lax.axis_index("mp")
+    rows, width = tokens.shape
+    bucket = rows // groups
+    units = w_down.shape[0] // groups
+    chip, core = me // 2, me % 2
+    pad_head = LANES - HEAD_DIM
+
+    target = route // TOK_DEV
+    earlier = jnp.arange(rows, dtype=jnp.int32)
+    same = (target[:, None] == target[None, :]) & (earlier[None, :] < earlier[:, None])
+    send_at = target * bucket + jnp.sum(same.astype(jnp.int32), axis=1)
+    sorting = send_at[None, :] == earlier[:, None]
+    slots_own = jnp.sum(jnp.where(sorting, (route % rows)[None, :], 0), axis=1)
+    sort_hot = sorting.astype(BF16)
+    tokens_b = jnp.dot(sort_hot, tokens, preferred_element_type=F32).astype(BF16)
+    cotangent_b = jnp.dot(sort_hot, cotangent, preferred_element_type=F32).astype(BF16)
+
+    mask_window = lax.dynamic_slice_in_dim(
+        jnp.concatenate([jnp.zeros((WINDOW,), jnp.int32), key_mask]), z * rows, rows + WINDOW
+    )
+    notes = jnp.concatenate([slots_own, mask_window, lengths[0]])
+    notes = jnp.pad(notes, (0, -notes.shape[0] % LANES))
+    notes_all = lax.all_gather(notes, "dp")
+    slots = (
+        notes_all[:, :rows].reshape(groups, groups, bucket).transpose(1, 0, 2).reshape(groups, rows)
+    )
+    flags = notes_all[:, rows : 2 * rows + WINDOW]
+    lengths_all = notes_all[:, 2 * rows + WINDOW : 2 * rows + WINDOW + 3]
+
+    def unit_columns(weight):
+        return lax.dynamic_slice_in_dim(weight, me * units, units, 1)
+
+    both_own = jnp.concatenate([unit_columns(w_gate), unit_columns(w_up)], axis=1)
+    down_own = lax.dynamic_slice_in_dim(w_down, me * units, units, 0)
+    both_all = lax.all_gather(both_own, "mp")
+    down_all = lax.all_gather(down_own, "mp", axis=0, tiled=True)
+    w_both = both_all.transpose(1, 0, 2).reshape(width, members * 2 * units)
+
+    def head_columns(weight):
+        head = lax.dynamic_slice_in_dim(weight, chip * HEAD_DIM, HEAD_DIM, 1)
+        return jnp.pad(head, ((0, 0), (0, pad_head)))
+
+    qkv_share = jnp.stack([head_columns(w_query), head_columns(w_key), head_columns(w_value)])
+    out_share = jnp.pad(
+        lax.dynamic_slice_in_dim(w_out, chip * HEAD_DIM, HEAD_DIM, 0), ((0, pad_head), (0, 0))
+    )
+
+    normed, _ = norm_rows(tokens_b.astype(F32))
+    hidden_own = (normed * norm1_gain).astype(BF16)
+    hidden_one, cotangent_all, w_qkv, w_proj = gather_first(
+        hidden_own, cotangent_b, qkv_share, out_share
+    )
+    count = groups * rows
+    hidden_one = hidden_one.reshape(count, width)
+    cotangent_all = cotangent_all.reshape(count, width)
+    qkv = jnp.dot(hidden_one, w_qkv, preferred_element_type=F32).astype(BF16)
+    scale = HEAD_DIM ** (-0.5)
+    mixed, kept = attend_ahead(
+        lengths_all, qkv.reshape(groups, groups, bucket, 6 * LANES), slots, flags, scale
+    )
+    mixed = mixed.reshape(count, 2 * LANES)
+    middle, hidden_two = project_middle(mixed, w_proj, tokens_b, norm2_gain[None])
+    hidden_two = hidden_two.reshape(count, width)
+    both_grad, activated = feed(hidden_two, cotangent_all, w_both, down_all)
+
+    down_sum = jnp.einsum("tf,td->fd", activated, cotangent_all, preferred_element_type=F32)
+    both_sum = jnp.einsum("td,tf->df", hidden_two, both_grad, preferred_element_type=F32)
+    both_sum = both_sum.astype(BF16).reshape(width, members, 2 * units).transpose(1, 0, 2)
+    down_part = lax.psum_scatter(down_sum.astype(BF16), "mp", scatter_dimension=0, tiled=True)
+    both_part = lax.psum_scatter(both_sum, "mp", scatter_dimension=0)
+
+    middle_grad, branch_all, sums_two = project_branch(
+        both_grad, w_both, middle, cotangent_b, norm2_gain[None]
+    )
+    branch_all = branch_all.reshape(count, width)
+    mixed_grad = jnp.einsum(
+        "td,cd->tc", branch_all, w_proj, preferred_element_type=F32
+    ).astype(BF16)
+    qkv_grad = attend_back(
+        lengths_all, kept, mixed_grad.reshape(groups, groups, bucket, 2 * LANES), slots, flags, scale
+    ).reshape(count, 6 * LANES)
+    proj_sum = jnp.einsum("tc,td->cd", mixed, branch_all, preferred_element_type=F32).astype(BF16)
+    qkv_sum = jnp.einsum("td,tc->dc", hidden_one, qkv_grad, preferred_element_type=F32).astype(BF16)
+
+    spread = jnp.arange(members, dtype=jnp.int32)
+    mine = (spread // 2 == core)[:, None, None]
+    qkv_heads = qkv_sum.reshape(width, 3, 2, LANES)[..., :HEAD_DIM].transpose(2, 0, 1, 3)
+    qkv_heads = qkv_heads.reshape(2, width, 3 * HEAD_DIM)
+    proj_heads = proj_sum.reshape(2, LANES, width)[:, :HEAD_DIM]
+    none = jnp.zeros((), BF16)
+    qkv_part = lax.psum_scatter(
+        jnp.where(mine, jnp.tile(qkv_heads, (2, 1, 1)), none), "mp", scatter_dimension=0
+    )
+    proj_part = lax.psum_scatter(
+        jnp.where(mine, jnp.tile(proj_heads, (2, 1, 1)), none), "mp", scatter_dimension=0
+    )
+    input_rows, sums_one = project_input(qkv_grad, w_qkv, tokens_b, middle_grad, norm1_gain[None])
+    output_rows = project_output(activated, down_all, middle)
+
+    gain_sums = lax.psum(
+        jnp.stack([jnp.sum(sums_one, axis=0), jnp.sum(sums_two, axis=0)]), ("dp", "mp")
+    )
+    pick = z // 2
+    both_whole = lax.all_gather(both_part, "dp").astype(F32)
+    down_grad = lax.all_gather(down_part, "dp", axis=0, tiled=True).astype(F32)
+    gate_grad = both_whole[:, :, :units].transpose(1, 0, 2).reshape(width, groups * units)
+    up_grad = both_whole[:, :, units:].transpose(1, 0, 2).reshape(width, groups * units)
+    qkv_whole = lax.all_gather(qkv_part, "dp").reshape(groups // 2, 2, width, 3, HEAD_DIM)
+    qkv_whole = lax.dynamic_index_in_dim(qkv_whole, pick, 1, keepdims=False).astype(F32)
+    proj_whole = lax.all_gather(proj_part, "dp").reshape(groups // 2, 2, HEAD_DIM, width)
+    proj_whole = lax.dynamic_index_in_dim(proj_whole, pick, 1, keepdims=False).astype(F32)
+    head_grads = qkv_whole.transpose(2, 1, 0, 3).reshape(3, width, groups // 2 * HEAD_DIM)
+
+    unsort = (((0,), (0,)), ((), ()))
+    return (
+        lax.dot_general(sort_hot, output_rows, unsort, preferred_element_type=F32).astype(BF16),
+        lax.dot_general(sort_hot, input_rows, unsort, preferred_element_type=F32).astype(BF16),
+        gain_sums[0],
+        gain_sums[1],
+        head_grads[0],
+        head_grads[1],
+        head_grads[2],
+        proj_whole.reshape(groups // 2 * HEAD_DIM, width),
+        gate_grad,
+        up_grad,
+        down_grad,
+    )
+
+
 def solution(mesh):
     in_specs = (
         P(("dp", "mp"), None),
@@ -361,4 +1289,5 @@
         P(None, "mp"),
         P("mp", None),
     )
-    return jax.shard_map(local, mesh=mesh, in_specs=in_specs, out_specs=out_specs, check_vma=False)
+    body = swapped if (mesh.shape["dp"], mesh.shape["mp"]) == (8, 4) else local
+    return jax.shard_map(body, mesh=mesh, in_specs=in_specs, out_specs=out_specs, check_vma=False)

time: 1740 us -> 1060 us (0.61)
  waiting for transfers between devices: 1200 us -> 143 us
  Pallas kernels: 0 us -> 658 us
  matrix products: 226 us -> 82.8 us
  other arithmetic: 74.3 us -> 19.9 us
  local copies, waits for them, and re-layouts: 130 us -> 79 us
    pallas_call x0 -> x8, Pallas kernels: none -> 658 us  [the longest x1 144 us: gather_first(): pl.pallas_call(first_kernel, out_shape=(jax.ShapeDtypeStruct((groups, row...]
    psum x2 -> x0, waiting for transfers between devices: 555 us -> none  [the longest x1 341 us: local(): lax.psum(jnp.dot(mixed_flat, w_out, preferred_element_type=jnp.float32),...]
    all_gather x3 -> x6, waiting for transfers between devices: 272 us -> 0.03 us  [the longest x1 0.02 us: swapped(): both_all = lax.all_gather(both_own, 'mp')]
    reduce_scatter x3 -> x4, waiting for transfers between devices: 323 us -> 142 us  [the longest x1 89.7 us: swapped(): lax.psum_scatter(jnp.where(mine, jnp.tile(qkv_heads, (2, 1, 1)), none), '...]
    dot_general x42 -> x10, matrix products: 226 us -> 82.8 us  [the longest x1 18.3 us: swapped(): jnp.einsum('td,tf->df', hidden_two, both_grad, preferred_element_type=F32)]
    dynamic_update_slice x6 -> x0, local copies, waits for them, and re-layouts: 55.3 us -> none  [the longest x3 27.7 us: one_block(): lax.dynamic_update_slice_in_dim(value_grad, lax.dynamic_slice_in_dim(valu...]
    all_to_all x4 -> x0, waiting for transfers between devices: 48.4 us -> none  [the longest x1 30.8 us: local(): lax.all_to_all(out_rows.astype(jnp.bfloat16)[arrival_slot], 'dp', split_a...]
    convert_element_type x15 -> x3, other arithmetic: 40 us -> 9.14 us  [the longest x1 5.68 us: swapped(): down_grad = lax.all_gather(down_part, 'dp', axis=0, tiled=True).astype(F32)]
  transfers between devices with their start and end apart: 12 -> 10, of which waited for: 10 -> 2; matrix products, arithmetic and copies ran while one was open for 8% -> 15% of each run, Pallas kernels for 0% -> 49%
where the time goes in v1:
time: 1060 us; the launch traced here: 1050 us
  Pallas kernels  658 us (62%)
  waiting for transfers between devices  143 us (13%)
  matrix products  82.8 us (8%)
  local copies, waits for them, and re-layouts  79 us (7%)
  blocking collectives  50.6 us (5%)
  other arithmetic  19.9 us (2%)
  between operations  15 us (1%)
    pallas_call x1, Pallas kernels, gather_first(): pl.pallas_call(first_kernel, out_shape=(jax.ShapeDtypeStruct((groups, row...  144 us
    pallas_call x1, Pallas kernels, project_branch(): pl.pallas_call(branch_kernel, out_shape=(jax.ShapeDtypeStruct((rows, widt...  121 us
    pallas_call x1, Pallas kernels, project_middle(): pl.pallas_call(middle_kernel, out_shape=(jax.ShapeDtypeStruct((rows, widt...  112 us
    reduce_scatter x1, waiting for transfers between devices, swapped(): lax.psum_scatter(jnp.where(mine, jnp.tile(qkv_heads, (2, 1, 1)), none), '...  89.7 us
    pallas_call x1, Pallas kernels, project_input(): pl.pallas_call(input_kernel, out_shape=(jax.ShapeDtypeStruct((rows, width...  88.6 us
    pallas_call x1, Pallas kernels, project_output(): pl.pallas_call(output_kernel, out_shape=jax.ShapeDtypeStruct((rows, width...  88.5 us
    reduce_scatter x1, waiting for transfers between devices, swapped(): both_part = lax.psum_scatter(both_sum, 'mp', scatter_dimension=0)  52.3 us
    pallas_call x1, Pallas kernels, attend_back(): pl.pallas_call(functools.partial(backward_kernel, scale=scale, groups=gro...  41.1 us
  transfers between devices with their start and end apart: 10, of which 2 were waited for; matrix products, arithmetic and copies ran while one was open for 15% of the time, Pallas kernels for 49%

profile of v1, /device:TPU:0, one launch (start us, length us, event | category | flops | bytes accessed | tf_op | source)
XLA Modules:
  0.0 1049.9 jit_solution(11175526470501298830)
XLA Ops:
  12.2 10.5 %all-gather.2 = s32[8,1,896]{2,1,0:T(1,128)S(1)} all-gather(s32[1,1,896]{2,1,0:T(1,128)S(1)} %reshape.146), channel_id=2, replica_groups=mesh['dp'=8,'mp'=4] {'dp'}, dimensions={0}, use_global_device_ids=true | all-gather | bytes 32256 | tf_op jit(solution)/shard_map/all_gather | solution.py:1155
  28.8 3.4 convolution_convert_fusion.7.cotangent
  36.7 144.5 %gather_first.1 = (bf16[8,384,1792]{2,1,0:T(8,128)(2,1)}, bf16[8,384,1792]{2,1,0:T(8,128)(2,1)}, bf16[1792,768]{1,0:T(8,128)(2,1)}, bf16[256,1792]{1,0:T(8,128)(2,1)}) custom-call(bf16[384,1792]{1,0:T(8,128)(2,1)} %fusion.2.hidden, bf16[384,1792]{1,0:T(8,128)(2,1)} %convolution_convert_fusion.7.cotangent, bf16[3,1792,128]{2,1,0:T(8,128)(2,1)} %pad_maximum_fusion.qkv_share, ...), custom_call_target="tpu_custom_call" | custom-call | bytes 300000000 | tf_op jit(solution)/shard_map/gather_first/pallas_call | solution.py:532
  181.1 13.8 %convolution_convert_fusion = bf16[3072,768]{1,0:T(8,128)(2,1)} fusion(bf16[3072,1792]{1,0:T(8,128)(2,1)} %bitcast.98, bf16[1792,768]{1,0:T(8,128)(2,1)} %get-tuple-element.27.w_qkv), kind=kOutput, calls=%fused_computation.1 | convolution fusion | flops 8458076160 | bytes 18481152 | tf_op jit(solution)/shard_map/dot_general | solution.py:1188
  194.9 37.5 %attend_ahead.1 = (bf16[8,8,48,256]{3,2,1,0:T(8,128)(2,1)}, bf16[8,448,768]{2,1,0:T(8,128)(2,1)}) custom-call(s32[8,3]{1,0:T(8,128)} %slice.51.lengths, bf16[8,8,48,768]{3,2,1,0:T(8,128)(2,1)} %bitcast.82, s32[8,384]{1,0:T(8,128)} %reshape.127.slots, s32[8,448]{1,0:T(8,128)} %slice.53.flags), custom_call_target="tpu_custom_call" | custom-call | bytes 70000000 | tf_op jit(solution)/shard_map/attend_ahead/pallas_call | solution.py:658
  232.5 112.2 %project_middle.1 = (f32[384,1792]{1,0:T(8,128)}, bf16[8,384,1792]{2,1,0:T(8,128)(2,1)}) custom-call(bf16[3072,256]{1,0:T(8,128)(2,1)} %bitcast.79, bf16[256,1792]{1,0:T(8,128)(2,1)} %get-tuple-element.29.w_out, bf16[384,1792]{1,0:T(8,128)(2,1)} %copy-done.2, f32[1,1792]{1,0:T(1,128)} %broadcast_in_dim.56.gain), custom_call_target="tpu_custom_call" | custom-call | bytes 300000000 | tf_op jit(solution)/shard_map/project_middle/pallas_call | solution.py:994
  344.7 15.3 %copy.61 = bf16[4,1792,256]{2,0,1:T(4,128)(2,1)S(1)} copy(bf16[4,1792,256]{2,1,0:T(8,128)(2,1)} %bitcast.83) | data formatting | bytes 7340032 | tf_op jit(solution)/shard_map/all_gather | solution.py:1167
  360.0 2.7 copy.72
  362.7 24.7 %feed.1 = (bf16[3072,1024]{1,0:T(8,128)(2,1)}, bf16[3072,512]{1,0:T(8,128)(2,1)}) custom-call(bf16[3072,1792]{1,0:T(8,128)(2,1)} %bitcast.102, bf16[3072,1792]{1,0:T(8,128)(2,1)} %bitcast.100, bf16[1792,1024]{1,0:T(8,128)(2,1)} %bitcast.77, bf16[512,1792]{1,0:T(8,128)(2,1)} %all-gather.10.cloned.1.call-done.w_down), custom_call_target="tpu_custom_call" | custom-call | flops 16911433728 | bytes 50000000 | tf_op jit(solution)/shard_map/feed/pallas_call | solution.py:802
  387.4 121.1 %project_branch.1 = (f32[384,1792]{1,0:T(8,128)}, bf16[8,384,1792]{2,1,0:T(8,128)(2,1)}, f32[8,1792]{1,0:T(8,128)}) custom-call(bf16[3072,1024]{1,0:T(8,128)(2,1)} %get-tuple-element.35.both_grad, bf16[1792,1024]{1,0:T(8,128)(2,1)} %bitcast.78, f32[384,1792]{1,0:T(8,128)} %get-tuple-element.33.middle, bf16[384,1792]{1,0:T(8,128)(2,1)} %convolution_convert_fusion.7.cotangent, ...), custom_call_target="tpu_custom_call" | custom-call | bytes 300000000 | tf_op jit(solution)/shard_map/project_branch/pallas_call | solution.py:1047
  508.5 7.2 convolution_convert_fusion.9
  517.2 11.7 %convolution_convert_fusion.4 = bf16[512,1792]{1,0:T(8,128)(2,1)} fusion(bf16[3072,512]{1,0:T(8,128)(2,1)} %get-tuple-element.32.activated, bf16[3072,1792]{1,0:T(8,128)(2,1)} %bitcast.101), kind=kOutput, calls=%fused_computation.8 | convolution fusion | flops 5638062080 | bytes 15990784 | tf_op jit(solution)/shard_map/tf,td->fd/dot_general | solution.py:1198
  528.9 18.3 %convolution_convert_fusion.2 = bf16[1792,1024]{0,1:T(8,128)(2,1)} fusion(bf16[3072,1792]{1,0:T(8,128)(2,1)} %bitcast.103, bf16[3072,1024]{1,0:T(8,128)(2,1)} %get-tuple-element.35.both_grad), kind=kOutput, calls=%fused_computation.4 | convolution fusion | flops 11276124160 | bytes 20971520 | tf_op jit(solution)/shard_map/td,tf->df/dot_general | solution.py:1199
  547.2 5.9 copy.63
  554.3 8.3 convolution_convert_fusion.1
  562.7 41.1 %attend_back.1 = bf16[8,8,48,768]{3,2,1,0:T(8,128)(2,1)} custom-call(s32[8,3]{1,0:T(8,128)} %slice.51.lengths, bf16[8,448,768]{2,1,0:T(8,128)(2,1)} %get-tuple-element.34.kept, bf16[8,8,48,256]{3,2,1,0:T(8,128)(2,1)} %bitcast.91, s32[8,384]{1,0:T(8,128)} %reshape.127.slots, s32[8,448]{1,0:T(8,128)} %slice.53.flags), custom_call_target="tpu_custom_call" | custom-call | bytes 120000000 | tf_op jit(solution)/shard_map/attend_back/pallas_call | solution.py:759
  603.7 13.9 %convolution_convert_fusion.3 = bf16[1792,768]{0,1:T(8,128)(2,1)S(1)} fusion(bf16[3072,1792]{1,0:T(8,128)(2,1)} %bitcast.99, bf16[3072,768]{1,0:T(8,128)(2,1)} %bitcast.73), kind=kOutput, calls=%fused_computation.7 | convolution fusion | flops 8457093120 | bytes 18481152 | tf_op jit(solution)/shard_map/td,tc->dc/dot_general | solution.py:1215
  618.0 2.6 bitcast_select_fusion
  622.2 52.3 %reduce-scatter.9.cloned.1.call-done = bf16[1,1792,256]{2,1,0:T(8,128)(2,1)} async-done(((bf16[4,1792,256]{2,1,0:T(8,128)(2,1)}), bf16[1,1792,256]{2,1,0:T(8,128)(2,1)}) %reduce-scatter.9.cloned.1.call-update) | async-done | bytes 917520 | tf_op jit(solution)/shard_map/reduce_scatter | solution.py:1202
  674.7 89.7 %reduce-scatter.5.cloned.1.call-done = bf16[1,1792,336]{1,2,0:T(8,128)(2,1)} async-done(((bf16[4,1792,336]{1,2,0:T(8,128)(2,1)}), bf16[1,1792,336]{1,2,0:T(8,128)(2,1)}) %reduce-scatter.5.cloned.1.call-update) | async-done | bytes 1204240 | tf_op jit(solution)/shard_map/reduce_scatter | solution.py:1223
  765.1 88.6 %project_input.1 = (bf16[384,1792]{1,0:T(8,128)(2,1)}, f32[8,1792]{1,0:T(8,128)}) custom-call(bf16[3072,768]{1,0:T(8,128)(2,1)} %bitcast.74, bf16[1792,768]{1,0:T(8,128)(2,1)} %get-tuple-element.27.w_qkv, bf16[384,1792]{1,0:T(8,128)(2,1)} %copy-done.2, f32[384,1792]{1,0:T(8,128)} %get-tuple-element.37.middle_grad, f32[1,1792]{1,0:T(1,128)} %broadcast_in_dim.57.gain), custom_call_target="tpu_custom_call" | custom-call | bytes 150000000 | tf_op jit(solution)/shard_map/project_input/pallas_call | solution.py:1083
  854.6 88.5 %project_output.1 = bf16[384,1792]{1,0:T(8,128)(2,1)} custom-call(bf16[3072,512]{1,0:T(8,128)(2,1)} %get-tuple-element.32.activated, bf16[512,1792]{1,0:T(8,128)(2,1)} %all-gather.10.cloned.1.call-done.w_down, f32[384,1792]{1,0:T(8,128)} %get-tuple-element.33.middle), custom_call_target="tpu_custom_call" | custom-call | bytes 150000000 | tf_op jit(solution)/shard_map/project_output/pallas_call | solution.py:1114
  943.1 40.1 %psum.7 = f32[2,1792]{1,0:T(2,128)S(1)} all-reduce(f32[2,1792]{1,0:T(2,128)S(1)} %pad_maximum_fusion.2), channel_id=1, replica_groups=mesh['dp'=8,'mp'=4] {'dp','mp'}, use_global_device_ids=true, to_apply=%region_5.6 | all-reduce | flops 3584 | bytes 28672 | tf_op jit(solution)/shard_map/psum | solution.py:1232
  983.9 2.0 convolution_convert_fusion.5
  985.9 3.3 convolution_convert_fusion.6
  992.8 5.7 convert_element_type.80
  998.5 9.9 copy.64
  1008.4 10.1 fusion.11
  1018.5 8.4 copy.66
  1026.9 8.4 copy.65
  1035.3 3.3 convert_bitcast_fusion
  1038.5 4.1 fusion.10
  (101 shorter events, 26.0 us)
Async XLA Ops:
  7.2 18.2 %copy-start = (bf16[1792,448]{0,1:T(8,128)(2,1)S(1)}, bf16[1792,448]{0,1:T(8,128)(2,1)}, u32[]{:S(2)}) copy-start(bf16[1792,448]{0,1:T(8,128)(2,1)} %param.21) | copy-start | bytes 4816900
  7.2 4.4 copy-start.10
  7.2 4.7 copy-start.8
  7.2 4.9 copy-start.11
  7.2 16.8 %copy-start.9 = (f32[1792]{0:T(1024)S(1)}, f32[1792]{0:T(1024)}, u32[]{:S(2)}) copy-start(f32[1792]{0:T(1024)} %param.20) | copy-start | bytes 21508
  7.2 337.4 %all-gather.20.cloned.1.call-start = ((), (), s32[]{:S(2)}) async-start(), calls=%async_computation.13 | async-start | bytes 4587520 | tf_op jit(solution)/shard_map/all_gather | solution.py:1167
  9.7 353.0 %all-gather.10.cloned.1.call-start = ((), (), s32[]{:S(2)}) async-start(), calls=%async_computation.4 | async-start | bytes 2293760 | tf_op jit(solution)/shard_map/all_gather | solution.py:1168
  11.6 609.1 %reduce-scatter.7.cloned.1.call-start = ((), (), s32[]{:S(2)}) async-start(), calls=%async_computation.7 | async-start | bytes 2007040 | tf_op jit(solution)/shard_map/reduce_scatter | solution.py:1226
  28.7 3.5 copy-start.12
  32.1 3.1 copy-start.7
  33.1 3.6 copy-start.2
  387.4 121.1 %copy-start.3 = (bf16[8,8,48,256]{3,2,1,0:T(8,128)(2,1)S(1)}, bf16[8,8,48,256]{3,2,1,0:T(8,128)(2,1)}, u32[]{:S(2)}) copy-start(bf16[8,8,48,256]{3,2,1,0:T(8,128)(2,1)} %get-tuple-element.28) | copy-start | bytes 4718596
  517.1 104.3 %reduce-scatter.11.cloned.1.call-start = ((), (), s32[]{:S(2)}) async-start(), calls=%async_computation.11 | async-start | bytes 2293760 | tf_op jit(solution)/shard_map/reduce_scatter | solution.py:1201
  528.8 145.6 %reduce-scatter.9.cloned.1.call-start = ((), (), s32[]{:S(2)}) async-start(), calls=%async_computation.9 | async-start | bytes 4587520 | tf_op jit(solution)/shard_map/reduce_scatter | solution.py:1202
  553.2 1.2 copy-start.5
  553.2 211.2 %reduce-scatter.5.cloned.1.call-start = ((), (), s32[]{:S(2)}) async-start(), calls=%async_computation.5 | async-start | bytes 6021120 | tf_op jit(solution)/shard_map/reduce_scatter | solution.py:1223
  620.6 368.6 %all-gather.14.cloned.1.call-start = ((), (), s32[]{:S(2)}) async-start(), calls=%async_computation.8 | async-start | bytes 3612672 | tf_op jit(solution)/shard_map/all_gather | solution.py:1242
  621.4 371.5 %all-gather.18.cloned.1.call-start = ((), (), s32[]{:S(2)}) async-start(), calls=%async_computation.12 | async-start | bytes 4128768 | tf_op jit(solution)/shard_map/all_gather | solution.py:1237
  622.1 376.4 %all-gather.16.cloned.1.call-start = ((), (), s32[]{:S(2)}) async-start(), calls=%async_computation.10 | async-start | bytes 8257536 | tf_op jit(solution)/shard_map/all_gather | solution.py:1236
  674.4 360.8 %all-gather.12.cloned.1.call-start = ((), (), s32[]{:S(2)}) async-start(), calls=%async_computation.6 | async-start | bytes 10838016 | tf_op jit(solution)/shard_map/all_gather | solution.py:1240
  765.1 89.5 %copy-start.6 = (f32[8,1792]{1,0:T(8,128)S(1)}, f32[8,1792]{1,0:T(8,128)}, u32[]{:S(2)}) copy-start(f32[8,1792]{1,0:T(8,128)} %get-tuple-element.40) | copy-start | bytes 172036
  854.6 129.3 %copy-start.4 = (bf16[384,1792]{1,0:T(8,128)(2,1)S(1)}, bf16[384,1792]{1,0:T(8,128)(2,1)}, u32[]{:S(2)}) copy-start(bf16[384,1792]{1,0:T(8,128)(2,1)} %get-tuple-element.38) | copy-start | bytes 4128772
  1038.5 4.1 copy-start.1
Sparse Core Ops, SparseCore 0:
  10.2 124.7 all-gather.19
  137.1 46.9 all-gather.9
  517.2 34.3 reduce-scatter.6
  554.4 49.6 reduce-scatter.10
  606.8 67.5 reduce-scatter.8
  677.2 87.2 reduce-scatter.4
  766.3 41.8 all-gather.13
  810.1 44.7 all-gather.17
  856.7 77.9 all-gather.15
  936.5 61.0 all-gather.11

commit v2 on v1

--- a/solution.py
+++ b/solution.py
@@ -442,69 +442,145 @@
         self.keep.wait()
 
 
+def greet_all(barrier):
+    me, z = lax.axis_index("dp"), lax.axis_index("mp")
+    for step in range(1, 8):
+        pl.semaphore_signal(
+            barrier, inc=1, device_id={"dp": lax.rem(me + step, 8)}, device_id_type=MESH
+        )
+    core = lax.rem(me, 2)
+    for step in range(1, 4):
+        for other in (me, me + 1 - 2 * core):
+            pl.semaphore_signal(
+                barrier,
+                inc=1,
+                device_id={"dp": other, "mp": lax.rem(z + step, 4)},
+                device_id_type=MESH,
+            )
+    pl.semaphore_wait(barrier, 13)
+
+
+def swap_all(source, target, send, recv):
+    me = lax.axis_index("dp")
+    return [
+        to_dp(source, target.at[me], send.at[step - 1], recv.at[step - 1], lax.rem(me + step, 8))
+        for step in range(1, 8)
+    ]
+
+
+class Spread:
+    def __init__(self, qkv_share, out_share, w_qkv, w_out, send, recv, local):
+        me, z = lax.axis_index("dp"), lax.axis_index("mp")
+        core = lax.rem(me, 2)
+        self.place = z + core * (3 - 2 * z)
+        self.send, self.recv, self.local = send, recv, local
+        self.shares = [qkv_share.at[0], qkv_share.at[1], qkv_share.at[2], out_share]
+        self.slots = (core, 1 - core)
+        self.core = core
+        self.w_qkv, self.w_out = w_qkv, w_out
+
+    def target(self, which, piece):
+        slot = self.slots[which]
+        if piece == 3:
+            return self.w_out.at[pl.ds(pl.multiple_of(slot * LANES, LANES), LANES)]
+        columns = pl.ds(pl.multiple_of((2 * piece + slot) * LANES, LANES), LANES)
+        return self.w_qkv.at[:, columns]
+
+    def hop(self, which, piece, number, place, own):
+        source = self.shares[piece] if own else self.target(which, piece)
+        z = place + self.core * (3 - 2 * place)
+        return to_mp(
+            source,
+            self.target(which, piece),
+            self.send.at[number * 4 + piece],
+            self.recv.at[which * 4 + piece],
+            z,
+        )
+
+    def keep(self, which, piece):
+        return pltpu.make_async_copy(
+            self.shares[piece], self.target(which, piece), self.local.at[piece]
+        )
+
+    def start(self):
+        @pl.when(self.place == 0)
+        def _():
+            for piece in range(4):
+                self.hop(0, piece, 0, 1, True).start()
+                self.keep(0, piece).start()
+
+        @pl.when(self.place == 1)
+        def _():
+            for piece in range(4):
+                self.hop(1, piece, 0, 0, True).start()
+                self.hop(1, piece, 1, 2, True).start()
+                self.keep(1, piece).start()
+
+    def pass_on(self):
+        @pl.when(self.place == 1)
+        def _():
+            for piece in range(4):
+                self.hop(0, piece, 2, 2, False).wait_recv()
+                self.hop(0, piece, 2, 2, False).start()
+
+        @pl.when(self.place == 2)
+        def _():
+            for piece in range(4):
+                for which in (1, 0):
+                    self.hop(which, piece, which, 3, False).wait_recv()
+                    self.hop(which, piece, which, 3, False).start()
+
+    def finish(self):
+        @pl.when(self.place == 0)
+        def _():
+            for piece in range(4):
+                self.hop(1, piece, 0, 1, False).wait_recv()
+                self.hop(0, piece, 0, 1, True).wait_send()
+                self.keep(0, piece).wait()
+
+        @pl.when(self.place == 1)
+        def _():
+            for piece in range(4):
+                self.hop(1, piece, 0, 0, True).wait_send()
+                self.hop(1, piece, 1, 2, True).wait_send()
+                self.hop(0, piece, 2, 2, False).wait_send()
+                self.keep(1, piece).wait()
+
+        @pl.when(self.place == 2)
+        def _():
+            for piece in range(4):
+                for which in (1, 0):
+                    self.hop(which, piece, which, 3, False).wait_send()
+
+        @pl.when(self.place == 3)
+        def _():
+            for piece in range(4):
+                for which in (1, 0):
+                    self.hop(which, piece, which, 3, False).wait_recv()
+
+
 def first_kernel(
-    hidden, cotangent, qkv_share, out_share,
-    hidden_all, cotangent_all, w_qkv, w_out,
-    send_a, recv_a, send_b, recv_b, send_w, recv_w, local,
+    hidden, qkv_share, out_share, notes,
+    hidden_all, w_qkv, w_out, notes_all,
+    send_a, recv_a, send_w, recv_w, send_n, recv_n, local,
 ):
-    me, _, _, _, _ = plane()
-    z = lax.axis_index("mp")
-    core = lax.rem(me, 2)
-    barrier = greet_plane()
-    for step in (1, 2, 3):
-        pl.semaphore_signal(
-            barrier, inc=1, device_id={"mp": lax.rem(z + step, 4)}, device_id_type=MESH
-        )
-    pl.semaphore_wait(barrier, 6)
-    first = Gather(hidden, hidden_all, send_a, recv_a, local.at[0])
-    second = Gather(cotangent, cotangent_all, send_b, recv_b, local.at[1])
-    first.start()
-    place = lax.rem(z, 2)
-    owner = lax.div(z, 2) == core
-
-    def pieces(slot):
-        found = []
-        for part in range(3):
-            columns = pl.ds(pl.multiple_of((2 * part + slot) * LANES, LANES), LANES)
-            found.append((qkv_share.at[part], w_qkv.at[:, columns]))
-        rows = pl.ds(pl.multiple_of(slot * LANES, LANES), LANES)
-        found.append((out_share, w_out.at[rows]))
-        return found
-
-    @pl.when(owner)
-    def _():
-        for number, (source, target) in enumerate(pieces(place)):
-            pltpu.make_async_copy(source, target, local.at[2 + number]).start()
-        for step in (1, 2, 3):
-            other = lax.rem(z + step, 4)
-            for number, (source, target) in enumerate(pieces(place)):
-                index = (step - 1) * 4 + number
-                to_mp(source, target, send_w.at[index], recv_w.at[index], other).start()
-
-    second.start()
-    first.pass_on()
-    second.pass_on()
-    first.finish()
-    second.finish()
-
-    for step in (1, 2, 3):
-        source_z = lax.rem(z + 4 - step, 4)
-
-        @pl.when(lax.div(source_z, 2) == core)
-        def _():
-            for number, (source, target) in enumerate(pieces(lax.rem(source_z, 2))):
-                index = (step - 1) * 4 + number
-                to_mp(source, target, send_w.at[index], recv_w.at[index], source_z).wait_recv()
-
-    @pl.when(owner)
-    def _():
-        for step in (1, 2, 3):
-            other = lax.rem(z + step, 4)
-            for number, (source, target) in enumerate(pieces(place)):
-                index = (step - 1) * 4 + number
-                to_mp(source, target, send_w.at[index], recv_w.at[index], other).wait_send()
-        for number, (source, target) in enumerate(pieces(place)):
-            pltpu.make_async_copy(source, target, local.at[2 + number]).wait()
+    greet_all(pltpu.get_barrier_semaphore())
+    spread = Spread(qkv_share, out_share, w_qkv, w_out, send_w, recv_w, local)
+    gather = Gather(hidden, hidden_all, send_a, recv_a, local.at[4])
+    spread.start()
+    gather.start()
+    swaps = swap_all(notes, notes_all, send_n, recv_n)
+    for copy in swaps:
+        copy.start()
+    keep = pltpu.make_async_copy(notes, notes_all.at[lax.axis_index("dp")], local.at[5])
+    keep.start()
+    spread.pass_on()
+    gather.pass_on()
+    gather.finish()
+    spread.finish()
+    for copy in swaps:
+        copy.wait()
+    keep.wait()
 
 
 def anywhere():
@@ -525,7 +601,7 @@
     )
 
 
-def gather_first(hidden, cotangent, qkv_share, out_share):
+def gather_first(hidden, qkv_share, out_share, notes):
     rows, width = hidden.shape
     groups = lax.axis_size("dp")
     dma = pltpu.SemaphoreType.DMA
@@ -533,19 +609,19 @@
         first_kernel,
         out_shape=(
             jax.ShapeDtypeStruct((groups, rows, width), BF16),
-            jax.ShapeDtypeStruct((groups, rows, width), BF16),
             jax.ShapeDtypeStruct((width, 6 * LANES), BF16),
             jax.ShapeDtypeStruct((2 * LANES, width), BF16),
+            jax.ShapeDtypeStruct((groups,) + notes.shape, notes.dtype),
         ),
-        in_specs=[anywhere()] * 4,
+        in_specs=[on_chip()] * 4,
         out_specs=(anywhere(),) * 4,
         scratch_shapes=[
-            dma((13,)), dma((13,)), dma((13,)), dma((13,)), dma((12,)), dma((12,)), dma((6,)),
+            dma((13,)), dma((13,)), dma((12,)), dma((8,)), dma((7,)), dma((7,)), dma((6,)),
         ],
         compiler_params=remote_params(1),
-        cost_estimate=pl.CostEstimate(flops=0, bytes_accessed=300_000_000, transcendentals=0),
+        cost_estimate=pl.CostEstimate(flops=0, bytes_accessed=200_000_000, transcendentals=0),
         name="gather_first",
-    )(hidden, cotangent, qkv_share, out_share)
+    )(hidden, qkv_share, out_share, notes)
 
 
 def one_hot(slots, k, size):
@@ -573,11 +649,12 @@
 
 
 def forward_kernel(
-    lengths, qkv, slots, flags, mixed, kept, send, recv, *, scale, groups, rows
+    lengths, qkv, slots, flags, cotangent, mixed, kept, cotangent_all,
+    send, recv, send_g, recv_g, local, *, scale, groups, rows
 ):
     z = lax.axis_index("mp")
     members = lax.axis_size("mp")
-    barrier = pltpu.get_barrier_semaphore()
+    barrier = greet_plane()
 
     @pl.when(z > 0)
     def _():
@@ -585,7 +662,14 @@
 
     @pl.when(z < members - 1)
     def _():
-        pl.semaphore_wait(barrier, 1)
+        pl.semaphore_wait(barrier, 4)
+
+    @pl.when(z == members - 1)
+    def _():
+        pl.semaphore_wait(barrier, 3)
+
+    gather = Gather(cotangent, cotangent_all, send_g, recv_g, local)
+    gather.start()
 
     def halo(k, other):
         return to_mp(
@@ -640,7 +724,10 @@
         mixed[:, pl.ds(k, 1)] = back.reshape(groups, 1, rows // groups, 256)
         return carry
 
-    lax.fori_loop(0, groups, attend, 0)
+    lax.fori_loop(0, groups - 2, attend, 0)
+    gather.pass_on()
+    lax.fori_loop(groups - 2, groups, attend, 0)
+    gather.finish()
 
     @pl.when(z < members - 1)
     def _():
@@ -651,7 +738,7 @@
         lax.fori_loop(0, groups, done, 0)
 
 
-def attend_ahead(lengths, qkv, slots, flags, scale):
+def attend_ahead(lengths, qkv, slots, flags, cotangent, scale):
     groups = qkv.shape[0]
     rows = slots.shape[1]
     dma = pltpu.SemaphoreType.DMA
@@ -660,32 +747,340 @@
         out_shape=(
             jax.ShapeDtypeStruct((groups, groups, rows // groups, 256), BF16),
             jax.ShapeDtypeStruct((groups, rows + 64, 768), BF16),
+            jax.ShapeDtypeStruct((groups,) + cotangent.shape, BF16),
         ),
-        in_specs=[in_scalar(), on_chip(), on_chip(), on_chip()],
-        out_specs=(on_chip(), on_chip()),
-        scratch_shapes=[dma((groups,)), dma((groups,))],
+        in_specs=[in_scalar()] + [on_chip()] * 4,
+        out_specs=(on_chip(), on_chip(), anywhere()),
+        scratch_shapes=[dma((groups,)), dma((groups,)), dma((13,)), dma((13,)), dma(())],
         compiler_params=remote_params(2),
-        cost_estimate=pl.CostEstimate(flops=0, bytes_accessed=70_000_000, transcendentals=0),
+        cost_estimate=pl.CostEstimate(flops=0, bytes_accessed=150_000_000, transcendentals=0),
         name="attend_ahead",
-    )(lengths, qkv, slots, flags)
+    )(lengths, qkv, slots, flags, cotangent)
+
+
+def feed_kernel(hidden, cotangent, w_both, w_down, both_grad, activated, *, members):
+    rows = hidden[...]
+    grad = lax.dot_general(cotangent[...], w_down[...], NT, preferred_element_type=F32)
+    for part in range(members):
+        raw = jnp.dot(rows, w_both[part], preferred_element_type=F32)
+        gate, upward = raw[:, :128], raw[:, 128:]
+        active_grad = grad[:, part * 128 : part * 128 + 128]
+        sigmoid = jax.nn.sigmoid(gate)
+        activated[:, part * 128 : part * 128 + 128] = (gate * sigmoid * upward).astype(BF16)
+        both_grad[:, part * 256 : part * 256 + 128] = (
+            active_grad * upward * sigmoid * (1.0 + gate * (1.0 - sigmoid))
+        ).astype(BF16)
+        both_grad[:, part * 256 + 128 : part * 256 + 256] = (
+            active_grad * gate * sigmoid
+        ).astype(BF16)
+
+
+def feed(hidden, cotangent, w_both, w_down):
+    count, width = hidden.shape
+    wide = w_both.shape[0] * 256
+    units = w_down.shape[0]
+    tile = 256
+    return pl.pallas_call(
+        functools.partial(feed_kernel, members=wide // 256),
+        grid=(count // tile,),
+        out_shape=(
+            jax.ShapeDtypeStruct((count, wide), BF16),
+            jax.ShapeDtypeStruct((count, units), BF16),
+        ),
+        in_specs=[
+            pl.BlockSpec((tile, width), lambda i: (i, 0)),
+            pl.BlockSpec((tile, width), lambda i: (i, 0)),
+            pl.BlockSpec(w_both.shape, lambda i: (0, 0, 0)),
+            pl.BlockSpec((units, width), lambda i: (0, 0)),
+        ],
+        out_specs=(
+            pl.BlockSpec((tile, wide), lambda i: (i, 0)),
+            pl.BlockSpec((tile, units), lambda i: (i, 0)),
+        ),
+        compiler_params=pltpu.CompilerParams(vmem_limit_bytes=VMEM_LIMIT),
+        cost_estimate=pl.CostEstimate(
+            flops=2 * count * width * (wide + units), bytes_accessed=50_000_000, transcendentals=0
+        ),
+        name="feed",
+    )(hidden, cotangent, w_both, w_down)
+
+
+CHUNK = 32
+
+
+def each_chunk(rows, body):
+    def step(i, carry):
+        body(pl.ds(pl.multiple_of(i * CHUNK, CHUNK), CHUNK))
+        return carry
+
+    lax.fori_loop(0, rows // CHUNK, step, 0)
+
+
+class Reduce:
+    COUNT = 10
+
+    def __init__(self, left, right, across, part, from_side, from_corner, from_near, send, recv):
+        self.left, self.right, self.across, self.part = left, right, across, part
+        self.from_side, self.from_corner, self.from_near = from_side, from_corner, from_near
+        self.send, self.recv = send, recv
+        self.rows = part.shape[1]
+
+    def product(self, owner, slot):
+        rows, width = self.rows, self.part.shape[2]
+        picked = pl.ds(pl.multiple_of(owner * rows, rows), rows)
+
+        def tile(t, carry):
+            columns = pl.ds(pl.multiple_of(t * 256, 256), 256)
+            if self.across == 3:
+                value = sum(
+                    lax.dot_general(
+                        self.left[picked, part * 256 : part * 256 + 256],
+                        self.right[part, columns, :],
+                        NT,
+                        preferred_element_type=F32,
+                    )
+                    for part in range(self.right.shape[0])
+                )
+            elif self.across == 2:
+                value = lax.dot_general(
+                    self.left[picked, :], self.right[columns, :], NT, preferred_element_type=F32
+                )
+            else:
+                value = jnp.dot(
+                    self.left[picked, :], self.right[:, columns], preferred_element_type=F32
+                )
+            self.part[slot, :, columns] = value.astype(BF16)
+            return carry
+
+        lax.fori_loop(0, width // 256, tile, 0)
+
+    def prepare(self):
+        _, side, over_x, over_y, corner = plane()
+        part, near = self.part, self.from_near
+        half = self.rows // 2
+        low, high = pl.ds(0, half), pl.ds(half, half)
+
+        def hop(number, source, target, index):
+            return to_dp(source, target, self.send.at[number], self.recv.at[number], index)
+
+        self.shares = [hop(i, part.at[4 + i], self.from_side.at[i], side) for i in range(4)]
+        self.corners = [
+            hop(4, part.at[0, low], self.from_corner.at[0], over_x),
+            hop(5, part.at[0, high], self.from_corner.at[1], over_y),
+        ]
+        self.nears = [
+            hop(6, part.at[1, low], near.at[0, low], over_x),
+            hop(7, part.at[1, high], near.at[0, high], over_x),
+            hop(8, part.at[2, high], near.at[1, high], over_y),
+            hop(9, part.at[2, low], near.at[1, low], over_y),
+        ]
+
+    def add_side(self, slot):
+        self.shares[slot].wait_recv()
+
+        def body(span):
+            self.part[slot, span, :] = (
+                self.part[slot, span, :].astype(F32) + self.from_side[slot, span, :].astype(F32)
+            ).astype(BF16)
+
+        each_chunk(self.rows, body)
+
+    def add_corner(self, slot, offset, which):
+        self.corners[which].wait_recv()
+
+        def body(span):
+            target = pl.ds(pl.multiple_of(offset + span.start, CHUNK), CHUNK)
+            self.part[slot, target, :] = (
+                self.part[slot, target, :].astype(F32)
+                + self.from_corner[which, span, :].astype(F32)
+            ).astype(BF16)
+
+        each_chunk(self.rows // 2, body)
+
+    def begin(self):
+        self.prepare()
+        me, _, over_x, over_y, corner = plane()
+        owners = (corner, over_x, over_y, me)
+        turn = 1 - 2 * lax.rem(me, 2)
+        self.product(corner + turn, 4)
+        self.shares[0].start()
+        self.product(corner, 0)
+        self.product(over_x + turn, 5)
+        self.shares[1].start()
+        self.add_side(0)
+        self.corners[0].start()
+        self.corners[1].start()
+        self.product(over_x, 1)
+        self.product(over_y + turn, 6)
+        self.shares[2].start()
+        self.add_side(1)
+        self.nears[0].start()
+        self.product(over_y, 2)
+        self.product(me + turn, 7)
+        self.shares[3].start()
+        self.add_side(2)
+        self.nears[2].start()
+        self.product(me, 3)
+
+    def middle(self):
+        self.add_corner(2, 0, 0)
+        self.nears[3].start()
+        self.add_corner(1, self.rows // 2, 1)
+        self.nears[1].start()
+
+    def end(self):
+        self.shares[3].wait_recv()
+        for copy in self.nears:
+            copy.wait_recv()
+
+    def run(self):
+        self.begin()
+        self.middle()
+        self.end()
+
+    def rows_of(self, span):
+        return (
+            self.part[3, span, :].astype(F32)
+            + self.from_side[3, span, :].astype(F32)
+            + self.from_near[0, span, :].astype(F32)
+            + self.from_near[1, span, :].astype(F32)
+        )
+
+    def finish(self):
+        for copy in self.shares + self.corners + self.nears:
+            copy.wait_send()
+
+
+def reduce_scratch(rows, width):
+    dma = pltpu.SemaphoreType.DMA
+    return [
+        pltpu.VMEM((8, rows, width), BF16),
+        pltpu.VMEM((4, rows, width), BF16),
+        pltpu.VMEM((2, rows // 2, width), BF16),
+        pltpu.VMEM((2, rows, width), BF16),
+        dma((10,)),
+        dma((10,)),
+    ]
+
+
+def gather_scratch(rows, width):
+    dma = pltpu.SemaphoreType.DMA
+    return [pltpu.VMEM((rows, width), BF16), dma((13,)), dma((13,)), dma(())]
+
+
+def mean_rows(values):
+    return jnp.mean(values, axis=-1, keepdims=True)
+
+
+class Heads:
+    def __init__(self, source, arrive, send, recv, views):
+        me, z = lax.axis_index("dp"), lax.axis_index("mp")
+        self.me, self.z = me, z
+        self.core = lax.rem(me, 2)
+        self.source, self.arrive, self.send, self.recv, self.views = source, arrive, send, recv, views
+        self.owner = lax.div(z, 2)
+
+    def copy(self, slot, half, number):
+        target_z = 2 * self.core + slot
+        index = (slot * 2 + half) * self.views + number
+        return to_at(
+            self.view(slot, half, number),
+            self.arrive.at[self.z, number],
+            self.send.at[index],
+            self.recv.at[self.z * self.views + number],
+            self.me - self.core + half,
+            target_z,
+        )
+
+    def view(self, slot, half, number):
+        if self.views == 1:
+            rows = pl.ds(pl.multiple_of(slot * LANES, LANES), LANES)
+            return self.source.at[rows, pl.ds(half * 896, 896)]
+        columns = pl.ds(pl.multiple_of((2 * number + slot) * LANES, LANES), LANES)
+        return self.source.at[pl.ds(half * 896, 896), columns]
+
+    def each(self, action):
+        for slot in range(2):
+            for half in range(2):
+                mine = (2 * self.core + slot == self.z) & (self.core == half)
+
+                @pl.when(jnp.logical_not(mine))
+                def _():
+                    for number in range(self.views):
+                        action(self.copy(slot, half, number))
+
+    def start(self):
+        self.each(lambda copy: copy.start())
+
+    def finish_send(self):
+        self.each(lambda copy: copy.wait_send())
+
+    def total(self, out):
+        me, z = self.me, self.z
+        for number in range(self.views):
+            for other in range(4):
+                waiting = to_at(
+                    self.view(0, 0, number),
+                    self.arrive.at[other, number],
+                    self.send.at[0],
+                    self.recv.at[other * self.views + number],
+                    me,
+                    other,
+                )
+
+                @pl.when((z != other) | (self.core != self.owner))
+                def _():
+                    waiting.wait_recv()
+
+                @pl.when((z == other) & (self.core == self.owner))
+                def _():
+                    half = self.core
+                    slot = lax.rem(z, 2)
+                    if self.views == 1:
+                        rows = pl.ds(pl.multiple_of(slot * LANES, LANES), LANES)
+                        columns = pl.ds(pl.multiple_of(half * 896, LANES), 896)
+                        self.arrive[other, number] = self.source[rows, columns]
+                    else:
+                        rows = pl.ds(pl.multiple_of(half * 896, LANES), 896)
+                        columns = pl.ds(pl.multiple_of((2 * number + slot) * LANES, LANES), LANES)
+                        self.arrive[other, number] = self.source[rows, columns]
+
+            count = self.arrive.shape[2]
+
+            def body(span):
+                found = self.arrive[0, number, span, :].astype(F32)
+                for other in range(1, 4):
+                    found = found + self.arrive[other, number, span, :].astype(F32)
+                out[number, span, :] = found.astype(BF16)
+
+            each_chunk(count, body)
+
+
+def to_at(source, target, send_sem, recv_sem, dp, mp):
+    return pltpu.make_async_remote_copy(
+        src_ref=source,
+        dst_ref=target,
+        send_sem=send_sem,
+        recv_sem=recv_sem,
+        device_id={"dp": dp, "mp": mp},
+        device_id_type=MESH,
+    )
 
 
 def backward_kernel(
-    lengths, kept, mixed_grad, slots, flags, out,
-    totals, query_part, key_value, leaving, arriving, send, recv,
+    lengths, kept, mixed_grad, slots, flags, activated, w_down, middle, proj_sum,
+    out, result, proj_part,
+    totals, query_part, key_value, ending, leaving, arriving, send, recv,
+    part, from_side, from_corner, from_near, send_r, recv_r, arrive, send_h, recv_h,
     *, scale, groups, rows,
 ):
     z = lax.axis_index("mp")
     members = lax.axis_size("mp")
-    barrier = pltpu.get_barrier_semaphore()
-
-    @pl.when(z < members - 1)
-    def _():
-        pl.semaphore_signal(barrier, inc=1, device_id={"mp": z + 1}, device_id_type=MESH)
-
-    @pl.when(z > 0)
-    def _():
-        pl.semaphore_wait(barrier, 1)
+    greet_all(pltpu.get_barrier_semaphore())
+    heads = Heads(proj_sum, arrive, send_h, recv_h, 1)
+    heads.start()
+    reduce = Reduce(activated, w_down, 0, part, from_side, from_corner, from_near, send_r, recv_r)
+    reduce.begin()
 
     def halo(k, other):
         return to_mp(leaving.at[k], arriving.at[k], send.at[k], recv.at[k], other)
@@ -718,7 +1113,8 @@
                 totals[pl.ds(block * 128, 192), pl.ds(256 + head * 128, 128)] += lax.dot_general(
                     again.astype(BF16), grad, TN, preferred_element_type=F32
                 )
-        key_value[k] = totals[pl.ds(64, rows), :]
+        key_value[k] = totals[pl.ds(64, rows), :].astype(BF16)
+        ending[k] = totals[pl.ds(rows, 64), :]
 
         @pl.when(z > 0)
         def _():
@@ -727,21 +1123,34 @@
 
         return carry
 
-    lax.fori_loop(0, groups, attend, 0)
+    lax.fori_loop(0, groups - 5, attend, 0)
+    reduce.middle()
+    lax.fori_loop(groups - 5, groups, attend, 0)
 
     def restore(k, carry):
         @pl.when(z < members - 1)
         def _():
             halo(k, z).wait_recv()
-            key_value[k, pl.ds(rows - 64, 64), :] += arriving[k].astype(F32)
+            key_value[k, pl.ds(rows - 64, 64), :] = (
+                ending[k] + arriving[k].astype(F32)
+            ).astype(BF16)
 
         hot = one_hot(slots, k, rows)
-        ordered = jnp.concatenate([query_part[k], key_value[k].astype(BF16)], axis=1)
+        ordered = jnp.concatenate([query_part[k], key_value[k]], axis=1)
         back = lax.dot_general(hot, ordered, TN, preferred_element_type=F32).astype(BF16)
         out[:, pl.ds(k, 1)] = back.reshape(groups, 1, rows // groups, 768)
         return carry
 
     lax.fori_loop(0, groups, restore, 0)
+    reduce.end()
+
+    def body(span):
+        result[span, :] = (middle[span, :] + reduce.rows_of(span)).astype(BF16)
+
+    each_chunk(rows, body)
+    heads.total(proj_part)
+    heads.finish_send()
+    reduce.finish()
 
     @pl.when(z > 0)
     def _():
@@ -752,218 +1161,37 @@
         lax.fori_loop(0, groups, done, 0)
 
 
-def attend_back(lengths, kept, mixed_grad, slots, flags, scale):
+def attend_back(
+    lengths, kept, mixed_grad, slots, flags, activated, w_down, middle, proj_sum, scale
+):
     groups = kept.shape[0]
-    rows = slots.shape[1]
+    rows, width = middle.shape
     dma = pltpu.SemaphoreType.DMA
     return pl.pallas_call(
         functools.partial(backward_kernel, scale=scale, groups=groups, rows=rows),
-        out_shape=jax.ShapeDtypeStruct((groups, groups, rows // groups, 768), BF16),
-        in_specs=[in_scalar()] + [on_chip()] * 4,
-        out_specs=on_chip(),
+        out_shape=(
+            jax.ShapeDtypeStruct((groups, groups, rows // groups, 768), BF16),
+            jax.ShapeDtypeStruct((rows, width), BF16),
+            jax.ShapeDtypeStruct((1, LANES, width // 2), BF16),
+        ),
+        in_specs=[in_scalar()] + [on_chip()] * 8,
+        out_specs=(on_chip(), on_chip(), on_chip()),
         scratch_shapes=[
             pltpu.VMEM((rows + 64, 512), F32),
             pltpu.VMEM((groups, rows, 256), BF16),
-            pltpu.VMEM((groups, rows, 512), F32),
+            pltpu.VMEM((groups, rows, 512), BF16),
+            pltpu.VMEM((groups, 64, 512), F32),
             pltpu.VMEM((groups, 64, 512), BF16),
             pltpu.VMEM((groups, 64, 512), BF16),
             dma((groups,)),
             dma((groups,)),
-        ],
-        compiler_params=remote_params(3),
-        cost_estimate=pl.CostEstimate(flops=0, bytes_accessed=120_000_000, transcendentals=0),
+        ]
+        + reduce_scratch(rows, width)
+        + [pltpu.VMEM((4, 1, LANES, width // 2), BF16), dma((4,)), dma((4,))],
+        compiler_params=remote_params(3, 62 * 1024 * 1024),
+        cost_estimate=pl.CostEstimate(flops=0, bytes_accessed=200_000_000, transcendentals=0),
         name="attend_back",
-    )(lengths, kept, mixed_grad, slots, flags)
-
-
-def feed_kernel(hidden, cotangent, w_both, w_down, both_grad, activated, *, members):
-    rows = hidden[...]
-    raw = jnp.dot(rows, w_both[...], preferred_element_type=F32)
-    grad = lax.dot_general(cotangent[...], w_down[...], NT, preferred_element_type=F32)
-    for part in range(members):
-        gate = raw[:, part * 256 : part * 256 + 128]
-        upward = raw[:, part * 256 + 128 : part * 256 + 256]
-        active_grad = grad[:, part * 128 : part * 128 + 128]
-        sigmoid = jax.nn.sigmoid(gate)
-        activated[:, part * 128 : part * 128 + 128] = (gate * sigmoid * upward).astype(BF16)
-        both_grad[:, part * 256 : part * 256 + 128] = (
-            active_grad * upward * sigmoid * (1.0 + gate * (1.0 - sigmoid))
-        ).astype(BF16)
-        both_grad[:, part * 256 + 128 : part * 256 + 256] = (
-            active_grad * gate * sigmoid
-        ).astype(BF16)
-
-
-def feed(hidden, cotangent, w_both, w_down):
-    count, width = hidden.shape
-    wide = w_both.shape[1]
-    units = w_down.shape[0]
-    tile = 256
-    return pl.pallas_call(
-        functools.partial(feed_kernel, members=wide // 256),
-        grid=(count // tile,),
-        out_shape=(
-            jax.ShapeDtypeStruct((count, wide), BF16),
-            jax.ShapeDtypeStruct((count, units), BF16),
-        ),
-        in_specs=[
-            pl.BlockSpec((tile, width), lambda i: (i, 0)),
-            pl.BlockSpec((tile, width), lambda i: (i, 0)),
-            pl.BlockSpec((width, wide), lambda i: (0, 0)),
-            pl.BlockSpec((units, width), lambda i: (0, 0)),
-        ],
-        out_specs=(
-            pl.BlockSpec((tile, wide), lambda i: (i, 0)),
-            pl.BlockSpec((tile, units), lambda i: (i, 0)),
-        ),
-        compiler_params=pltpu.CompilerParams(vmem_limit_bytes=VMEM_LIMIT),
-        cost_estimate=pl.CostEstimate(
-            flops=2 * count * width * (wide + units), bytes_accessed=50_000_000, transcendentals=0
-        ),
-        name="feed",
-    )(hidden, cotangent, w_both, w_down)
-
-
-CHUNK = 32
-
-
-def each_chunk(rows, body):
-    def step(i, carry):
-        body(pl.ds(pl.multiple_of(i * CHUNK, CHUNK), CHUNK))
-        return carry
-
-    lax.fori_loop(0, rows // CHUNK, step, 0)
-
-
-class Reduce:
-    COUNT = 10
-
-    def __init__(self, left, right, across, part, from_side, from_corner, from_near, send, recv):
-        self.left, self.right, self.across, self.part = left, right, across, part
-        self.from_side, self.from_corner, self.from_near = from_side, from_corner, from_near
-        self.send, self.recv = send, recv
-        self.rows = part.shape[1]
-
-    def product(self, owner, slot):
-        rows, width = self.rows, self.part.shape[2]
-        picked = pl.ds(pl.multiple_of(owner * rows, rows), rows)
-
-        def tile(t, carry):
-            columns = pl.ds(pl.multiple_of(t * 256, 256), 256)
-            if self.across:
-                value = lax.dot_general(
-                    self.left[picked, :], self.right[columns, :], NT, preferred_element_type=F32
-                )
-            else:
-                value = jnp.dot(
-                    self.left[picked, :], self.right[:, columns], preferred_element_type=F32
-                )
-            self.part[slot, :, columns] = value.astype(BF16)
-            return carry
-
-        lax.fori_loop(0, width // 256, tile, 0)
-
-    def run(self):
-        me, side, over_x, over_y, corner = plane()
-        part, near, rows = self.part, self.from_near, self.rows
-        half = rows // 2
-        low, high = pl.ds(0, half), pl.ds(half, half)
-
-        def hop(number, source, target, index):
-            return to_dp(source, target, self.send.at[number], self.recv.at[number], index)
-
-        shares = [hop(i, part.at[4 + i], self.from_side.at[i], side) for i in range(4)]
-        corners = [
-            hop(4, part.at[0, low], self.from_corner.at[0], over_x),
-            hop(5, part.at[0, high], self.from_corner.at[1], over_y),
-        ]
-        nears = [
-            hop(6, part.at[1, low], near.at[0, low], over_x),
-            hop(7, part.at[1, high], near.at[0, high], over_x),
-            hop(8, part.at[2, high], near.at[1, high], over_y),
-            hop(9, part.at[2, low], near.at[1, low], over_y),
-        ]
-        owners = [corner, over_x, over_y, me]
-        for slot in range(4):
-            other = owners[slot] + 1 - 2 * lax.rem(me, 2)
-            self.product(other, 4 + slot)
-            shares[slot].start()
-
-        def add_side(slot):
-            shares[slot].wait_recv()
-
-            def body(span):
-                part[slot, span, :] = (
-                    part[slot, span, :].astype(F32) + self.from_side[slot, span, :].astype(F32)
-                ).astype(BF16)
-
-            each_chunk(rows, body)
-
-        self.product(corner, 0)
-        add_side(0)
-        corners[0].start()
-        corners[1].start()
-        self.product(over_x, 1)
-        add_side(1)
-        nears[0].start()
-        self.product(over_y, 2)
-        add_side(2)
-        nears[2].start()
-        self.product(me, 3)
-
-        def add_corner(slot, offset, which):
-            def body(span):
-                target = pl.ds(pl.multiple_of(offset + span.start, CHUNK), CHUNK)
-                part[slot, target, :] = (
-                    part[slot, target, :].astype(F32)
-                    + self.from_corner[which, span, :].astype(F32)
-                ).astype(BF16)
-
-            each_chunk(half, body)
-
-        corners[0].wait_recv()
-        add_corner(2, 0, 0)
-        nears[3].start()
-        corners[1].wait_recv()
-        add_corner(1, half, 1)
-        nears[1].start()
-        shares[3].wait_recv()
-        for copy in nears:
-            copy.wait_recv()
-        self.pending = shares + corners + nears
-
-    def rows_of(self, span):
-        return (
-            self.part[3, span, :].astype(F32)
-            + self.from_side[3, span, :].astype(F32)
-            + self.from_near[0, span, :].astype(F32)
-            + self.from_near[1, span, :].astype(F32)
-        )
-
-    def finish(self):
-        for copy in self.pending:
-            copy.wait_send()
-
-
-def reduce_scratch(rows, width):
-    dma = pltpu.SemaphoreType.DMA
-    return [
-        pltpu.VMEM((8, rows, width), BF16),
-        pltpu.VMEM((4, rows, width), BF16),
-        pltpu.VMEM((2, rows // 2, width), BF16),
-        pltpu.VMEM((2, rows, width), BF16),
-        dma((10,)),
-        dma((10,)),
-    ]
-
-
-def gather_scratch(rows, width):
-    dma = pltpu.SemaphoreType.DMA
-    return [pltpu.VMEM((rows, width), BF16), dma((13,)), dma((13,)), dma(())]
-
-
-def mean_rows(values):
-    return jnp.mean(values, axis=-1, keepdims=True)
+    )(lengths, kept, mixed_grad, slots, flags, activated, w_down, middle, proj_sum)
 
 
 def middle_kernel(
@@ -971,7 +1199,7 @@
     part, from_side, from_corner, from_near, send, recv, own, send_g, recv_g, local,
 ):
     pl.semaphore_wait(greet_plane(), 3)
-    reduce = Reduce(mixed, w_out, False, part, from_side, from_corner, from_near, send, recv)
+    reduce = Reduce(mixed, w_out, 0, part, from_side, from_corner, from_near, send, recv)
     reduce.run()
 
     def body(span):
@@ -1023,7 +1251,7 @@
     part, from_side, from_corner, from_near, send, recv, own, send_g, recv_g, local,
 ):
     pl.semaphore_wait(greet_plane(), 3)
-    reduce = Reduce(both_grad, w_both, True, part, from_side, from_corner, from_near, send, recv)
+    reduce = Reduce(both_grad, w_both, 3, part, from_side, from_corner, from_near, send, recv)
     reduce.run()
     sums[...] = jnp.zeros_like(sums)
 
@@ -1061,11 +1289,15 @@
 
 
 def input_kernel(
-    qkv_grad, w_qkv, tokens, middle_grad, gain, result, sums,
-    part, from_side, from_corner, from_near, send, recv,
+    qkv_grad, w_qkv, tokens, middle_grad, gain, sums_two, qkv_sum, result, qkv_part, gains,
+    part, from_side, from_corner, from_near, send, recv, sums,
+    arrive, send_h, recv_h, own, plane_sums, column_sums, send_s, recv_s,
 ):
-    pl.semaphore_wait(greet_plane(), 3)
-    reduce = Reduce(qkv_grad, w_qkv, True, part, from_side, from_corner, from_near, send, recv)
+    me, z = lax.axis_index("dp"), lax.axis_index("mp")
+    greet_all(pltpu.get_barrier_semaphore())
+    heads = Heads(qkv_sum, arrive, send_h, recv_h, 3)
+    heads.start()
+    reduce = Reduce(qkv_grad, w_qkv, 2, part, from_side, from_corner, from_near, send, recv)
     reduce.run()
     sums[...] = jnp.zeros_like(sums)
 
@@ -1075,52 +1307,117 @@
         result[span, :] = (middle_grad[span, :] + change).astype(BF16)
 
     each_chunk(result.shape[0], body)
+    own[...] = jnp.concatenate(
+        [
+            jnp.sum(sums[...], axis=0, keepdims=True),
+            jnp.sum(sums_two[...], axis=0, keepdims=True),
+        ],
+        axis=0,
+    )
+    swaps = swap_all(own, plane_sums, send_s, recv_s)
+    for copy in swaps:
+        copy.start()
+    plane_sums[me] = own[...]
+    for copy in swaps:
+        copy.wait()
+    found = plane_sums[0]
+    for other in range(1, 8):
+        found = found + plane_sums[other]
+    column_sums[z] = found
+    passes = [
+        to_mp(
+            column_sums.at[z],
+            column_sums.at[z],
+            send_s.at[6 + step],
+            recv_s.at[6 + step],
+            lax.rem(z + step, 4),
+        )
+        for step in range(1, 4)
+    ]
+    for copy in passes:
+        copy.start()
+    for copy in passes:
+        copy.wait()
+    gains[...] = (column_sums[0] + column_sums[1]) + (column_sums[2] + column_sums[3])
+    heads.total(qkv_part)
+    heads.finish_send()
     reduce.finish()
 
 
-def project_input(qkv_grad, w_qkv, tokens, middle_grad, gain):
+def project_input(qkv_grad, w_qkv, tokens, middle_grad, gain, sums_two, qkv_sum):
     rows, width = tokens.shape
+    dma = pltpu.SemaphoreType.DMA
     return pl.pallas_call(
         input_kernel,
         out_shape=(
             jax.ShapeDtypeStruct((rows, width), BF16),
-            jax.ShapeDtypeStruct((8, width), F32),
+            jax.ShapeDtypeStruct((3, width // 2, LANES), BF16),
+            jax.ShapeDtypeStruct((2, width), F32),
         ),
-        in_specs=[on_chip()] * 5,
-        out_specs=(on_chip(), on_chip()),
-        scratch_shapes=reduce_scratch(rows, width),
+        in_specs=[on_chip()] * 7,
+        out_specs=(on_chip(),) * 3,
+        scratch_shapes=reduce_scratch(rows, width)
+        + [
+            pltpu.VMEM((8, width), F32),
+            pltpu.VMEM((4, 3, width // 2, LANES), BF16),
+            dma((12,)),
+            dma((12,)),
+            pltpu.VMEM((2, width), F32),
+            pltpu.VMEM((8, 2, width), F32),
+            pltpu.VMEM((4, 2, width), F32),
+            dma((10,)),
+            dma((10,)),
+        ],
         compiler_params=remote_params(6),
-        cost_estimate=pl.CostEstimate(flops=0, bytes_accessed=150_000_000, transcendentals=0),
+        cost_estimate=pl.CostEstimate(flops=0, bytes_accessed=200_000_000, transcendentals=0),
         name="project_input",
-    )(qkv_grad, w_qkv, tokens, middle_grad, gain)
-
-
-def output_kernel(
-    activated, w_down, middle, result, part, from_side, from_corner, from_near, send, recv
-):
-    pl.semaphore_wait(greet_plane(), 3)
-    reduce = Reduce(activated, w_down, False, part, from_side, from_corner, from_near, send, recv)
-    reduce.run()
-
-    def body(span):
-        result[span, :] = (middle[span, :] + reduce.rows_of(span)).astype(BF16)
-
-    each_chunk(result.shape[0], body)
-    reduce.finish()
-
-
-def project_output(activated, w_down, middle):
-    rows, width = middle.shape
+    )(qkv_grad, w_qkv, tokens, middle_grad, gain, sums_two, qkv_sum)
+
+
+def units_kernel(both, gate, upward):
+    for d in range(both.shape[0]):
+        gate[:, d * 128 : d * 128 + 128] = both[d, :, :128].astype(F32)
+        upward[:, d * 128 : d * 128 + 128] = both[d, :, 128:].astype(F32)
+
+
+def assemble_units(both):
+    groups, width, wide = both.shape
+    tile = 256
+    shape = jax.ShapeDtypeStruct((width, groups * wide // 2), F32)
+    spec = pl.BlockSpec((tile, groups * wide // 2), lambda i: (i, 0))
     return pl.pallas_call(
-        output_kernel,
-        out_shape=jax.ShapeDtypeStruct((rows, width), BF16),
-        in_specs=[on_chip()] * 3,
-        out_specs=on_chip(),
-        scratch_shapes=reduce_scratch(rows, width),
-        compiler_params=remote_params(7),
-        cost_estimate=pl.CostEstimate(flops=0, bytes_accessed=150_000_000, transcendentals=0),
-        name="project_output",
-    )(activated, w_down, middle)
+        units_kernel,
+        grid=(width // tile,),
+        out_shape=(shape, shape),
+        in_specs=[pl.BlockSpec((groups, tile, wide), lambda i: (0, i, 0))],
+        out_specs=(spec, spec),
+        cost_estimate=pl.CostEstimate(flops=0, bytes_accessed=22_000_000, transcendentals=0),
+        name="assemble_units",
+    )(both)
+
+
+def heads_kernel(whole, query, keys, values):
+    for part, out in enumerate((query, keys, values)):
+        out[...] = jnp.concatenate(
+            [whole[c, 0, part, :, :HEAD_DIM].astype(F32) for c in range(whole.shape[0])], axis=1
+        )
+
+
+def assemble_heads(whole):
+    chips, halves, _, rows, _ = whole.shape
+    tile = 448
+    count = rows // tile
+    shape = jax.ShapeDtypeStruct((halves * rows, chips * HEAD_DIM), F32)
+    spec = pl.BlockSpec((tile, chips * HEAD_DIM), lambda h, i: (h * count + i, 0))
+    return pl.pallas_call(
+        heads_kernel,
+        grid=(halves, count),
+        out_shape=(shape,) * 3,
+        in_specs=[pl.BlockSpec((chips, 1, 3, tile, LANES), lambda h, i: (0, h, 0, i, 0))],
+        out_specs=(spec,) * 3,
+        cost_estimate=pl.CostEstimate(flops=0, bytes_accessed=15_000_000, transcendentals=0),
+        name="assemble_heads",
+    )(whole)
 
 
 def swapped(
@@ -1151,22 +1448,7 @@
         jnp.concatenate([jnp.zeros((WINDOW,), jnp.int32), key_mask]), z * rows, rows + WINDOW
     )
     notes = jnp.concatenate([slots_own, mask_window, lengths[0]])
-    notes = jnp.pad(notes, (0, -notes.shape[0] % LANES))
-    notes_all = lax.all_gather(notes, "dp")
-    slots = (
-        notes_all[:, :rows].reshape(groups, groups, bucket).transpose(1, 0, 2).reshape(groups, rows)
-    )
-    flags = notes_all[:, rows : 2 * rows + WINDOW]
-    lengths_all = notes_all[:, 2 * rows + WINDOW : 2 * rows + WINDOW + 3]
-
-    def unit_columns(weight):
-        return lax.dynamic_slice_in_dim(weight, me * units, units, 1)
-
-    both_own = jnp.concatenate([unit_columns(w_gate), unit_columns(w_up)], axis=1)
-    down_own = lax.dynamic_slice_in_dim(w_down, me * units, units, 0)
-    both_all = lax.all_gather(both_own, "mp")
-    down_all = lax.all_gather(down_own, "mp", axis=0, tiled=True)
-    w_both = both_all.transpose(1, 0, 2).reshape(width, members * 2 * units)
+    notes = jnp.pad(notes, (0, 8 * LANES - notes.shape[0])).reshape(8, LANES)
 
     def head_columns(weight):
         head = lax.dynamic_slice_in_dim(weight, chip * HEAD_DIM, HEAD_DIM, 1)
@@ -1179,17 +1461,37 @@
 
     normed, _ = norm_rows(tokens_b.astype(F32))
     hidden_own = (normed * norm1_gain).astype(BF16)
-    hidden_one, cotangent_all, w_qkv, w_proj = gather_first(
-        hidden_own, cotangent_b, qkv_share, out_share
-    )
+    hidden_one, w_qkv, w_proj, notes_all = gather_first(hidden_own, qkv_share, out_share, notes)
+    notes_all = notes_all.reshape(groups, 8 * LANES)
+    slots = (
+        notes_all[:, :rows].reshape(groups, groups, bucket).transpose(1, 0, 2).reshape(groups, rows)
+    )
+    flags = notes_all[:, rows : 2 * rows + WINDOW]
+    lengths_all = notes_all[:, 2 * rows + WINDOW : 2 * rows + WINDOW + 3]
+
+    w_gate, w_up, w_down, hidden_one = lax.optimization_barrier((w_gate, w_up, w_down, hidden_one))
+
+    def unit_columns(weight):
+        return lax.dynamic_slice_in_dim(weight, me * units, units, 1)
+
+    both_own = jnp.concatenate([unit_columns(w_gate), unit_columns(w_up)], axis=1)
+    down_own = lax.dynamic_slice_in_dim(w_down, me * units, units, 0)
+    w_both = lax.all_gather(both_own, "mp")
+    down_all = lax.all_gather(down_own, "mp", axis=0, tiled=True)
+
     count = groups * rows
     hidden_one = hidden_one.reshape(count, width)
-    cotangent_all = cotangent_all.reshape(count, width)
     qkv = jnp.dot(hidden_one, w_qkv, preferred_element_type=F32).astype(BF16)
     scale = HEAD_DIM ** (-0.5)
-    mixed, kept = attend_ahead(
-        lengths_all, qkv.reshape(groups, groups, bucket, 6 * LANES), slots, flags, scale
-    )
+    mixed, kept, cotangent_all = attend_ahead(
+        lengths_all,
+        qkv.reshape(groups, groups, bucket, 6 * LANES),
+        slots,
+        flags,
+        cotangent_b,
+        scale,
+    )
+    cotangent_all = cotangent_all.reshape(count, width)
     mixed = mixed.reshape(count, 2 * LANES)
     middle, hidden_two = project_middle(mixed, w_proj, tokens_b, norm2_gain[None])
     hidden_two = hidden_two.reshape(count, width)
@@ -1198,50 +1500,53 @@
     down_sum = jnp.einsum("tf,td->fd", activated, cotangent_all, preferred_element_type=F32)
     both_sum = jnp.einsum("td,tf->df", hidden_two, both_grad, preferred_element_type=F32)
     both_sum = both_sum.astype(BF16).reshape(width, members, 2 * units).transpose(1, 0, 2)
-    down_part = lax.psum_scatter(down_sum.astype(BF16), "mp", scatter_dimension=0, tiled=True)
+    down_sum, both_sum, both_grad = lax.optimization_barrier(
+        (down_sum.astype(BF16), both_sum, both_grad)
+    )
+    down_part = lax.psum_scatter(down_sum, "mp", scatter_dimension=0, tiled=True)
     both_part = lax.psum_scatter(both_sum, "mp", scatter_dimension=0)
 
     middle_grad, branch_all, sums_two = project_branch(
         both_grad, w_both, middle, cotangent_b, norm2_gain[None]
     )
+    down_part, both_part, branch_all = lax.optimization_barrier((down_part, both_part, branch_all))
+    both_whole = lax.all_gather(both_part, "dp")
+    down_whole = lax.all_gather(down_part, "dp", axis=0, tiled=True)
     branch_all = branch_all.reshape(count, width)
     mixed_grad = jnp.einsum(
         "td,cd->tc", branch_all, w_proj, preferred_element_type=F32
     ).astype(BF16)
-    qkv_grad = attend_back(
-        lengths_all, kept, mixed_grad.reshape(groups, groups, bucket, 2 * LANES), slots, flags, scale
-    ).reshape(count, 6 * LANES)
     proj_sum = jnp.einsum("tc,td->cd", mixed, branch_all, preferred_element_type=F32).astype(BF16)
+    qkv_grad, output_rows, proj_part = attend_back(
+        lengths_all,
+        kept,
+        mixed_grad.reshape(groups, groups, bucket, 2 * LANES),
+        slots,
+        flags,
+        activated,
+        down_all,
+        middle,
+        proj_sum,
+        scale,
+    )
+    qkv_grad = qkv_grad.reshape(count, 6 * LANES)
     qkv_sum = jnp.einsum("td,tc->dc", hidden_one, qkv_grad, preferred_element_type=F32).astype(BF16)
-
-    spread = jnp.arange(members, dtype=jnp.int32)
-    mine = (spread // 2 == core)[:, None, None]
-    qkv_heads = qkv_sum.reshape(width, 3, 2, LANES)[..., :HEAD_DIM].transpose(2, 0, 1, 3)
-    qkv_heads = qkv_heads.reshape(2, width, 3 * HEAD_DIM)
-    proj_heads = proj_sum.reshape(2, LANES, width)[:, :HEAD_DIM]
-    none = jnp.zeros((), BF16)
-    qkv_part = lax.psum_scatter(
-        jnp.where(mine, jnp.tile(qkv_heads, (2, 1, 1)), none), "mp", scatter_dimension=0
-    )
-    proj_part = lax.psum_scatter(
-        jnp.where(mine, jnp.tile(proj_heads, (2, 1, 1)), none), "mp", scatter_dimension=0
-    )
-    input_rows, sums_one = project_input(qkv_grad, w_qkv, tokens_b, middle_grad, norm1_gain[None])
-    output_rows = project_output(activated, down_all, middle)
-
-    gain_sums = lax.psum(
-        jnp.stack([jnp.sum(sums_one, axis=0), jnp.sum(sums_two, axis=0)]), ("dp", "mp")
-    )
-    pick = z // 2
-    both_whole = lax.all_gather(both_part, "dp").astype(F32)
-    down_grad = lax.all_gather(down_part, "dp", axis=0, tiled=True).astype(F32)
-    gate_grad = both_whole[:, :, :units].transpose(1, 0, 2).reshape(width, groups * units)
-    up_grad = both_whole[:, :, units:].transpose(1, 0, 2).reshape(width, groups * units)
-    qkv_whole = lax.all_gather(qkv_part, "dp").reshape(groups // 2, 2, width, 3, HEAD_DIM)
-    qkv_whole = lax.dynamic_index_in_dim(qkv_whole, pick, 1, keepdims=False).astype(F32)
-    proj_whole = lax.all_gather(proj_part, "dp").reshape(groups // 2, 2, HEAD_DIM, width)
-    proj_whole = lax.dynamic_index_in_dim(proj_whole, pick, 1, keepdims=False).astype(F32)
-    head_grads = qkv_whole.transpose(2, 1, 0, 3).reshape(3, width, groups // 2 * HEAD_DIM)
+    input_rows, qkv_part, gain_sums = project_input(
+        qkv_grad, w_qkv, tokens_b, middle_grad, norm1_gain[None], sums_two, qkv_sum
+    )
+    proj_part, qkv_part, both_whole, down_whole = lax.optimization_barrier(
+        (proj_part, qkv_part, both_whole, down_whole)
+    )
+    chips = groups // 2
+    qkv_whole = lax.all_gather(qkv_part.reshape(3 * width // 2, LANES), "dp")
+    proj_whole = lax.all_gather(proj_part[0], "dp")
+    gate_grad, up_grad = assemble_units(both_whole)
+    down_grad = down_whole.astype(F32)
+    query_grad, key_grad, value_grad = assemble_heads(
+        qkv_whole.reshape(chips, 2, 3, width // 2, LANES)
+    )
+    proj_grad = proj_whole.reshape(chips, 2, LANES, width // 2)[:, :, :HEAD_DIM]
+    proj_grad = proj_grad.transpose(0, 2, 1, 3).reshape(chips * HEAD_DIM, width).astype(F32)
 
     unsort = (((0,), (0,)), ((), ()))
     return (
@@ -1249,10 +1554,10 @@
         lax.dot_general(sort_hot, input_rows, unsort, preferred_element_type=F32).astype(BF16),
         gain_sums[0],
         gain_sums[1],
-        head_grads[0],
-        head_grads[1],
-        head_grads[2],
-        proj_whole.reshape(groups // 2 * HEAD_DIM, width),
+        query_grad,
+        key_grad,
+        value_grad,
+        proj_grad,
         gate_grad,
         up_grad,
         down_grad,

time: 1060 us -> 774 us (0.73)
  Pallas kernels: 658 us -> 557 us
  waiting for transfers between devices: 143 us -> 44.1 us
  blocking collectives: 50.6 us -> 0 us
  local copies, waits for them, and re-layouts: 79 us -> 43.2 us
    reduce_scatter x3 -> x1, waiting for transfers between devices: 89.7 us -> 0.02 us  [swapped(): lax.psum_scatter(down_sum, 'mp', scatter_dimension=0, tiled=True)]
    pallas_call x1, Pallas kernels: 144 us -> 57.9 us  [gather_first(): pl.pallas_call(first_kernel, out_shape=(jax.ShapeDtypeStruct((groups, row...]
    pallas_call x1 -> x2, Pallas kernels: 88.5 us -> 17 us  [the longest x1 9.68 us: assemble_units(): pl.pallas_call(units_kernel, grid=(width // tile,), out_shape=(shape, sha...]
    reduce_scatter x1, waiting for transfers between devices: 52.3 us -> 0.02 us  [swapped(): both_part = lax.psum_scatter(both_sum, 'mp', scatter_dimension=0)]
    pallas_call x1, Pallas kernels: 41.1 us -> 91.6 us  [attend_back(): pl.pallas_call(functools.partial(backward_kernel, scale=scale, groups=gro...]
    all_gather x5, waiting for transfers between devices: 0.03 us -> 42.4 us  [the longest x1 39 us: swapped(): qkv_whole = lax.all_gather(qkv_part.reshape(3 * width // 2, LANES), 'dp')]
    psum x1 -> x0, blocking collectives: 40.1 us -> none  [swapped(): lax.psum(jnp.stack([jnp.sum(sums_one, axis=0), jnp.sum(sums_two, axis=0)]...]
    pallas_call x1, Pallas kernels: 37.5 us -> 69.4 us  [attend_ahead(): pl.pallas_call(functools.partial(forward_kernel, scale=scale, groups=grou...]
  transfers between devices with their start and end apart: 10 -> 8, of which waited for: 2 -> 2; matrix products, arithmetic and copies ran while one was open for 15% -> 9% of each run, Pallas kernels for 49% -> 61%
where the time goes in v2:
time: 774 us; the launch traced here: 766 us
  Pallas kernels  557 us (72%)
  matrix products  82.6 us (11%)
  waiting for transfers between devices  44.1 us (6%)
  local copies, waits for them, and re-layouts  43.2 us (6%)
  between operations  14.9 us (2%)
  other arithmetic  12.5 us (2%)
  starting transfers between devices  11 us (1%)
    pallas_call x1, Pallas kernels, project_branch(): pl.pallas_call(branch_kernel, out_shape=(jax.ShapeDtypeStruct((rows, widt...  116 us
    pallas_call x1, Pallas kernels, project_middle(): pl.pallas_call(middle_kernel, out_shape=(jax.ShapeDtypeStruct((rows, widt...  107 us
    pallas_call x1, Pallas kernels, attend_back(): pl.pallas_call(functools.partial(backward_kernel, scale=scale, groups=gro...  91.6 us
    pallas_call x1, Pallas kernels, project_input(): pl.pallas_call(input_kernel, out_shape=(jax.ShapeDtypeStruct((rows, width...  73.7 us
    pallas_call x1, Pallas kernels, attend_ahead(): pl.pallas_call(functools.partial(forward_kernel, scale=scale, groups=grou...  69.4 us
    pallas_call x1, Pallas kernels, gather_first(): pl.pallas_call(first_kernel, out_shape=(jax.ShapeDtypeStruct((groups, row...  57.9 us
    all_gather x1, waiting for transfers between devices, swapped(): qkv_whole = lax.all_gather(qkv_part.reshape(3 * width // 2, LANES), 'dp')  39 us
    pallas_call x1, Pallas kernels, feed(): pl.pallas_call(functools.partial(feed_kernel, members=wide // 256), grid=...  24.8 us
  transfers between devices with their start and end apart: 8, of which 2 were waited for; matrix products, arithmetic and copies ran while one was open for 9% of the time, Pallas kernels for 61%

profile of v2, /device:TPU:0, one launch (start us, length us, event | category | flops | bytes accessed | tf_op | source)
XLA Modules:
  0.0 765.8 jit_solution(7481514159225907658)
XLA Ops:
  8.3 2.3 fusion
  10.6 2.5 constant_dynamic-slice_fusion.4
  23.4 57.9 %gather_first.1 = (bf16[8,384,1792]{2,1,0:T(8,128)(2,1)}, bf16[1792,768]{1,0:T(8,128)(2,1)}, bf16[256,1792]{1,0:T(8,128)(2,1)}, s32[8,8,128]{2,1,0:T(8,128)}) custom-call(bf16[384,1792]{1,0:T(8,128)(2,1)} %fusion.2.hidden, bf16[3,1792,128]{2,1,0:T(8,128)(2,1)} %pad_maximum_fusion.qkv_share, bf16[128,1792]{1,0:T(8,128)(2,1)} %pad.22.out_share, ...), custom_call_target="tpu_custom_call" | custom-call | bytes 200000000 | tf_op jit(solution)/shard_map/gather_first/pallas_call | solution.py:608
  81.3 1.8 constant_dynamic-slice_fusion
  89.2 1.9 convolution_convert_fusion.7.cotangent
  91.1 13.8 %convolution_convert_fusion = bf16[3072,768]{1,0:T(8,128)(2,1)} fusion(bf16[3072,1792]{1,0:T(8,128)(2,1)} %bitcast.76, bf16[1792,768]{1,0:T(8,128)(2,1)} %get-tuple-element.53.w_qkv), kind=kOutput, calls=%fused_computation | convolution fusion | flops 8458076160 | bytes 18481152 | tf_op jit(solution)/shard_map/dot_general | solution.py:1484
  104.9 69.4 %attend_ahead.1 = (bf16[8,8,48,256]{3,2,1,0:T(8,128)(2,1)}, bf16[8,448,768]{2,1,0:T(8,128)(2,1)}, bf16[8,384,1792]{2,1,0:T(8,128)(2,1)}) custom-call(s32[8,3]{1,0:T(8,128)} %slice.24.lengths, bf16[8,8,48,768]{3,2,1,0:T(8,128)(2,1)} %bitcast.61, s32[8,384]{1,0:T(8,128)} %reshape.88.slots, s32[8,448]{1,0:T(8,128)} %slice.26.flags, ...), custom_call_target="tpu_custom_call" | custom-call | bytes 150000000 | tf_op jit(solution)/shard_map/attend_ahead/pallas_call | solution.py:745
  174.2 107.4 %project_middle.1 = (f32[384,1792]{1,0:T(8,128)}, bf16[8,384,1792]{2,1,0:T(8,128)(2,1)}) custom-call(bf16[3072,256]{1,0:T(8,128)(2,1)} %bitcast.55, bf16[256,1792]{1,0:T(8,128)(2,1)} %get-tuple-element.56.w_out, bf16[384,1792]{1,0:T(8,128)(2,1)} %copy-done.2, f32[1,1792]{1,0:T(1,128)} %broadcast_in_dim.18.gain), custom_call_target="tpu_custom_call" | custom-call | bytes 300000000 | tf_op jit(solution)/shard_map/project_middle/pallas_call | solution.py:1222
  281.7 24.8 %feed.1 = (bf16[3072,1024]{1,0:T(8,128)(2,1)}, bf16[3072,512]{1,0:T(8,128)(2,1)}) custom-call(bf16[3072,1792]{1,0:T(8,128)(2,1)} %bitcast.80, bf16[3072,1792]{1,0:T(8,128)(2,1)} %bitcast.78, bf16[4,1792,256]{2,1,0:T(8,128)(2,1)} %bitcast.63, bf16[512,1792]{1,0:T(8,128)(2,1)} %all-gather.9.cloned.1.call-done.w_down), custom_call_target="tpu_custom_call" | custom-call | flops 16911433728 | bytes 50000000 | tf_op jit(solution)/shard_map/feed/pallas_call | solution.py:783
  306.6 11.6 %convolution_convert_fusion.4 = bf16[512,1792]{1,0:T(8,128)(2,1)} fusion(bf16[3072,512]{1,0:T(8,128)(2,1)} %get-tuple-element.62.activated, bf16[3072,1792]{1,0:T(8,128)(2,1)} %bitcast.79), kind=kOutput, calls=%fused_computation.7 | convolution fusion | flops 5638062080 | bytes 15990784 | tf_op jit(solution)/shard_map/tf,td->fd/dot_general | solution.py:1500
  318.2 18.2 %convolution_convert_fusion.2 = bf16[1792,1024]{0,1:T(8,128)(2,1)} fusion(bf16[3072,1792]{1,0:T(8,128)(2,1)} %bitcast.81, bf16[3072,1024]{1,0:T(8,128)(2,1)} %get-tuple-element.66.both_grad), kind=kOutput, calls=%fused_computation.2 | convolution fusion | flops 11276124160 | bytes 20971520 | tf_op jit(solution)/shard_map/td,tf->df/dot_general | solution.py:1501
  336.4 5.9 copy.47
  343.0 10.5 %all-gather.11.cloned.1.call-start = ((), (), s32[]{:S(2)}) async-start(), calls=%async_computation.5 | async-start | bytes 4128768 | tf_op jit(solution)/shard_map/all_gather | solution.py:1514
  353.5 115.5 %project_branch.1 = (f32[384,1792]{1,0:T(8,128)}, bf16[8,384,1792]{2,1,0:T(8,128)(2,1)}, f32[8,1792]{1,0:T(8,128)}) custom-call(bf16[3072,1024]{1,0:T(8,128)(2,1)} %get-tuple-element.66.both_grad, bf16[4,1792,256]{2,1,0:T(8,128)(2,1)} %bitcast.64, f32[384,1792]{1,0:T(8,128)} %get-tuple-element.67.middle, ...), custom_call_target="tpu_custom_call" | custom-call | bytes 300000000 | tf_op jit(solution)/shard_map/project_branch/pallas_call | solution.py:1275
  470.3 8.2 %convolution_convert_fusion.9.proj_sum = bf16[256,1792]{1,0:T(8,128)(2,1)} fusion(bf16[3072,256]{1,0:T(8,128)(2,1)S(1)} %bitcast.56, bf16[3072,1792]{1,0:T(8,128)(2,1)} %bitcast.51), kind=kOutput, calls=%fused_computation.15 | convolution fusion | flops 2819031040 | bytes 13500416 | tf_op jit(solution)/shard_map/tc,td->cd/dot_general | solution.py:1519
  478.5 8.3 %convolution_convert_fusion.1 = bf16[3072,256]{1,0:T(8,128)(2,1)} fusion(bf16[3072,1792]{1,0:T(8,128)(2,1)} %bitcast.52, bf16[256,1792]{1,0:T(8,128)(2,1)S(1)} %copy-done.9), kind=kOutput, calls=%fused_computation.1 | convolution fusion | flops 2819358720 | bytes 13500416 | tf_op jit(solution)/shard_map/td,cd->tc/dot_general | solution.py:1516
  486.8 91.6 %attend_back.1 = (bf16[8,8,48,768]{3,2,1,0:T(8,128)(2,1)}, bf16[384,1792]{1,0:T(8,128)(2,1)}, bf16[1,128,896]{2,1,0:T(8,128)(2,1)}) custom-call(s32[8,3]{1,0:T(8,128)} %slice.24.lengths, bf16[8,448,768]{2,1,0:T(8,128)(2,1)} %get-tuple-element.54.kept, bf16[8,8,48,256]{3,2,1,0:T(8,128)(2,1)} %bitcast.66, s32[8,384]{1,0:T(8,128)} %reshape.88.slots, ...), custom_call_target="tpu_custom_call" | custom-call | bytes 200000000 | tf_op jit(solution)/shard_map/attend_back/pallas_call | solution.py:1170
  578.5 14.2 %convolution_convert_fusion.3.qkv_sum = bf16[1792,768]{1,0:T(8,128)(2,1)} fusion(bf16[3072,1792]{1,0:T(8,128)(2,1)} %bitcast.77, bf16[3072,768]{1,0:T(8,128)(2,1)} %bitcast.59), kind=kOutput, calls=%fused_computation.5 | convolution fusion | flops 8457093120 | bytes 18481152 | tf_op jit(solution)/shard_map/td,tc->dc/dot_general | solution.py:1533
  592.7 73.7 %project_input.1 = (bf16[384,1792]{1,0:T(8,128)(2,1)}, bf16[3,896,128]{2,1,0:T(8,128)(2,1)}, f32[2,1792]{1,0:T(2,128)}) custom-call(bf16[3072,768]{1,0:T(8,128)(2,1)} %bitcast.60, bf16[1792,768]{1,0:T(8,128)(2,1)} %get-tuple-element.53.w_qkv, bf16[384,1792]{1,0:T(8,128)(2,1)} %copy-done.2, f32[384,1792]{1,0:T(8,128)} %get-tuple-element.72.middle_grad, ...), custom_call_target="tpu_custom_call" | custom-call | bytes 200000000 | tf_op jit(solution)/shard_map/project_input/pallas_call | solution.py:1350
  668.7 2.0 convolution_convert_fusion.6
  670.7 2.0 convolution_convert_fusion.5
  672.7 9.7 %assemble_units.1 = (f32[1792,1024]{1,0:T(8,128)}, f32[1792,1024]{1,0:T(8,128)}) custom-call(bf16[8,1792,256]{2,1,0:T(8,128)(2,1)} %bitcast.57), custom_call_target="tpu_custom_call" | custom-call | bytes 22000000 | tf_op jit(solution)/shard_map/assemble_units/pallas_call | solution.py:1388
  682.4 5.9 convert_element_type.74
  688.3 3.4 all-gather.15.cloned.1.call-done
  691.8 1.6 convert_bitcast_fusion
  693.4 1.7 copy.48
  695.1 1.9 copy.56
  697.0 39.0 %all-gather.13.cloned.1.call-done = bf16[8,2688,128]{2,1,0:T(8,128)(2,1)} async-done(((bf16[1,2688,128]{2,1,0:T(8,128)(2,1)}), bf16[8,2688,128]{2,1,0:T(8,128)(2,1)}) %all-gather.13.cloned.1.call-update) | async-done | bytes 5505040 | tf_op jit(solution)/shard_map/all_gather | solution.py:1541
  735.9 7.4 assemble_heads.1
  743.3 5.0 copy.49
  748.3 5.0 copy.50
  753.3 5.2 copy.51
  (83 shorter events, 21.4 us)
Async XLA Ops:
  7.2 10.3 %copy-start = (bf16[1792,448]{0,1:T(8,128)(2,1)S(1)}, bf16[1792,448]{0,1:T(8,128)(2,1)}, u32[]{:S(2)}) copy-start(bf16[1792,448]{0,1:T(8,128)(2,1)} %param.21) | copy-start | bytes 4816900
  7.2 274.5 %all-gather.9.cloned.1.call-start = ((), (), s32[]{:S(2)}) async-start(), calls=%async_computation.2 | async-start | bytes 2293760 | tf_op jit(solution)/shard_map/all_gather | solution.py:1480
  10.6 10.1 %copy-start.2 = (bf16[384,1792]{1,0:T(8,128)(2,1)}, bf16[384,1792]{1,0:T(8,128)(2,1)S(1)}, u32[]{:S(2)}) copy-start(bf16[384,1792]{1,0:T(8,128)(2,1)S(1)} %get-tuple-element.127.tokens) | copy-start | bytes 4128772
  15.3 3.9 copy-start.12
  15.3 3.9 copy-start.14
  16.6 4.1 copy-start.10
  17.8 4.4 copy-start.4
  17.8 4.4 copy-start.5
  83.1 3.4 copy-start.11
  83.1 5.5 copy-start.13
  83.1 6.1 copy-start.6
  83.1 198.6 %all-gather.17.cloned.1.call-start = ((), (), s32[]{:S(2)}) async-start(), calls=%async_computation.8 | async-start | bytes 4587520 | tf_op jit(solution)/shard_map/all_gather | solution.py:1479
  86.4 382.6 %reduce-scatter.3.cloned.1.call-start = ((), (), s32[]{:S(2)}) async-start(), calls=%async_computation.3 | async-start | bytes 2293760 | tf_op jit(solution)/shard_map/reduce_scatter | solution.py:1506
  342.4 126.7 %reduce-scatter.5.cloned.1.call-start = ((), (), s32[]{:S(2)}) async-start(), calls=%async_computation.4 | async-start | bytes 4587520 | tf_op jit(solution)/shard_map/reduce_scatter | solution.py:1507
  343.0 323.5 %all-gather.11.cloned.1.call-start = ((), (), s32[]{:S(2)}) async-start(), calls=%async_computation.5 | async-start | bytes 4128768 | tf_op jit(solution)/shard_map/all_gather | solution.py:1514
  353.5 116.8 %copy-start.3 = (bf16[8,8,48,256]{3,2,1,0:T(8,128)(2,1)S(1)}, bf16[8,8,48,256]{3,2,1,0:T(8,128)(2,1)}, u32[]{:S(2)}) copy-start(bf16[8,8,48,256]{3,2,1,0:T(8,128)(2,1)} %get-tuple-element.55) | copy-start | bytes 4718596
  469.1 197.4 %all-gather.19.cloned.1.call-start = ((), (), s32[]{:S(2)}) async-start(), calls=%async_computation.9 | async-start | bytes 8257536 | tf_op jit(solution)/shard_map/all_gather | solution.py:1513
  469.7 222.1 %all-gather.15.cloned.1.call-start = ((), (), s32[]{:S(2)}) async-start(), calls=%async_computation.7 | async-start | bytes 2064384 | tf_op jit(solution)/shard_map/all_gather | solution.py:1542
  470.3 8.2 %copy-start.9 = (bf16[256,1792]{1,0:T(8,128)(2,1)S(1)}, bf16[256,1792]{1,0:T(8,128)(2,1)}, u32[]{:S(2)}) copy-start(bf16[256,1792]{1,0:T(8,128)(2,1)} %get-tuple-element.56.w_out) | copy-start | bytes 2752516
  592.7 76.0 %copy-start.7 = (bf16[384,1792]{1,0:T(8,128)(2,1)S(1)}, bf16[384,1792]{1,0:T(8,128)(2,1)}, u32[]{:S(2)}) copy-start(bf16[384,1792]{1,0:T(8,128)(2,1)} %get-tuple-element.70) | copy-start | bytes 4128772
  666.4 4.3 copy-start.8
  666.5 69.4 %all-gather.13.cloned.1.call-start = ((), (), s32[]{:S(2)}) async-start(), calls=%async_computation.6 | async-start | bytes 6193152 | tf_op jit(solution)/shard_map/all_gather | solution.py:1541
  753.3 5.2 copy-start.1
Sparse Core Ops, SparseCore 0:
  83.3 62.5 all-gather.8
  148.0 72.4 all-gather.16
  342.5 39.9 reduce-scatter.2
  385.2 67.5 reduce-scatter.4
  469.2 35.8 all-gather.10
  506.8 73.6 all-gather.18
  666.6 25.0 all-gather.14
  693.6 42.2 all-gather.12

commit v3 on v2

--- a/solution.py
+++ b/solution.py
@@ -382,64 +382,62 @@
 
 
 class Gather:
-    COUNT = 13
-
-    def __init__(self, own, out, send, recv, local):
+    AFTER = {0: (5, 6), 1: (7, 8), 2: (9,), 3: (10,), 5: (11,), 7: (12,)}
+
+    def __init__(self, own, out, send, recv, local=None):
         me, side, over_x, over_y, corner = plane()
-        half = own.shape[0] // 2
+        half = out.shape[1] // 2
         low, high = pl.ds(0, half), pl.ds(half, half)
+        self.keep = None if own is None else pltpu.make_async_copy(own, out.at[me], local)
+        own = out.at[me] if own is None else own
 
         def hop(number, source, target, index):
             return to_dp(source, target, send.at[number], recv.at[number], index)
 
-        self.keep = pltpu.make_async_copy(own, out.at[me], local)
-        self.first = [
+        def onward(number, owner, part, index):
+            place = out.at[owner, part]
+            return hop(number, place, place, index)
+
+        self.copies = [
             hop(0, own.at[low], out.at[me, low], over_x),
             hop(1, own.at[high], out.at[me, high], over_y),
             hop(2, own.at[high], out.at[me, high], over_x),
             hop(3, own.at[low], out.at[me, low], over_y),
             hop(4, own, out.at[me], side),
+            onward(5, over_x, low, over_y),
+            onward(6, over_x, low, side),
+            onward(7, over_y, high, over_x),
+            onward(8, over_y, high, side),
+            onward(9, over_x, high, side),
+            onward(10, over_y, low, side),
+            onward(11, corner, low, side),
+            onward(12, corner, high, side),
         ]
-        self.onward = [
-            (0, hop(5, out.at[over_x, low], out.at[over_x, low], over_y)),
-            (0, hop(6, out.at[over_x, low], out.at[over_x, low], side)),
-            (1, hop(7, out.at[over_y, high], out.at[over_y, high], over_x)),
-            (1, hop(8, out.at[over_y, high], out.at[over_y, high], side)),
-            (2, hop(9, out.at[over_x, high], out.at[over_x, high], side)),
-            (3, hop(10, out.at[over_y, low], out.at[over_y, low], side)),
-        ]
-        self.last = [
-            (5, hop(11, out.at[corner, low], out.at[corner, low], side)),
-            (7, hop(12, out.at[corner, high], out.at[corner, high], side)),
-        ]
-        self.by_number = dict(enumerate(self.first))
-        for number, copy in zip((5, 6, 7, 8, 9, 10), [c for _, c in self.onward]):
-            self.by_number[number] = copy
-        for number, copy in zip((11, 12), [c for _, c in self.last]):
-            self.by_number[number] = copy
 
     def start(self):
-        for copy in self.first:
-            copy.start()
-        self.keep.start()
+        for number in range(5):
+            self.copies[number].start()
+        if self.keep is not None:
+            self.keep.start()
+
+    def arrive(self, *numbers):
+        for number in numbers:
+            self.copies[number].wait_recv()
+            for later in self.AFTER.get(number, ()):
+                self.copies[later].start()
 
     def pass_on(self):
-        seen = set()
-        for after, copy in self.onward:
-            if after not in seen:
-                self.by_number[after].wait_recv()
-                seen.add(after)
-            copy.start()
+        self.arrive(0, 1, 2, 3)
+
+    def sent(self):
+        for copy in self.copies:
+            copy.wait_send()
+        if self.keep is not None:
+            self.keep.wait()
 
     def finish(self):
-        for after, copy in self.last:
-            self.by_number[after].wait_recv()
-            copy.start()
-        for number in (4, 6, 8, 9, 10, 11, 12):
-            self.by_number[number].wait_recv()
-        for number in range(self.COUNT):
-            self.by_number[number].wait_send()
-        self.keep.wait()
+        self.arrive(5, 7, 4, 6, 8, 9, 10, 11, 12)
+        self.sent()
 
 
 def greet_all(barrier):
@@ -469,22 +467,21 @@
 
 
 class Spread:
-    def __init__(self, qkv_share, out_share, w_qkv, w_out, send, recv, local):
+    def __init__(self, share, w_qkv, w_out, send, recv, local):
         me, z = lax.axis_index("dp"), lax.axis_index("mp")
         core = lax.rem(me, 2)
         self.place = z + core * (3 - 2 * z)
         self.send, self.recv, self.local = send, recv, local
-        self.shares = [qkv_share.at[0], qkv_share.at[1], qkv_share.at[2], out_share]
+        self.shares = [share.at[0], share.at[1], share.at[2], share.at[3]]
         self.slots = (core, 1 - core)
         self.core = core
         self.w_qkv, self.w_out = w_qkv, w_out
 
     def target(self, which, piece):
         slot = self.slots[which]
-        if piece == 3:
-            return self.w_out.at[pl.ds(pl.multiple_of(slot * LANES, LANES), LANES)]
-        columns = pl.ds(pl.multiple_of((2 * piece + slot) * LANES, LANES), LANES)
-        return self.w_qkv.at[:, columns]
+        block = slot if piece == 3 else 2 * piece + slot
+        rows = pl.ds(pl.multiple_of(block * LANES, LANES), HEAD_DIM)
+        return (self.w_out if piece == 3 else self.w_qkv).at[rows]
 
     def hop(self, which, piece, number, place, own):
         source = self.shares[piece] if own else self.target(which, piece)
@@ -560,26 +557,49 @@
 
 
 def first_kernel(
-    hidden, qkv_share, out_share, notes,
+    hidden, query, keys, values, project, notes,
     hidden_all, w_qkv, w_out, notes_all,
-    send_a, recv_a, send_w, recv_w, send_n, recv_n, local,
+    share, none, send_a, recv_a, send_w, recv_w, send_n, recv_n, local,
 ):
+    me = lax.axis_index("dp")
+    head = pl.ds(pl.multiple_of(lax.div(me, 2) * HEAD_DIM, 16), HEAD_DIM)
+    loads = [
+        pltpu.make_async_copy(source.at[head], share.at[piece], local.at[piece])
+        for piece, source in enumerate((query, keys, values, project))
+    ]
+    for copy in loads:
+        copy.start()
+    none[...] = jnp.zeros_like(none)
     greet_all(pltpu.get_barrier_semaphore())
-    spread = Spread(qkv_share, out_share, w_qkv, w_out, send_w, recv_w, local)
     gather = Gather(hidden, hidden_all, send_a, recv_a, local.at[4])
-    spread.start()
     gather.start()
     swaps = swap_all(notes, notes_all, send_n, recv_n)
     for copy in swaps:
         copy.start()
-    keep = pltpu.make_async_copy(notes, notes_all.at[lax.axis_index("dp")], local.at[5])
+    keep = pltpu.make_async_copy(notes, notes_all.at[me], local.at[5])
     keep.start()
+    pads = [
+        pltpu.make_async_copy(
+            none, weight.at[pl.ds(block * LANES + HEAD_DIM, LANES - HEAD_DIM)], local.at[6 + number]
+        )
+        for number, (weight, block) in enumerate(
+            [(w_qkv, block) for block in range(6)] + [(w_out, block) for block in range(2)]
+        )
+    ]
+    for copy in pads:
+        copy.start()
+    for copy in loads:
+        copy.wait()
+    spread = Spread(share, w_qkv, w_out, send_w, recv_w, local)
+    spread.start()
     spread.pass_on()
     gather.pass_on()
     gather.finish()
     spread.finish()
     for copy in swaps:
         copy.wait()
+    for copy in pads:
+        copy.wait()
     keep.wait()
 
 
@@ -601,7 +621,7 @@
     )
 
 
-def gather_first(hidden, qkv_share, out_share, notes):
+def gather_first(hidden, query, keys, values, project, notes):
     rows, width = hidden.shape
     groups = lax.axis_size("dp")
     dma = pltpu.SemaphoreType.DMA
@@ -609,19 +629,21 @@
         first_kernel,
         out_shape=(
             jax.ShapeDtypeStruct((groups, rows, width), BF16),
-            jax.ShapeDtypeStruct((width, 6 * LANES), BF16),
+            jax.ShapeDtypeStruct((6 * LANES, width), BF16),
             jax.ShapeDtypeStruct((2 * LANES, width), BF16),
             jax.ShapeDtypeStruct((groups,) + notes.shape, notes.dtype),
         ),
-        in_specs=[on_chip()] * 4,
+        in_specs=[on_chip()] + [anywhere()] * 4 + [on_chip()],
         out_specs=(anywhere(),) * 4,
         scratch_shapes=[
-            dma((13,)), dma((13,)), dma((12,)), dma((8,)), dma((7,)), dma((7,)), dma((6,)),
+            pltpu.VMEM((4, HEAD_DIM, width), BF16),
+            pltpu.VMEM((LANES - HEAD_DIM, width), BF16),
+            dma((13,)), dma((13,)), dma((12,)), dma((8,)), dma((7,)), dma((7,)), dma((14,)),
         ],
         compiler_params=remote_params(1),
         cost_estimate=pl.CostEstimate(flops=0, bytes_accessed=200_000_000, transcendentals=0),
         name="gather_first",
-    )(hidden, qkv_share, out_share, notes)
+    )(hidden, query, keys, values, project, notes)
 
 
 def one_hot(slots, k, size):
@@ -649,8 +671,8 @@
 
 
 def forward_kernel(
-    lengths, qkv, slots, flags, cotangent, mixed, kept, cotangent_all,
-    send, recv, send_g, recv_g, local, *, scale, groups, rows
+    lengths, hidden_all, w_qkv, slots, flags, cotangent, mixed, kept, cotangent_all,
+    qkv, shard, shard_sem, send, recv, send_g, recv_g, local, *, scale, groups, rows
 ):
     z = lax.axis_index("mp")
     members = lax.axis_size("mp")
@@ -670,6 +692,26 @@
 
     gather = Gather(cotangent, cotangent_all, send_g, recv_g, local)
     gather.start()
+
+    def load(g):
+        slot = lax.rem(g, 2)
+        return pltpu.make_async_copy(hidden_all.at[g], shard.at[slot], shard_sem.at[slot])
+
+    load(0).start()
+
+    def multiply(g, carry):
+        @pl.when(g < groups - 1)
+        def _():
+            load(g + 1).start()
+
+        load(g).wait()
+        product = lax.dot_general(
+            shard[lax.rem(g, 2)], w_qkv[...], NT, preferred_element_type=F32
+        ).astype(BF16)
+        qkv[g] = product.reshape(groups, rows // groups, 768)
+        return carry
+
+    lax.fori_loop(0, groups, multiply, 0)
 
     def halo(k, other):
         return to_mp(
@@ -724,9 +766,9 @@
         mixed[:, pl.ds(k, 1)] = back.reshape(groups, 1, rows // groups, 256)
         return carry
 
-    lax.fori_loop(0, groups - 2, attend, 0)
+    lax.fori_loop(0, groups // 4, attend, 0)
     gather.pass_on()
-    lax.fori_loop(groups - 2, groups, attend, 0)
+    lax.fori_loop(groups // 4, groups, attend, 0)
     gather.finish()
 
     @pl.when(z < members - 1)
@@ -738,9 +780,8 @@
         lax.fori_loop(0, groups, done, 0)
 
 
-def attend_ahead(lengths, qkv, slots, flags, cotangent, scale):
-    groups = qkv.shape[0]
-    rows = slots.shape[1]
+def attend_ahead(lengths, hidden_all, w_qkv, slots, flags, cotangent, scale):
+    groups, rows, width = hidden_all.shape
     dma = pltpu.SemaphoreType.DMA
     return pl.pallas_call(
         functools.partial(forward_kernel, scale=scale, groups=groups, rows=rows),
@@ -749,71 +790,33 @@
             jax.ShapeDtypeStruct((groups, rows + 64, 768), BF16),
             jax.ShapeDtypeStruct((groups,) + cotangent.shape, BF16),
         ),
-        in_specs=[in_scalar()] + [on_chip()] * 4,
+        in_specs=[in_scalar(), anywhere()] + [on_chip()] * 4,
         out_specs=(on_chip(), on_chip(), anywhere()),
-        scratch_shapes=[dma((groups,)), dma((groups,)), dma((13,)), dma((13,)), dma(())],
+        scratch_shapes=[
+            pltpu.VMEM((groups, groups, rows // groups, 768), BF16),
+            pltpu.VMEM((2, rows, width), BF16),
+            dma((2,)),
+            dma((groups,)),
+            dma((groups,)),
+            dma((13,)),
+            dma((13,)),
+            dma(()),
+        ],
         compiler_params=remote_params(2),
-        cost_estimate=pl.CostEstimate(flops=0, bytes_accessed=150_000_000, transcendentals=0),
+        cost_estimate=pl.CostEstimate(flops=0, bytes_accessed=200_000_000, transcendentals=0),
         name="attend_ahead",
-    )(lengths, qkv, slots, flags, cotangent)
-
-
-def feed_kernel(hidden, cotangent, w_both, w_down, both_grad, activated, *, members):
-    rows = hidden[...]
-    grad = lax.dot_general(cotangent[...], w_down[...], NT, preferred_element_type=F32)
-    for part in range(members):
-        raw = jnp.dot(rows, w_both[part], preferred_element_type=F32)
-        gate, upward = raw[:, :128], raw[:, 128:]
-        active_grad = grad[:, part * 128 : part * 128 + 128]
-        sigmoid = jax.nn.sigmoid(gate)
-        activated[:, part * 128 : part * 128 + 128] = (gate * sigmoid * upward).astype(BF16)
-        both_grad[:, part * 256 : part * 256 + 128] = (
-            active_grad * upward * sigmoid * (1.0 + gate * (1.0 - sigmoid))
-        ).astype(BF16)
-        both_grad[:, part * 256 + 128 : part * 256 + 256] = (
-            active_grad * gate * sigmoid
-        ).astype(BF16)
-
-
-def feed(hidden, cotangent, w_both, w_down):
-    count, width = hidden.shape
-    wide = w_both.shape[0] * 256
-    units = w_down.shape[0]
-    tile = 256
-    return pl.pallas_call(
-        functools.partial(feed_kernel, members=wide // 256),
-        grid=(count // tile,),
-        out_shape=(
-            jax.ShapeDtypeStruct((count, wide), BF16),
-            jax.ShapeDtypeStruct((count, units), BF16),
-        ),
-        in_specs=[
-            pl.BlockSpec((tile, width), lambda i: (i, 0)),
-            pl.BlockSpec((tile, width), lambda i: (i, 0)),
-            pl.BlockSpec(w_both.shape, lambda i: (0, 0, 0)),
-            pl.BlockSpec((units, width), lambda i: (0, 0)),
-        ],
-        out_specs=(
-            pl.BlockSpec((tile, wide), lambda i: (i, 0)),
-            pl.BlockSpec((tile, units), lambda i: (i, 0)),
-        ),
-        compiler_params=pltpu.CompilerParams(vmem_limit_bytes=VMEM_LIMIT),
-        cost_estimate=pl.CostEstimate(
-            flops=2 * count * width * (wide + units), bytes_accessed=50_000_000, transcendentals=0
-        ),
-        name="feed",
-    )(hidden, cotangent, w_both, w_down)
+    )(lengths, hidden_all, w_qkv, slots, flags, cotangent)
 
 
 CHUNK = 32
 
 
-def each_chunk(rows, body):
+def each_chunk(rows, body, chunk=CHUNK):
     def step(i, carry):
-        body(pl.ds(pl.multiple_of(i * CHUNK, CHUNK), CHUNK))
+        body(pl.ds(pl.multiple_of(i * chunk, chunk), chunk))
         return carry
 
-    lax.fori_loop(0, rows // CHUNK, step, 0)
+    lax.fori_loop(0, rows // chunk, step, 0)
 
 
 class Reduce:
@@ -831,17 +834,7 @@
 
         def tile(t, carry):
             columns = pl.ds(pl.multiple_of(t * 256, 256), 256)
-            if self.across == 3:
-                value = sum(
-                    lax.dot_general(
-                        self.left[picked, part * 256 : part * 256 + 256],
-                        self.right[part, columns, :],
-                        NT,
-                        preferred_element_type=F32,
-                    )
-                    for part in range(self.right.shape[0])
-                )
-            elif self.across == 2:
+            if self.across:
                 value = lax.dot_general(
                     self.left[picked, :], self.right[columns, :], NT, preferred_element_type=F32
                 )
@@ -993,11 +986,9 @@
         )
 
     def view(self, slot, half, number):
-        if self.views == 1:
-            rows = pl.ds(pl.multiple_of(slot * LANES, LANES), LANES)
-            return self.source.at[rows, pl.ds(half * 896, 896)]
-        columns = pl.ds(pl.multiple_of((2 * number + slot) * LANES, LANES), LANES)
-        return self.source.at[pl.ds(half * 896, 896), columns]
+        rows = pl.ds(pl.multiple_of((2 * number + slot) * LANES, LANES), HEAD_DIM)
+        columns = self.source.shape[1] // 2
+        return self.source.at[rows, pl.ds(pl.multiple_of(half * columns, LANES), columns)]
 
     def each(self, action):
         for slot in range(2):
@@ -1034,16 +1025,7 @@
 
                 @pl.when((z == other) & (self.core == self.owner))
                 def _():
-                    half = self.core
-                    slot = lax.rem(z, 2)
-                    if self.views == 1:
-                        rows = pl.ds(pl.multiple_of(slot * LANES, LANES), LANES)
-                        columns = pl.ds(pl.multiple_of(half * 896, LANES), 896)
-                        self.arrive[other, number] = self.source[rows, columns]
-                    else:
-                        rows = pl.ds(pl.multiple_of(half * 896, LANES), 896)
-                        columns = pl.ds(pl.multiple_of((2 * number + slot) * LANES, LANES), LANES)
-                        self.arrive[other, number] = self.source[rows, columns]
+                    self.arrive[other, number] = self.view(lax.rem(z, 2), self.core, number)[...]
 
             count = self.arrive.shape[2]
 
@@ -1053,7 +1035,7 @@
                     found = found + self.arrive[other, number, span, :].astype(F32)
                 out[number, span, :] = found.astype(BF16)
 
-            each_chunk(count, body)
+            each_chunk(count, body, 16)
 
 
 def to_at(source, target, send_sem, recv_sem, dp, mp):
@@ -1079,7 +1061,7 @@
     greet_all(pltpu.get_barrier_semaphore())
     heads = Heads(proj_sum, arrive, send_h, recv_h, 1)
     heads.start()
-    reduce = Reduce(activated, w_down, 0, part, from_side, from_corner, from_near, send_r, recv_r)
+    reduce = Reduce(activated, w_down, False, part, from_side, from_corner, from_near, send_r, recv_r)
     reduce.begin()
 
     def halo(k, other):
@@ -1172,7 +1154,7 @@
         out_shape=(
             jax.ShapeDtypeStruct((groups, groups, rows // groups, 768), BF16),
             jax.ShapeDtypeStruct((rows, width), BF16),
-            jax.ShapeDtypeStruct((1, LANES, width // 2), BF16),
+            jax.ShapeDtypeStruct((1, HEAD_DIM, width // 2), BF16),
         ),
         in_specs=[in_scalar()] + [on_chip()] * 8,
         out_specs=(on_chip(), on_chip(), on_chip()),
@@ -1187,7 +1169,7 @@
             dma((groups,)),
         ]
         + reduce_scratch(rows, width)
-        + [pltpu.VMEM((4, 1, LANES, width // 2), BF16), dma((4,)), dma((4,))],
+        + [pltpu.VMEM((4, 1, HEAD_DIM, width // 2), BF16), dma((4,)), dma((4,))],
         compiler_params=remote_params(3, 62 * 1024 * 1024),
         cost_estimate=pl.CostEstimate(flops=0, bytes_accessed=200_000_000, transcendentals=0),
         name="attend_back",
@@ -1195,41 +1177,36 @@
 
 
 def middle_kernel(
-    mixed, w_out, tokens, gain, middle, hidden_all,
-    part, from_side, from_corner, from_near, send, recv, own, send_g, recv_g, local,
+    mixed, w_out, tokens, gain, middle, hidden,
+    part, from_side, from_corner, from_near, send, recv,
 ):
     pl.semaphore_wait(greet_plane(), 3)
-    reduce = Reduce(mixed, w_out, 0, part, from_side, from_corner, from_near, send, recv)
+    reduce = Reduce(mixed, w_out, False, part, from_side, from_corner, from_near, send, recv)
     reduce.run()
 
     def body(span):
         values = tokens[span, :].astype(F32) + reduce.rows_of(span)
         middle[span, :] = values
         inverse = lax.rsqrt(mean_rows(values * values) + EPSILON)
-        own[span, :] = (values * inverse * gain[...]).astype(BF16)
-
-    each_chunk(own.shape[0], body)
-    gather = Gather(own, hidden_all, send_g, recv_g, local)
-    gather.start()
-    gather.pass_on()
-    gather.finish()
+        hidden[span, :] = (values * inverse * gain[...]).astype(BF16)
+
+    each_chunk(hidden.shape[0], body)
     reduce.finish()
 
 
 def project_middle(mixed, w_out, tokens, gain):
     rows, width = tokens.shape
-    groups = lax.axis_size("dp")
     return pl.pallas_call(
         middle_kernel,
         out_shape=(
             jax.ShapeDtypeStruct((rows, width), F32),
-            jax.ShapeDtypeStruct((groups, rows, width), BF16),
+            jax.ShapeDtypeStruct((rows, width), BF16),
         ),
         in_specs=[on_chip()] * 4,
-        out_specs=(on_chip(), anywhere()),
-        scratch_shapes=reduce_scratch(rows, width) + gather_scratch(rows, width),
+        out_specs=(on_chip(), on_chip()),
+        scratch_shapes=reduce_scratch(rows, width),
         compiler_params=remote_params(4),
-        cost_estimate=pl.CostEstimate(flops=0, bytes_accessed=300_000_000, transcendentals=0),
+        cost_estimate=pl.CostEstimate(flops=0, bytes_accessed=150_000_000, transcendentals=0),
         name="project_middle",
     )(mixed, w_out, tokens, gain)
 
@@ -1246,58 +1223,287 @@
     return inverse * (scaled - normed * mean_rows(scaled * normed))
 
 
-def branch_kernel(
-    both_grad, w_both, middle, cotangent, gain, middle_grad, branch_all, sums,
-    part, from_side, from_corner, from_near, send, recv, own, send_g, recv_g, local,
+def feed_kernel(
+    hidden_own, cotangent_all, middle, cotangent, gain, w_both, w_down,
+    middle_grad, branch_all, sums, activated, both_sum, down_sum,
+    hidden_all, both_grad, part, from_side, from_corner, from_near, send_r, recv_r,
+    send_a, recv_a, send_b, recv_b, cot_half, cot_tile, stage_both, stage_down, load_sem, local,
 ):
+    groups, rows, width = hidden_all.shape
+    members = w_both.shape[0]
+    half_rows = rows // 2
+    me, side, over_x, over_y, _ = plane()
+    own = pltpu.make_async_copy(hidden_own, hidden_all.at[me], local.at[0])
+    own.start()
+    start_middle = pltpu.make_async_copy(middle, middle_grad, local.at[1])
+    start_middle.start()
+
+    def place_of(step):
+        block = step // 4
+        near = ((block + 1) // 2) % 2
+        far = block // 3
+        mixed_order = near * (1 - block // 2)
+        second = mixed_order * (step % 2) + (1 - mixed_order) * ((step // 2) % 2)
+        half = mixed_order * ((step % 2 + (step // 2) % 2) % 2) + (1 - mixed_order) * (step % 2)
+        other = (1 - near) * second + (block // 2) * near
+        in_x = near * (1 - second) + far
+        in_y = near * second + far
+        owner = me + in_x * (over_x - me) + in_y * (over_y - me) + other * (side - me)
+        slot = 4 * other + 3 * (1 - near) * (1 - far) + near * (1 + second)
+        return owner, half, slot
+
+    def load_cotangent(step):
+        owner, half, _ = place_of(step)
+        span = pl.ds(pl.multiple_of(half * half_rows, half_rows), half_rows)
+        return pltpu.make_async_copy(
+            cotangent_all.at[owner, span], cot_half.at[step % 2], load_sem.at[step % 2]
+        )
+
+    load_cotangent(0).start()
     pl.semaphore_wait(greet_plane(), 3)
-    reduce = Reduce(both_grad, w_both, 3, part, from_side, from_corner, from_near, send, recv)
-    reduce.run()
+    own.wait()
+    gather = Gather(None, hidden_all, send_a, recv_a)
+    gather.start()
+    reduce = Reduce(None, None, False, part, from_side, from_corner, from_near, send_r, recv_r)
+    reduce.prepare()
+
+    def before(step, *numbers):
+        return (step, lambda: gather.arrive(*numbers))
+
+    def nears():
+        reduce.add_side(1)
+        reduce.nears[0].start()
+        reduce.add_side(2)
+        reduce.nears[2].start()
+
+    early = [
+        before(2, 4),
+        before(4, 0),
+        before(5, 1),
+        before(6, 2),
+        before(7, 3),
+        before(8, 6, 9),
+        before(10, 8, 10),
+        before(12, 5, 7),
+        (13, nears),
+        before(14, 11, 12),
+    ]
+    late = [(3, 3), (9, 1), (11, 2), (15, 0)]
+
+    def unit(step, carry):
+        for number, action in early:
+            pl.when(step == number)(action)
+
+        @pl.when(step < 15)
+        def _():
+            load_cotangent(step + 1).start()
+
+        load_cotangent(step).wait()
+        owner, half, slot = place_of(step)
+        span = pl.ds(pl.multiple_of(half * half_rows, half_rows), half_rows)
+        mine = hidden_all[owner, span, :]
+        grads = cot_half[step % 2]
+        for z in range(members):
+            raw = jnp.dot(mine, w_both[z], preferred_element_type=F32)
+            units = pl.ds(z * 128, 128)
+            if z % 2 == 0:
+                pair = lax.dot_general(
+                    grads, w_down[pl.ds(z * 128, 256), :], NT, preferred_element_type=F32
+                )
+            active_grad = pair[:, 128 * (z % 2) : 128 * (z % 2) + 128]
+            gate, upward = raw[:, :128], raw[:, 128:]
+            sigmoid = jax.nn.sigmoid(gate)
+            activated[owner, span, units] = (gate * sigmoid * upward).astype(BF16)
+            both_grad[owner, span, pl.ds(z * 256, 128)] = (
+                active_grad * upward * sigmoid * (1.0 + gate * (1.0 - sigmoid))
+            ).astype(BF16)
+            both_grad[owner, span, pl.ds(z * 256 + 128, 128)] = (
+                active_grad * gate * sigmoid
+            ).astype(BF16)
+
+        def tile(t, inner):
+            columns = pl.ds(pl.multiple_of(t * 256, 256), 256)
+            value = sum(
+                lax.dot_general(
+                    both_grad[owner, span, pl.ds(z * 256, 256)],
+                    w_both[z, columns, :],
+                    NT,
+                    preferred_element_type=F32,
+                )
+                for z in range(members)
+            )
+            part[slot, span, columns] = value.astype(BF16)
+            return inner
+
+        lax.fori_loop(0, width // 256, tile, 0)
+        for number, share in late:
+            pl.when(step == number)(reduce.shares[share].start)
+        return carry
+
+    lax.fori_loop(0, 16, unit, 0)
+
+    def load_tile(t):
+        columns = pl.ds(pl.multiple_of(t * 256, 256), 256)
+        return pltpu.make_async_copy(
+            cotangent_all.at[:, :, columns], cot_tile.at[t % 2], load_sem.at[2 + t % 2]
+        )
+
+    def store_both(t):
+        columns = pl.ds(pl.multiple_of(t * 256, 256), 256)
+        return pltpu.make_async_copy(
+            stage_both.at[t % 2], both_sum.at[:, columns], load_sem.at[4 + t % 2]
+        )
+
+    def store_down(t):
+        columns = pl.ds(pl.multiple_of(t * 256, 256), 256)
+        return pltpu.make_async_copy(
+            stage_down.at[t % 2], down_sum.at[:, columns], load_sem.at[6 + t % 2]
+        )
+
+    tiles = width // 256
+    count = groups * rows
+
+    def weight_tile(t, carry):
+        columns = pl.ds(pl.multiple_of(t * 256, 256), 256)
+
+        @pl.when(t < tiles - 1)
+        def _():
+            load_tile(t + 1).start()
+
+        load_tile(t).wait()
+
+        @pl.when(t >= 2)
+        def _():
+            store_both(t - 2).wait()
+            store_down(t - 2).wait()
+
+        value = lax.dot_general(
+            hidden_all[:, :, columns].reshape(count, 256),
+            both_grad[...].reshape(count, members * 256),
+            TN,
+            preferred_element_type=F32,
+        )
+        for z in range(members):
+            stage_both[t % 2, z] = value[:, z * 256 : z * 256 + 256].astype(BF16)
+        stage_down[t % 2] = lax.dot_general(
+            activated[...].reshape(count, members * 128),
+            cot_tile[t % 2].reshape(count, 256),
+            TN,
+            preferred_element_type=F32,
+        ).astype(BF16)
+        store_both(t).start()
+        store_down(t).start()
+        return carry
+
+    load_tile(0).start()
+    reduce.add_side(0)
+    reduce.corners[0].start()
+    reduce.corners[1].start()
+    lax.fori_loop(0, 4, weight_tile, 0)
+    reduce.middle()
+    lax.fori_loop(4, tiles, weight_tile, 0)
+    reduce.end()
+    start_middle.wait()
     sums[...] = jnp.zeros_like(sums)
+    for copy in reduce.corners:
+        copy.wait_send()
 
     def body(span):
-        change = norm_back_rows(reduce.rows_of(span), middle[span, :], gain[...], sums, span)
+        change = norm_back_rows(reduce.rows_of(span), middle_grad[span, :], gain[...], sums, span)
         total = cotangent[span, :].astype(F32) + change
         middle_grad[span, :] = total
-        own[span, :] = total.astype(BF16)
-
-    each_chunk(own.shape[0], body)
-    gather = Gather(own, branch_all, send_g, recv_g, local)
-    gather.start()
-    gather.pass_on()
-    gather.finish()
-    reduce.finish()
-
-
-def project_branch(both_grad, w_both, middle, cotangent, gain):
-    rows, width = middle.shape
-    groups = lax.axis_size("dp")
+        part[0, span, :] = total.astype(BF16)
+
+    each_chunk(rows, body)
+    branch = Gather(part.at[0], branch_all, send_b, recv_b, local.at[2])
+    branch.start()
+    branch.pass_on()
+    branch.finish()
+    for copy in reduce.shares + reduce.nears:
+        copy.wait_send()
+    gather.sent()
+    for t in (tiles - 2, tiles - 1):
+        store_both(t).wait()
+        store_down(t).wait()
+
+
+def feed(hidden_own, cotangent_all, middle, cotangent, gain, w_both, w_down):
+    groups, rows, width = cotangent_all.shape
+    members = w_both.shape[0]
+    dma = pltpu.SemaphoreType.DMA
+    units = members * 128
     return pl.pallas_call(
-        branch_kernel,
+        feed_kernel,
         out_shape=(
             jax.ShapeDtypeStruct((rows, width), F32),
             jax.ShapeDtypeStruct((groups, rows, width), BF16),
             jax.ShapeDtypeStruct((8, width), F32),
+            jax.ShapeDtypeStruct((groups, rows, units), BF16),
+            jax.ShapeDtypeStruct((members, width, 256), BF16),
+            jax.ShapeDtypeStruct((units, width), BF16),
         ),
-        in_specs=[on_chip()] * 5,
-        out_specs=(on_chip(), anywhere(), on_chip()),
-        scratch_shapes=reduce_scratch(rows, width) + gather_scratch(rows, width),
-        compiler_params=remote_params(5),
-        cost_estimate=pl.CostEstimate(flops=0, bytes_accessed=300_000_000, transcendentals=0),
-        name="project_branch",
-    )(both_grad, w_both, middle, cotangent, gain)
+        in_specs=[anywhere()] * 3 + [on_chip()] * 4,
+        out_specs=(on_chip(), anywhere(), on_chip(), on_chip(), anywhere(), anywhere()),
+        scratch_shapes=[
+            pltpu.VMEM((groups, rows, width), BF16),
+            pltpu.VMEM((groups, rows, 2 * units), BF16),
+        ]
+        + reduce_scratch(rows, width)
+        + [
+            dma((13,)),
+            dma((13,)),
+            dma((13,)),
+            dma((13,)),
+            pltpu.VMEM((2, rows // 2, width), BF16),
+            pltpu.VMEM((2, groups, rows, 256), BF16),
+            pltpu.VMEM((2, members, 256, 256), BF16),
+            pltpu.VMEM((2, units, 256), BF16),
+            dma((8,)),
+            dma((3,)),
+        ],
+        compiler_params=remote_params(5, 62 * 1024 * 1024),
+        cost_estimate=pl.CostEstimate(flops=0, bytes_accessed=400_000_000, transcendentals=0),
+        name="feed",
+    )(hidden_own, cotangent_all, middle, cotangent, gain, w_both, w_down)
 
 
 def input_kernel(
-    qkv_grad, w_qkv, tokens, middle_grad, gain, sums_two, qkv_sum, result, qkv_part, gains,
+    qkv_grad, w_qkv, hidden_all, tokens, middle_grad, gain, sums_two, proj_part, result, heads_part, gains,
     part, from_side, from_corner, from_near, send, recv, sums,
     arrive, send_h, recv_h, own, plane_sums, column_sums, send_s, recv_s,
+    qkv_sum, hidden_tile, tile_sem,
 ):
     me, z = lax.axis_index("dp"), lax.axis_index("mp")
+    count = qkv_grad.shape[0]
+    tiles = tokens.shape[1] // 256
+
+    def load(t):
+        columns = pl.ds(pl.multiple_of(t * 256, 256), 256)
+        return pltpu.make_async_copy(
+            hidden_all.at[:, :, columns], hidden_tile.at[t % 2], tile_sem.at[t % 2]
+        )
+
+    load(0).start()
+
+    def weight_tile(t, carry):
+        columns = pl.ds(pl.multiple_of(t * 256, 256), 256)
+
+        @pl.when(t < tiles - 1)
+        def _():
+            load(t + 1).start()
+
+        load(t).wait()
+        qkv_sum[:, columns] = lax.dot_general(
+            qkv_grad[...], hidden_tile[t % 2].reshape(count, 256), TN, preferred_element_type=F32
+        ).astype(BF16)
+        return carry
+
+    lax.fori_loop(0, tiles, weight_tile, 0)
     greet_all(pltpu.get_barrier_semaphore())
     heads = Heads(qkv_sum, arrive, send_h, recv_h, 3)
     heads.start()
-    reduce = Reduce(qkv_grad, w_qkv, 2, part, from_side, from_corner, from_near, send, recv)
+    heads_part[3] = proj_part[0]
+    reduce = Reduce(qkv_grad, w_qkv, False, part, from_side, from_corner, from_near, send, recv)
     reduce.run()
     sums[...] = jnp.zeros_like(sums)
 
@@ -1339,27 +1545,28 @@
     for copy in passes:
         copy.wait()
     gains[...] = (column_sums[0] + column_sums[1]) + (column_sums[2] + column_sums[3])
-    heads.total(qkv_part)
+    heads.total(heads_part)
     heads.finish_send()
     reduce.finish()
 
 
-def project_input(qkv_grad, w_qkv, tokens, middle_grad, gain, sums_two, qkv_sum):
+def project_input(qkv_grad, w_qkv, hidden_all, tokens, middle_grad, gain, sums_two, proj_part):
     rows, width = tokens.shape
+    groups = hidden_all.shape[0]
     dma = pltpu.SemaphoreType.DMA
     return pl.pallas_call(
         input_kernel,
         out_shape=(
             jax.ShapeDtypeStruct((rows, width), BF16),
-            jax.ShapeDtypeStruct((3, width // 2, LANES), BF16),
+            jax.ShapeDtypeStruct((4, HEAD_DIM, width // 2), BF16),
             jax.ShapeDtypeStruct((2, width), F32),
         ),
-        in_specs=[on_chip()] * 7,
+        in_specs=[on_chip()] * 2 + [anywhere()] + [on_chip()] * 5,
         out_specs=(on_chip(),) * 3,
         scratch_shapes=reduce_scratch(rows, width)
         + [
             pltpu.VMEM((8, width), F32),
-            pltpu.VMEM((4, 3, width // 2, LANES), BF16),
+            pltpu.VMEM((4, 3, HEAD_DIM, width // 2), BF16),
             dma((12,)),
             dma((12,)),
             pltpu.VMEM((2, width), F32),
@@ -1367,11 +1574,37 @@
             pltpu.VMEM((4, 2, width), F32),
             dma((10,)),
             dma((10,)),
+            pltpu.VMEM((6 * LANES, width), BF16),
+            pltpu.VMEM((2, groups, rows, 256), BF16),
+            dma((2,)),
         ],
         compiler_params=remote_params(6),
-        cost_estimate=pl.CostEstimate(flops=0, bytes_accessed=200_000_000, transcendentals=0),
+        cost_estimate=pl.CostEstimate(flops=0, bytes_accessed=250_000_000, transcendentals=0),
         name="project_input",
-    )(qkv_grad, w_qkv, tokens, middle_grad, gain, sums_two, qkv_sum)
+    )(qkv_grad, w_qkv, hidden_all, tokens, middle_grad, gain, sums_two, proj_part)
+
+
+def units_gather_kernel(both, both_all, send, recv, local):
+    pl.semaphore_wait(greet_plane(), 3)
+    gather = Gather(both, both_all, send, recv, local)
+    gather.start()
+    gather.pass_on()
+    gather.finish()
+
+
+def gather_units(part, number):
+    groups = lax.axis_size("dp")
+    dma = pltpu.SemaphoreType.DMA
+    return pl.pallas_call(
+        units_gather_kernel,
+        out_shape=jax.ShapeDtypeStruct((groups,) + part.shape, BF16),
+        in_specs=[on_chip()],
+        out_specs=anywhere(),
+        scratch_shapes=[dma((13,)), dma((13,)), dma(())],
+        compiler_params=remote_params(number),
+        cost_estimate=pl.CostEstimate(flops=0, bytes_accessed=100_000_000, transcendentals=0),
+        name="gather_units",
+    )(part)
 
 
 def units_kernel(both, gate, upward):
@@ -1396,26 +1629,24 @@
     )(both)
 
 
-def heads_kernel(whole, query, keys, values):
-    for part, out in enumerate((query, keys, values)):
-        out[...] = jnp.concatenate(
-            [whole[c, 0, part, :, :HEAD_DIM].astype(F32) for c in range(whole.shape[0])], axis=1
-        )
+def heads_kernel(whole, *outs):
+    columns = whole.shape[4]
+    for kind, out in enumerate(outs):
+        for half in range(whole.shape[1]):
+            out[:, half * columns : half * columns + columns] = whole[0, half, kind].astype(F32)
 
 
 def assemble_heads(whole):
-    chips, halves, _, rows, _ = whole.shape
-    tile = 448
-    count = rows // tile
-    shape = jax.ShapeDtypeStruct((halves * rows, chips * HEAD_DIM), F32)
-    spec = pl.BlockSpec((tile, chips * HEAD_DIM), lambda h, i: (h * count + i, 0))
+    chips, halves, kinds, rows, columns = whole.shape
+    shape = jax.ShapeDtypeStruct((chips * rows, halves * columns), F32)
+    spec = pl.BlockSpec((rows, halves * columns), lambda c: (c, 0))
     return pl.pallas_call(
         heads_kernel,
-        grid=(halves, count),
-        out_shape=(shape,) * 3,
-        in_specs=[pl.BlockSpec((chips, 1, 3, tile, LANES), lambda h, i: (0, h, 0, i, 0))],
-        out_specs=(spec,) * 3,
-        cost_estimate=pl.CostEstimate(flops=0, bytes_accessed=15_000_000, transcendentals=0),
+        grid=(chips,),
+        out_shape=(shape,) * kinds,
+        in_specs=[pl.BlockSpec((1, halves, kinds, rows, columns), lambda c: (c, 0, 0, 0, 0))],
+        out_specs=(spec,) * kinds,
+        cost_estimate=pl.CostEstimate(flops=0, bytes_accessed=20_000_000, transcendentals=0),
         name="assemble_heads",
     )(whole)
 
@@ -1431,8 +1662,6 @@
     rows, width = tokens.shape
     bucket = rows // groups
     units = w_down.shape[0] // groups
-    chip, core = me // 2, me % 2
-    pad_head = LANES - HEAD_DIM
 
     target = route // TOK_DEV
     earlier = jnp.arange(rows, dtype=jnp.int32)
@@ -1450,18 +1679,11 @@
     notes = jnp.concatenate([slots_own, mask_window, lengths[0]])
     notes = jnp.pad(notes, (0, 8 * LANES - notes.shape[0])).reshape(8, LANES)
 
-    def head_columns(weight):
-        head = lax.dynamic_slice_in_dim(weight, chip * HEAD_DIM, HEAD_DIM, 1)
-        return jnp.pad(head, ((0, 0), (0, pad_head)))
-
-    qkv_share = jnp.stack([head_columns(w_query), head_columns(w_key), head_columns(w_value)])
-    out_share = jnp.pad(
-        lax.dynamic_slice_in_dim(w_out, chip * HEAD_DIM, HEAD_DIM, 0), ((0, pad_head), (0, 0))
-    )
-
     normed, _ = norm_rows(tokens_b.astype(F32))
     hidden_own = (normed * norm1_gain).astype(BF16)
-    hidden_one, w_qkv, w_proj, notes_all = gather_first(hidden_own, qkv_share, out_share, notes)
+    hidden_one, w_qkv, w_proj, notes_all = gather_first(
+        hidden_own, w_query.T, w_key.T, w_value.T, w_out, notes
+    )
     notes_all = notes_all.reshape(groups, 8 * LANES)
     slots = (
         notes_all[:, :rows].reshape(groups, groups, bucket).transpose(1, 0, 2).reshape(groups, rows)
@@ -1480,73 +1702,48 @@
     down_all = lax.all_gather(down_own, "mp", axis=0, tiled=True)
 
     count = groups * rows
-    hidden_one = hidden_one.reshape(count, width)
-    qkv = jnp.dot(hidden_one, w_qkv, preferred_element_type=F32).astype(BF16)
     scale = HEAD_DIM ** (-0.5)
     mixed, kept, cotangent_all = attend_ahead(
-        lengths_all,
-        qkv.reshape(groups, groups, bucket, 6 * LANES),
-        slots,
-        flags,
-        cotangent_b,
-        scale,
-    )
-    cotangent_all = cotangent_all.reshape(count, width)
+        lengths_all, hidden_one, w_qkv, slots, flags, cotangent_b, scale
+    )
     mixed = mixed.reshape(count, 2 * LANES)
     middle, hidden_two = project_middle(mixed, w_proj, tokens_b, norm2_gain[None])
-    hidden_two = hidden_two.reshape(count, width)
-    both_grad, activated = feed(hidden_two, cotangent_all, w_both, down_all)
-
-    down_sum = jnp.einsum("tf,td->fd", activated, cotangent_all, preferred_element_type=F32)
-    both_sum = jnp.einsum("td,tf->df", hidden_two, both_grad, preferred_element_type=F32)
-    both_sum = both_sum.astype(BF16).reshape(width, members, 2 * units).transpose(1, 0, 2)
-    down_sum, both_sum, both_grad = lax.optimization_barrier(
-        (down_sum.astype(BF16), both_sum, both_grad)
+    middle_grad, branch_all, sums_two, activated, both_sum, down_sum = feed(
+        hidden_two, cotangent_all, middle, cotangent_b, norm2_gain[None], w_both, down_all
     )
     down_part = lax.psum_scatter(down_sum, "mp", scatter_dimension=0, tiled=True)
     both_part = lax.psum_scatter(both_sum, "mp", scatter_dimension=0)
 
-    middle_grad, branch_all, sums_two = project_branch(
-        both_grad, w_both, middle, cotangent_b, norm2_gain[None]
-    )
-    down_part, both_part, branch_all = lax.optimization_barrier((down_part, both_part, branch_all))
-    both_whole = lax.all_gather(both_part, "dp")
-    down_whole = lax.all_gather(down_part, "dp", axis=0, tiled=True)
-    branch_all = branch_all.reshape(count, width)
+    branch_rows = branch_all.reshape(count, width)
     mixed_grad = jnp.einsum(
-        "td,cd->tc", branch_all, w_proj, preferred_element_type=F32
+        "td,cd->tc", branch_rows, w_proj, preferred_element_type=F32
     ).astype(BF16)
-    proj_sum = jnp.einsum("tc,td->cd", mixed, branch_all, preferred_element_type=F32).astype(BF16)
+    proj_sum = jnp.einsum("tc,td->cd", mixed, branch_rows, preferred_element_type=F32).astype(BF16)
     qkv_grad, output_rows, proj_part = attend_back(
         lengths_all,
         kept,
         mixed_grad.reshape(groups, groups, bucket, 2 * LANES),
         slots,
         flags,
-        activated,
+        activated.reshape(count, units * members),
         down_all,
         middle,
         proj_sum,
         scale,
     )
     qkv_grad = qkv_grad.reshape(count, 6 * LANES)
-    qkv_sum = jnp.einsum("td,tc->dc", hidden_one, qkv_grad, preferred_element_type=F32).astype(BF16)
-    input_rows, qkv_part, gain_sums = project_input(
-        qkv_grad, w_qkv, tokens_b, middle_grad, norm1_gain[None], sums_two, qkv_sum
-    )
-    proj_part, qkv_part, both_whole, down_whole = lax.optimization_barrier(
-        (proj_part, qkv_part, both_whole, down_whole)
-    )
-    chips = groups // 2
-    qkv_whole = lax.all_gather(qkv_part.reshape(3 * width // 2, LANES), "dp")
-    proj_whole = lax.all_gather(proj_part[0], "dp")
+    input_rows, heads_part, gain_sums = project_input(
+        qkv_grad, w_qkv, hidden_one, tokens_b, middle_grad, norm1_gain[None], sums_two, proj_part
+    )
+    down_part, both_part, heads_part = lax.optimization_barrier((down_part, both_part, heads_part))
+    heads_whole = lax.all_gather(heads_part.reshape(4 * HEAD_DIM, width // 2), "dp")
+    both_whole = gather_units(both_part, 7)
+    down_whole = gather_units(down_part, 8)
     gate_grad, up_grad = assemble_units(both_whole)
-    down_grad = down_whole.astype(F32)
-    query_grad, key_grad, value_grad = assemble_heads(
-        qkv_whole.reshape(chips, 2, 3, width // 2, LANES)
-    )
-    proj_grad = proj_whole.reshape(chips, 2, LANES, width // 2)[:, :, :HEAD_DIM]
-    proj_grad = proj_grad.transpose(0, 2, 1, 3).reshape(chips * HEAD_DIM, width).astype(F32)
+    down_grad = down_whole.astype(F32).reshape(groups * units, width)
+    query_grad, key_grad, value_grad, proj_grad = assemble_heads(
+        heads_whole.reshape(groups // 2, 2, 4, HEAD_DIM, width // 2)
+    )
 
     unsort = (((0,), (0,)), ((), ()))
     return (
@@ -1554,9 +1751,9 @@
         lax.dot_general(sort_hot, input_rows, unsort, preferred_element_type=F32).astype(BF16),
         gain_sums[0],
         gain_sums[1],
-        query_grad,
-        key_grad,
-        value_grad,
+        query_grad.T,
+        key_grad.T,
+        value_grad.T,
         proj_grad,
         gate_grad,
         up_grad,

time: 774 us -> 664 us (0.86)
  matrix products: 82.6 us -> 23.8 us
  Pallas kernels: 557 us -> 603 us
  waiting for transfers between devices: 44.1 us -> 3.9 us
  local copies, waits for them, and re-layouts: 43.2 us -> 8.95 us
  starting transfers between devices: 11 us -> 0.42 us
    pallas_call x3 -> x4, Pallas kernels: 148 us -> 255 us  [the longest x1 168 us: feed(): pl.pallas_call(feed_kernel, out_shape=(jax.ShapeDtypeStruct((rows, width)...]
    dot_general x6 -> x2, matrix products: 74.3 us -> 16.9 us  [the longest x1 8.53 us: swapped(): jnp.einsum('tc,td->cd', mixed, branch_rows, preferred_element_type=F32)]
    pallas_call x1, Pallas kernels: 107 us -> 58.8 us  [project_middle(): pl.pallas_call(middle_kernel, out_shape=(jax.ShapeDtypeStruct((rows, widt...]
    all_gather x4 -> x1, waiting for transfers between devices: 42.4 us -> 0.01 us  [swapped(): lax.all_gather(heads_part.reshape(4 * HEAD_DIM, width // 2), 'dp')]
    pallas_call x1, Pallas kernels: 91.6 us -> 63.7 us  [attend_back(): pl.pallas_call(functools.partial(backward_kernel, scale=scale, groups=gro...]
    pallas_call x1, Pallas kernels: 73.7 us -> 97.1 us  [project_input(): pl.pallas_call(input_kernel, out_shape=(jax.ShapeDtypeStruct((rows, width...]
    unnamed x38 -> x27, local copies, waits for them, and re-layouts: 20 us -> 0.31 us
    all_gather x4 -> x1, starting transfers between devices: 10.9 us -> 0.26 us  [swapped(): lax.all_gather(heads_part.reshape(4 * HEAD_DIM, width // 2), 'dp')]
  transfers between devices with their start and end apart: 8 -> 5, of which waited for: 2 -> 1; matrix products, arithmetic and copies ran while one was open for 9% -> 5% of each run, Pallas kernels for 61% -> 56%
where the time goes in v3:
time: 664 us; the launch traced here: 663 us
  Pallas kernels  603 us (91%)
  matrix products  23.8 us (4%)
  between operations  14 us (2%)
  other arithmetic  9.36 us (1%)
  local copies, waits for them, and re-layouts  8.95 us (1%)
    pallas_call x1, Pallas kernels, feed(): pl.pallas_call(feed_kernel, out_shape=(jax.ShapeDtypeStruct((rows, width)...  168 us
    pallas_call x1, Pallas kernels, project_input(): pl.pallas_call(input_kernel, out_shape=(jax.ShapeDtypeStruct((rows, width...  97.1 us
    pallas_call x2, Pallas kernels, gather_units(): pl.pallas_call(units_gather_kernel, out_shape=jax.ShapeDtypeStruct((group...  79.1 us
    pallas_call x1, Pallas kernels, attend_back(): pl.pallas_call(functools.partial(backward_kernel, scale=scale, groups=gro...  63.7 us
    pallas_call x1, Pallas kernels, attend_ahead(): pl.pallas_call(functools.partial(forward_kernel, scale=scale, groups=grou...  60.9 us
    pallas_call x1, Pallas kernels, project_middle(): pl.pallas_call(middle_kernel, out_shape=(jax.ShapeDtypeStruct((rows, widt...  58.8 us
    pallas_call x1, Pallas kernels, gather_first(): pl.pallas_call(first_kernel, out_shape=(jax.ShapeDtypeStruct((groups, row...  57.5 us
  transfers between devices with their start and end apart: 5, of which 1 were waited for; matrix products, arithmetic and copies ran while one was open for 5% of the time, Pallas kernels for 56%

profile of v3, /device:TPU:0, one launch (start us, length us, event | category | flops | bytes accessed | tf_op | source)
XLA Modules:
  0.0 663.3 jit_solution(17752780428597826912)
XLA Ops:
  7.3 0.8 add_select_fusion
  8.5 0.9 fusion
  9.8 0.7 pad_bitcast_fusion.notes
  10.5 1.5 fusion.2.hidden
  12.0 57.5 %gather_first.1 = (bf16[8,384,1792]{2,1,0:T(8,128)(2,1)}, bf16[768,1792]{1,0:T(8,128)(2,1)}, bf16[256,1792]{1,0:T(8,128)(2,1)}, s32[8,8,128]{2,1,0:T(8,128)}) custom-call(bf16[384,1792]{1,0:T(8,128)(2,1)} %fusion.2.hidden, bf16[448,1792]{1,0:T(8,128)(2,1)} %bitcast.42, bf16[448,1792]{1,0:T(8,128)(2,1)} %bitcast.43, bf16[448,1792]{1,0:T(8,128)(2,1)} %bitcast.44, ...), custom_call_target="tpu_custom_call" | custom-call | bytes 200000000 | tf_op jit(solution)/shard_map/gather_first/pallas_call | solution.py:628
  69.5 1.8 constant_dynamic-slice_fusion
  71.4 1.3 constant_dynamic-slice_fusion.1
  72.7 1.0 pad_maximum_fusion
  73.9 0.7 slice.20.lengths
  74.5 0.6 slice.22.flags
  75.2 0.7 reshape.74.slots
  75.9 0.6 broadcast_in_dim.18.gain
  76.5 1.9 convolution_convert_fusion.3.cotangent
  78.4 60.9 %attend_ahead.1 = (bf16[8,8,48,256]{3,2,1,0:T(8,128)(2,1)}, bf16[8,448,768]{2,1,0:T(8,128)(2,1)}, bf16[8,384,1792]{2,1,0:T(8,128)(2,1)}) custom-call(s32[8,3]{1,0:T(8,128)} %slice.20.lengths, bf16[8,384,1792]{2,1,0:T(8,128)(2,1)} %get-tuple-element.47.hidden_all, bf16[768,1792]{1,0:T(8,128)(2,1)} %get-tuple-element.48.w_qkv, s32[8,384]{1,0:T(8,128)} %reshape.74.slots, ...), custom_call_target="tpu_custom_call" | custom-call | bytes 200000000 | tf_op jit(solution)/shard_map/attend_ahead/pallas_call | solution.py:786
  139.4 58.8 %project_middle.1 = (f32[384,1792]{1,0:T(8,128)}, bf16[384,1792]{1,0:T(8,128)(2,1)}) custom-call(bf16[3072,256]{1,0:T(8,128)(2,1)} %bitcast.36, bf16[256,1792]{1,0:T(8,128)(2,1)} %get-tuple-element.51.w_out, bf16[384,1792]{1,0:T(8,128)(2,1)} %copy-done.2, f32[1,1792]{1,0:T(1,128)} %broadcast_in_dim.18.gain), custom_call_target="tpu_custom_call" | custom-call | bytes 150000000 | tf_op jit(solution)/shard_map/project_middle/pallas_call | solution.py:1199
  198.2 3.2 all-gather.9.cloned.1.call-done
  201.4 168.2 %feed.1 = (f32[384,1792]{1,0:T(8,128)}, bf16[8,384,1792]{2,1,0:T(8,128)(2,1)}, f32[8,1792]{1,0:T(8,128)}, bf16[8,384,512]{2,1,0:T(8,128)(2,1)}, bf16[4,1792,256]...) custom-call(bf16[384,1792]{1,0:T(8,128)(2,1)} %get-tuple-element.52.hidden_own, ...), custom_call_target="tpu_custom_call" | custom-call | bytes 400000000 | tf_op jit(solution)/shard_map/feed/pallas_call | solution.py:1435
  369.7 0.5 reduce-scatter.5.cloned.1.call-update
  370.2 0.3 all-gather.7.cloned.1.call-start
  370.5 0.6 broadcast_in_dim.19.gain
  371.1 8.5 %convolution_convert_fusion.5.proj_sum = bf16[256,1792]{1,0:T(8,128)(2,1)} fusion(bf16[3072,256]{1,0:T(8,128)(2,1)S(1)} %bitcast.37, bf16[3072,1792]{1,0:T(8,128)(2,1)} %bitcast.34), kind=kOutput, calls=%fused_computation.11 | convolution fusion | flops 2819031040 | bytes 13500416 | tf_op jit(solution)/shard_map/tc,td->cd/dot_general | solution.py:1721
  379.6 8.4 %convolution_convert_fusion = bf16[3072,256]{1,0:T(8,128)(2,1)} fusion(bf16[3072,1792]{1,0:T(8,128)(2,1)} %bitcast.35, bf16[256,1792]{1,0:T(8,128)(2,1)S(1)} %copy-done.7), kind=kOutput, calls=%fused_computation | convolution fusion | flops 2819358720 | bytes 13500416 | tf_op jit(solution)/shard_map/td,cd->tc/dot_general | solution.py:1718
  388.0 63.7 %attend_back.1 = (bf16[8,8,48,768]{3,2,1,0:T(8,128)(2,1)}, bf16[384,1792]{1,0:T(8,128)(2,1)}, bf16[1,112,896]{2,1,0:T(8,128)(2,1)}) custom-call(s32[8,3]{1,0:T(8,128)} %slice.20.lengths, bf16[8,448,768]{2,1,0:T(8,128)(2,1)} %get-tuple-element.49.kept, bf16[8,8,48,256]{3,2,1,0:T(8,128)(2,1)} %bitcast.45, s32[8,384]{1,0:T(8,128)} %reshape.74.slots, ...), custom_call_target="tpu_custom_call" | custom-call | bytes 200000000 | tf_op jit(solution)/shard_map/attend_back/pallas_call | solution.py:1152
  451.8 97.1 %project_input.1 = (bf16[384,1792]{1,0:T(8,128)(2,1)}, bf16[4,112,896]{2,1,0:T(8,128)(2,1)}, f32[2,1792]{1,0:T(2,128)}) custom-call(bf16[3072,768]{1,0:T(8,128)(2,1)} %bitcast.39, bf16[768,1792]{1,0:T(8,128)(2,1)} %get-tuple-element.48.w_qkv, bf16[8,384,1792]{2,1,0:T(8,128)(2,1)} %get-tuple-element.47.hidden_all, bf16[384,1792]{1,0:T(8,128)(2,1)} %copy-done.2, ...), custom_call_target="tpu_custom_call" | custom-call | bytes 250000000 | tf_op jit(solution)/shard_map/project_input/pallas_call | solution.py:1557
  549.0 1.5 slice_reduce_fusion
  550.4 2.0 convolution_convert_fusion.2
  552.4 2.0 convolution_convert_fusion.1
  554.5 58.2 %gather_units.2.both = bf16[8,1792,256]{2,1,0:T(8,128)(2,1)} custom-call(bf16[1792,256]{1,0:T(8,128)(2,1)} %bitcast.46), custom_call_target="tpu_custom_call" | custom-call | bytes 100000000 | tf_op jit(solution)/shard_map/gather_units/pallas_call | solution.py:1598
  612.6 9.7 %assemble_units.1 = (f32[1792,1024]{1,0:T(8,128)}, f32[1792,1024]{1,0:T(8,128)}) custom-call(bf16[8,1792,256]{2,1,0:T(8,128)(2,1)} %gather_units.2.both), custom_call_target="tpu_custom_call" | custom-call | bytes 22000000 | tf_op jit(solution)/shard_map/assemble_units/pallas_call | solution.py:1621
  622.3 20.9 %gather_units.3 = bf16[8,128,1792]{2,1,0:T(8,128)(2,1)} custom-call(bf16[128,1792]{1,0:T(8,128)(2,1)} %reduce-scatter.3.cloned.1.call-done.both), custom_call_target="tpu_custom_call" | custom-call | bytes 100000000 | tf_op jit(solution)/shard_map/gather_units/pallas_call | solution.py:1598
  643.2 5.6 bitcast_convert_fusion
  648.9 7.9 %assemble_heads.1 = (f32[448,1792]{1,0:T(8,128)}, f32[448,1792]{1,0:T(8,128)}, f32[448,1792]{1,0:T(8,128)}, f32[448,1792]{1,0:T(8,128)}) custom-call(bf16[4,2,4,112,896]{4,3,2,1,0:T(8,128)(2,1)} %bitcast.38), custom_call_target="tpu_custom_call" | custom-call | bytes 20000000 | tf_op jit(solution)/shard_map/assemble_heads/pallas_call | solution.py:1643
  (48 shorter events, 1.2 us)
Async XLA Ops:
  7.2 1.4 copy-start
  7.2 2.5 copy-start.10
  7.2 2.5 copy-start.12
  7.2 3.3 copy-start.8
  7.2 190.9 %all-gather.5.cloned.1.call-start = ((), (), s32[]{:S(2)}) async-start(), calls=%async_computation.2 | async-start | bytes 2293760 | tf_op jit(solution)/shard_map/all_gather | solution.py:1702
  9.5 60.0 %copy-start.2 = (bf16[384,1792]{1,0:T(8,128)(2,1)}, bf16[384,1792]{1,0:T(8,128)(2,1)S(1)}, u32[]{:S(2)}) copy-start(bf16[384,1792]{1,0:T(8,128)(2,1)S(1)} %get-tuple-element.84.tokens) | copy-start | bytes 4128772
  71.3 2.5 copy-start.9
  71.3 4.6 copy-start.11
  71.3 5.2 copy-start.4
  71.3 130.1 %all-gather.9.cloned.1.call-start = ((), (), s32[]{:S(2)}) async-start(), calls=%async_computation.6 | async-start | bytes 4587520 | tf_op jit(solution)/shard_map/all_gather | solution.py:1701
  73.8 475.1 %reduce-scatter.3.cloned.1.call-start = ((), (), s32[]{:S(2)}) async-start(), calls=%async_computation.3 | async-start | bytes 2293760 | tf_op jit(solution)/shard_map/reduce_scatter | solution.py:1714
  369.6 1.5 copy-start.3
  369.7 179.3 %reduce-scatter.5.cloned.1.call-start = ((), (), s32[]{:S(2)}) async-start(), calls=%async_computation.4 | async-start | bytes 4587520 | tf_op jit(solution)/shard_map/reduce_scatter | solution.py:1715
  370.2 278.6 %all-gather.7.cloned.1.call-start = ((), (), s32[]{:S(2)}) async-start(), calls=%async_computation.5 | async-start | bytes 7225344 | tf_op jit(solution)/shard_map/all_gather | solution.py:1739
  371.1 8.5 %copy-start.7 = (bf16[256,1792]{1,0:T(8,128)(2,1)S(1)}, bf16[256,1792]{1,0:T(8,128)(2,1)}, u32[]{:S(2)}) copy-start(bf16[256,1792]{1,0:T(8,128)(2,1)} %get-tuple-element.51.w_out) | copy-start | bytes 2752516
  451.8 98.7 %copy-start.5 = (bf16[384,1792]{1,0:T(8,128)(2,1)S(1)}, bf16[384,1792]{1,0:T(8,128)(2,1)}, u32[]{:S(2)}) copy-start(bf16[384,1792]{1,0:T(8,128)(2,1)} %get-tuple-element.60) | copy-start | bytes 4128772
  548.9 3.6 copy-start.6
  648.9 7.9 %copy-start.1 = (bf16[384,1792]{1,0:T(8,128)(2,1)S(1)}, bf16[384,1792]{1,0:T(8,128)(2,1)}, u32[]{:S(2)}) copy-start(bf16[384,1792]{1,0:T(8,128)(2,1)} %param.14) | copy-start | bytes 4128772
Sparse Core Ops, SparseCore 0:
  71.5 55.2 all-gather.4
  128.9 72.4 all-gather.8
  369.8 46.5 reduce-scatter.2
  418.5 85.9 reduce-scatter.4
  549.1 66.2 all-gather.6

commit v4 on v3

--- a/solution.py
+++ b/solution.py
@@ -557,8 +557,8 @@
 
 
 def first_kernel(
-    hidden, query, keys, values, project, notes,
-    hidden_all, w_qkv, w_out, notes_all,
+    hidden, query, keys, values, project, gate, upward, down, notes,
+    hidden_all, w_qkv, w_out, notes_all, both_own, down_own,
     share, none, send_a, recv_a, send_w, recv_w, send_n, recv_n, local,
 ):
     me = lax.axis_index("dp")
@@ -566,6 +566,12 @@
     loads = [
         pltpu.make_async_copy(source.at[head], share.at[piece], local.at[piece])
         for piece, source in enumerate((query, keys, values, project))
+    ]
+    units = pl.ds(pl.multiple_of(me * LANES, LANES), LANES)
+    loads += [
+        pltpu.make_async_copy(gate.at[:, units], both_own.at[:, pl.ds(0, LANES)], local.at[14]),
+        pltpu.make_async_copy(upward.at[:, units], both_own.at[:, pl.ds(LANES, LANES)], local.at[15]),
+        pltpu.make_async_copy(down.at[units], down_own, local.at[16]),
     ]
     for copy in loads:
         copy.start()
@@ -588,7 +594,7 @@
     ]
     for copy in pads:
         copy.start()
-    for copy in loads:
+    for copy in loads[:4]:
         copy.wait()
     spread = Spread(share, w_qkv, w_out, send_w, recv_w, local)
     spread.start()
@@ -598,7 +604,7 @@
     spread.finish()
     for copy in swaps:
         copy.wait()
-    for copy in pads:
+    for copy in pads + loads[4:]:
         copy.wait()
     keep.wait()
 
@@ -621,7 +627,7 @@
     )
 
 
-def gather_first(hidden, query, keys, values, project, notes):
+def gather_first(hidden, query, keys, values, project, gate, upward, down, notes):
     rows, width = hidden.shape
     groups = lax.axis_size("dp")
     dma = pltpu.SemaphoreType.DMA
@@ -632,18 +638,20 @@
             jax.ShapeDtypeStruct((6 * LANES, width), BF16),
             jax.ShapeDtypeStruct((2 * LANES, width), BF16),
             jax.ShapeDtypeStruct((groups,) + notes.shape, notes.dtype),
+            jax.ShapeDtypeStruct((width, 2 * LANES), BF16),
+            jax.ShapeDtypeStruct((LANES, width), BF16),
         ),
-        in_specs=[on_chip()] + [anywhere()] * 4 + [on_chip()],
-        out_specs=(anywhere(),) * 4,
+        in_specs=[on_chip()] + [anywhere()] * 7 + [on_chip()],
+        out_specs=(anywhere(),) * 4 + (on_chip(),) * 2,
         scratch_shapes=[
             pltpu.VMEM((4, HEAD_DIM, width), BF16),
             pltpu.VMEM((LANES - HEAD_DIM, width), BF16),
-            dma((13,)), dma((13,)), dma((12,)), dma((8,)), dma((7,)), dma((7,)), dma((14,)),
+            dma((13,)), dma((13,)), dma((12,)), dma((8,)), dma((7,)), dma((7,)), dma((17,)),
         ],
         compiler_params=remote_params(1),
         cost_estimate=pl.CostEstimate(flops=0, bytes_accessed=200_000_000, transcendentals=0),
         name="gather_first",
-    )(hidden, query, keys, values, project, notes)
+    )(hidden, query, keys, values, project, gate, upward, down, notes)
 
 
 def one_hot(slots, k, size):
@@ -1224,10 +1232,10 @@
 
 
 def feed_kernel(
-    hidden_own, cotangent_all, middle, cotangent, gain, w_both, w_down,
-    middle_grad, branch_all, sums, activated, both_sum, down_sum,
+    hidden_own, cotangent_all, middle, cotangent, gain, w_both, w_down, mixed, w_out,
+    middle_grad, mixed_grad, sums, activated, both_sum, down_sum, proj_sum,
     hidden_all, both_grad, part, from_side, from_corner, from_near, send_r, recv_r,
-    send_a, recv_a, send_b, recv_b, cot_half, cot_tile, stage_both, stage_down, load_sem, local,
+    send_a, recv_a, send_b, recv_b, cot_half, cot_tile, stage_both, stage_down, load_sem, local, ready,
 ):
     groups, rows, width = hidden_all.shape
     members = w_both.shape[0]
@@ -1405,29 +1413,67 @@
     reduce.end()
     start_middle.wait()
     sums[...] = jnp.zeros_like(sums)
-    for copy in reduce.corners:
-        copy.wait_send()
+
+    gather.sent()
+    for other in (side, over_x, over_y):
+        pl.semaphore_signal(ready, inc=1, device_id={"dp": other}, device_id_type=MESH)
 
     def body(span):
         change = norm_back_rows(reduce.rows_of(span), middle_grad[span, :], gain[...], sums, span)
         total = cotangent[span, :].astype(F32) + change
         middle_grad[span, :] = total
-        part[0, span, :] = total.astype(BF16)
+        hidden_all[me, span, :] = total.astype(BF16)
 
     each_chunk(rows, body)
-    branch = Gather(part.at[0], branch_all, send_b, recv_b, local.at[2])
+    pl.semaphore_wait(ready, 3)
+    branch = Gather(None, hidden_all, send_b, recv_b)
     branch.start()
-    branch.pass_on()
-    branch.finish()
-    for copy in reduce.shares + reduce.nears:
-        copy.wait_send()
-    gather.sent()
+    arrivals = [
+        (1, (4,)),
+        (2, (0, 1, 2)),
+        (3, (3,)),
+        (4, (6, 9)),
+        (5, (8, 10)),
+        (6, (5, 7)),
+        (7, (11, 12)),
+    ]
+
+    def spread_back(turn, carry):
+        for number, numbers in arrivals:
+            pl.when(turn == number)(functools.partial(branch.arrive, *numbers))
+        block = turn // 2
+        near = ((block + 1) // 2) % 2
+        far = block // 3
+        second = turn % 2
+        other = (1 - near) * second + (block // 2) * near
+        owner = me + (near * (1 - second) + far) * (over_x - me)
+        owner = owner + (near * second + far) * (over_y - me) + other * (side - me)
+        mixed_grad[owner] = lax.dot_general(
+            hidden_all[owner], w_out[...], NT, preferred_element_type=F32
+        ).astype(BF16)
+        return carry
+
+    lax.fori_loop(0, 8, spread_back, 0)
+
+    def project_tile(t, carry):
+        columns = pl.ds(pl.multiple_of(t * 256, 256), 256)
+        proj_sum[:, columns] = lax.dot_general(
+            mixed[...],
+            hidden_all[:, :, columns].reshape(count, 256),
+            TN,
+            preferred_element_type=F32,
+        ).astype(BF16)
+        return carry
+
+    lax.fori_loop(0, tiles, project_tile, 0)
+    branch.sent()
+    reduce.finish()
     for t in (tiles - 2, tiles - 1):
         store_both(t).wait()
         store_down(t).wait()
 
 
-def feed(hidden_own, cotangent_all, middle, cotangent, gain, w_both, w_down):
+def feed(hidden_own, cotangent_all, middle, cotangent, gain, w_both, w_down, mixed, w_out):
     groups, rows, width = cotangent_all.shape
     members = w_both.shape[0]
     dma = pltpu.SemaphoreType.DMA
@@ -1436,14 +1482,15 @@
         feed_kernel,
         out_shape=(
             jax.ShapeDtypeStruct((rows, width), F32),
-            jax.ShapeDtypeStruct((groups, rows, width), BF16),
+            jax.ShapeDtypeStruct((groups, rows, 2 * LANES), BF16),
             jax.ShapeDtypeStruct((8, width), F32),
             jax.ShapeDtypeStruct((groups, rows, units), BF16),
             jax.ShapeDtypeStruct((members, width, 256), BF16),
             jax.ShapeDtypeStruct((units, width), BF16),
+            jax.ShapeDtypeStruct((2 * LANES, width), BF16),
         ),
-        in_specs=[anywhere()] * 3 + [on_chip()] * 4,
-        out_specs=(on_chip(), anywhere(), on_chip(), on_chip(), anywhere(), anywhere()),
+        in_specs=[anywhere()] * 3 + [on_chip()] * 6,
+        out_specs=(on_chip(),) * 4 + (anywhere(),) * 2 + (on_chip(),),
         scratch_shapes=[
             pltpu.VMEM((groups, rows, width), BF16),
             pltpu.VMEM((groups, rows, 2 * units), BF16),
@@ -1459,19 +1506,21 @@
             pltpu.VMEM((2, members, 256, 256), BF16),
             pltpu.VMEM((2, units, 256), BF16),
             dma((8,)),
-            dma((3,)),
+            dma((2,)),
+            pltpu.SemaphoreType.REGULAR,
         ],
         compiler_params=remote_params(5, 62 * 1024 * 1024),
         cost_estimate=pl.CostEstimate(flops=0, bytes_accessed=400_000_000, transcendentals=0),
         name="feed",
-    )(hidden_own, cotangent_all, middle, cotangent, gain, w_both, w_down)
+    )(hidden_own, cotangent_all, middle, cotangent, gain, w_both, w_down, mixed, w_out)
 
 
 def input_kernel(
-    qkv_grad, w_qkv, hidden_all, tokens, middle_grad, gain, sums_two, proj_part, result, heads_part, gains,
+    qkv_grad, w_qkv, hidden_all, tokens, middle_grad, gain, sums_two, proj_part, down_part,
+    result, heads_part, gains, down_all,
     part, from_side, from_corner, from_near, send, recv, sums,
     arrive, send_h, recv_h, own, plane_sums, column_sums, send_s, recv_s,
-    qkv_sum, hidden_tile, tile_sem,
+    qkv_sum, hidden_tile, tile_sem, send_g, recv_g, local,
 ):
     me, z = lax.axis_index("dp"), lax.axis_index("mp")
     count = qkv_grad.shape[0]
@@ -1498,8 +1547,11 @@
         ).astype(BF16)
         return carry
 
+    greet_all(pltpu.get_barrier_semaphore())
+    down = Gather(down_part, down_all, send_g, recv_g, local)
+    down.start()
     lax.fori_loop(0, tiles, weight_tile, 0)
-    greet_all(pltpu.get_barrier_semaphore())
+    down.pass_on()
     heads = Heads(qkv_sum, arrive, send_h, recv_h, 3)
     heads.start()
     heads_part[3] = proj_part[0]
@@ -1524,6 +1576,7 @@
     for copy in swaps:
         copy.start()
     plane_sums[me] = own[...]
+    down.finish()
     for copy in swaps:
         copy.wait()
     found = plane_sums[0]
@@ -1542,15 +1595,17 @@
     ]
     for copy in passes:
         copy.start()
+    heads.total(heads_part)
     for copy in passes:
         copy.wait()
     gains[...] = (column_sums[0] + column_sums[1]) + (column_sums[2] + column_sums[3])
-    heads.total(heads_part)
     heads.finish_send()
     reduce.finish()
 
 
-def project_input(qkv_grad, w_qkv, hidden_all, tokens, middle_grad, gain, sums_two, proj_part):
+def project_input(
+    qkv_grad, w_qkv, hidden_all, tokens, middle_grad, gain, sums_two, proj_part, down_part
+):
     rows, width = tokens.shape
     groups = hidden_all.shape[0]
     dma = pltpu.SemaphoreType.DMA
@@ -1560,9 +1615,10 @@
             jax.ShapeDtypeStruct((rows, width), BF16),
             jax.ShapeDtypeStruct((4, HEAD_DIM, width // 2), BF16),
             jax.ShapeDtypeStruct((2, width), F32),
+            jax.ShapeDtypeStruct((groups,) + down_part.shape, BF16),
         ),
-        in_specs=[on_chip()] * 2 + [anywhere()] + [on_chip()] * 5,
-        out_specs=(on_chip(),) * 3,
+        in_specs=[on_chip()] * 2 + [anywhere()] + [on_chip()] * 6,
+        out_specs=(on_chip(),) * 3 + (anywhere(),),
         scratch_shapes=reduce_scratch(rows, width)
         + [
             pltpu.VMEM((8, width), F32),
@@ -1577,11 +1633,14 @@
             pltpu.VMEM((6 * LANES, width), BF16),
             pltpu.VMEM((2, groups, rows, 256), BF16),
             dma((2,)),
+            dma((13,)),
+            dma((13,)),
+            dma(()),
         ],
         compiler_params=remote_params(6),
         cost_estimate=pl.CostEstimate(flops=0, bytes_accessed=250_000_000, transcendentals=0),
         name="project_input",
-    )(qkv_grad, w_qkv, hidden_all, tokens, middle_grad, gain, sums_two, proj_part)
+    )(qkv_grad, w_qkv, hidden_all, tokens, middle_grad, gain, sums_two, proj_part, down_part)
 
 
 def units_gather_kernel(both, both_all, send, recv, local):
@@ -1681,8 +1740,8 @@
 
     normed, _ = norm_rows(tokens_b.astype(F32))
     hidden_own = (normed * norm1_gain).astype(BF16)
-    hidden_one, w_qkv, w_proj, notes_all = gather_first(
-        hidden_own, w_query.T, w_key.T, w_value.T, w_out, notes
+    hidden_one, w_qkv, w_proj, notes_all, both_own, down_own = gather_first(
+        hidden_own, w_query.T, w_key.T, w_value.T, w_out, w_gate, w_up, w_down, notes
     )
     notes_all = notes_all.reshape(groups, 8 * LANES)
     slots = (
@@ -1691,13 +1750,6 @@
     flags = notes_all[:, rows : 2 * rows + WINDOW]
     lengths_all = notes_all[:, 2 * rows + WINDOW : 2 * rows + WINDOW + 3]
 
-    w_gate, w_up, w_down, hidden_one = lax.optimization_barrier((w_gate, w_up, w_down, hidden_one))
-
-    def unit_columns(weight):
-        return lax.dynamic_slice_in_dim(weight, me * units, units, 1)
-
-    both_own = jnp.concatenate([unit_columns(w_gate), unit_columns(w_up)], axis=1)
-    down_own = lax.dynamic_slice_in_dim(w_down, me * units, units, 0)
     w_both = lax.all_gather(both_own, "mp")
     down_all = lax.all_gather(down_own, "mp", axis=0, tiled=True)
 
@@ -1708,17 +1760,20 @@
     )
     mixed = mixed.reshape(count, 2 * LANES)
     middle, hidden_two = project_middle(mixed, w_proj, tokens_b, norm2_gain[None])
-    middle_grad, branch_all, sums_two, activated, both_sum, down_sum = feed(
-        hidden_two, cotangent_all, middle, cotangent_b, norm2_gain[None], w_both, down_all
+    middle_grad, mixed_grad, sums_two, activated, both_sum, down_sum, proj_sum = feed(
+        hidden_two,
+        cotangent_all,
+        middle,
+        cotangent_b,
+        norm2_gain[None],
+        w_both,
+        down_all,
+        mixed,
+        w_proj,
     )
     down_part = lax.psum_scatter(down_sum, "mp", scatter_dimension=0, tiled=True)
     both_part = lax.psum_scatter(both_sum, "mp", scatter_dimension=0)
 
-    branch_rows = branch_all.reshape(count, width)
-    mixed_grad = jnp.einsum(
-        "td,cd->tc", branch_rows, w_proj, preferred_element_type=F32
-    ).astype(BF16)
-    proj_sum = jnp.einsum("tc,td->cd", mixed, branch_rows, preferred_element_type=F32).astype(BF16)
     qkv_grad, output_rows, proj_part = attend_back(
         lengths_all,
         kept,
@@ -1732,13 +1787,20 @@
         scale,
     )
     qkv_grad = qkv_grad.reshape(count, 6 * LANES)
-    input_rows, heads_part, gain_sums = project_input(
-        qkv_grad, w_qkv, hidden_one, tokens_b, middle_grad, norm1_gain[None], sums_two, proj_part
-    )
-    down_part, both_part, heads_part = lax.optimization_barrier((down_part, both_part, heads_part))
+    input_rows, heads_part, gain_sums, down_whole = project_input(
+        qkv_grad,
+        w_qkv,
+        hidden_one,
+        tokens_b,
+        middle_grad,
+        norm1_gain[None],
+        sums_two,
+        proj_part,
+        down_part,
+    )
+    both_part, heads_part = lax.optimization_barrier((both_part, heads_part))
     heads_whole = lax.all_gather(heads_part.reshape(4 * HEAD_DIM, width // 2), "dp")
     both_whole = gather_units(both_part, 7)
-    down_whole = gather_units(down_part, 8)
     gate_grad, up_grad = assemble_units(both_whole)
     down_grad = down_whole.astype(F32).reshape(groups * units, width)
     query_grad, key_grad, value_grad, proj_grad = assemble_heads(

time: 664 us -> 649 us (0.977)
  matrix products: 23.8 us -> 6.9 us
  Pallas kernels: 603 us -> 610 us
    pallas_call x2 -> x1, Pallas kernels: 79.1 us -> 56.2 us  [gather_units(): pl.pallas_call(units_gather_kernel, out_shape=jax.ShapeDtypeStruct((group...]
    pallas_call x1, Pallas kernels: 97.1 us -> 120 us  [project_input(): pl.pallas_call(input_kernel, out_shape=(jax.ShapeDtypeStruct((rows, width...]
    dot_general x2 -> x0, matrix products: 16.9 us -> none  [the longest x1 8.53 us: swapped(): jnp.einsum('tc,td->cd', mixed, branch_rows, preferred_element_type=F32)]
  transfers between devices with their start and end apart: 5 -> 5, of which waited for: 1 -> 1; matrix products, arithmetic and copies ran while one was open for 5% -> 2% of each run, Pallas kernels for 56% -> 57%
where the time goes in v4:
time: 649 us; the launch traced here: 648 us
  Pallas kernels  610 us (94%)
  between operations  14 us (2%)
  matrix products  6.9 us (1%)
  other arithmetic  6.54 us (1%)
    pallas_call x1, Pallas kernels, feed(): pl.pallas_call(feed_kernel, out_shape=(jax.ShapeDtypeStruct((rows, width)...  174 us
    pallas_call x1, Pallas kernels, project_input(): pl.pallas_call(input_kernel, out_shape=(jax.ShapeDtypeStruct((rows, width...  120 us
    pallas_call x1, Pallas kernels, attend_back(): pl.pallas_call(functools.partial(backward_kernel, scale=scale, groups=gro...  63.9 us
    pallas_call x1, Pallas kernels, attend_ahead(): pl.pallas_call(functools.partial(forward_kernel, scale=scale, groups=grou...  60.7 us
    pallas_call x1, Pallas kernels, project_middle(): pl.pallas_call(middle_kernel, out_shape=(jax.ShapeDtypeStruct((rows, widt...  58.8 us
    pallas_call x1, Pallas kernels, gather_first(): pl.pallas_call(first_kernel, out_shape=(jax.ShapeDtypeStruct((groups, row...  58.8 us
    pallas_call x1, Pallas kernels, gather_units(): pl.pallas_call(units_gather_kernel, out_shape=jax.ShapeDtypeStruct((group...  56.2 us
  transfers between devices with their start and end apart: 5, of which 1 were waited for; matrix products, arithmetic and copies ran while one was open for 2% of the time, Pallas kernels for 57%

profile of v4, /device:TPU:0, one launch (start us, length us, event | category | flops | bytes accessed | tf_op | source)
XLA Modules:
  0.0 648.2 jit_solution(13819174314701568999)
XLA Ops:
  7.3 0.8 add_select_fusion
  8.1 0.2 convert_reduce_fusion
  8.3 0.2 copy-done
  8.5 0.9 fusion
  9.5 0.1 select_reduce_fusion
  9.7 0.1 pad_dynamic-slice_fusion
  9.8 0.7 pad_bitcast_fusion.notes
  10.5 1.5 fusion.2.hidden
  12.0 58.8 %gather_first.1 = (bf16[8,384,1792]{2,1,0:T(8,128)(2,1)}, bf16[768,1792]{1,0:T(8,128)(2,1)}, bf16[256,1792]{1,0:T(8,128)(2,1)}, s32[8,8,128]{2,1,0:T(8,128)}, bf...) custom-call(bf16[384,1792]{1,0:T(8,128)(2,1)} %fusion.2.hidden, bf16[448,1792]{1,0:T(8,128)(2,1)} %bitcast.35, ...), custom_call_target="tpu_custom_call" | custom-call | bytes 200000000 | tf_op jit(solution)/shard_map/gather_first/pallas_call | solution.py:634
  70.9 0.7 all-gather.9.cloned.1.call-update
  71.7 0.8 copy.30
  72.4 0.7 slice.20.lengths
  73.1 0.6 slice.22.flags
  73.8 0.7 reshape.71.slots
  74.5 0.6 broadcast_in_dim.18.gain
  75.1 1.9 convolution_convert_fusion.2.cotangent
  77.0 60.7 %attend_ahead.1 = (bf16[8,8,48,256]{3,2,1,0:T(8,128)(2,1)}, bf16[8,448,768]{2,1,0:T(8,128)(2,1)}, bf16[8,384,1792]{2,1,0:T(8,128)(2,1)}) custom-call(s32[8,3]{1,0:T(8,128)} %slice.20.lengths, bf16[8,384,1792]{2,1,0:T(8,128)(2,1)} %get-tuple-element.45.hidden_all, bf16[768,1792]{1,0:T(8,128)(2,1)} %get-tuple-element.46.w_qkv, s32[8,384]{1,0:T(8,128)} %reshape.71.slots, ...), custom_call_target="tpu_custom_call" | custom-call | bytes 200000000 | tf_op jit(solution)/shard_map/attend_ahead/pallas_call | solution.py:794
  137.7 58.8 %project_middle.1 = (f32[384,1792]{1,0:T(8,128)}, bf16[384,1792]{1,0:T(8,128)(2,1)}) custom-call(bf16[3072,256]{1,0:T(8,128)(2,1)} %bitcast.30, bf16[256,1792]{1,0:T(8,128)(2,1)} %get-tuple-element.49.w_out, bf16[384,1792]{1,0:T(8,128)(2,1)} %copy-done.2, f32[1,1792]{1,0:T(1,128)} %broadcast_in_dim.18.gain), custom_call_target="tpu_custom_call" | custom-call | bytes 150000000 | tf_op jit(solution)/shard_map/project_middle/pallas_call | solution.py:1207
  196.6 3.7 all-gather.9.cloned.1.call-done
  200.3 173.6 %feed.1 = (f32[384,1792]{1,0:T(8,128)}, bf16[8,384,256]{2,1,0:T(8,128)(2,1)}, f32[8,1792]{1,0:T(8,128)}, bf16[8,384,512]{2,1,0:T(8,128)(2,1)}, bf16[4,1792,256]{...) custom-call(bf16[384,1792]{1,0:T(8,128)(2,1)} %get-tuple-element.50.hidden_own, ...), custom_call_target="tpu_custom_call" | custom-call | bytes 400000000 | tf_op jit(solution)/shard_map/feed/pallas_call | solution.py:1481
  374.0 0.5 reduce-scatter.5.cloned.1.call-update
  374.5 0.3 all-gather.7.cloned.1.call-start
  374.8 0.6 broadcast_in_dim.19.gain
  375.4 63.9 %attend_back.1 = (bf16[8,8,48,768]{3,2,1,0:T(8,128)(2,1)}, bf16[384,1792]{1,0:T(8,128)(2,1)}, bf16[1,112,896]{2,1,0:T(8,128)(2,1)}) custom-call(s32[8,3]{1,0:T(8,128)} %slice.20.lengths, bf16[8,448,768]{2,1,0:T(8,128)(2,1)} %get-tuple-element.47.kept, bf16[8,8,48,256]{3,2,1,0:T(8,128)(2,1)} %bitcast.38, s32[8,384]{1,0:T(8,128)} %reshape.71.slots, ...), custom_call_target="tpu_custom_call" | custom-call | bytes 200000000 | tf_op jit(solution)/shard_map/attend_back/pallas_call | solution.py:1160
  439.4 119.9 %project_input.1 = (bf16[384,1792]{1,0:T(8,128)(2,1)}, bf16[4,112,896]{2,1,0:T(8,128)(2,1)}, f32[2,1792]{1,0:T(2,128)}, bf16[8,128,1792]{2,1,0:T(8,128)(2,1)}) custom-call(bf16[3072,768]{1,0:T(8,128)(2,1)} %bitcast.32, bf16[768,1792]{1,0:T(8,128)(2,1)} %get-tuple-element.46.w_qkv, bf16[8,384,1792]{2,1,0:T(8,128)(2,1)} %get-tuple-element.45.hidden_all, ...), custom_call_target="tpu_custom_call" | custom-call | bytes 250000000 | tf_op jit(solution)/shard_map/project_input/pallas_call | solution.py:1612
  559.4 2.0 convolution_convert_fusion.1
  561.4 0.6 slice_reduce_fusion
  562.0 2.0 convolution_convert_fusion
  564.0 3.8 bitcast_convert_fusion
  567.8 56.2 %gather_units.1.both = bf16[8,1792,256]{2,1,0:T(8,128)(2,1)} custom-call(bf16[1792,256]{1,0:T(8,128)(2,1)} %bitcast.39), custom_call_target="tpu_custom_call" | custom-call | bytes 100000000 | tf_op jit(solution)/shard_map/gather_units/pallas_call | solution.py:1657
  624.0 9.7 %assemble_units.1 = (f32[1792,1024]{1,0:T(8,128)}, f32[1792,1024]{1,0:T(8,128)}) custom-call(bf16[8,1792,256]{2,1,0:T(8,128)(2,1)} %gather_units.1.both), custom_call_target="tpu_custom_call" | custom-call | bytes 22000000 | tf_op jit(solution)/shard_map/assemble_units/pallas_call | solution.py:1680
  633.7 7.9 %assemble_heads.1 = (f32[448,1792]{1,0:T(8,128)}, f32[448,1792]{1,0:T(8,128)}, f32[448,1792]{1,0:T(8,128)}, f32[448,1792]{1,0:T(8,128)}) custom-call(bf16[4,2,4,112,896]{4,3,2,1,0:T(8,128)(2,1)} %bitcast.29), custom_call_target="tpu_custom_call" | custom-call | bytes 20000000 | tf_op jit(solution)/shard_map/assemble_heads/pallas_call | solution.py:1702
  (40 shorter events, 0.5 us)
Async XLA Ops:
  7.2 1.4 copy-start
  7.2 2.5 copy-start.9
  7.2 2.5 copy-start.11
  7.2 3.3 copy-start.7
  7.2 189.4 %all-gather.5.cloned.1.call-start = ((), (), s32[]{:S(2)}) async-start(), calls=%async_computation.2 | async-start | bytes 2293760 | tf_op jit(solution)/shard_map/all_gather | solution.py:1754
  9.5 61.3 %copy-start.2 = (bf16[384,1792]{1,0:T(8,128)(2,1)}, bf16[384,1792]{1,0:T(8,128)(2,1)S(1)}, u32[]{:S(2)}) copy-start(bf16[384,1792]{1,0:T(8,128)(2,1)S(1)} %get-tuple-element.82.tokens) | copy-start | bytes 4128772
  12.0 62.5 %copy-start.10 = (f32[1792]{0:T(1024)S(1)}, f32[1792]{0:T(1024)}, u32[]{:S(2)}) copy-start(f32[1792]{0:T(1024)} %param.20) | copy-start | bytes 21508
  12.0 63.1 %copy-start.4 = (bf16[384,1792]{1,0:T(8,128)(2,1)S(1)}, bf16[384,1792]{1,0:T(8,128)(2,1)}, u32[]{:S(2)}) copy-start(bf16[384,1792]{1,0:T(8,128)(2,1)} %param.15) | copy-start | bytes 4128772
  70.9 129.4 %all-gather.9.cloned.1.call-start = ((), (), s32[]{:S(2)}) async-start(), calls=%async_computation.6 | async-start | bytes 4587520 | tf_op jit(solution)/shard_map/all_gather | solution.py:1753
  71.6 367.8 %reduce-scatter.3.cloned.1.call-start = ((), (), s32[]{:S(2)}) async-start(), calls=%async_computation.3 | async-start | bytes 2293760 | tf_op jit(solution)/shard_map/reduce_scatter | solution.py:1774
  374.0 185.3 %reduce-scatter.5.cloned.1.call-start = ((), (), s32[]{:S(2)}) async-start(), calls=%async_computation.4 | async-start | bytes 4587520 | tf_op jit(solution)/shard_map/reduce_scatter | solution.py:1775
  374.5 259.2 %all-gather.7.cloned.1.call-start = ((), (), s32[]{:S(2)}) async-start(), calls=%async_computation.5 | async-start | bytes 7225344 | tf_op jit(solution)/shard_map/all_gather | solution.py:1802
  439.4 120.0 %copy-start.5 = (bf16[384,1792]{1,0:T(8,128)(2,1)S(1)}, bf16[384,1792]{1,0:T(8,128)(2,1)}, u32[]{:S(2)}) copy-start(bf16[384,1792]{1,0:T(8,128)(2,1)} %get-tuple-element.58) | copy-start | bytes 4128772
  559.3 2.1 copy-start.8
  559.3 2.7 copy-start.6
  559.3 4.7 copy-start.3
  633.7 7.9 %copy-start.1 = (bf16[384,1792]{1,0:T(8,128)(2,1)S(1)}, bf16[384,1792]{1,0:T(8,128)(2,1)}, u32[]{:S(2)}) copy-start(bf16[384,1792]{1,0:T(8,128)(2,1)} %param.14) | copy-start | bytes 4128772
Sparse Core Ops, SparseCore 0:
  71.0 55.2 all-gather.4
  127.9 72.3 all-gather.8
  374.1 59.8 reduce-scatter.2
  436.1 104.2 reduce-scatter.4
  559.5 66.6 all-gather.6

commit v5 on v3

--- a/solution.py
+++ b/solution.py
@@ -381,6 +381,28 @@
     return barrier
 
 
+def owner_at(turn):
+    me, side, over_x, over_y, _ = plane()
+    block = turn // 2
+    near = ((block + 1) // 2) % 2
+    far = block // 3
+    second = turn % 2
+    other = (1 - near) * second + (block // 2) * near
+    owner = me + (near * (1 - second) + far) * (over_x - me)
+    return owner + (near * second + far) * (over_y - me) + other * (side - me)
+
+
+ARRIVALS = (
+    (1, (4,)),
+    (2, (0, 1, 2)),
+    (3, (3,)),
+    (4, (6, 9)),
+    (5, (8, 10)),
+    (6, (5, 7)),
+    (7, (11, 12)),
+)
+
+
 class Gather:
     AFTER = {0: (5, 6), 1: (7, 8), 2: (9,), 3: (10,), 5: (11,), 7: (12,)}
 
@@ -557,8 +579,8 @@
 
 
 def first_kernel(
-    hidden, query, keys, values, project, notes,
-    hidden_all, w_qkv, w_out, notes_all,
+    hidden, query, keys, values, project, gate, upward, down, notes,
+    hidden_all, w_qkv, w_out, notes_all, both_own, down_own,
     share, none, send_a, recv_a, send_w, recv_w, send_n, recv_n, local,
 ):
     me = lax.axis_index("dp")
@@ -566,6 +588,12 @@
     loads = [
         pltpu.make_async_copy(source.at[head], share.at[piece], local.at[piece])
         for piece, source in enumerate((query, keys, values, project))
+    ]
+    units = pl.ds(pl.multiple_of(me * LANES, LANES), LANES)
+    loads += [
+        pltpu.make_async_copy(gate.at[:, units], both_own.at[:, pl.ds(0, LANES)], local.at[14]),
+        pltpu.make_async_copy(upward.at[:, units], both_own.at[:, pl.ds(LANES, LANES)], local.at[15]),
+        pltpu.make_async_copy(down.at[units], down_own, local.at[16]),
     ]
     for copy in loads:
         copy.start()
@@ -588,7 +616,7 @@
     ]
     for copy in pads:
         copy.start()
-    for copy in loads:
+    for copy in loads[:4]:
         copy.wait()
     spread = Spread(share, w_qkv, w_out, send_w, recv_w, local)
     spread.start()
@@ -598,7 +626,7 @@
     spread.finish()
     for copy in swaps:
         copy.wait()
-    for copy in pads:
+    for copy in pads + loads[4:]:
         copy.wait()
     keep.wait()
 
@@ -621,7 +649,7 @@
     )
 
 
-def gather_first(hidden, query, keys, values, project, notes):
+def gather_first(hidden, query, keys, values, project, gate, upward, down, notes):
     rows, width = hidden.shape
     groups = lax.axis_size("dp")
     dma = pltpu.SemaphoreType.DMA
@@ -632,18 +660,20 @@
             jax.ShapeDtypeStruct((6 * LANES, width), BF16),
             jax.ShapeDtypeStruct((2 * LANES, width), BF16),
             jax.ShapeDtypeStruct((groups,) + notes.shape, notes.dtype),
+            jax.ShapeDtypeStruct((width, 2 * LANES), BF16),
+            jax.ShapeDtypeStruct((LANES, width), BF16),
         ),
-        in_specs=[on_chip()] + [anywhere()] * 4 + [on_chip()],
-        out_specs=(anywhere(),) * 4,
+        in_specs=[on_chip()] + [anywhere()] * 7 + [on_chip()],
+        out_specs=(anywhere(),) * 4 + (on_chip(),) * 2,
         scratch_shapes=[
             pltpu.VMEM((4, HEAD_DIM, width), BF16),
             pltpu.VMEM((LANES - HEAD_DIM, width), BF16),
-            dma((13,)), dma((13,)), dma((12,)), dma((8,)), dma((7,)), dma((7,)), dma((14,)),
+            dma((13,)), dma((13,)), dma((12,)), dma((8,)), dma((7,)), dma((7,)), dma((17,)),
         ],
         compiler_params=remote_params(1),
         cost_estimate=pl.CostEstimate(flops=0, bytes_accessed=200_000_000, transcendentals=0),
         name="gather_first",
-    )(hidden, query, keys, values, project, notes)
+    )(hidden, query, keys, values, project, gate, upward, down, notes)
 
 
 def one_hot(slots, k, size):
@@ -890,10 +920,28 @@
 
         each_chunk(self.rows // 2, body)
 
+    def products(self):
+        self.prepare()
+        me, _, over_x, over_y, corner = plane()
+        turn = 1 - 2 * lax.rem(me, 2)
+        for slot, owner in enumerate((corner, over_x, over_y, me)):
+            self.product(owner + turn, 4 + slot)
+            self.shares[slot].start()
+        for slot, owner in enumerate((corner, over_x, over_y, me)):
+            self.product(owner, slot)
+
+    def launch(self):
+        self.add_side(0)
+        self.corners[0].start()
+        self.corners[1].start()
+        self.add_side(1)
+        self.nears[0].start()
+        self.add_side(2)
+        self.nears[2].start()
+
     def begin(self):
         self.prepare()
         me, _, over_x, over_y, corner = plane()
-        owners = (corner, over_x, over_y, me)
         turn = 1 - 2 * lax.rem(me, 2)
         self.product(corner + turn, 4)
         self.shares[0].start()
@@ -1049,20 +1097,194 @@
     )
 
 
+class Units:
+    def __init__(self, both_sum, down_sum, both_in, down_in, both_stage, down_stage, send, recv, local):
+        self.z = lax.axis_index("mp")
+        self.sums = (both_sum, down_sum)
+        self.inputs = (both_in, down_in)
+        self.stages = (both_stage, down_stage)
+        self.send, self.recv, self.local = send, recv, local
+        z = self.z
+        self.outer = (z == 0) | (z == 3)
+        self.far = 3 - z
+        self.near = 1 + lax.div(z, 3)
+        self.second = 3 - self.near
+        self.edge = 3 * (z - 1)
+
+    def part(self, kind, z):
+        if kind == 0:
+            return self.sums[0].at[z]
+        return self.sums[1].at[pl.ds(pl.multiple_of(z * LANES, LANES), LANES)]
+
+    def straight(self, kind, number, target):
+        return to_mp(
+            self.part(kind, target),
+            self.inputs[kind].at[self.z],
+            self.send.at[number * 2 + kind],
+            self.recv.at[self.z * 2 + kind],
+            target,
+        )
+
+    def staged(self, kind):
+        return to_mp(
+            self.part(kind, self.far),
+            self.stages[kind].at[0],
+            self.send.at[4 + kind],
+            self.recv.at[8 + kind],
+            self.near,
+        )
+
+    def summed(self, kind):
+        return to_mp(
+            self.stages[kind].at[1],
+            self.inputs[kind].at[self.z],
+            self.send.at[4 + kind],
+            self.recv.at[self.z * 2 + kind],
+            3 - self.edge,
+        )
+
+    def mine(self, kind):
+        return pltpu.make_async_copy(
+            self.part(kind, 3 - self.edge), self.stages[kind].at[1], self.local.at[kind]
+        )
+
+    def start(self):
+        @pl.when(self.outer)
+        def _():
+            for kind in range(2):
+                self.staged(kind).start()
+            for kind in range(2):
+                self.straight(kind, 0, self.near).start()
+                self.straight(kind, 1, self.second).start()
+
+        @pl.when(jnp.logical_not(self.outer))
+        def _():
+            for kind in range(2):
+                self.mine(kind).start()
+                self.straight(kind, 0, 3 - self.z).start()
+                self.straight(kind, 1, self.edge).start()
+
+    def add(self):
+        @pl.when(jnp.logical_not(self.outer))
+        def _():
+            for kind in range(2):
+                stage = self.stages[kind]
+                self.mine(kind).wait()
+                to_mp(
+                    self.part(kind, 0),
+                    stage.at[0],
+                    self.send.at[4 + kind],
+                    self.recv.at[8 + kind],
+                    self.edge,
+                ).wait_recv()
+
+                def body(span):
+                    stage[1, span, :] = (
+                        stage[0, span, :].astype(F32) + stage[1, span, :].astype(F32)
+                    ).astype(BF16)
+
+                each_chunk(stage.shape[1], body)
+                self.summed(kind).start()
+
+    def arrived(self, kind, source):
+        to_mp(
+            self.part(kind, 0),
+            self.inputs[kind].at[source],
+            self.send.at[kind],
+            self.recv.at[source * 2 + kind],
+            source,
+        ).wait_recv()
+
+    def finish(self):
+        @pl.when(self.outer)
+        def _():
+            for kind in range(2):
+                self.arrived(kind, 1)
+                self.arrived(kind, 2)
+                self.straight(kind, 0, self.near).wait_send()
+                self.straight(kind, 1, self.second).wait_send()
+                self.staged(kind).wait_send()
+
+        @pl.when(jnp.logical_not(self.outer))
+        def _():
+            for kind in range(2):
+                self.arrived(kind, 0)
+                self.arrived(kind, 3)
+                self.arrived(kind, 3 - self.z)
+                self.straight(kind, 0, 3 - self.z).wait_send()
+                self.straight(kind, 1, self.edge).wait_send()
+                self.summed(kind).wait_send()
+
+
 def backward_kernel(
-    lengths, kept, mixed_grad, slots, flags, activated, w_down, middle, proj_sum,
-    out, result, proj_part,
+    lengths, kept, branch, mixed, w_out, slots, flags, activated, w_down, middle, both_sum, down_sum,
+    out, result, proj_part, branch_all, both_in, down_in,
     totals, query_part, key_value, ending, leaving, arriving, send, recv,
     part, from_side, from_corner, from_near, send_r, recv_r, arrive, send_h, recv_h,
+    mixed_grad, proj_sum, shard, branch_tile, load_sem, send_g, recv_g,
+    both_stage, down_stage, send_u, recv_u, local,
     *, scale, groups, rows,
 ):
     z = lax.axis_index("mp")
     members = lax.axis_size("mp")
+    count, width = groups * rows, middle.shape[1]
     greet_all(pltpu.get_barrier_semaphore())
+    units = Units(
+        both_sum, down_sum, both_in, down_in, both_stage, down_stage, send_u, recv_u, local
+    )
+    gather = Gather(branch, branch_all, send_g, recv_g, local.at[2])
+    gather.start()
+    units.start()
+    reduce = Reduce(activated, w_down, False, part, from_side, from_corner, from_near, send_r, recv_r)
+    reduce.products()
+
+    def spread_back(turn, carry):
+        for number, numbers in ARRIVALS:
+            pl.when(turn == number)(functools.partial(gather.arrive, *numbers))
+
+        @pl.when(turn == 0)
+        def _():
+            gather.keep.wait()
+
+        owner = owner_at(turn)
+        load = pltpu.make_async_copy(branch_all.at[owner], shard, load_sem.at[0])
+        load.start()
+        load.wait()
+        mixed_grad[owner] = (
+            lax.dot_general(shard[...], w_out[...], NT, preferred_element_type=F32)
+            .astype(BF16)
+            .reshape(groups, rows // groups, 256)
+        )
+        return carry
+
+    lax.fori_loop(0, 8, spread_back, 0)
+    reduce.launch()
+    units.add()
+
+    def load_tile(t):
+        columns = pl.ds(pl.multiple_of(t * 256, 256), 256)
+        return pltpu.make_async_copy(
+            branch_all.at[:, :, columns], branch_tile.at[t % 2], load_sem.at[1 + t % 2]
+        )
+
+    load_tile(0).start()
+
+    def project_tile(t, carry):
+        columns = pl.ds(pl.multiple_of(t * 256, 256), 256)
+
+        @pl.when(t < width // 256 - 1)
+        def _():
+            load_tile(t + 1).start()
+
+        load_tile(t).wait()
+        proj_sum[:, columns] = lax.dot_general(
+            mixed[...], branch_tile[t % 2].reshape(count, 256), TN, preferred_element_type=F32
+        ).astype(BF16)
+        return carry
+
+    lax.fori_loop(0, width // 256, project_tile, 0)
     heads = Heads(proj_sum, arrive, send_h, recv_h, 1)
     heads.start()
-    reduce = Reduce(activated, w_down, False, part, from_side, from_corner, from_near, send_r, recv_r)
-    reduce.begin()
 
     def halo(k, other):
         return to_mp(leaving.at[k], arriving.at[k], send.at[k], recv.at[k], other)
@@ -1105,9 +1327,9 @@
 
         return carry
 
-    lax.fori_loop(0, groups - 5, attend, 0)
+    lax.fori_loop(0, 3, attend, 0)
     reduce.middle()
-    lax.fori_loop(groups - 5, groups, attend, 0)
+    lax.fori_loop(3, groups, attend, 0)
 
     def restore(k, carry):
         @pl.when(z < members - 1)
@@ -1132,6 +1354,9 @@
     each_chunk(rows, body)
     heads.total(proj_part)
     heads.finish_send()
+    units.finish()
+    for copy in gather.copies:
+        copy.wait_send()
     reduce.finish()
 
     @pl.when(z > 0)
@@ -1144,20 +1369,26 @@
 
 
 def attend_back(
-    lengths, kept, mixed_grad, slots, flags, activated, w_down, middle, proj_sum, scale
+    lengths, kept, branch, mixed, w_out, slots, flags, activated, w_down, middle,
+    both_sum, down_sum, scale,
 ):
     groups = kept.shape[0]
     rows, width = middle.shape
+    members = both_sum.shape[0]
     dma = pltpu.SemaphoreType.DMA
+    shape = jax.ShapeDtypeStruct
     return pl.pallas_call(
         functools.partial(backward_kernel, scale=scale, groups=groups, rows=rows),
         out_shape=(
-            jax.ShapeDtypeStruct((groups, groups, rows // groups, 768), BF16),
-            jax.ShapeDtypeStruct((rows, width), BF16),
-            jax.ShapeDtypeStruct((1, HEAD_DIM, width // 2), BF16),
+            shape((groups, groups, rows // groups, 768), BF16),
+            shape((rows, width), BF16),
+            shape((1, HEAD_DIM, width // 2), BF16),
+            shape((groups, rows, width), BF16),
+            shape((members, width, 256), BF16),
+            shape((members, LANES, width), BF16),
         ),
-        in_specs=[in_scalar()] + [on_chip()] * 8,
-        out_specs=(on_chip(), on_chip(), on_chip()),
+        in_specs=[in_scalar()] + [on_chip()] * 9 + [anywhere()] * 2,
+        out_specs=(on_chip(),) * 3 + (anywhere(),) * 3,
         scratch_shapes=[
             pltpu.VMEM((rows + 64, 512), F32),
             pltpu.VMEM((groups, rows, 256), BF16),
@@ -1169,11 +1400,30 @@
             dma((groups,)),
         ]
         + reduce_scratch(rows, width)
-        + [pltpu.VMEM((4, 1, HEAD_DIM, width // 2), BF16), dma((4,)), dma((4,))],
-        compiler_params=remote_params(3, 62 * 1024 * 1024),
-        cost_estimate=pl.CostEstimate(flops=0, bytes_accessed=200_000_000, transcendentals=0),
+        + [
+            pltpu.VMEM((4, 1, HEAD_DIM, width // 2), BF16),
+            dma((4,)),
+            dma((4,)),
+            pltpu.VMEM((groups, groups, rows // groups, 256), BF16),
+            pltpu.VMEM((2 * LANES, width), BF16),
+            pltpu.VMEM((rows, width), BF16),
+            pltpu.VMEM((2, groups, rows, 256), BF16),
+            dma((3,)),
+            dma((13,)),
+            dma((13,)),
+            pltpu.VMEM((2, width, 256), BF16),
+            pltpu.VMEM((2, LANES, width), BF16),
+            dma((6,)),
+            dma((10,)),
+            dma((3,)),
+        ],
+        compiler_params=remote_params(3, 63 * 1024 * 1024),
+        cost_estimate=pl.CostEstimate(flops=0, bytes_accessed=300_000_000, transcendentals=0),
         name="attend_back",
-    )(lengths, kept, mixed_grad, slots, flags, activated, w_down, middle, proj_sum)
+    )(
+        lengths, kept, branch, mixed, w_out, slots, flags, activated, w_down, middle,
+        both_sum, down_sum,
+    )
 
 
 def middle_kernel(
@@ -1225,9 +1475,9 @@
 
 def feed_kernel(
     hidden_own, cotangent_all, middle, cotangent, gain, w_both, w_down,
-    middle_grad, branch_all, sums, activated, both_sum, down_sum,
+    middle_grad, branch, sums, activated, both_sum, down_sum,
     hidden_all, both_grad, part, from_side, from_corner, from_near, send_r, recv_r,
-    send_a, recv_a, send_b, recv_b, cot_half, cot_tile, stage_both, stage_down, load_sem, local,
+    send_a, recv_a, cot_half, cot_tile, stage_both, stage_down, load_sem, local,
 ):
     groups, rows, width = hidden_all.shape
     members = w_both.shape[0]
@@ -1405,23 +1655,16 @@
     reduce.end()
     start_middle.wait()
     sums[...] = jnp.zeros_like(sums)
-    for copy in reduce.corners:
-        copy.wait_send()
 
     def body(span):
         change = norm_back_rows(reduce.rows_of(span), middle_grad[span, :], gain[...], sums, span)
         total = cotangent[span, :].astype(F32) + change
         middle_grad[span, :] = total
-        part[0, span, :] = total.astype(BF16)
+        branch[span, :] = total.astype(BF16)
 
     each_chunk(rows, body)
-    branch = Gather(part.at[0], branch_all, send_b, recv_b, local.at[2])
-    branch.start()
-    branch.pass_on()
-    branch.finish()
-    for copy in reduce.shares + reduce.nears:
-        copy.wait_send()
     gather.sent()
+    reduce.finish()
     for t in (tiles - 2, tiles - 1):
         store_both(t).wait()
         store_down(t).wait()
@@ -1436,14 +1679,14 @@
         feed_kernel,
         out_shape=(
             jax.ShapeDtypeStruct((rows, width), F32),
-            jax.ShapeDtypeStruct((groups, rows, width), BF16),
+            jax.ShapeDtypeStruct((rows, width), BF16),
             jax.ShapeDtypeStruct((8, width), F32),
             jax.ShapeDtypeStruct((groups, rows, units), BF16),
             jax.ShapeDtypeStruct((members, width, 256), BF16),
             jax.ShapeDtypeStruct((units, width), BF16),
         ),
         in_specs=[anywhere()] * 3 + [on_chip()] * 4,
-        out_specs=(on_chip(), anywhere(), on_chip(), on_chip(), anywhere(), anywhere()),
+        out_specs=(on_chip(),) * 4 + (anywhere(),) * 2,
         scratch_shapes=[
             pltpu.VMEM((groups, rows, width), BF16),
             pltpu.VMEM((groups, rows, 2 * units), BF16),
@@ -1452,14 +1695,12 @@
         + [
             dma((13,)),
             dma((13,)),
-            dma((13,)),
-            dma((13,)),
             pltpu.VMEM((2, rows // 2, width), BF16),
             pltpu.VMEM((2, groups, rows, 256), BF16),
             pltpu.VMEM((2, members, 256, 256), BF16),
             pltpu.VMEM((2, units, 256), BF16),
             dma((8,)),
-            dma((3,)),
+            dma((2,)),
         ],
         compiler_params=remote_params(5, 62 * 1024 * 1024),
         cost_estimate=pl.CostEstimate(flops=0, bytes_accessed=400_000_000, transcendentals=0),
@@ -1468,10 +1709,12 @@
 
 
 def input_kernel(
-    qkv_grad, w_qkv, hidden_all, tokens, middle_grad, gain, sums_two, proj_part, result, heads_part, gains,
+    qkv_grad, w_qkv, hidden_all, tokens, middle_grad, gain, sums_two, proj_part,
+    both_sum, down_sum, both_in, down_in,
+    result, heads_part, gains, both_all, down_all,
     part, from_side, from_corner, from_near, send, recv, sums,
     arrive, send_h, recv_h, own, plane_sums, column_sums, send_s, recv_s,
-    qkv_sum, hidden_tile, tile_sem,
+    qkv_sum, hidden_tile, tile_sem, send_b, recv_b, send_d, recv_d, both_found, down_found, local,
 ):
     me, z = lax.axis_index("dp"), lax.axis_index("mp")
     count = qkv_grad.shape[0]
@@ -1498,13 +1741,64 @@
         ).astype(BF16)
         return carry
 
+    outer = (z == 0) | (z == 3)
+    inner = 3 - z
+    rows_down = pl.ds(pl.multiple_of(z * LANES, LANES), LANES)
+    sources = [(outer, 1), (outer, 2), (z == 1, 0), (z == 1, 2), (z == 1, 3)]
+    sources += [(z == 2, 0), (z == 2, 1), (z == 2, 3)]
+    places = [1, 2, 1, 2, 3, 1, 2, 3]
+
+    def found(source, place):
+        return (
+            pltpu.make_async_copy(both_in.at[source], both_found.at[place], local.at[2 * place]),
+            pltpu.make_async_copy(down_in.at[source], down_found.at[place], local.at[2 * place + 1]),
+        )
+
+    own_parts = (
+        pltpu.make_async_copy(both_sum.at[z], both_found.at[0], local.at[0]),
+        pltpu.make_async_copy(down_sum.at[rows_down], down_found.at[0], local.at[1]),
+    )
+    for copy in own_parts:
+        copy.start()
+    for (here, source), place in zip(sources, places):
+        @pl.when(here)
+        def _():
+            for copy in found(source, place):
+                copy.start()
+
+    @pl.when(outer)
+    def _():
+        both_found[3] = jnp.zeros_like(both_found[3])
+        down_found[3] = jnp.zeros_like(down_found[3])
+
+    greet_all(pltpu.get_barrier_semaphore())
+    reduce = Reduce(qkv_grad, w_qkv, False, part, from_side, from_corner, from_near, send, recv)
+    reduce.begin()
     lax.fori_loop(0, tiles, weight_tile, 0)
-    greet_all(pltpu.get_barrier_semaphore())
     heads = Heads(qkv_sum, arrive, send_h, recv_h, 3)
     heads.start()
     heads_part[3] = proj_part[0]
-    reduce = Reduce(qkv_grad, w_qkv, False, part, from_side, from_corner, from_near, send, recv)
-    reduce.run()
+    reduce.middle()
+    for copy in own_parts:
+        copy.wait()
+    for (here, source), place in zip(sources, places):
+        @pl.when(here)
+        def _():
+            for copy in found(source, place):
+                copy.wait()
+
+    for buffer in (both_found, down_found):
+        def add(span):
+            value = buffer[0, span, :].astype(F32) + buffer[1, span, :].astype(F32)
+            value = value + buffer[2, span, :].astype(F32) + buffer[3, span, :].astype(F32)
+            buffer[0, span, :] = value.astype(BF16)
+
+        each_chunk(buffer.shape[1], add)
+    both = Gather(both_found.at[0], both_all, send_b, recv_b, local.at[8])
+    down = Gather(down_found.at[0], down_all, send_d, recv_d, local.at[9])
+    both.start()
+    down.start()
+    reduce.end()
     sums[...] = jnp.zeros_like(sums)
 
     def body(span):
@@ -1524,6 +1818,8 @@
     for copy in swaps:
         copy.start()
     plane_sums[me] = own[...]
+    both.pass_on()
+    down.pass_on()
     for copy in swaps:
         copy.wait()
     found = plane_sums[0]
@@ -1542,15 +1838,20 @@
     ]
     for copy in passes:
         copy.start()
+    heads.total(heads_part)
     for copy in passes:
         copy.wait()
     gains[...] = (column_sums[0] + column_sums[1]) + (column_sums[2] + column_sums[3])
-    heads.total(heads_part)
+    both.finish()
+    down.finish()
     heads.finish_send()
     reduce.finish()
 
 
-def project_input(qkv_grad, w_qkv, hidden_all, tokens, middle_grad, gain, sums_two, proj_part):
+def project_input(
+    qkv_grad, w_qkv, hidden_all, tokens, middle_grad, gain, sums_two, proj_part,
+    both_sum, down_sum, both_in, down_in,
+):
     rows, width = tokens.shape
     groups = hidden_all.shape[0]
     dma = pltpu.SemaphoreType.DMA
@@ -1560,9 +1861,11 @@
             jax.ShapeDtypeStruct((rows, width), BF16),
             jax.ShapeDtypeStruct((4, HEAD_DIM, width // 2), BF16),
             jax.ShapeDtypeStruct((2, width), F32),
+            jax.ShapeDtypeStruct((groups, width, 256), BF16),
+            jax.ShapeDtypeStruct((groups, LANES, width), BF16),
         ),
-        in_specs=[on_chip()] * 2 + [anywhere()] + [on_chip()] * 5,
-        out_specs=(on_chip(),) * 3,
+        in_specs=[on_chip()] * 2 + [anywhere()] + [on_chip()] * 5 + [anywhere()] * 4,
+        out_specs=(on_chip(),) * 3 + (anywhere(),) * 2,
         scratch_shapes=reduce_scratch(rows, width)
         + [
             pltpu.VMEM((8, width), F32),
@@ -1577,34 +1880,21 @@
             pltpu.VMEM((6 * LANES, width), BF16),
             pltpu.VMEM((2, groups, rows, 256), BF16),
             dma((2,)),
+            dma((13,)),
+            dma((13,)),
+            dma((13,)),
+            dma((13,)),
+            pltpu.VMEM((4, width, 256), BF16),
+            pltpu.VMEM((4, LANES, width), BF16),
+            dma((10,)),
         ],
-        compiler_params=remote_params(6),
+        compiler_params=remote_params(6, 62 * 1024 * 1024),
         cost_estimate=pl.CostEstimate(flops=0, bytes_accessed=250_000_000, transcendentals=0),
         name="project_input",
-    )(qkv_grad, w_qkv, hidden_all, tokens, middle_grad, gain, sums_two, proj_part)
-
-
-def units_gather_kernel(both, both_all, send, recv, local):
-    pl.semaphore_wait(greet_plane(), 3)
-    gather = Gather(both, both_all, send, recv, local)
-    gather.start()
-    gather.pass_on()
-    gather.finish()
-
-
-def gather_units(part, number):
-    groups = lax.axis_size("dp")
-    dma = pltpu.SemaphoreType.DMA
-    return pl.pallas_call(
-        units_gather_kernel,
-        out_shape=jax.ShapeDtypeStruct((groups,) + part.shape, BF16),
-        in_specs=[on_chip()],
-        out_specs=anywhere(),
-        scratch_shapes=[dma((13,)), dma((13,)), dma(())],
-        compiler_params=remote_params(number),
-        cost_estimate=pl.CostEstimate(flops=0, bytes_accessed=100_000_000, transcendentals=0),
-        name="gather_units",
-    )(part)
+    )(
+        qkv_grad, w_qkv, hidden_all, tokens, middle_grad, gain, sums_two, proj_part,
+        both_sum, down_sum, both_in, down_in,
+    )
 
 
 def units_kernel(both, gate, upward):
@@ -1681,8 +1971,8 @@
 
     normed, _ = norm_rows(tokens_b.astype(F32))
     hidden_own = (normed * norm1_gain).astype(BF16)
-    hidden_one, w_qkv, w_proj, notes_all = gather_first(
-        hidden_own, w_query.T, w_key.T, w_value.T, w_out, notes
+    hidden_one, w_qkv, w_proj, notes_all, both_own, down_own = gather_first(
+        hidden_own, w_query.T, w_key.T, w_value.T, w_out, w_gate, w_up, w_down, notes
     )
     notes_all = notes_all.reshape(groups, 8 * LANES)
     slots = (
@@ -1691,13 +1981,6 @@
     flags = notes_all[:, rows : 2 * rows + WINDOW]
     lengths_all = notes_all[:, 2 * rows + WINDOW : 2 * rows + WINDOW + 3]
 
-    w_gate, w_up, w_down, hidden_one = lax.optimization_barrier((w_gate, w_up, w_down, hidden_one))
-
-    def unit_columns(weight):
-        return lax.dynamic_slice_in_dim(weight, me * units, units, 1)
-
-    both_own = jnp.concatenate([unit_columns(w_gate), unit_columns(w_up)], axis=1)
-    down_own = lax.dynamic_slice_in_dim(w_down, me * units, units, 0)
     w_both = lax.all_gather(both_own, "mp")
     down_all = lax.all_gather(down_own, "mp", axis=0, tiled=True)
 
@@ -1708,37 +1991,40 @@
     )
     mixed = mixed.reshape(count, 2 * LANES)
     middle, hidden_two = project_middle(mixed, w_proj, tokens_b, norm2_gain[None])
-    middle_grad, branch_all, sums_two, activated, both_sum, down_sum = feed(
+    middle_grad, branch, sums_two, activated, both_sum, down_sum = feed(
         hidden_two, cotangent_all, middle, cotangent_b, norm2_gain[None], w_both, down_all
     )
-    down_part = lax.psum_scatter(down_sum, "mp", scatter_dimension=0, tiled=True)
-    both_part = lax.psum_scatter(both_sum, "mp", scatter_dimension=0)
-
-    branch_rows = branch_all.reshape(count, width)
-    mixed_grad = jnp.einsum(
-        "td,cd->tc", branch_rows, w_proj, preferred_element_type=F32
-    ).astype(BF16)
-    proj_sum = jnp.einsum("tc,td->cd", mixed, branch_rows, preferred_element_type=F32).astype(BF16)
-    qkv_grad, output_rows, proj_part = attend_back(
+    qkv_grad, output_rows, proj_part, _, both_in, down_in = attend_back(
         lengths_all,
         kept,
-        mixed_grad.reshape(groups, groups, bucket, 2 * LANES),
+        branch,
+        mixed,
+        w_proj,
         slots,
         flags,
         activated.reshape(count, units * members),
         down_all,
         middle,
-        proj_sum,
+        both_sum,
+        down_sum,
         scale,
     )
     qkv_grad = qkv_grad.reshape(count, 6 * LANES)
-    input_rows, heads_part, gain_sums = project_input(
-        qkv_grad, w_qkv, hidden_one, tokens_b, middle_grad, norm1_gain[None], sums_two, proj_part
-    )
-    down_part, both_part, heads_part = lax.optimization_barrier((down_part, both_part, heads_part))
+    input_rows, heads_part, gain_sums, both_whole, down_whole = project_input(
+        qkv_grad,
+        w_qkv,
+        hidden_one,
+        tokens_b,
+        middle_grad,
+        norm1_gain[None],
+        sums_two,
+        proj_part,
+        both_sum,
+        down_sum,
+        both_in,
+        down_in,
+    )
     heads_whole = lax.all_gather(heads_part.reshape(4 * HEAD_DIM, width // 2), "dp")
-    both_whole = gather_units(both_part, 7)
-    down_whole = gather_units(down_part, 8)
     gate_grad, up_grad = assemble_units(both_whole)
     down_grad = down_whole.astype(F32).reshape(groups * units, width)
     query_grad, key_grad, value_grad, proj_grad = assemble_heads(

time: 664 us -> 643 us (0.968)
  waiting for transfers between devices: 3.9 us -> 30.4 us
  Pallas kernels: 603 us -> 577 us
  matrix products: 23.8 us -> 8.26 us
    pallas_call x2 -> x0, Pallas kernels: 79.1 us -> none  [gather_units(): pl.pallas_call(units_gather_kernel, out_shape=jax.ShapeDtypeStruct((group...]
    pallas_call x1, Pallas kernels: 63.7 us -> 136 us  [attend_back(): pl.pallas_call(functools.partial(backward_kernel, scale=scale, groups=gro...]
    pallas_call x1, Pallas kernels: 168 us -> 119 us  [feed(): pl.pallas_call(feed_kernel, out_shape=(jax.ShapeDtypeStruct((rows, width)...]
    pallas_call x1, Pallas kernels: 97.1 us -> 126 us  [project_input(): pl.pallas_call(input_kernel, out_shape=(jax.ShapeDtypeStruct((rows, width...]
    all_gather x1, waiting for transfers between devices: 0.01 us -> 26.6 us  [swapped(): lax.all_gather(heads_part.reshape(4 * HEAD_DIM, width // 2), 'dp')]
    dot_general x2 -> x0, matrix products: 16.9 us -> none  [the longest x1 8.53 us: swapped(): jnp.einsum('tc,td->cd', mixed, branch_rows, preferred_element_type=F32)]
  transfers between devices with their start and end apart: 5 -> 3, of which waited for: 1 -> 2; matrix products, arithmetic and copies ran while one was open for 5% -> 2% of each run, Pallas kernels for 56% -> 20%
where the time goes in v5:
time: 643 us; the launch traced here: 641 us
  Pallas kernels  577 us (90%)
  waiting for transfers between devices  30.4 us (5%)
  between operations  13.9 us (2%)
  matrix products  8.26 us (1%)
  other arithmetic  6.44 us (1%)
    pallas_call x1, Pallas kernels, attend_back(): pl.pallas_call(functools.partial(backward_kernel, scale=scale, groups=gro...  136 us
    pallas_call x1, Pallas kernels, project_input(): pl.pallas_call(input_kernel, out_shape=(jax.ShapeDtypeStruct((rows, width...  126 us
    pallas_call x1, Pallas kernels, feed(): pl.pallas_call(feed_kernel, out_shape=(jax.ShapeDtypeStruct((rows, width)...  119 us
    pallas_call x1, Pallas kernels, attend_ahead(): pl.pallas_call(functools.partial(forward_kernel, scale=scale, groups=grou...  60.8 us
    pallas_call x1, Pallas kernels, gather_first(): pl.pallas_call(first_kernel, out_shape=(jax.ShapeDtypeStruct((groups, row...  58.8 us
    pallas_call x1, Pallas kernels, project_middle(): pl.pallas_call(middle_kernel, out_shape=(jax.ShapeDtypeStruct((rows, widt...  58.7 us
    all_gather x1, waiting for transfers between devices, swapped(): lax.all_gather(heads_part.reshape(4 * HEAD_DIM, width // 2), 'dp')  26.6 us
  transfers between devices with their start and end apart: 3, of which 2 were waited for; matrix products, arithmetic and copies ran while one was open for 2% of the time, Pallas kernels for 20%

profile of v5, /device:TPU:0, one launch (start us, length us, event | category | flops | bytes accessed | tf_op | source)
XLA Modules:
  0.0 641.5 jit_solution(8900483318192890038)
XLA Ops:
  7.3 0.7 add_select_fusion
  8.0 0.2 convert_reduce_fusion
  8.2 2.3 fusion
  10.5 0.1 select_reduce_fusion
  10.7 0.1 pad_dynamic-slice_fusion
  10.7 0.1 pad_add_fusion
  10.8 0.7 pad_bitcast_fusion.notes
  11.5 1.5 fusion.2.hidden
  13.0 58.8 %gather_first.1 = (bf16[8,384,1792]{2,1,0:T(8,128)(2,1)}, bf16[768,1792]{1,0:T(8,128)(2,1)}, bf16[256,1792]{1,0:T(8,128)(2,1)}, s32[8,8,128]{2,1,0:T(8,128)}, bf...) custom-call(bf16[384,1792]{1,0:T(8,128)(2,1)} %fusion.2.hidden, bf16[448,1792]{1,0:T(8,128)(2,1)} %bitcast.33, ...), custom_call_target="tpu_custom_call" | custom-call | bytes 200000000 | tf_op jit(solution)/shard_map/gather_first/pallas_call | solution.py:656
  71.8 0.0 all-gather.9.cloned.1.call-start
  71.9 0.7 all-gather.9.cloned.1.call-update
  72.6 0.8 copy.30
  73.4 0.6 slice.22.flags
  74.0 0.7 slice.20.lengths
  74.7 0.6 broadcast_in_dim.19.gain
  75.3 0.1 reshape.67
  75.4 0.7 reshape.68.slots
  76.1 0.6 broadcast_in_dim.18.gain
  76.7 2.0 convolution_convert_fusion.2.cotangent
  78.6 60.8 %attend_ahead.1 = (bf16[8,8,48,256]{3,2,1,0:T(8,128)(2,1)}, bf16[8,448,768]{2,1,0:T(8,128)(2,1)}, bf16[8,384,1792]{2,1,0:T(8,128)(2,1)}) custom-call(s32[8,3]{1,0:T(8,128)} %slice.20.lengths, bf16[8,384,1792]{2,1,0:T(8,128)(2,1)} %get-tuple-element.45.hidden_all, bf16[768,1792]{1,0:T(8,128)(2,1)} %get-tuple-element.46.w_qkv, s32[8,384]{1,0:T(8,128)} %reshape.68.slots, ...), custom_call_target="tpu_custom_call" | custom-call | bytes 200000000 | tf_op jit(solution)/shard_map/attend_ahead/pallas_call | solution.py:816
  139.5 58.7 %project_middle.1 = (f32[384,1792]{1,0:T(8,128)}, bf16[384,1792]{1,0:T(8,128)(2,1)}) custom-call(bf16[3072,256]{1,0:T(8,128)(2,1)} %bitcast.28, bf16[256,1792]{1,0:T(8,128)(2,1)} %get-tuple-element.49.w_out, bf16[384,1792]{1,0:T(8,128)(2,1)} %copy-done, f32[1,1792]{1,0:T(1,128)} %broadcast_in_dim.18.gain), custom_call_target="tpu_custom_call" | custom-call | bytes 150000000 | tf_op jit(solution)/shard_map/project_middle/pallas_call | solution.py:1449
  198.2 3.1 all-gather.9.cloned.1.call-done
  201.3 118.9 %feed.1 = (f32[384,1792]{1,0:T(8,128)}, bf16[384,1792]{1,0:T(8,128)(2,1)}, f32[8,1792]{1,0:T(8,128)}, bf16[8,384,512]{2,1,0:T(8,128)(2,1)}, bf16[4,1792,256]{2,1,0:T(8,128)(2,1)}, /*index=5*/bf16[512,1792]{1,0:T(8,128)(2,1)}) custom-call(bf16[384,1792]{1,0:T(8,128)(2,1)} %get-tuple-element.50.hidden_own, ...), custom_call_target="tpu_custom_call" | custom-call | bytes 400000000 | tf_op jit(solution)/shard_map/feed/pallas_call | solution.py:1678
  320.2 136.0 %attend_back.1 = (bf16[8,8,48,768]{3,2,1,0:T(8,128)(2,1)}, bf16[384,1792]{1,0:T(8,128)(2,1)}, bf16[1,112,896]{2,1,0:T(8,128)(2,1)}, bf16[8,384,1792]{2,1,0:T(8,1...) custom-call(s32[8,3]{1,0:T(8,128)} %slice.20.lengths, ...), custom_call_target="tpu_custom_call" | custom-call | bytes 300000000 | tf_op jit(solution)/shard_map/attend_back/pallas_call | solution.py:1380
  456.2 125.8 %project_input.1 = (bf16[384,1792]{1,0:T(8,128)(2,1)}, bf16[4,112,896]{2,1,0:T(8,128)(2,1)}, f32[2,1792]{1,0:T(2,128)}, bf16[8,1792,256]{2,1,0:T(8,128)(2,1)}, bf16[8,128,1792]{2,1,0:T(8,128)(2,1)}) custom-call(bf16[3072,768]{1,0:T(8,128)(2,1)} %bitcast.30, bf16[768,1792]{1,0:T(8,128)(2,1)} %get-tuple-element.46.w_qkv, ...), custom_call_target="tpu_custom_call" | custom-call | bytes 250000000 | tf_op jit(solution)/shard_map/project_input/pallas_call | solution.py:1858
  582.1 10.0 %assemble_units.1 = (f32[1792,1024]{1,0:T(8,128)}, f32[1792,1024]{1,0:T(8,128)}) custom-call(bf16[8,1792,256]{2,1,0:T(8,128)(2,1)} %get-tuple-element.73.both), custom_call_target="tpu_custom_call" | custom-call | bytes 22000000 | tf_op jit(solution)/shard_map/assemble_units/pallas_call | solution.py:1911
  592.0 0.6 slice_reduce_fusion
  592.7 2.0 convolution_convert_fusion
  594.7 2.0 convolution_convert_fusion.1
  596.7 3.8 bitcast_convert_fusion
  600.5 26.6 %all-gather.7.cloned.1.call-done = bf16[8,448,896]{2,1,0:T(8,128)(2,1)} async-done(((bf16[1,448,896]{2,1,0:T(8,128)(2,1)}), bf16[8,448,896]{2,1,0:T(8,128)(2,1)}) %all-gather.7.cloned.1.call-update) | async-done | bytes 6422544 | tf_op jit(solution)/shard_map/all_gather | solution.py:2027
  627.1 7.8 %assemble_heads.1 = (f32[448,1792]{1,0:T(8,128)}, f32[448,1792]{1,0:T(8,128)}, f32[448,1792]{1,0:T(8,128)}, f32[448,1792]{1,0:T(8,128)}) custom-call(bf16[4,2,4,112,896]{4,3,2,1,0:T(8,128)(2,1)} %bitcast.27), custom_call_target="tpu_custom_call" | custom-call | bytes 20000000 | tf_op jit(solution)/shard_map/assemble_heads/pallas_call | solution.py:1933
  (29 shorter events, 0.2 us)
Async XLA Ops:
  7.2 3.5 copy-start.7
  7.2 3.6 copy-start.9
  7.2 4.3 copy-start.5
  7.2 191.0 %all-gather.5.cloned.1.call-start = ((), (), s32[]{:S(2)}) async-start(), calls=%async_computation | async-start | bytes 2293760 | tf_op jit(solution)/shard_map/all_gather | solution.py:1985
  10.5 61.3 %copy-start = (bf16[384,1792]{1,0:T(8,128)(2,1)}, bf16[384,1792]{1,0:T(8,128)(2,1)S(1)}, u32[]{:S(2)}) copy-start(bf16[384,1792]{1,0:T(8,128)(2,1)S(1)} %get-tuple-element.82.tokens) | copy-start | bytes 4128772
  13.0 63.1 %copy-start.8 = (f32[1792]{0:T(1024)S(1)}, f32[1792]{0:T(1024)}, u32[]{:S(2)}) copy-start(f32[1792]{0:T(1024)} %param.20) | copy-start | bytes 21508
  13.0 63.7 %copy-start.2 = (bf16[384,1792]{1,0:T(8,128)(2,1)S(1)}, bf16[384,1792]{1,0:T(8,128)(2,1)}, u32[]{:S(2)}) copy-start(bf16[384,1792]{1,0:T(8,128)(2,1)} %param.15) | copy-start | bytes 4128772
  71.8 129.4 %all-gather.9.cloned.1.call-start = ((), (), s32[]{:S(2)}) async-start(), calls=%async_computation.2 | async-start | bytes 4587520 | tf_op jit(solution)/shard_map/all_gather | solution.py:1984
  72.6 554.5 %all-gather.7.cloned.1.call-start = ((), (), s32[]{:S(2)}) async-start(), calls=%async_computation.1 | async-start | bytes 7225344 | tf_op jit(solution)/shard_map/all_gather | solution.py:2027
  582.0 10.0 %copy-start.6 = (f32[2,1792]{1,0:T(2,128)S(1)}, f32[2,1792]{1,0:T(2,128)}, u32[]{:S(2)}) copy-start(f32[2,1792]{1,0:T(2,128)} %get-tuple-element.67) | copy-start | bytes 43012
  582.0 10.6 %copy-start.4 = (bf16[384,1792]{1,0:T(8,128)(2,1)S(1)}, bf16[384,1792]{1,0:T(8,128)(2,1)}, u32[]{:S(2)}) copy-start(bf16[384,1792]{1,0:T(8,128)(2,1)} %get-tuple-element.66) | copy-start | bytes 4128772
  592.0 2.7 copy-start.3
  592.7 4.0 copy-start.1
Sparse Core Ops, SparseCore 0:
  72.0 55.2 all-gather.4
  128.9 72.3 all-gather.8
  582.2 44.9 all-gather.6

commit v6 on v5

--- a/solution.py
+++ b/solution.py
@@ -1014,76 +1014,155 @@
 
 
 class Heads:
-    def __init__(self, source, arrive, send, recv, views):
+    def __init__(self, source, stage, arrive, send, recv_stage, recv):
         me, z = lax.axis_index("dp"), lax.axis_index("mp")
         self.me, self.z = me, z
         self.core = lax.rem(me, 2)
-        self.source, self.arrive, self.send, self.recv, self.views = source, arrive, send, recv, views
-        self.owner = lax.div(z, 2)
-
-    def copy(self, slot, half, number):
-        target_z = 2 * self.core + slot
-        index = (slot * 2 + half) * self.views + number
+        self.source, self.stage, self.arrive = source, stage, arrive
+        self.send, self.recv_stage, self.recv = send, recv_stage, recv
+        self.place = z + self.core * (3 - 2 * z)
+        self.columns = source.shape[1] // 2
+
+    def z_of(self, place):
+        return place + self.core * (3 - 2 * place)
+
+    def slot_of(self, place):
+        return self.core if place == 0 else 1 - self.core
+
+    def rows_of(self, place, kind):
+        block = 2 * kind + self.slot_of(place)
+        return self.source.at[pl.ds(pl.multiple_of(block * LANES, LANES), HEAD_DIM)]
+
+    def half_of(self, ref, half):
+        return ref.at[:, pl.ds(pl.multiple_of(half * self.columns, LANES), self.columns)]
+
+    def to_stage(self, place, kind):
         return to_at(
-            self.view(slot, half, number),
-            self.arrive.at[self.z, number],
-            self.send.at[index],
-            self.recv.at[self.z * self.views + number],
+            self.rows_of(place, kind),
+            self.stage.at[place, kind],
+            self.send.at[place * 4 + kind],
+            self.recv_stage.at[place * 4 + kind],
+            self.me,
+            self.z_of(2),
+        )
+
+    def to_owner(self, place, kind, half, way, ref, number):
+        return to_at(
+            self.half_of(ref, half),
+            self.arrive.at[way, kind],
+            self.send.at[number],
+            self.recv.at[way * 4 + kind],
             self.me - self.core + half,
-            target_z,
-        )
-
-    def view(self, slot, half, number):
-        rows = pl.ds(pl.multiple_of((2 * number + slot) * LANES, LANES), HEAD_DIM)
-        columns = self.source.shape[1] // 2
-        return self.source.at[rows, pl.ds(pl.multiple_of(half * columns, LANES), columns)]
-
-    def each(self, action):
-        for slot in range(2):
-            for half in range(2):
-                mine = (2 * self.core + slot == self.z) & (self.core == half)
-
-                @pl.when(jnp.logical_not(mine))
+            self.z_of(place),
+        )
+
+    def sums(self, kind):
+        return [
+            self.to_owner(
+                place, kind, half, 2, self.stage.at[place, kind], place * 8 + kind * 2 + half
+            )
+            for place in (0, 1)
+            for half in (0, 1)
+        ]
+
+    def cross(self, own, kind):
+        other = 1 - own
+        copies = [
+            self.to_owner(other, kind, half, 0, self.rows_of(other, kind), kind * 2 + half)
+            for half in (0, 1)
+        ]
+        copies.append(
+            to_at(
+                self.half_of(self.rows_of(own, kind), 1 - self.core),
+                self.arrive.at[1, kind],
+                self.send.at[8 + kind],
+                self.recv.at[4 + kind],
+                self.me + 1 - 2 * self.core,
+                self.z,
+            )
+        )
+        return copies
+
+    def start(self, kinds):
+        @pl.when(self.place == 3)
+        def _():
+            for kind in kinds:
+                self.to_stage(0, kind).start()
+                self.to_stage(1, kind).start()
+
+        for own in (0, 1):
+            @pl.when(self.place == own)
+            def _():
+                for kind in kinds:
+                    for copy in self.cross(own, kind):
+                        copy.start()
+
+    def add(self, kinds):
+        @pl.when(self.place == 2)
+        def _():
+            for kind in kinds:
+                for place in (0, 1):
+                    self.to_stage(place, kind).wait_recv()
+                    mine = self.rows_of(place, kind)
+
+                    def body(span):
+                        self.stage[place, kind, span, :] = (
+                            self.stage[place, kind, span, :].astype(F32)
+                            + mine[span, :].astype(F32)
+                        ).astype(BF16)
+
+                    each_chunk(HEAD_DIM, body, 16)
+                for copy in self.sums(kind):
+                    copy.start()
+
+    def total(self, out):
+        owner = lax.div(self.z, 2) == self.core
+        for kind in range(4):
+            for own in (0, 1):
+                @pl.when(self.place == own)
                 def _():
-                    for number in range(self.views):
-                        action(self.copy(slot, half, number))
-
-    def start(self):
-        self.each(lambda copy: copy.start())
+                    self.arrive[1, kind] = self.half_of(self.rows_of(own, kind), self.core)[...]
+
+            for way in range(3):
+                waiting = to_at(
+                    self.half_of(self.rows_of(0, kind), 0),
+                    self.arrive.at[way, kind],
+                    self.send.at[0],
+                    self.recv.at[way * 4 + kind],
+                    self.me,
+                    lax.rem(self.z + 1, 4),
+                )
+                if way == 1:
+                    pl.when(jnp.logical_not(owner))(waiting.wait_recv)
+                else:
+                    waiting.wait_recv()
+
+            def body(span):
+                found = self.arrive[0, kind, span, :].astype(F32)
+                found = found + self.arrive[1, kind, span, :].astype(F32)
+                found = found + self.arrive[2, kind, span, :].astype(F32)
+                target = pl.ds(pl.multiple_of(kind * HEAD_DIM + span.start, 16), 16)
+                out[target, :] = found.astype(BF16)
+
+            each_chunk(HEAD_DIM, body, 16)
 
     def finish_send(self):
-        self.each(lambda copy: copy.wait_send())
-
-    def total(self, out):
-        me, z = self.me, self.z
-        for number in range(self.views):
-            for other in range(4):
-                waiting = to_at(
-                    self.view(0, 0, number),
-                    self.arrive.at[other, number],
-                    self.send.at[0],
-                    self.recv.at[other * self.views + number],
-                    me,
-                    other,
-                )
-
-                @pl.when((z != other) | (self.core != self.owner))
+        for kind in range(4):
+            @pl.when(self.place == 3)
+            def _():
+                self.to_stage(0, kind).wait_send()
+                self.to_stage(1, kind).wait_send()
+
+            @pl.when(self.place == 2)
+            def _():
+                for copy in self.sums(kind):
+                    copy.wait_send()
+
+            for own in (0, 1):
+                @pl.when(self.place == own)
                 def _():
-                    waiting.wait_recv()
-
-                @pl.when((z == other) & (self.core == self.owner))
-                def _():
-                    self.arrive[other, number] = self.view(lax.rem(z, 2), self.core, number)[...]
-
-            count = self.arrive.shape[2]
-
-            def body(span):
-                found = self.arrive[0, number, span, :].astype(F32)
-                for other in range(1, 4):
-                    found = found + self.arrive[other, number, span, :].astype(F32)
-                out[number, span, :] = found.astype(BF16)
-
-            each_chunk(count, body, 16)
+                    for copy in self.cross(own, kind):
+                        copy.wait_send()
 
 
 def to_at(source, target, send_sem, recv_sem, dp, mp):
@@ -1098,11 +1177,11 @@
 
 
 class Units:
-    def __init__(self, both_sum, down_sum, both_in, down_in, both_stage, down_stage, send, recv, local):
+    def __init__(self, both_sum, both_in, both_stage, send, recv, local):
         self.z = lax.axis_index("mp")
-        self.sums = (both_sum, down_sum)
-        self.inputs = (both_in, down_in)
-        self.stages = (both_stage, down_stage)
+        self.sums = (both_sum,)
+        self.inputs = (both_in,)
+        self.stages = (both_stage,)
         self.send, self.recv, self.local = send, recv, local
         z = self.z
         self.outer = (z == 0) | (z == 3)
@@ -1112,9 +1191,7 @@
         self.edge = 3 * (z - 1)
 
     def part(self, kind, z):
-        if kind == 0:
-            return self.sums[0].at[z]
-        return self.sums[1].at[pl.ds(pl.multiple_of(z * LANES, LANES), LANES)]
+        return self.sums[kind].at[z]
 
     def straight(self, kind, number, target):
         return to_mp(
@@ -1151,15 +1228,15 @@
     def start(self):
         @pl.when(self.outer)
         def _():
-            for kind in range(2):
+            for kind in range(1):
                 self.staged(kind).start()
-            for kind in range(2):
+            for kind in range(1):
                 self.straight(kind, 0, self.near).start()
                 self.straight(kind, 1, self.second).start()
 
         @pl.when(jnp.logical_not(self.outer))
         def _():
-            for kind in range(2):
+            for kind in range(1):
                 self.mine(kind).start()
                 self.straight(kind, 0, 3 - self.z).start()
                 self.straight(kind, 1, self.edge).start()
@@ -1167,7 +1244,7 @@
     def add(self):
         @pl.when(jnp.logical_not(self.outer))
         def _():
-            for kind in range(2):
+            for kind in range(1):
                 stage = self.stages[kind]
                 self.mine(kind).wait()
                 to_mp(
@@ -1198,7 +1275,7 @@
     def finish(self):
         @pl.when(self.outer)
         def _():
-            for kind in range(2):
+            for kind in range(1):
                 self.arrived(kind, 1)
                 self.arrived(kind, 2)
                 self.straight(kind, 0, self.near).wait_send()
@@ -1207,7 +1284,7 @@
 
         @pl.when(jnp.logical_not(self.outer))
         def _():
-            for kind in range(2):
+            for kind in range(1):
                 self.arrived(kind, 0)
                 self.arrived(kind, 3)
                 self.arrived(kind, 3 - self.z)
@@ -1217,26 +1294,38 @@
 
 
 def backward_kernel(
-    lengths, kept, branch, mixed, w_out, slots, flags, activated, w_down, middle, both_sum, down_sum,
-    out, result, proj_part, branch_all, both_in, down_in,
+    lengths, kept, branch, w_out, slots, flags, activated, w_down, middle, both_sum, down_in,
+    out, result, branch_all, both_in, down_all,
     totals, query_part, key_value, ending, leaving, arriving, send, recv,
-    part, from_side, from_corner, from_near, send_r, recv_r, arrive, send_h, recv_h,
-    mixed_grad, proj_sum, shard, branch_tile, load_sem, send_g, recv_g,
-    both_stage, down_stage, send_u, recv_u, local,
+    part, from_side, from_corner, from_near, send_r, recv_r,
+    mixed_grad, shard, load_sem, send_g, recv_g,
+    both_stage, send_u, recv_u, local, down_found, send_d, recv_d,
     *, scale, groups, rows,
 ):
     z = lax.axis_index("mp")
     members = lax.axis_size("mp")
-    count, width = groups * rows, middle.shape[1]
+    load_down = pltpu.make_async_copy(down_in, down_found, load_sem.at[2])
+    load_down.start()
     greet_all(pltpu.get_barrier_semaphore())
-    units = Units(
-        both_sum, down_sum, both_in, down_in, both_stage, down_stage, send_u, recv_u, local
-    )
+    units = Units(both_sum, both_in, both_stage, send_u, recv_u, local)
     gather = Gather(branch, branch_all, send_g, recv_g, local.at[2])
     gather.start()
     units.start()
     reduce = Reduce(activated, w_down, False, part, from_side, from_corner, from_near, send_r, recv_r)
     reduce.products()
+    load_down.wait()
+
+    def add_down(span):
+        value = down_found[0, span, :].astype(F32) + down_found[1, span, :].astype(F32)
+        value = value + down_found[2, span, :].astype(F32) + down_found[3, span, :].astype(F32)
+        down_found[0, span, :] = value.astype(BF16)
+
+    each_chunk(down_found.shape[1], add_down)
+    down = Gather(down_found.at[0], down_all, send_d, recv_d, local.at[1])
+
+    def load_shard(turn):
+        slot = turn % 2
+        return pltpu.make_async_copy(branch_all.at[owner_at(turn)], shard.at[slot], load_sem.at[slot])
 
     def spread_back(turn, carry):
         for number, numbers in ARRIVALS:
@@ -1246,12 +1335,10 @@
         def _():
             gather.keep.wait()
 
-        owner = owner_at(turn)
-        load = pltpu.make_async_copy(branch_all.at[owner], shard, load_sem.at[0])
-        load.start()
-        load.wait()
-        mixed_grad[owner] = (
-            lax.dot_general(shard[...], w_out[...], NT, preferred_element_type=F32)
+        load_shard(turn).start()
+        load_shard(turn).wait()
+        mixed_grad[owner_at(turn)] = (
+            lax.dot_general(shard[turn % 2], w_out[...], NT, preferred_element_type=F32)
             .astype(BF16)
             .reshape(groups, rows // groups, 256)
         )
@@ -1259,32 +1346,9 @@
 
     lax.fori_loop(0, 8, spread_back, 0)
     reduce.launch()
+    down.start()
     units.add()
 
-    def load_tile(t):
-        columns = pl.ds(pl.multiple_of(t * 256, 256), 256)
-        return pltpu.make_async_copy(
-            branch_all.at[:, :, columns], branch_tile.at[t % 2], load_sem.at[1 + t % 2]
-        )
-
-    load_tile(0).start()
-
-    def project_tile(t, carry):
-        columns = pl.ds(pl.multiple_of(t * 256, 256), 256)
-
-        @pl.when(t < width // 256 - 1)
-        def _():
-            load_tile(t + 1).start()
-
-        load_tile(t).wait()
-        proj_sum[:, columns] = lax.dot_general(
-            mixed[...], branch_tile[t % 2].reshape(count, 256), TN, preferred_element_type=F32
-        ).astype(BF16)
-        return carry
-
-    lax.fori_loop(0, width // 256, project_tile, 0)
-    heads = Heads(proj_sum, arrive, send_h, recv_h, 1)
-    heads.start()
 
     def halo(k, other):
         return to_mp(leaving.at[k], arriving.at[k], send.at[k], recv.at[k], other)
@@ -1329,7 +1393,9 @@
 
     lax.fori_loop(0, 3, attend, 0)
     reduce.middle()
-    lax.fori_loop(3, groups, attend, 0)
+    lax.fori_loop(3, 7, attend, 0)
+    down.pass_on()
+    lax.fori_loop(7, groups, attend, 0)
 
     def restore(k, carry):
         @pl.when(z < members - 1)
@@ -1352,8 +1418,7 @@
         result[span, :] = (middle[span, :] + reduce.rows_of(span)).astype(BF16)
 
     each_chunk(rows, body)
-    heads.total(proj_part)
-    heads.finish_send()
+    down.finish()
     units.finish()
     for copy in gather.copies:
         copy.wait_send()
@@ -1369,8 +1434,7 @@
 
 
 def attend_back(
-    lengths, kept, branch, mixed, w_out, slots, flags, activated, w_down, middle,
-    both_sum, down_sum, scale,
+    lengths, kept, branch, w_out, slots, flags, activated, w_down, middle, both_sum, down_in, scale
 ):
     groups = kept.shape[0]
     rows, width = middle.shape
@@ -1382,13 +1446,12 @@
         out_shape=(
             shape((groups, groups, rows // groups, 768), BF16),
             shape((rows, width), BF16),
-            shape((1, HEAD_DIM, width // 2), BF16),
             shape((groups, rows, width), BF16),
             shape((members, width, 256), BF16),
-            shape((members, LANES, width), BF16),
+            shape((groups, LANES, width), BF16),
         ),
-        in_specs=[in_scalar()] + [on_chip()] * 9 + [anywhere()] * 2,
-        out_specs=(on_chip(),) * 3 + (anywhere(),) * 3,
+        in_specs=[in_scalar()] + [on_chip()] * 8 + [anywhere()] * 2,
+        out_specs=(on_chip(),) * 2 + (anywhere(),) * 3,
         scratch_shapes=[
             pltpu.VMEM((rows + 64, 512), F32),
             pltpu.VMEM((groups, rows, 256), BF16),
@@ -1401,29 +1464,23 @@
         ]
         + reduce_scratch(rows, width)
         + [
-            pltpu.VMEM((4, 1, HEAD_DIM, width // 2), BF16),
-            dma((4,)),
-            dma((4,)),
             pltpu.VMEM((groups, groups, rows // groups, 256), BF16),
-            pltpu.VMEM((2 * LANES, width), BF16),
-            pltpu.VMEM((rows, width), BF16),
-            pltpu.VMEM((2, groups, rows, 256), BF16),
+            pltpu.VMEM((2, rows, width), BF16),
             dma((3,)),
             dma((13,)),
             dma((13,)),
             pltpu.VMEM((2, width, 256), BF16),
-            pltpu.VMEM((2, LANES, width), BF16),
             dma((6,)),
             dma((10,)),
             dma((3,)),
+            pltpu.VMEM((members, LANES, width), BF16),
+            dma((13,)),
+            dma((13,)),
         ],
         compiler_params=remote_params(3, 63 * 1024 * 1024),
         cost_estimate=pl.CostEstimate(flops=0, bytes_accessed=300_000_000, transcendentals=0),
         name="attend_back",
-    )(
-        lengths, kept, branch, mixed, w_out, slots, flags, activated, w_down, middle,
-        both_sum, down_sum,
-    )
+    )(lengths, kept, branch, w_out, slots, flags, activated, w_down, middle, both_sum, down_in)
 
 
 def middle_kernel(
@@ -1475,9 +1532,9 @@
 
 def feed_kernel(
     hidden_own, cotangent_all, middle, cotangent, gain, w_both, w_down,
-    middle_grad, branch, sums, activated, both_sum, down_sum,
+    middle_grad, branch, sums, activated, both_sum, down_in,
     hidden_all, both_grad, part, from_side, from_corner, from_near, send_r, recv_r,
-    send_a, recv_a, cot_half, cot_tile, stage_both, stage_down, load_sem, local,
+    send_a, recv_a, cot_half, cot_tile, stage_both, down_sum, load_sem, local, send_z, recv_z,
 ):
     groups, rows, width = hidden_all.shape
     members = w_both.shape[0]
@@ -1510,7 +1567,7 @@
         )
 
     load_cotangent(0).start()
-    pl.semaphore_wait(greet_plane(), 3)
+    greet_all(pltpu.get_barrier_semaphore())
     own.wait()
     gather = Gather(None, hidden_all, send_a, recv_a)
     gather.start()
@@ -1604,28 +1661,48 @@
             stage_both.at[t % 2], both_sum.at[:, columns], load_sem.at[4 + t % 2]
         )
 
-    def store_down(t):
-        columns = pl.ds(pl.multiple_of(t * 256, 256), 256)
-        return pltpu.make_async_copy(
-            stage_down.at[t % 2], down_sum.at[:, columns], load_sem.at[6 + t % 2]
-        )
-
     tiles = width // 256
     count = groups * rows
 
+    def down_tile(t, carry):
+        columns = pl.ds(pl.multiple_of(t * 256, 256), 256)
+
+        @pl.when(t < tiles - 1)
+        def _():
+            load_tile(t + 1).start()
+
+        load_tile(t).wait()
+        down_sum[:, columns] = lax.dot_general(
+            activated[...].reshape(count, members * 128),
+            cot_tile[t % 2].reshape(count, 256),
+            TN,
+            preferred_element_type=F32,
+        ).astype(BF16)
+        return carry
+
+    z = lax.axis_index("mp")
+
+    def down_rows(owner):
+        return down_sum.at[pl.ds(pl.multiple_of(owner * LANES, LANES), LANES)]
+
+    keep_down = pltpu.make_async_copy(down_rows(z), down_in.at[z], local.at[2])
+    pass_down = [
+        to_mp(
+            down_rows(lax.rem(z + step, members)),
+            down_in.at[z],
+            send_z.at[step - 1],
+            recv_z.at[step - 1],
+            lax.rem(z + step, members),
+        )
+        for step in range(1, members)
+    ]
+
     def weight_tile(t, carry):
         columns = pl.ds(pl.multiple_of(t * 256, 256), 256)
 
-        @pl.when(t < tiles - 1)
-        def _():
-            load_tile(t + 1).start()
-
-        load_tile(t).wait()
-
         @pl.when(t >= 2)
         def _():
             store_both(t - 2).wait()
-            store_down(t - 2).wait()
 
         value = lax.dot_general(
             hidden_all[:, :, columns].reshape(count, 256),
@@ -1635,23 +1712,20 @@
         )
         for z in range(members):
             stage_both[t % 2, z] = value[:, z * 256 : z * 256 + 256].astype(BF16)
-        stage_down[t % 2] = lax.dot_general(
-            activated[...].reshape(count, members * 128),
-            cot_tile[t % 2].reshape(count, 256),
-            TN,
-            preferred_element_type=F32,
-        ).astype(BF16)
         store_both(t).start()
-        store_down(t).start()
         return carry
 
     load_tile(0).start()
     reduce.add_side(0)
     reduce.corners[0].start()
     reduce.corners[1].start()
-    lax.fori_loop(0, 4, weight_tile, 0)
+    lax.fori_loop(0, tiles, down_tile, 0)
+    keep_down.start()
+    for copy in pass_down:
+        copy.start()
+    lax.fori_loop(0, 2, weight_tile, 0)
     reduce.middle()
-    lax.fori_loop(4, tiles, weight_tile, 0)
+    lax.fori_loop(2, tiles, weight_tile, 0)
     reduce.end()
     start_middle.wait()
     sums[...] = jnp.zeros_like(sums)
@@ -1667,7 +1741,9 @@
     reduce.finish()
     for t in (tiles - 2, tiles - 1):
         store_both(t).wait()
-        store_down(t).wait()
+    keep_down.wait()
+    for copy in pass_down:
+        copy.wait()
 
 
 def feed(hidden_own, cotangent_all, middle, cotangent, gain, w_both, w_down):
@@ -1683,7 +1759,7 @@
             jax.ShapeDtypeStruct((8, width), F32),
             jax.ShapeDtypeStruct((groups, rows, units), BF16),
             jax.ShapeDtypeStruct((members, width, 256), BF16),
-            jax.ShapeDtypeStruct((units, width), BF16),
+            jax.ShapeDtypeStruct((members, LANES, width), BF16),
         ),
         in_specs=[anywhere()] * 3 + [on_chip()] * 4,
         out_specs=(on_chip(),) * 4 + (anywhere(),) * 2,
@@ -1698,9 +1774,11 @@
             pltpu.VMEM((2, rows // 2, width), BF16),
             pltpu.VMEM((2, groups, rows, 256), BF16),
             pltpu.VMEM((2, members, 256, 256), BF16),
-            pltpu.VMEM((2, units, 256), BF16),
-            dma((8,)),
-            dma((2,)),
+            pltpu.VMEM((units, width), BF16),
+            dma((6,)),
+            dma((3,)),
+            dma((3,)),
+            dma((3,)),
         ],
         compiler_params=remote_params(5, 62 * 1024 * 1024),
         cost_estimate=pl.CostEstimate(flops=0, bytes_accessed=400_000_000, transcendentals=0),
@@ -1709,95 +1787,93 @@
 
 
 def input_kernel(
-    qkv_grad, w_qkv, hidden_all, tokens, middle_grad, gain, sums_two, proj_part,
-    both_sum, down_sum, both_in, down_in,
-    result, heads_part, gains, both_all, down_all,
+    qkv_grad, w_qkv, hidden_all, branch_all, mixed, tokens, middle_grad, gain, sums_two,
+    both_sum, both_in,
+    result, gains, both_all, heads_all,
     part, from_side, from_corner, from_near, send, recv, sums,
-    arrive, send_h, recv_h, own, plane_sums, column_sums, send_s, recv_s,
-    qkv_sum, hidden_tile, tile_sem, send_b, recv_b, send_d, recv_d, both_found, down_found, local,
+    stage, arrive, send_h, recv_s, recv_h, own, plane_sums, column_sums, send_p, recv_p,
+    weight_sum, row_tile, tile_sem, send_b, recv_b, send_t, recv_t, both_found, heads_own, local,
 ):
     me, z = lax.axis_index("dp"), lax.axis_index("mp")
     count = qkv_grad.shape[0]
     tiles = tokens.shape[1] // 256
-
-    def load(t):
-        columns = pl.ds(pl.multiple_of(t * 256, 256), 256)
+    outer = (z == 0) | (z == 3)
+
+    def columns_of(t):
+        return pl.ds(pl.multiple_of(lax.rem(t, tiles) * 256, 256), 256)
+
+    def load(t, source):
         return pltpu.make_async_copy(
-            hidden_all.at[:, :, columns], hidden_tile.at[t % 2], tile_sem.at[t % 2]
-        )
-
-    load(0).start()
-
-    def weight_tile(t, carry):
-        columns = pl.ds(pl.multiple_of(t * 256, 256), 256)
-
-        @pl.when(t < tiles - 1)
-        def _():
-            load(t + 1).start()
-
-        load(t).wait()
-        qkv_sum[:, columns] = lax.dot_general(
-            qkv_grad[...], hidden_tile[t % 2].reshape(count, 256), TN, preferred_element_type=F32
-        ).astype(BF16)
-        return carry
-
-    outer = (z == 0) | (z == 3)
-    inner = 3 - z
-    rows_down = pl.ds(pl.multiple_of(z * LANES, LANES), LANES)
-    sources = [(outer, 1), (outer, 2), (z == 1, 0), (z == 1, 2), (z == 1, 3)]
-    sources += [(z == 2, 0), (z == 2, 1), (z == 2, 3)]
-    places = [1, 2, 1, 2, 3, 1, 2, 3]
-
-    def found(source, place):
-        return (
-            pltpu.make_async_copy(both_in.at[source], both_found.at[place], local.at[2 * place]),
-            pltpu.make_async_copy(down_in.at[source], down_found.at[place], local.at[2 * place + 1]),
-        )
-
-    own_parts = (
-        pltpu.make_async_copy(both_sum.at[z], both_found.at[0], local.at[0]),
-        pltpu.make_async_copy(down_sum.at[rows_down], down_found.at[0], local.at[1]),
-    )
-    for copy in own_parts:
-        copy.start()
-    for (here, source), place in zip(sources, places):
-        @pl.when(here)
-        def _():
-            for copy in found(source, place):
-                copy.start()
+            source.at[:, :, columns_of(t)], row_tile.at[t % 2], tile_sem.at[t % 2]
+        )
+
+    own_part = pltpu.make_async_copy(both_sum.at[z], both_found.at[0], local.at[0])
+    own_part.start()
+    ways = [(outer, 1, 1), (outer, 2, 2)]
+    ways += [(z == 1, 0, 1), (z == 1, 2, 2), (z == 1, 3, 3)]
+    ways += [(z == 2, 0, 1), (z == 2, 1, 2), (z == 2, 3, 3)]
+
+    def came(source, place):
+        return pltpu.make_async_copy(both_in.at[source], both_found.at[place], local.at[place])
+
+    for here, source, place in ways:
+        pl.when(here)(came(source, place).start)
 
     @pl.when(outer)
     def _():
         both_found[3] = jnp.zeros_like(both_found[3])
-        down_found[3] = jnp.zeros_like(down_found[3])
-
+
+    load(0, branch_all).start()
     greet_all(pltpu.get_barrier_semaphore())
+    own_part.wait()
+    for here, source, place in ways:
+        pl.when(here)(came(source, place).wait)
+
+    def add(span):
+        value = both_found[0, span, :].astype(F32) + both_found[1, span, :].astype(F32)
+        value = value + both_found[2, span, :].astype(F32) + both_found[3, span, :].astype(F32)
+        both_found[0, span, :] = value.astype(BF16)
+
+    each_chunk(both_found.shape[1], add)
+    both = Gather(both_found.at[0], both_all, send_b, recv_b, local.at[4])
+    both.start()
+
+    def weight_tile(t, carry):
+        @pl.when(t < tiles - 1)
+        def _():
+            load(t + 1, branch_all).start()
+
+        @pl.when((t >= tiles - 1) & (t < 2 * tiles - 1))
+        def _():
+            load(t + 1, hidden_all).start()
+
+        load(t, hidden_all).wait()
+
+        @pl.when(t < tiles)
+        def _():
+            weight_sum[pl.ds(768, 256), columns_of(t)] = lax.dot_general(
+                mixed[...], row_tile[t % 2].reshape(count, 256), TN, preferred_element_type=F32
+            ).astype(BF16)
+
+        @pl.when(t >= tiles)
+        def _():
+            weight_sum[pl.ds(0, 768), columns_of(t)] = lax.dot_general(
+                qkv_grad[...], row_tile[t % 2].reshape(count, 256), TN, preferred_element_type=F32
+            ).astype(BF16)
+
+        return carry
+
+    heads = Heads(weight_sum, stage, arrive, send_h, recv_s, recv_h)
+    lax.fori_loop(0, tiles, weight_tile, 0)
+    heads.start((3,))
+    lax.fori_loop(tiles, 2 * tiles, weight_tile, 0)
+    heads.start((0, 1, 2))
     reduce = Reduce(qkv_grad, w_qkv, False, part, from_side, from_corner, from_near, send, recv)
     reduce.begin()
-    lax.fori_loop(0, tiles, weight_tile, 0)
-    heads = Heads(qkv_sum, arrive, send_h, recv_h, 3)
-    heads.start()
-    heads_part[3] = proj_part[0]
+    both.pass_on()
+    heads.add((3, 0))
     reduce.middle()
-    for copy in own_parts:
-        copy.wait()
-    for (here, source), place in zip(sources, places):
-        @pl.when(here)
-        def _():
-            for copy in found(source, place):
-                copy.wait()
-
-    for buffer in (both_found, down_found):
-        def add(span):
-            value = buffer[0, span, :].astype(F32) + buffer[1, span, :].astype(F32)
-            value = value + buffer[2, span, :].astype(F32) + buffer[3, span, :].astype(F32)
-            buffer[0, span, :] = value.astype(BF16)
-
-        each_chunk(buffer.shape[1], add)
-    both = Gather(both_found.at[0], both_all, send_b, recv_b, local.at[8])
-    down = Gather(down_found.at[0], down_all, send_d, recv_d, local.at[9])
-    both.start()
-    down.start()
+    heads.add((1, 2))
     reduce.end()
     sums[...] = jnp.zeros_like(sums)
 
@@ -1814,12 +1890,13 @@
         ],
         axis=0,
     )
-    swaps = swap_all(own, plane_sums, send_s, recv_s)
+    swaps = swap_all(own, plane_sums, send_p, recv_p)
     for copy in swaps:
         copy.start()
     plane_sums[me] = own[...]
-    both.pass_on()
-    down.pass_on()
+    heads.total(heads_own)
+    gather = Gather(heads_own, heads_all, send_t, recv_t, local.at[5])
+    gather.start()
     for copy in swaps:
         copy.wait()
     found = plane_sums[0]
@@ -1830,54 +1907,56 @@
         to_mp(
             column_sums.at[z],
             column_sums.at[z],
-            send_s.at[6 + step],
-            recv_s.at[6 + step],
+            send_p.at[6 + step],
+            recv_p.at[6 + step],
             lax.rem(z + step, 4),
         )
         for step in range(1, 4)
     ]
     for copy in passes:
         copy.start()
-    heads.total(heads_part)
+    both.finish()
     for copy in passes:
         copy.wait()
     gains[...] = (column_sums[0] + column_sums[1]) + (column_sums[2] + column_sums[3])
-    both.finish()
-    down.finish()
+    gather.pass_on()
     heads.finish_send()
     reduce.finish()
+    gather.finish()
 
 
 def project_input(
-    qkv_grad, w_qkv, hidden_all, tokens, middle_grad, gain, sums_two, proj_part,
-    both_sum, down_sum, both_in, down_in,
+    qkv_grad, w_qkv, hidden_all, branch_all, mixed, tokens, middle_grad, gain, sums_two,
+    both_sum, both_in,
 ):
     rows, width = tokens.shape
     groups = hidden_all.shape[0]
     dma = pltpu.SemaphoreType.DMA
+    shape = jax.ShapeDtypeStruct
     return pl.pallas_call(
         input_kernel,
         out_shape=(
-            jax.ShapeDtypeStruct((rows, width), BF16),
-            jax.ShapeDtypeStruct((4, HEAD_DIM, width // 2), BF16),
-            jax.ShapeDtypeStruct((2, width), F32),
-            jax.ShapeDtypeStruct((groups, width, 256), BF16),
-            jax.ShapeDtypeStruct((groups, LANES, width), BF16),
+            shape((rows, width), BF16),
+            shape((2, width), F32),
+            shape((groups, width, 256), BF16),
+            shape((groups, 4 * HEAD_DIM, width // 2), BF16),
         ),
-        in_specs=[on_chip()] * 2 + [anywhere()] + [on_chip()] * 5 + [anywhere()] * 4,
-        out_specs=(on_chip(),) * 3 + (anywhere(),) * 2,
+        in_specs=[on_chip()] * 2 + [anywhere()] * 2 + [on_chip()] * 5 + [anywhere()] * 2,
+        out_specs=(on_chip(),) * 2 + (anywhere(),) * 2,
         scratch_shapes=reduce_scratch(rows, width)
         + [
             pltpu.VMEM((8, width), F32),
-            pltpu.VMEM((4, 3, HEAD_DIM, width // 2), BF16),
-            dma((12,)),
+            pltpu.VMEM((2, 4, HEAD_DIM, width), BF16),
+            pltpu.VMEM((3, 4, HEAD_DIM, width // 2), BF16),
+            dma((16,)),
+            dma((8,)),
             dma((12,)),
             pltpu.VMEM((2, width), F32),
             pltpu.VMEM((8, 2, width), F32),
             pltpu.VMEM((4, 2, width), F32),
             dma((10,)),
             dma((10,)),
-            pltpu.VMEM((6 * LANES, width), BF16),
+            pltpu.VMEM((8 * LANES, width), BF16),
             pltpu.VMEM((2, groups, rows, 256), BF16),
             dma((2,)),
             dma((13,)),
@@ -1885,15 +1964,15 @@
             dma((13,)),
             dma((13,)),
             pltpu.VMEM((4, width, 256), BF16),
-            pltpu.VMEM((4, LANES, width), BF16),
-            dma((10,)),
+            pltpu.VMEM((4 * HEAD_DIM, width // 2), BF16),
+            dma((6,)),
         ],
-        compiler_params=remote_params(6, 62 * 1024 * 1024),
+        compiler_params=remote_params(6, 63 * 1024 * 1024),
         cost_estimate=pl.CostEstimate(flops=0, bytes_accessed=250_000_000, transcendentals=0),
         name="project_input",
     )(
-        qkv_grad, w_qkv, hidden_all, tokens, middle_grad, gain, sums_two, proj_part,
-        both_sum, down_sum, both_in, down_in,
+        qkv_grad, w_qkv, hidden_all, branch_all, mixed, tokens, middle_grad, gain, sums_two,
+        both_sum, both_in,
     )
 
 
@@ -1991,14 +2070,13 @@
     )
     mixed = mixed.reshape(count, 2 * LANES)
     middle, hidden_two = project_middle(mixed, w_proj, tokens_b, norm2_gain[None])
-    middle_grad, branch, sums_two, activated, both_sum, down_sum = feed(
+    middle_grad, branch, sums_two, activated, both_sum, down_in = feed(
         hidden_two, cotangent_all, middle, cotangent_b, norm2_gain[None], w_both, down_all
     )
-    qkv_grad, output_rows, proj_part, _, both_in, down_in = attend_back(
+    qkv_grad, output_rows, branch_all, both_in, down_whole = attend_back(
         lengths_all,
         kept,
         branch,
-        mixed,
         w_proj,
         slots,
         flags,
@@ -2006,25 +2084,23 @@
         down_all,
         middle,
         both_sum,
-        down_sum,
+        down_in,
         scale,
     )
     qkv_grad = qkv_grad.reshape(count, 6 * LANES)
-    input_rows, heads_part, gain_sums, both_whole, down_whole = project_input(
+    input_rows, gain_sums, both_whole, heads_whole = project_input(
         qkv_grad,
         w_qkv,
         hidden_one,
+        branch_all,
+        mixed,
         tokens_b,
         middle_grad,
         norm1_gain[None],
         sums_two,
-        proj_part,
         both_sum,
-        down_sum,
         both_in,
-        down_in,
-    )
-    heads_whole = lax.all_gather(heads_part.reshape(4 * HEAD_DIM, width // 2), "dp")
+    )
     gate_grad, up_grad = assemble_units(both_whole)
     down_grad = down_whole.astype(F32).reshape(groups * units, width)
     query_grad, key_grad, value_grad, proj_grad = assemble_heads(

time: 643 us -> 622 us (0.967)
  waiting for transfers between devices: 30.4 us -> 3.92 us
    all_gather x1 -> x0, waiting for transfers between devices: 26.6 us -> none  [swapped(): lax.all_gather(heads_part.reshape(4 * HEAD_DIM, width // 2), 'dp')]
  transfers between devices with their start and end apart: 3 -> 2, of which waited for: 2 -> 1; matrix products, arithmetic and copies ran while one was open for 2% -> 1% of each run, Pallas kernels for 20% -> 19%
where the time goes in v6:
time: 622 us; the launch traced here: 620 us
  Pallas kernels  580 us (93%)
  between operations  14.2 us (2%)
  other arithmetic  8.35 us (1%)
  matrix products  8.25 us (1%)
    pallas_call x1, Pallas kernels, attend_back(): pl.pallas_call(functools.partial(backward_kernel, scale=scale, groups=gro...  135 us
    pallas_call x1, Pallas kernels, project_input(): pl.pallas_call(input_kernel, out_shape=(shape((rows, width), BF16), shape...  126 us
    pallas_call x1, Pallas kernels, feed(): pl.pallas_call(feed_kernel, out_shape=(jax.ShapeDtypeStruct((rows, width)...  123 us
    pallas_call x1, Pallas kernels, attend_ahead(): pl.pallas_call(functools.partial(forward_kernel, scale=scale, groups=grou...  60.8 us
    pallas_call x1, Pallas kernels, project_middle(): pl.pallas_call(middle_kernel, out_shape=(jax.ShapeDtypeStruct((rows, widt...  58.7 us
    pallas_call x1, Pallas kernels, gather_first(): pl.pallas_call(first_kernel, out_shape=(jax.ShapeDtypeStruct((groups, row...  58.7 us
  transfers between devices with their start and end apart: 2, of which 1 were waited for; matrix products, arithmetic and copies ran while one was open for 1% of the time, Pallas kernels for 19%

profile of v6, /device:TPU:0, one launch (start us, length us, event | category | flops | bytes accessed | tf_op | source)
XLA Modules:
  0.0 620.2 jit_solution(6183004024361081623)
XLA Ops:
  7.2 0.0 all-gather.4.cloned.1.call-start
  7.3 0.7 add_select_fusion
  8.0 0.2 convert_reduce_fusion
  8.2 2.3 fusion
  10.5 0.1 select_reduce_fusion
  10.7 0.1 pad_dynamic-slice_fusion
  10.7 0.1 pad_add_fusion
  10.8 0.7 pad_bitcast_fusion.notes
  11.5 1.5 fusion.2.hidden
  13.0 58.7 %gather_first.1 = (bf16[8,384,1792]{2,1,0:T(8,128)(2,1)}, bf16[768,1792]{1,0:T(8,128)(2,1)}, bf16[256,1792]{1,0:T(8,128)(2,1)}, s32[8,8,128]{2,1,0:T(8,128)}, bf...) custom-call(bf16[384,1792]{1,0:T(8,128)(2,1)} %fusion.2.hidden, bf16[448,1792]{1,0:T(8,128)(2,1)} %bitcast.32, ...), custom_call_target="tpu_custom_call" | custom-call | bytes 200000000 | tf_op jit(solution)/shard_map/gather_first/pallas_call | solution.py:656
  71.8 0.0 all-gather.6.cloned.1.call-start
  71.8 0.7 all-gather.6.cloned.1.call-update
  72.5 0.8 copy.29
  73.3 0.6 slice.22.flags
  73.9 0.7 slice.20.lengths
  74.6 0.6 broadcast_in_dim.19.gain
  75.2 0.1 reshape.67
  75.2 0.7 reshape.68.slots
  75.9 0.6 broadcast_in_dim.18.gain
  76.5 1.9 convolution_convert_fusion.2.cotangent
  78.5 60.8 %attend_ahead.1 = (bf16[8,8,48,256]{3,2,1,0:T(8,128)(2,1)}, bf16[8,448,768]{2,1,0:T(8,128)(2,1)}, bf16[8,384,1792]{2,1,0:T(8,128)(2,1)}) custom-call(s32[8,3]{1,0:T(8,128)} %slice.20.lengths, bf16[8,384,1792]{2,1,0:T(8,128)(2,1)} %get-tuple-element.44.hidden_all, bf16[768,1792]{1,0:T(8,128)(2,1)} %get-tuple-element.45.w_qkv, s32[8,384]{1,0:T(8,128)} %reshape.68.slots, ...), custom_call_target="tpu_custom_call" | custom-call | bytes 200000000 | tf_op jit(solution)/shard_map/attend_ahead/pallas_call | solution.py:816
  139.3 58.7 %project_middle.1 = (f32[384,1792]{1,0:T(8,128)}, bf16[384,1792]{1,0:T(8,128)(2,1)}) custom-call(bf16[3072,256]{1,0:T(8,128)(2,1)} %bitcast.27, bf16[256,1792]{1,0:T(8,128)(2,1)} %get-tuple-element.48.w_out, bf16[384,1792]{1,0:T(8,128)(2,1)} %copy-done, f32[1,1792]{1,0:T(1,128)} %broadcast_in_dim.18.gain), custom_call_target="tpu_custom_call" | custom-call | bytes 150000000 | tf_op jit(solution)/shard_map/project_middle/pallas_call | solution.py:1506
  198.1 3.2 all-gather.6.cloned.1.call-done
  201.3 123.3 %feed.1 = (f32[384,1792]{1,0:T(8,128)}, bf16[384,1792]{1,0:T(8,128)(2,1)}, f32[8,1792]{1,0:T(8,128)}, bf16[8,384,512]{2,1,0:T(8,128)(2,1)}, bf16[4,1792,256]{2,1...) custom-call(bf16[384,1792]{1,0:T(8,128)(2,1)} %get-tuple-element.49.hidden_own, ...), custom_call_target="tpu_custom_call" | custom-call | bytes 400000000 | tf_op jit(solution)/shard_map/feed/pallas_call | solution.py:1754
  324.5 134.9 %attend_back.1 = (bf16[8,8,48,768]{3,2,1,0:T(8,128)(2,1)}, bf16[384,1792]{1,0:T(8,128)(2,1)}, bf16[8,384,1792]{2,1,0:T(8,128)(2,1)}, bf16[4,1792,256]{2,1,0:T(8,128)(2,1)}, bf16[8,128,1792]{2,1,0:T(8,128)(2,1)}) custom-call(s32[8,3]{1,0:T(8,128)} %slice.20.lengths, bf16[8,448,768]{2,1,0:T(8,128)(2,1)} %get-tuple-element.46.kept, ...), custom_call_target="tpu_custom_call" | custom-call | bytes 300000000 | tf_op jit(solution)/shard_map/attend_back/pallas_call | solution.py:1444
  459.4 125.9 %project_input.1 = (bf16[384,1792]{1,0:T(8,128)(2,1)}, f32[2,1792]{1,0:T(2,128)}, bf16[8,1792,256]{2,1,0:T(8,128)(2,1)}, bf16[8,448,896]{2,1,0:T(8,128)(2,1)}) custom-call(bf16[3072,768]{1,0:T(8,128)(2,1)} %bitcast.29, bf16[768,1792]{1,0:T(8,128)(2,1)} %get-tuple-element.45.w_qkv, bf16[8,384,1792]{2,1,0:T(8,128)(2,1)} %get-tuple-element.44.hidden_all, ...), custom_call_target="tpu_custom_call" | custom-call | bytes 250000000 | tf_op jit(solution)/shard_map/project_input/pallas_call | solution.py:1936
  585.4 9.7 %assemble_units.1 = (f32[1792,1024]{1,0:T(8,128)}, f32[1792,1024]{1,0:T(8,128)}) custom-call(bf16[8,1792,256]{2,1,0:T(8,128)(2,1)} %get-tuple-element.71.both), custom_call_target="tpu_custom_call" | custom-call | bytes 22000000 | tf_op jit(solution)/shard_map/assemble_units/pallas_call | solution.py:1990
  595.1 7.9 %assemble_heads.1 = (f32[448,1792]{1,0:T(8,128)}, f32[448,1792]{1,0:T(8,128)}, f32[448,1792]{1,0:T(8,128)}, f32[448,1792]{1,0:T(8,128)}) custom-call(bf16[4,2,4,112,896]{4,3,2,1,0:T(8,128)(2,1)} %bitcast.26), custom_call_target="tpu_custom_call" | custom-call | bytes 20000000 | tf_op jit(solution)/shard_map/assemble_heads/pallas_call | solution.py:2012
  603.0 2.0 convolution_convert_fusion
  605.0 0.6 slice_reduce_fusion
  605.6 5.7 bitcast_convert_fusion
  611.4 2.0 convolution_convert_fusion.1
  (24 shorter events, 0.1 us)
Async XLA Ops:
  7.2 3.5 copy-start.6
  7.2 3.6 copy-start.8
  7.2 4.3 copy-start.4
  7.2 190.9 %all-gather.4.cloned.1.call-start = ((), (), s32[]{:S(2)}) async-start(), calls=%async_computation | async-start | bytes 2293760 | tf_op jit(solution)/shard_map/all_gather | solution.py:2064
  10.5 61.2 %copy-start = (bf16[384,1792]{1,0:T(8,128)(2,1)}, bf16[384,1792]{1,0:T(8,128)(2,1)S(1)}, u32[]{:S(2)}) copy-start(bf16[384,1792]{1,0:T(8,128)(2,1)S(1)} %get-tuple-element.80.tokens) | copy-start | bytes 4128772
  13.0 62.9 %copy-start.7 = (f32[1792]{0:T(1024)S(1)}, f32[1792]{0:T(1024)}, u32[]{:S(2)}) copy-start(f32[1792]{0:T(1024)} %param.20) | copy-start | bytes 21508
  13.0 63.5 %copy-start.1 = (bf16[384,1792]{1,0:T(8,128)(2,1)S(1)}, bf16[384,1792]{1,0:T(8,128)(2,1)}, u32[]{:S(2)}) copy-start(bf16[384,1792]{1,0:T(8,128)(2,1)} %param.15) | copy-start | bytes 4128772
  71.8 129.5 %all-gather.6.cloned.1.call-start = ((), (), s32[]{:S(2)}) async-start(), calls=%async_computation.1 | async-start | bytes 4587520 | tf_op jit(solution)/shard_map/all_gather | solution.py:2063
  595.1 7.9 %copy-start.3 = (bf16[384,1792]{1,0:T(8,128)(2,1)S(1)}, bf16[384,1792]{1,0:T(8,128)(2,1)}, u32[]{:S(2)}) copy-start(bf16[384,1792]{1,0:T(8,128)(2,1)} %get-tuple-element.64) | copy-start | bytes 4128772
  603.0 2.0 copy-start.5
  605.6 5.7 copy-start.2
Sparse Core Ops, SparseCore 0:
  71.9 55.2 all-gather.3
  128.8 72.4 all-gather.5

commit v7 on v6

--- a/solution.py
+++ b/solution.py
@@ -535,16 +535,16 @@
                 self.hop(1, piece, 1, 2, True).start()
                 self.keep(1, piece).start()
 
-    def pass_on(self):
+    def pass_on(self, pieces):
         @pl.when(self.place == 1)
         def _():
-            for piece in range(4):
+            for piece in pieces:
                 self.hop(0, piece, 2, 2, False).wait_recv()
                 self.hop(0, piece, 2, 2, False).start()
 
         @pl.when(self.place == 2)
         def _():
-            for piece in range(4):
+            for piece in pieces:
                 for which in (1, 0):
                     self.hop(which, piece, which, 3, False).wait_recv()
                     self.hop(which, piece, which, 3, False).start()
@@ -578,167 +578,168 @@
                     self.hop(which, piece, which, 3, False).wait_recv()
 
 
-def first_kernel(
-    hidden, query, keys, values, project, gate, upward, down, notes,
-    hidden_all, w_qkv, w_out, notes_all, both_own, down_own,
-    share, none, send_a, recv_a, send_w, recv_w, send_n, recv_n, local,
+class Chain:
+    def __init__(self, own, out, send, recv, local):
+        self.z = lax.axis_index("mp")
+        self.own, self.out, self.send, self.recv = own, out, send, recv
+        self.keep = pltpu.make_async_copy(own, out.at[self.z], local)
+
+    def hop(self, way, distance):
+        z = self.z
+        source = z - way * distance
+        return to_mp(
+            self.own if distance == 0 else self.out.at[source],
+            self.out.at[source],
+            self.send.at[3 * (way > 0) + distance],
+            self.recv.at[3 * (way > 0) + distance],
+            z + way,
+        )
+
+    def ways(self, distance):
+        z = self.z
+        return (
+            (1, z >= distance, (z >= distance) & (z < 3)),
+            (-1, z <= 3 - distance, (z <= 3 - distance) & (z > 0)),
+        )
+
+    def step(self, distance):
+        if distance == 0:
+            self.keep.start()
+        for way, there, onward in self.ways(distance):
+            if distance > 0:
+                pl.when(there)(self.hop(way, distance - 1).wait_recv)
+            if distance < 3:
+                pl.when(onward)(self.hop(way, distance).start)
+
+    def finish(self):
+        self.step(3)
+        for distance in range(3):
+            for way, _, onward in self.ways(distance):
+                pl.when(onward)(self.hop(way, distance).wait_send)
+        self.keep.wait()
+
+
+def anywhere():
+    return pl.BlockSpec(memory_space=pl.ANY)
+
+
+def on_chip():
+    return pl.BlockSpec(memory_space=pltpu.VMEM)
+
+
+def remote_params(number, limit=VMEM_LIMIT):
+    return pltpu.CompilerParams(
+        collective_id=number, has_side_effects=True, vmem_limit_bytes=limit
+    )
+
+
+def hot_of(notes, k, size):
+    own = notes[:, 0:48, :].reshape(size, LANES)
+    lane = lax.broadcasted_iota(jnp.int32, (size, LANES), 1)
+    slot = jnp.sum(jnp.where(lane == k, own, 0.0), axis=1, keepdims=True)
+    return (lax.broadcasted_iota(jnp.int32, (size, size), 1).astype(F32) == slot).astype(BF16)
+
+
+def block_mask(notes, k, block, z, rows):
+    position = rows * z + block * 128 + lax.broadcasted_iota(jnp.int32, (128, 1), 0)
+    position = position.astype(F32)
+    first_end = notes[k, 52:53, 0:1]
+    second_end = first_end + notes[k, 52:53, 1:2]
+    begin = jnp.where(position >= first_end, first_end, 0.0)
+    begin = jnp.where(position >= second_end, second_end, begin)
+    column = lax.broadcasted_iota(jnp.int32, (128, 192), 1)
+    distance = 64 + lax.broadcasted_iota(jnp.int32, (128, 192), 0) - column
+    key_position = (rows * z + block * 128 - 64 + column).astype(F32)
+    live = jnp.concatenate(
+        [notes[k, 48 + block : 49 + block, :], notes[k, 49 + block : 50 + block, 0:64]], axis=1
+    )
+    allowed = (distance >= 0) & (distance < WINDOW) & (key_position >= begin)
+    return allowed & ((live == 1.0) | (distance == 0))
+
+
+NT = (((1,), (1,)), ((), ()))
+TN = (((0,), (0,)), ((), ()))
+
+
+def forward_kernel(
+    tokens, cotangent, order_row, gain, notes, query, keys, values, project, gate, upward,
+    hidden_out, w_qkv, w_out, notes_all, w_both, mixed, kept, tokens_b, cotangent_b, cotangent_all,
+    hidden_all, qkv, share, both_own,
+    send, recv, send_a, recv_a, send_g, recv_g, send_w, recv_w, send_n, recv_n, send_c, recv_c,
+    local, out_sem, *, scale,
 ):
-    me = lax.axis_index("dp")
+    groups, rows, width = hidden_all.shape
+    me, z = lax.axis_index("dp"), lax.axis_index("mp")
+    members = lax.axis_size("mp")
     head = pl.ds(pl.multiple_of(lax.div(me, 2) * HEAD_DIM, 16), HEAD_DIM)
+    units = pl.ds(pl.multiple_of(me * LANES, LANES), LANES)
     loads = [
         pltpu.make_async_copy(source.at[head], share.at[piece], local.at[piece])
         for piece, source in enumerate((query, keys, values, project))
     ]
-    units = pl.ds(pl.multiple_of(me * LANES, LANES), LANES)
     loads += [
-        pltpu.make_async_copy(gate.at[:, units], both_own.at[:, pl.ds(0, LANES)], local.at[14]),
-        pltpu.make_async_copy(upward.at[:, units], both_own.at[:, pl.ds(LANES, LANES)], local.at[15]),
-        pltpu.make_async_copy(down.at[units], down_own, local.at[16]),
+        pltpu.make_async_copy(gate.at[:, units], both_own.at[:, pl.ds(0, LANES)], local.at[4]),
+        pltpu.make_async_copy(upward.at[:, units], both_own.at[:, pl.ds(LANES, LANES)], local.at[5]),
     ]
     for copy in loads:
         copy.start()
-    none[...] = jnp.zeros_like(none)
+    none = jnp.zeros((LANES - HEAD_DIM, width), BF16)
+    for block in range(6):
+        w_qkv[block * LANES + HEAD_DIM : block * LANES + LANES, :] = none
+    for block in range(2):
+        w_out[block * LANES + HEAD_DIM : block * LANES + LANES, :] = none
+
+    place = lax.broadcasted_iota(jnp.int32, (rows, rows), 0).astype(F32)
+    sort = (place == order_row[...]).astype(BF16)
+    tokens_b[...] = jnp.dot(sort, tokens[...], preferred_element_type=F32).astype(BF16)
+
+    def normalise(span):
+        value = tokens_b[span, :].astype(F32)
+        inverse = lax.rsqrt(mean_rows(value * value) + EPSILON)
+        hidden_all[me, span, :] = (value * inverse * gain[...]).astype(BF16)
+
+    each_chunk(rows, normalise)
+    notes_all[me] = notes[...]
     greet_all(pltpu.get_barrier_semaphore())
-    gather = Gather(hidden, hidden_all, send_a, recv_a, local.at[4])
+    gather = Gather(None, hidden_all, send_a, recv_a)
     gather.start()
     swaps = swap_all(notes, notes_all, send_n, recv_n)
     for copy in swaps:
-        copy.start()
-    keep = pltpu.make_async_copy(notes, notes_all.at[me], local.at[5])
-    keep.start()
-    pads = [
-        pltpu.make_async_copy(
-            none, weight.at[pl.ds(block * LANES + HEAD_DIM, LANES - HEAD_DIM)], local.at[6 + number]
-        )
-        for number, (weight, block) in enumerate(
-            [(w_qkv, block) for block in range(6)] + [(w_out, block) for block in range(2)]
-        )
-    ]
-    for copy in pads:
         copy.start()
     for copy in loads[:4]:
         copy.wait()
     spread = Spread(share, w_qkv, w_out, send_w, recv_w, local)
     spread.start()
-    spread.pass_on()
-    gather.pass_on()
-    gather.finish()
+    cotangent_b[...] = jnp.dot(sort, cotangent[...], preferred_element_type=F32).astype(BF16)
+    for copy in loads[4:]:
+        copy.wait()
+    chain = Chain(both_own, w_both, send_c, recv_c, local.at[4])
+    second = Gather(cotangent_b, cotangent_all, send_g, recv_g, local.at[5])
+    spread.pass_on((0, 1))
+    gather.arrive(0, 1)
+    spread.pass_on((2, 3))
+    gather.arrive(2, 3)
+    second.start()
+    chain.step(0)
     spread.finish()
     for copy in swaps:
         copy.wait()
-    for copy in pads + loads[4:]:
-        copy.wait()
-    keep.wait()
-
-
-def anywhere():
-    return pl.BlockSpec(memory_space=pl.ANY)
-
-
-def on_chip():
-    return pl.BlockSpec(memory_space=pltpu.VMEM)
-
-
-def in_scalar():
-    return pl.BlockSpec(memory_space=pltpu.SMEM)
-
-
-def remote_params(number, limit=VMEM_LIMIT):
-    return pltpu.CompilerParams(
-        collective_id=number, has_side_effects=True, vmem_limit_bytes=limit
-    )
-
-
-def gather_first(hidden, query, keys, values, project, gate, upward, down, notes):
-    rows, width = hidden.shape
-    groups = lax.axis_size("dp")
-    dma = pltpu.SemaphoreType.DMA
-    return pl.pallas_call(
-        first_kernel,
-        out_shape=(
-            jax.ShapeDtypeStruct((groups, rows, width), BF16),
-            jax.ShapeDtypeStruct((6 * LANES, width), BF16),
-            jax.ShapeDtypeStruct((2 * LANES, width), BF16),
-            jax.ShapeDtypeStruct((groups,) + notes.shape, notes.dtype),
-            jax.ShapeDtypeStruct((width, 2 * LANES), BF16),
-            jax.ShapeDtypeStruct((LANES, width), BF16),
-        ),
-        in_specs=[on_chip()] + [anywhere()] * 7 + [on_chip()],
-        out_specs=(anywhere(),) * 4 + (on_chip(),) * 2,
-        scratch_shapes=[
-            pltpu.VMEM((4, HEAD_DIM, width), BF16),
-            pltpu.VMEM((LANES - HEAD_DIM, width), BF16),
-            dma((13,)), dma((13,)), dma((12,)), dma((8,)), dma((7,)), dma((7,)), dma((17,)),
-        ],
-        compiler_params=remote_params(1),
-        cost_estimate=pl.CostEstimate(flops=0, bytes_accessed=200_000_000, transcendentals=0),
-        name="gather_first",
-    )(hidden, query, keys, values, project, gate, upward, down, notes)
-
-
-def one_hot(slots, k, size):
-    row = slots[pl.ds(k, 1), :]
-    place = lax.broadcasted_iota(jnp.int32, (size, size), 0)
-    return (place == row).astype(BF16)
-
-
-def block_mask(lengths, flags, k, block, z, rows):
-    position = rows * z + block * 128 + lax.broadcasted_iota(jnp.int32, (128, 1), 0)
-    first_end = lengths[k, 0]
-    second_end = first_end + lengths[k, 1]
-    begin = jnp.where(position >= first_end, first_end, 0)
-    begin = jnp.where(position >= second_end, second_end, begin)
-    column = lax.broadcasted_iota(jnp.int32, (128, 192), 1)
-    distance = 64 + lax.broadcasted_iota(jnp.int32, (128, 192), 0) - column
-    key_position = rows * z + block * 128 - 64 + column
-    live = flags[pl.ds(k, 1), block * 128 : block * 128 + 192]
-    allowed = (distance >= 0) & (distance < WINDOW) & (key_position >= begin)
-    return allowed & ((live == 1) | (distance == 0))
-
-
-NT = (((1,), (1,)), ((), ()))
-TN = (((0,), (0,)), ((), ()))
-
-
-def forward_kernel(
-    lengths, hidden_all, w_qkv, slots, flags, cotangent, mixed, kept, cotangent_all,
-    qkv, shard, shard_sem, send, recv, send_g, recv_g, local, *, scale, groups, rows
-):
-    z = lax.axis_index("mp")
-    members = lax.axis_size("mp")
-    barrier = greet_plane()
-
-    @pl.when(z > 0)
-    def _():
-        pl.semaphore_signal(barrier, inc=1, device_id={"mp": z - 1}, device_id_type=MESH)
-
-    @pl.when(z < members - 1)
-    def _():
-        pl.semaphore_wait(barrier, 4)
-
-    @pl.when(z == members - 1)
-    def _():
-        pl.semaphore_wait(barrier, 3)
-
-    gather = Gather(cotangent, cotangent_all, send_g, recv_g, local)
-    gather.start()
-
-    def load(g):
-        slot = lax.rem(g, 2)
-        return pltpu.make_async_copy(hidden_all.at[g], shard.at[slot], shard_sem.at[slot])
-
-    load(0).start()
-
-    def multiply(g, carry):
-        @pl.when(g < groups - 1)
-        def _():
-            load(g + 1).start()
-
-        load(g).wait()
+
+    def keep(turn):
+        owner = owner_at(turn)
+        return pltpu.make_async_copy(hidden_all.at[owner], hidden_out.at[owner], out_sem.at[turn])
+
+    def multiply(turn, carry):
+        for number, numbers in ARRIVALS:
+            left = tuple(n for n in numbers if n > 3)
+            if left:
+                pl.when(turn == number)(functools.partial(gather.arrive, *left))
+        owner = owner_at(turn)
+        keep(turn).start()
         product = lax.dot_general(
-            shard[lax.rem(g, 2)], w_qkv[...], NT, preferred_element_type=F32
+            hidden_all[owner], w_qkv[...], NT, preferred_element_type=F32
         ).astype(BF16)
-        qkv[g] = product.reshape(groups, rows // groups, 768)
+        qkv[owner] = product.reshape(groups, rows // groups, 768)
         return carry
 
     lax.fori_loop(0, groups, multiply, 0)
@@ -753,9 +754,11 @@
         )
 
     def order(k, carry):
-        hot = one_hot(slots, k, rows)
+        hot = hot_of(notes_all, k, rows)
         given = qkv[:, pl.ds(k, 1)].reshape(rows, 768)
-        kept[k, pl.ds(64, rows), :] = jnp.dot(hot, given, preferred_element_type=F32).astype(BF16)
+        kept[k, pl.ds(64, rows), :] = lax.dot_general(
+            hot, given, TN, preferred_element_type=F32
+        ).astype(BF16)
         kept[k, pl.ds(0, 64), pl.ds(0, 256)] = jnp.zeros((64, 256), BF16)
 
         @pl.when(z < members - 1)
@@ -775,10 +778,10 @@
         def _():
             halo(k, z).wait_recv()
 
-        hot = one_hot(slots, k, rows)
+        hot = hot_of(notes_all, k, rows)
         found = []
         for block in range(rows // 128):
-            allowed = block_mask(lengths, flags, k, block, z, rows)
+            allowed = block_mask(notes_all, k, block, z, rows)
             heads = []
             for head in range(2):
                 query = kept[k, pl.ds(64 + block * 128, 128), pl.ds(head * 128, 128)]
@@ -792,14 +795,24 @@
                 heads.append(jnp.dot(chances, values, preferred_element_type=F32).astype(BF16))
             found.append(jnp.concatenate(heads, axis=1))
         ordered = jnp.concatenate(found, axis=0)
-        back = lax.dot_general(hot, ordered, TN, preferred_element_type=F32).astype(BF16)
+        back = jnp.dot(hot, ordered, preferred_element_type=F32).astype(BF16)
         mixed[:, pl.ds(k, 1)] = back.reshape(groups, 1, rows // groups, 256)
         return carry
 
-    lax.fori_loop(0, groups // 4, attend, 0)
-    gather.pass_on()
-    lax.fori_loop(groups // 4, groups, attend, 0)
-    gather.finish()
+    chain.step(1)
+    lax.fori_loop(0, groups // 2, attend, 0)
+    second.pass_on()
+    chain.step(2)
+    lax.fori_loop(groups // 2, groups, attend, 0)
+    second.finish()
+    chain.finish()
+    gather.sent()
+
+    def kept_out(turn, carry):
+        keep(turn).wait()
+        return carry
+
+    lax.fori_loop(0, groups, kept_out, 0)
 
     @pl.when(z < members - 1)
     def _():
@@ -810,32 +823,57 @@
         lax.fori_loop(0, groups, done, 0)
 
 
-def attend_ahead(lengths, hidden_all, w_qkv, slots, flags, cotangent, scale):
-    groups, rows, width = hidden_all.shape
+def attend_ahead(
+    tokens, cotangent, order_row, gain, notes, query, keys, values, project, gate, upward, scale
+):
+    rows, width = tokens.shape
+    groups, members = lax.axis_size("dp"), lax.axis_size("mp")
     dma = pltpu.SemaphoreType.DMA
+    shape = jax.ShapeDtypeStruct
     return pl.pallas_call(
-        functools.partial(forward_kernel, scale=scale, groups=groups, rows=rows),
+        functools.partial(forward_kernel, scale=scale),
         out_shape=(
-            jax.ShapeDtypeStruct((groups, groups, rows // groups, 256), BF16),
-            jax.ShapeDtypeStruct((groups, rows + 64, 768), BF16),
-            jax.ShapeDtypeStruct((groups,) + cotangent.shape, BF16),
+            shape((groups, rows, width), BF16),
+            shape((6 * LANES, width), BF16),
+            shape((2 * LANES, width), BF16),
+            shape((groups,) + notes.shape, F32),
+            shape((members, width, 2 * LANES), BF16),
+            shape((groups, groups, rows // groups, 256), BF16),
+            shape((groups, rows + 64, 768), BF16),
+            shape((rows, width), BF16),
+            shape((rows, width), BF16),
+            shape((groups, rows, width), BF16),
         ),
-        in_specs=[in_scalar(), anywhere()] + [on_chip()] * 4,
-        out_specs=(on_chip(), on_chip(), anywhere()),
+        in_specs=[on_chip()] * 5 + [anywhere()] * 6,
+        out_specs=(anywhere(),)
+        + (on_chip(),) * 3
+        + (anywhere(),)
+        + (on_chip(),) * 4
+        + (anywhere(),),
         scratch_shapes=[
+            pltpu.VMEM((groups, rows, width), BF16),
             pltpu.VMEM((groups, groups, rows // groups, 768), BF16),
-            pltpu.VMEM((2, rows, width), BF16),
-            dma((2,)),
+            pltpu.VMEM((4, HEAD_DIM, width), BF16),
+            pltpu.VMEM((width, 2 * LANES), BF16),
             dma((groups,)),
             dma((groups,)),
             dma((13,)),
             dma((13,)),
-            dma(()),
+            dma((13,)),
+            dma((13,)),
+            dma((12,)),
+            dma((8,)),
+            dma((7,)),
+            dma((7,)),
+            dma((6,)),
+            dma((6,)),
+            dma((6,)),
+            dma((groups,)),
         ],
-        compiler_params=remote_params(2),
-        cost_estimate=pl.CostEstimate(flops=0, bytes_accessed=200_000_000, transcendentals=0),
+        compiler_params=remote_params(2, 60 * 1024 * 1024),
+        cost_estimate=pl.CostEstimate(flops=0, bytes_accessed=300_000_000, transcendentals=0),
         name="attend_ahead",
-    )(lengths, hidden_all, w_qkv, slots, flags, cotangent)
+    )(tokens, cotangent, order_row, gain, notes, query, keys, values, project, gate, upward)
 
 
 CHUNK = 32
@@ -1294,7 +1332,7 @@
 
 
 def backward_kernel(
-    lengths, kept, branch, w_out, slots, flags, activated, w_down, middle, both_sum, down_in,
+    kept, branch, w_out, notes_all, activated, w_down, middle, both_sum, down_in,
     out, result, branch_all, both_in, down_all,
     totals, query_part, key_value, ending, leaving, arriving, send, recv,
     part, from_side, from_corner, from_near, send_r, recv_r,
@@ -1354,12 +1392,12 @@
         return to_mp(leaving.at[k], arriving.at[k], send.at[k], recv.at[k], other)
 
     def attend(k, carry):
-        hot = one_hot(slots, k, rows)
+        hot = hot_of(notes_all, k, rows)
         given = mixed_grad[:, pl.ds(k, 1)].reshape(rows, 256)
-        grad_ordered = jnp.dot(hot, given, preferred_element_type=F32).astype(BF16)
+        grad_ordered = lax.dot_general(hot, given, TN, preferred_element_type=F32).astype(BF16)
         totals[...] = jnp.zeros_like(totals)
         for block in range(rows // 128):
-            allowed = block_mask(lengths, flags, k, block, z, rows)
+            allowed = block_mask(notes_all, k, block, z, rows)
             for head in range(2):
                 query = kept[k, pl.ds(64 + block * 128, 128), pl.ds(head * 128, 128)]
                 keys = kept[k, pl.ds(block * 128, 192), pl.ds(256 + head * 128, 128)]
@@ -1405,9 +1443,9 @@
                 ending[k] + arriving[k].astype(F32)
             ).astype(BF16)
 
-        hot = one_hot(slots, k, rows)
+        hot = hot_of(notes_all, k, rows)
         ordered = jnp.concatenate([query_part[k], key_value[k]], axis=1)
-        back = lax.dot_general(hot, ordered, TN, preferred_element_type=F32).astype(BF16)
+        back = jnp.dot(hot, ordered, preferred_element_type=F32).astype(BF16)
         out[:, pl.ds(k, 1)] = back.reshape(groups, 1, rows // groups, 768)
         return carry
 
@@ -1434,7 +1472,7 @@
 
 
 def attend_back(
-    lengths, kept, branch, w_out, slots, flags, activated, w_down, middle, both_sum, down_in, scale
+    kept, branch, w_out, notes_all, activated, w_down, middle, both_sum, down_in, scale
 ):
     groups = kept.shape[0]
     rows, width = middle.shape
@@ -1450,7 +1488,7 @@
             shape((members, width, 256), BF16),
             shape((groups, LANES, width), BF16),
         ),
-        in_specs=[in_scalar()] + [on_chip()] * 8 + [anywhere()] * 2,
+        in_specs=[on_chip()] * 7 + [anywhere()] * 2,
         out_specs=(on_chip(),) * 2 + (anywhere(),) * 3,
         scratch_shapes=[
             pltpu.VMEM((rows + 64, 512), F32),
@@ -1480,16 +1518,26 @@
         compiler_params=remote_params(3, 63 * 1024 * 1024),
         cost_estimate=pl.CostEstimate(flops=0, bytes_accessed=300_000_000, transcendentals=0),
         name="attend_back",
-    )(lengths, kept, branch, w_out, slots, flags, activated, w_down, middle, both_sum, down_in)
+    )(kept, branch, w_out, notes_all, activated, w_down, middle, both_sum, down_in)
 
 
 def middle_kernel(
-    mixed, w_out, tokens, gain, middle, hidden,
-    part, from_side, from_corner, from_near, send, recv,
+    mixed, w_out, tokens, gain, w_down, middle, hidden, down_all,
+    part, from_side, from_corner, from_near, send, recv, down_own, send_c, recv_c, local,
 ):
-    pl.semaphore_wait(greet_plane(), 3)
+    units = pl.ds(pl.multiple_of(lax.axis_index("dp") * LANES, LANES), LANES)
+    load = pltpu.make_async_copy(w_down.at[units], down_own, local.at[0])
+    load.start()
+    greet_all(pltpu.get_barrier_semaphore())
+    load.wait()
+    chain = Chain(down_own, down_all, send_c, recv_c, local.at[1])
+    chain.step(0)
     reduce = Reduce(mixed, w_out, False, part, from_side, from_corner, from_near, send, recv)
-    reduce.run()
+    reduce.begin()
+    chain.step(1)
+    reduce.middle()
+    chain.step(2)
+    reduce.end()
 
     def body(span):
         values = tokens[span, :].astype(F32) + reduce.rows_of(span)
@@ -1498,24 +1546,29 @@
         hidden[span, :] = (values * inverse * gain[...]).astype(BF16)
 
     each_chunk(hidden.shape[0], body)
+    chain.finish()
     reduce.finish()
 
 
-def project_middle(mixed, w_out, tokens, gain):
+def project_middle(mixed, w_out, tokens, gain, w_down):
     rows, width = tokens.shape
+    dma = pltpu.SemaphoreType.DMA
+    members = lax.axis_size("mp")
     return pl.pallas_call(
         middle_kernel,
         out_shape=(
             jax.ShapeDtypeStruct((rows, width), F32),
             jax.ShapeDtypeStruct((rows, width), BF16),
+            jax.ShapeDtypeStruct((members, LANES, width), BF16),
         ),
-        in_specs=[on_chip()] * 4,
-        out_specs=(on_chip(), on_chip()),
-        scratch_shapes=reduce_scratch(rows, width),
+        in_specs=[on_chip()] * 4 + [anywhere()],
+        out_specs=(on_chip(), on_chip(), anywhere()),
+        scratch_shapes=reduce_scratch(rows, width)
+        + [pltpu.VMEM((LANES, width), BF16), dma((6,)), dma((6,)), dma((2,))],
         compiler_params=remote_params(4),
         cost_estimate=pl.CostEstimate(flops=0, bytes_accessed=150_000_000, transcendentals=0),
         name="project_middle",
-    )(mixed, w_out, tokens, gain)
+    )(mixed, w_out, tokens, gain, w_down)
 
 
 def norm_back_rows(gradient, values, gain, sums, span):
@@ -2039,47 +2092,53 @@
     sorting = send_at[None, :] == earlier[:, None]
     slots_own = jnp.sum(jnp.where(sorting, (route % rows)[None, :], 0), axis=1)
     sort_hot = sorting.astype(BF16)
-    tokens_b = jnp.dot(sort_hot, tokens, preferred_element_type=F32).astype(BF16)
-    cotangent_b = jnp.dot(sort_hot, cotangent, preferred_element_type=F32).astype(BF16)
 
     mask_window = lax.dynamic_slice_in_dim(
         jnp.concatenate([jnp.zeros((WINDOW,), jnp.int32), key_mask]), z * rows, rows + WINDOW
     )
-    notes = jnp.concatenate([slots_own, mask_window, lengths[0]])
-    notes = jnp.pad(notes, (0, 8 * LANES - notes.shape[0])).reshape(8, LANES)
-
-    normed, _ = norm_rows(tokens_b.astype(F32))
-    hidden_own = (normed * norm1_gain).astype(BF16)
-    hidden_one, w_qkv, w_proj, notes_all, both_own, down_own = gather_first(
-        hidden_own, w_query.T, w_key.T, w_value.T, w_out, w_gate, w_up, w_down, notes
-    )
-    notes_all = notes_all.reshape(groups, 8 * LANES)
-    slots = (
-        notes_all[:, :rows].reshape(groups, groups, bucket).transpose(1, 0, 2).reshape(groups, rows)
-    )
-    flags = notes_all[:, rows : 2 * rows + WINDOW]
-    lengths_all = notes_all[:, 2 * rows + WINDOW : 2 * rows + WINDOW + 3]
-
-    w_both = lax.all_gather(both_own, "mp")
-    down_all = lax.all_gather(down_own, "mp", axis=0, tiled=True)
+    slot_rows = jnp.pad(slots_own.reshape(groups, bucket).T, ((0, 0), (0, LANES - groups)))
+    mask_rows = jnp.pad(mask_window, (0, 4 * LANES - rows - WINDOW)).reshape(4, LANES)
+    length_rows = jnp.pad(lengths, ((0, 3), (0, LANES - lengths.shape[1])))
+    notes = jnp.concatenate([slot_rows, mask_rows, length_rows], axis=0).astype(F32)
 
     count = groups * rows
     scale = HEAD_DIM ** (-0.5)
-    mixed, kept, cotangent_all = attend_ahead(
-        lengths_all, hidden_one, w_qkv, slots, flags, cotangent_b, scale
+    (
+        hidden_one,
+        w_qkv,
+        w_proj,
+        notes_all,
+        w_both,
+        mixed,
+        kept,
+        tokens_b,
+        cotangent_b,
+        cotangent_all,
+    ) = attend_ahead(
+        tokens,
+        cotangent,
+        send_at.astype(F32)[None],
+        norm1_gain[None],
+        notes,
+        w_query.T,
+        w_key.T,
+        w_value.T,
+        w_out,
+        w_gate,
+        w_up,
+        scale,
     )
     mixed = mixed.reshape(count, 2 * LANES)
-    middle, hidden_two = project_middle(mixed, w_proj, tokens_b, norm2_gain[None])
+    middle, hidden_two, down_all = project_middle(mixed, w_proj, tokens_b, norm2_gain[None], w_down)
+    down_all = down_all.reshape(members * units, width)
     middle_grad, branch, sums_two, activated, both_sum, down_in = feed(
         hidden_two, cotangent_all, middle, cotangent_b, norm2_gain[None], w_both, down_all
     )
     qkv_grad, output_rows, branch_all, both_in, down_whole = attend_back(
-        lengths_all,
         kept,
         branch,
         w_proj,
-        slots,
-        flags,
+        notes_all,
         activated.reshape(count, units * members),
         down_all,
         middle,

time: 622 us -> 627 us (level)
  Pallas kernels: 580 us -> 606 us
  between operations: 14.2 us -> 0.71 us
    pallas_call x2 -> x1, Pallas kernels: 120 us -> 139 us  [attend_ahead(): pl.pallas_call(functools.partial(forward_kernel, scale=scale), out_shape=...]
    pallas_call x1, Pallas kernels: 58.7 us -> 65.5 us  [project_middle(): pl.pallas_call(middle_kernel, out_shape=(jax.ShapeDtypeStruct((rows, widt...]
  transfers between devices with their start and end apart: 2 -> 0, of which waited for: 1 -> 0; matrix products, arithmetic and copies ran while one was open for 1% -> 0% of each run, Pallas kernels for 19% -> 0%
where the time goes in v7:
time: 627 us; the launch traced here: 626 us
  Pallas kernels  606 us (97%)
  other arithmetic  7.98 us (1%)
  matrix products  6.7 us (1%)
    pallas_call x1, Pallas kernels, attend_ahead(): pl.pallas_call(functools.partial(forward_kernel, scale=scale), out_shape=...  139 us
    pallas_call x1, Pallas kernels, attend_back(): pl.pallas_call(functools.partial(backward_kernel, scale=scale, groups=gro...  135 us
    pallas_call x1, Pallas kernels, project_input(): pl.pallas_call(input_kernel, out_shape=(shape((rows, width), BF16), shape...  125 us
    pallas_call x1, Pallas kernels, feed(): pl.pallas_call(feed_kernel, out_shape=(jax.ShapeDtypeStruct((rows, width)...  123 us
    pallas_call x1, Pallas kernels, project_middle(): pl.pallas_call(middle_kernel, out_shape=(jax.ShapeDtypeStruct((rows, widt...  65.5 us

profile of v7, /device:TPU:0, one launch (start us, length us, event | category | flops | bytes accessed | tf_op | source)
XLA Modules:
  0.0 625.7 jit_solution(9033367587824087947)
XLA Ops:
  0.6 0.8 pad_dynamic-slice_fusion
  1.4 0.7 add_select_fusion
  2.1 0.2 convert_reduce_fusion
  2.4 0.6 broadcast_in_dim.18.order_row
  2.9 0.1 select_reduce_fusion
  3.1 0.1 reshape.53
  3.2 1.3 broadcast_in_dim.19.gain
  4.5 1.3 broadcast_in_dim.35.gain
  5.8 0.1 copy.26
  5.9 1.3 fusion.3.notes
  7.1 139.3 %attend_ahead.1 = (bf16[8,384,1792]{2,1,0:T(8,128)(2,1)}, bf16[768,1792]{1,0:T(8,128)(2,1)}, bf16[256,1792]{1,0:T(8,128)(2,1)}, f32[8,56,128]{2,1,0:T(8,128)}, b...) custom-call(bf16[384,1792]{1,0:T(8,128)(2,1)} %tokens.1, ...), custom_call_target="tpu_custom_call" | custom-call | bytes 300000000 | tf_op jit(solution)/shard_map/attend_ahead/pallas_call | solution.py:833
  146.4 65.5 %project_middle.1 = (f32[384,1792]{1,0:T(8,128)}, bf16[384,1792]{1,0:T(8,128)(2,1)}, bf16[4,128,1792]{2,1,0:T(8,128)(2,1)}) custom-call(bf16[3072,256]{1,0:T(8,128)(2,1)} %bitcast.22, bf16[256,1792]{1,0:T(8,128)(2,1)} %get-tuple-element.47.w_out, bf16[384,1792]{1,0:T(8,128)(2,1)} %get-tuple-element.48.tokens, f32[1,1792]{1,0:T(1,128)} %broadcast_in_dim.35.gain, ...), custom_call_target="tpu_custom_call" | custom-call | bytes 150000000 | tf_op jit(solution)/shard_map/project_middle/pallas_call | solution.py:1557
  211.9 123.1 %feed.1 = (f32[384,1792]{1,0:T(8,128)}, bf16[384,1792]{1,0:T(8,128)(2,1)}, f32[8,1792]{1,0:T(8,128)}, bf16[8,384,512]{2,1,0:T(8,128)(2,1)}, bf16[4,1792,256]{2,1...) custom-call(bf16[384,1792]{1,0:T(8,128)(2,1)} %get-tuple-element.49.hidden_own, ...), custom_call_target="tpu_custom_call" | custom-call | bytes 400000000 | tf_op jit(solution)/shard_map/feed/pallas_call | solution.py:1807
  335.0 134.9 %attend_back.1 = (bf16[8,8,48,768]{3,2,1,0:T(8,128)(2,1)}, bf16[384,1792]{1,0:T(8,128)(2,1)}, bf16[8,384,1792]{2,1,0:T(8,128)(2,1)}, bf16[4,1792,256]{2,1,0:T(8,128)(2,1)}, bf16[8,128,1792]{2,1,0:T(8,128)(2,1)}) custom-call(bf16[8,448,768]{2,1,0:T(8,128)(2,1)} %get-tuple-element.45.kept, bf16[384,1792]{1,0:T(8,128)(2,1)} %get-tuple-element.55.branch, ...), custom_call_target="tpu_custom_call" | custom-call | bytes 300000000 | tf_op jit(solution)/shard_map/attend_back/pallas_call | solution.py:1482
  470.0 3.3 convolution_convert_fusion.1
  473.3 125.3 %project_input.1 = (bf16[384,1792]{1,0:T(8,128)(2,1)}, f32[2,1792]{1,0:T(2,128)}, bf16[8,1792,256]{2,1,0:T(8,128)(2,1)}, bf16[8,448,896]{2,1,0:T(8,128)(2,1)}) custom-call(bf16[3072,768]{1,0:T(8,128)(2,1)} %bitcast.24, bf16[768,1792]{1,0:T(8,128)(2,1)} %get-tuple-element.62.w_qkv, bf16[8,384,1792]{2,1,0:T(8,128)(2,1)} %get-tuple-element.63.hidden_all, ...), custom_call_target="tpu_custom_call" | custom-call | bytes 250000000 | tf_op jit(solution)/shard_map/project_input/pallas_call | solution.py:1989
  598.6 0.0 copy-start
  598.6 3.4 convolution_convert_fusion
  602.0 0.0 copy-done
  602.0 0.6 slice_reduce_fusion
  602.6 5.6 bitcast_convert_fusion
  608.2 7.8 %assemble_heads.1 = (f32[448,1792]{1,0:T(8,128)}, f32[448,1792]{1,0:T(8,128)}, f32[448,1792]{1,0:T(8,128)}, f32[448,1792]{1,0:T(8,128)}) custom-call(bf16[4,2,4,112,896]{4,3,2,1,0:T(8,128)(2,1)} %bitcast.21), custom_call_target="tpu_custom_call" | custom-call | bytes 20000000 | tf_op jit(solution)/shard_map/assemble_heads/pallas_call | solution.py:2065
  616.0 9.7 %assemble_units.1 = (f32[1792,1024]{1,0:T(8,128)}, f32[1792,1024]{1,0:T(8,128)}) custom-call(bf16[8,1792,256]{2,1,0:T(8,128)(2,1)} %get-tuple-element.75.both), custom_call_target="tpu_custom_call" | custom-call | bytes 22000000 | tf_op jit(solution)/shard_map/assemble_units/pallas_call | solution.py:2043
  (2 shorter events, 0.0 us)
Async XLA Ops:
  598.6 3.4 copy-start

commit v8 on v7

--- a/solution.py
+++ b/solution.py
@@ -521,16 +521,16 @@
             self.shares[piece], self.target(which, piece), self.local.at[piece]
         )
 
-    def start(self):
+    def start(self, pieces):
         @pl.when(self.place == 0)
         def _():
-            for piece in range(4):
+            for piece in pieces:
                 self.hop(0, piece, 0, 1, True).start()
                 self.keep(0, piece).start()
 
         @pl.when(self.place == 1)
         def _():
-            for piece in range(4):
+            for piece in pieces:
                 self.hop(1, piece, 0, 0, True).start()
                 self.hop(1, piece, 1, 2, True).start()
                 self.keep(1, piece).start()
@@ -544,22 +544,22 @@
 
         @pl.when(self.place == 2)
         def _():
-            for piece in pieces:
-                for which in (1, 0):
+            for which in (1, 0):
+                for piece in pieces:
                     self.hop(which, piece, which, 3, False).wait_recv()
                     self.hop(which, piece, which, 3, False).start()
 
-    def finish(self):
+    def finish(self, pieces):
         @pl.when(self.place == 0)
         def _():
-            for piece in range(4):
+            for piece in pieces:
                 self.hop(1, piece, 0, 1, False).wait_recv()
                 self.hop(0, piece, 0, 1, True).wait_send()
                 self.keep(0, piece).wait()
 
         @pl.when(self.place == 1)
         def _():
-            for piece in range(4):
+            for piece in pieces:
                 self.hop(1, piece, 0, 0, True).wait_send()
                 self.hop(1, piece, 1, 2, True).wait_send()
                 self.hop(0, piece, 2, 2, False).wait_send()
@@ -567,55 +567,80 @@
 
         @pl.when(self.place == 2)
         def _():
-            for piece in range(4):
+            for piece in pieces:
                 for which in (1, 0):
                     self.hop(which, piece, which, 3, False).wait_send()
 
         @pl.when(self.place == 3)
         def _():
-            for piece in range(4):
+            for piece in pieces:
                 for which in (1, 0):
                     self.hop(which, piece, which, 3, False).wait_recv()
 
 
-class Chain:
+class Column:
     def __init__(self, own, out, send, recv, local):
-        self.z = lax.axis_index("mp")
-        self.own, self.out, self.send, self.recv = own, out, send, recv
-        self.keep = pltpu.make_async_copy(own, out.at[self.z], local)
-
-    def hop(self, way, distance):
-        z = self.z
-        source = z - way * distance
+        z = lax.axis_index("mp")
+        self.z, self.own, self.out, self.send, self.recv = z, own, out, send, recv
+        self.outer = (z == 0) | (z == 3)
+        near = 1 + lax.div(z, 3)
+        self.from_outer = (near, 3 - near)
+        self.edge = 3 * (z - 1)
+        self.from_inner = (3 - z, 3 - self.edge, self.edge)
+        self.keep = pltpu.make_async_copy(own, out.at[z], local)
+
+    def straight(self, number, target):
         return to_mp(
-            self.own if distance == 0 else self.out.at[source],
-            self.out.at[source],
-            self.send.at[3 * (way > 0) + distance],
-            self.recv.at[3 * (way > 0) + distance],
-            z + way,
-        )
-
-    def ways(self, distance):
-        z = self.z
-        return (
-            (1, z >= distance, (z >= distance) & (z < 3)),
-            (-1, z <= 3 - distance, (z <= 3 - distance) & (z > 0)),
-        )
-
-    def step(self, distance):
-        if distance == 0:
-            self.keep.start()
-        for way, there, onward in self.ways(distance):
-            if distance > 0:
-                pl.when(there)(self.hop(way, distance - 1).wait_recv)
-            if distance < 3:
-                pl.when(onward)(self.hop(way, distance).start)
+            self.own, self.out.at[self.z], self.send.at[number], self.recv.at[self.z], target
+        )
+
+    def onward(self):
+        far = 3 - self.edge
+        return to_mp(
+            self.out.at[far], self.out.at[far], self.send.at[3], self.recv.at[far], self.edge
+        )
+
+    def came(self, source):
+        return to_mp(
+            self.own, self.out.at[source], self.send.at[0], self.recv.at[source], source
+        ).wait_recv
+
+    def start(self):
+        self.keep.start()
+
+        @pl.when(self.outer)
+        def _():
+            for number, target in enumerate(self.from_outer):
+                self.straight(number, target).start()
+
+        @pl.when(jnp.logical_not(self.outer))
+        def _():
+            for number, target in enumerate(self.from_inner):
+                self.straight(number, target).start()
+
+    def pass_on(self):
+        @pl.when(jnp.logical_not(self.outer))
+        def _():
+            self.came(3 - self.edge)()
+            self.onward().start()
 
     def finish(self):
-        self.step(3)
-        for distance in range(3):
-            for way, _, onward in self.ways(distance):
-                pl.when(onward)(self.hop(way, distance).wait_send)
+        @pl.when(self.outer)
+        def _():
+            for source in (1, 2):
+                self.came(source)()
+            self.came(3 - self.z)()
+            for number, target in enumerate(self.from_outer):
+                self.straight(number, target).wait_send()
+
+        @pl.when(jnp.logical_not(self.outer))
+        def _():
+            self.came(3 - self.z)()
+            self.came(self.edge)()
+            for number, target in enumerate(self.from_inner):
+                self.straight(number, target).wait_send()
+            self.onward().wait_send()
+
         self.keep.wait()
 
 
@@ -709,19 +734,19 @@
     for copy in loads[:4]:
         copy.wait()
     spread = Spread(share, w_qkv, w_out, send_w, recv_w, local)
-    spread.start()
+    spread.start((0, 1, 2))
     cotangent_b[...] = jnp.dot(sort, cotangent[...], preferred_element_type=F32).astype(BF16)
     for copy in loads[4:]:
         copy.wait()
-    chain = Chain(both_own, w_both, send_c, recv_c, local.at[4])
+    column = Column(both_own, w_both, send_c, recv_c, local.at[4])
     second = Gather(cotangent_b, cotangent_all, send_g, recv_g, local.at[5])
-    spread.pass_on((0, 1))
     gather.arrive(0, 1)
-    spread.pass_on((2, 3))
+    second.start()
+    spread.pass_on((0, 1, 2))
+    column.start()
     gather.arrive(2, 3)
-    second.start()
-    chain.step(0)
-    spread.finish()
+    spread.finish((0, 1, 2))
+    spread.start((3,))
     for copy in swaps:
         copy.wait()
 
@@ -799,13 +824,14 @@
         mixed[:, pl.ds(k, 1)] = back.reshape(groups, 1, rows // groups, 256)
         return carry
 
-    chain.step(1)
+    spread.pass_on((3,))
     lax.fori_loop(0, groups // 2, attend, 0)
     second.pass_on()
-    chain.step(2)
+    column.pass_on()
     lax.fori_loop(groups // 2, groups, attend, 0)
+    spread.finish((3,))
     second.finish()
-    chain.finish()
+    column.finish()
     gather.sent()
 
     def kept_out(turn, carry):
@@ -865,8 +891,8 @@
             dma((8,)),
             dma((7,)),
             dma((7,)),
-            dma((6,)),
-            dma((6,)),
+            dma((4,)),
+            dma((4,)),
             dma((6,)),
             dma((groups,)),
         ],
@@ -1530,13 +1556,12 @@
     load.start()
     greet_all(pltpu.get_barrier_semaphore())
     load.wait()
-    chain = Chain(down_own, down_all, send_c, recv_c, local.at[1])
-    chain.step(0)
+    column = Column(down_own, down_all, send_c, recv_c, local.at[1])
+    column.start()
     reduce = Reduce(mixed, w_out, False, part, from_side, from_corner, from_near, send, recv)
     reduce.begin()
-    chain.step(1)
     reduce.middle()
-    chain.step(2)
+    column.pass_on()
     reduce.end()
 
     def body(span):
@@ -1546,7 +1571,7 @@
         hidden[span, :] = (values * inverse * gain[...]).astype(BF16)
 
     each_chunk(hidden.shape[0], body)
-    chain.finish()
+    column.finish()
     reduce.finish()
 
 
@@ -1564,7 +1589,7 @@
         in_specs=[on_chip()] * 4 + [anywhere()],
         out_specs=(on_chip(), on_chip(), anywhere()),
         scratch_shapes=reduce_scratch(rows, width)
-        + [pltpu.VMEM((LANES, width), BF16), dma((6,)), dma((6,)), dma((2,))],
+        + [pltpu.VMEM((LANES, width), BF16), dma((4,)), dma((4,)), dma((2,))],
         compiler_params=remote_params(4),
         cost_estimate=pl.CostEstimate(flops=0, bytes_accessed=150_000_000, transcendentals=0),
         name="project_middle",
@@ -1584,41 +1609,37 @@
 
 
 def feed_kernel(
-    hidden_own, cotangent_all, middle, cotangent, gain, w_both, w_down,
+    hidden_own, cotangent_all, middle, w_parts, cotangent, gain, w_down,
     middle_grad, branch, sums, activated, both_sum, down_in,
     hidden_all, both_grad, part, from_side, from_corner, from_near, send_r, recv_r,
-    send_a, recv_a, cot_half, cot_tile, stage_both, down_sum, load_sem, local, send_z, recv_z,
+    send_a, recv_a, cot_shard, cot_tile, stage_both, down_sum, w_both, load_sem, local, send_z, recv_z,
 ):
     groups, rows, width = hidden_all.shape
-    members = w_both.shape[0]
-    half_rows = rows // 2
-    me, side, over_x, over_y, _ = plane()
+    members = w_parts.shape[0]
+    me = lax.axis_index("dp")
     own = pltpu.make_async_copy(hidden_own, hidden_all.at[me], local.at[0])
     own.start()
     start_middle = pltpu.make_async_copy(middle, middle_grad, local.at[1])
-    start_middle.start()
-
-    def place_of(step):
-        block = step // 4
+    loads = [
+        pltpu.make_async_copy(w_parts.at[z], w_both.at[:, pl.ds(z * 256, 256)], load_sem.at[6 + z])
+        for z in range(members)
+    ]
+
+    def slot_of(turn):
+        block = turn // 2
         near = ((block + 1) // 2) % 2
         far = block // 3
-        mixed_order = near * (1 - block // 2)
-        second = mixed_order * (step % 2) + (1 - mixed_order) * ((step // 2) % 2)
-        half = mixed_order * ((step % 2 + (step // 2) % 2) % 2) + (1 - mixed_order) * (step % 2)
+        second = turn % 2
         other = (1 - near) * second + (block // 2) * near
-        in_x = near * (1 - second) + far
-        in_y = near * second + far
-        owner = me + in_x * (over_x - me) + in_y * (over_y - me) + other * (side - me)
-        slot = 4 * other + 3 * (1 - near) * (1 - far) + near * (1 + second)
-        return owner, half, slot
-
-    def load_cotangent(step):
-        owner, half, _ = place_of(step)
-        span = pl.ds(pl.multiple_of(half * half_rows, half_rows), half_rows)
+        return 4 * other + 3 * (1 - near) * (1 - far) + near * (1 + second)
+
+    def load_cotangent(turn):
         return pltpu.make_async_copy(
-            cotangent_all.at[owner, span], cot_half.at[step % 2], load_sem.at[step % 2]
-        )
-
+            cotangent_all.at[owner_at(turn)], cot_shard.at[turn % 2], load_sem.at[turn % 2]
+        )
+
+    for copy in loads:
+        copy.start()
     load_cotangent(0).start()
     greet_all(pltpu.get_barrier_semaphore())
     own.wait()
@@ -1627,44 +1648,33 @@
     reduce = Reduce(None, None, False, part, from_side, from_corner, from_near, send_r, recv_r)
     reduce.prepare()
 
-    def before(step, *numbers):
-        return (step, lambda: gather.arrive(*numbers))
-
     def nears():
         reduce.add_side(1)
         reduce.nears[0].start()
         reduce.add_side(2)
         reduce.nears[2].start()
 
-    early = [
-        before(2, 4),
-        before(4, 0),
-        before(5, 1),
-        before(6, 2),
-        before(7, 3),
-        before(8, 6, 9),
-        before(10, 8, 10),
-        before(12, 5, 7),
-        (13, nears),
-        before(14, 11, 12),
-    ]
-    late = [(3, 3), (9, 1), (11, 2), (15, 0)]
-
-    def unit(step, carry):
+    early = [(turn, functools.partial(gather.arrive, *numbers)) for turn, numbers in ARRIVALS]
+    early += [(6, nears)]
+    late = [(1, 3), (4, 1), (5, 2), (7, 0)]
+    start_middle.start()
+    for copy in loads:
+        copy.wait()
+
+    def unit(turn, carry):
         for number, action in early:
-            pl.when(step == number)(action)
-
-        @pl.when(step < 15)
-        def _():
-            load_cotangent(step + 1).start()
-
-        load_cotangent(step).wait()
-        owner, half, slot = place_of(step)
-        span = pl.ds(pl.multiple_of(half * half_rows, half_rows), half_rows)
-        mine = hidden_all[owner, span, :]
-        grads = cot_half[step % 2]
+            pl.when(turn == number)(action)
+
+        @pl.when(turn < 7)
+        def _():
+            load_cotangent(turn + 1).start()
+
+        load_cotangent(turn).wait()
+        owner, slot = owner_at(turn), slot_of(turn)
+        mine = hidden_all[owner]
+        grads = cot_shard[turn % 2]
         for z in range(members):
-            raw = jnp.dot(mine, w_both[z], preferred_element_type=F32)
+            raw = jnp.dot(mine, w_both[:, z * 256 : z * 256 + 256], preferred_element_type=F32)
             units = pl.ds(z * 128, 128)
             if z % 2 == 0:
                 pair = lax.dot_general(
@@ -1673,34 +1683,27 @@
             active_grad = pair[:, 128 * (z % 2) : 128 * (z % 2) + 128]
             gate, upward = raw[:, :128], raw[:, 128:]
             sigmoid = jax.nn.sigmoid(gate)
-            activated[owner, span, units] = (gate * sigmoid * upward).astype(BF16)
-            both_grad[owner, span, pl.ds(z * 256, 128)] = (
+            activated[owner, :, units] = (gate * sigmoid * upward).astype(BF16)
+            both_grad[owner, :, pl.ds(z * 256, 128)] = (
                 active_grad * upward * sigmoid * (1.0 + gate * (1.0 - sigmoid))
             ).astype(BF16)
-            both_grad[owner, span, pl.ds(z * 256 + 128, 128)] = (
+            both_grad[owner, :, pl.ds(z * 256 + 128, 128)] = (
                 active_grad * gate * sigmoid
             ).astype(BF16)
 
         def tile(t, inner):
             columns = pl.ds(pl.multiple_of(t * 256, 256), 256)
-            value = sum(
-                lax.dot_general(
-                    both_grad[owner, span, pl.ds(z * 256, 256)],
-                    w_both[z, columns, :],
-                    NT,
-                    preferred_element_type=F32,
-                )
-                for z in range(members)
-            )
-            part[slot, span, columns] = value.astype(BF16)
+            part[slot, :, columns] = lax.dot_general(
+                both_grad[owner], w_both[columns, :], NT, preferred_element_type=F32
+            ).astype(BF16)
             return inner
 
         lax.fori_loop(0, width // 256, tile, 0)
         for number, share in late:
-            pl.when(step == number)(reduce.shares[share].start)
+            pl.when(turn == number)(reduce.shares[share].start)
         return carry
 
-    lax.fori_loop(0, 16, unit, 0)
+    lax.fori_loop(0, 8, unit, 0)
 
     def load_tile(t):
         columns = pl.ds(pl.multiple_of(t * 256, 256), 256)
@@ -1799,7 +1802,7 @@
         copy.wait()
 
 
-def feed(hidden_own, cotangent_all, middle, cotangent, gain, w_both, w_down):
+def feed(hidden_own, cotangent_all, middle, w_both, cotangent, gain, w_down):
     groups, rows, width = cotangent_all.shape
     members = w_both.shape[0]
     dma = pltpu.SemaphoreType.DMA
@@ -1814,7 +1817,7 @@
             jax.ShapeDtypeStruct((members, width, 256), BF16),
             jax.ShapeDtypeStruct((members, LANES, width), BF16),
         ),
-        in_specs=[anywhere()] * 3 + [on_chip()] * 4,
+        in_specs=[anywhere()] * 4 + [on_chip()] * 3,
         out_specs=(on_chip(),) * 4 + (anywhere(),) * 2,
         scratch_shapes=[
             pltpu.VMEM((groups, rows, width), BF16),
@@ -1824,19 +1827,20 @@
         + [
             dma((13,)),
             dma((13,)),
-            pltpu.VMEM((2, rows // 2, width), BF16),
+            pltpu.VMEM((2, rows, width), BF16),
             pltpu.VMEM((2, groups, rows, 256), BF16),
             pltpu.VMEM((2, members, 256, 256), BF16),
             pltpu.VMEM((units, width), BF16),
-            dma((6,)),
+            pltpu.VMEM((width, 2 * units), BF16),
+            dma((6 + members,)),
             dma((3,)),
             dma((3,)),
             dma((3,)),
         ],
-        compiler_params=remote_params(5, 62 * 1024 * 1024),
+        compiler_params=remote_params(5, 63 * 1024 * 1024),
         cost_estimate=pl.CostEstimate(flops=0, bytes_accessed=400_000_000, transcendentals=0),
         name="feed",
-    )(hidden_own, cotangent_all, middle, cotangent, gain, w_both, w_down)
+    )(hidden_own, cotangent_all, middle, w_both, cotangent, gain, w_down)
 
 
 def input_kernel(
@@ -1889,7 +1893,6 @@
 
     each_chunk(both_found.shape[1], add)
     both = Gather(both_found.at[0], both_all, send_b, recv_b, local.at[4])
-    both.start()
 
     def weight_tile(t, carry):
         @pl.when(t < tiles - 1)
@@ -1917,16 +1920,15 @@
         return carry
 
     heads = Heads(weight_sum, stage, arrive, send_h, recv_s, recv_h)
+    reduce = Reduce(qkv_grad, w_qkv, False, part, from_side, from_corner, from_near, send, recv)
+    reduce.begin()
     lax.fori_loop(0, tiles, weight_tile, 0)
     heads.start((3,))
+    reduce.middle()
+    both.start()
     lax.fori_loop(tiles, 2 * tiles, weight_tile, 0)
     heads.start((0, 1, 2))
-    reduce = Reduce(qkv_grad, w_qkv, False, part, from_side, from_corner, from_near, send, recv)
-    reduce.begin()
-    both.pass_on()
-    heads.add((3, 0))
-    reduce.middle()
-    heads.add((1, 2))
+    heads.add((3,))
     reduce.end()
     sums[...] = jnp.zeros_like(sums)
 
@@ -1947,6 +1949,8 @@
     for copy in swaps:
         copy.start()
     plane_sums[me] = own[...]
+    heads.add((0, 1, 2))
+    both.pass_on()
     heads.total(heads_own)
     gather = Gather(heads_own, heads_all, send_t, recv_t, local.at[5])
     gather.start()
@@ -2029,48 +2033,65 @@
     )
 
 
-def units_kernel(both, gate, upward):
+def assemble_kernel(
+    both, down, heads, order_column, output_b, input_b,
+    output, inputs, query, keys, values, project, gate, upward, down_out,
+):
     for d in range(both.shape[0]):
         gate[:, d * 128 : d * 128 + 128] = both[d, :, :128].astype(F32)
         upward[:, d * 128 : d * 128 + 128] = both[d, :, 128:].astype(F32)
-
-
-def assemble_units(both):
+    down_out[...] = down[0].astype(F32)
+    for kind, out in enumerate((query, keys, values, project)):
+        out[...] = heads[0, kind].astype(F32)
+    place = lax.broadcasted_iota(jnp.int32, (order_column.shape[0], output_b.shape[0]), 1)
+    unsort = (place.astype(F32) == order_column[...]).astype(BF16)
+    output[...] = jnp.dot(unsort, output_b[...], preferred_element_type=F32).astype(BF16)
+    inputs[...] = jnp.dot(unsort, input_b[...], preferred_element_type=F32).astype(BF16)
+
+
+def assemble(both, down, heads, order_column, output_b, input_b):
     groups, width, wide = both.shape
-    tile = 256
-    shape = jax.ShapeDtypeStruct((width, groups * wide // 2), F32)
-    spec = pl.BlockSpec((tile, groups * wide // 2), lambda i: (i, 0))
+    rows = output_b.shape[0]
+    units = down.shape[1]
+    chips = groups // 2
+    columns = heads.shape[3]
+    row_tile, tile = rows // groups, width // groups
+    shape = jax.ShapeDtypeStruct
+    head = shape((chips * HEAD_DIM, 2 * columns), F32)
+    head_spec = pl.BlockSpec((HEAD_DIM, columns), lambda i: (i // 2, i % 2))
+    wide_spec = pl.BlockSpec((tile, groups * units), lambda i: (i, 0))
+    row_spec = pl.BlockSpec((row_tile, width), lambda i: (i, 0))
+    whole_spec = pl.BlockSpec((rows, width), lambda i: (0, 0))
     return pl.pallas_call(
-        units_kernel,
-        grid=(width // tile,),
-        out_shape=(shape, shape),
-        in_specs=[pl.BlockSpec((groups, tile, wide), lambda i: (0, i, 0))],
-        out_specs=(spec, spec),
-        cost_estimate=pl.CostEstimate(flops=0, bytes_accessed=22_000_000, transcendentals=0),
-        name="assemble_units",
-    )(both)
-
-
-def heads_kernel(whole, *outs):
-    columns = whole.shape[4]
-    for kind, out in enumerate(outs):
-        for half in range(whole.shape[1]):
-            out[:, half * columns : half * columns + columns] = whole[0, half, kind].astype(F32)
-
-
-def assemble_heads(whole):
-    chips, halves, kinds, rows, columns = whole.shape
-    shape = jax.ShapeDtypeStruct((chips * rows, halves * columns), F32)
-    spec = pl.BlockSpec((rows, halves * columns), lambda c: (c, 0))
-    return pl.pallas_call(
-        heads_kernel,
-        grid=(chips,),
-        out_shape=(shape,) * kinds,
-        in_specs=[pl.BlockSpec((1, halves, kinds, rows, columns), lambda c: (c, 0, 0, 0, 0))],
-        out_specs=(spec,) * kinds,
-        cost_estimate=pl.CostEstimate(flops=0, bytes_accessed=20_000_000, transcendentals=0),
-        name="assemble_heads",
-    )(whole)
+        assemble_kernel,
+        grid=(groups,),
+        out_shape=(
+            shape((rows, width), BF16),
+            shape((rows, width), BF16),
+            head,
+            head,
+            head,
+            head,
+            shape((width, groups * units), F32),
+            shape((width, groups * units), F32),
+            shape((groups * units, width), F32),
+        ),
+        in_specs=[
+            pl.BlockSpec((groups, tile, wide), lambda i: (0, i, 0)),
+            pl.BlockSpec((1, units, width), lambda i: (i, 0, 0)),
+            pl.BlockSpec((1, 4, HEAD_DIM, columns), lambda i: (i, 0, 0, 0)),
+            pl.BlockSpec((row_tile, 1), lambda i: (i, 0)),
+            whole_spec,
+            whole_spec,
+        ],
+        out_specs=(
+            row_spec, row_spec, head_spec, head_spec, head_spec, head_spec, wide_spec, wide_spec,
+            pl.BlockSpec((units, width), lambda i: (i, 0)),
+        ),
+        compiler_params=pltpu.CompilerParams(vmem_limit_bytes=VMEM_LIMIT),
+        cost_estimate=pl.CostEstimate(flops=0, bytes_accessed=58_000_000, transcendentals=0),
+        name="assemble",
+    )(both, down, heads, order_column, output_b, input_b)
 
 
 def swapped(
@@ -2091,7 +2112,6 @@
     send_at = target * bucket + jnp.sum(same.astype(jnp.int32), axis=1)
     sorting = send_at[None, :] == earlier[:, None]
     slots_own = jnp.sum(jnp.where(sorting, (route % rows)[None, :], 0), axis=1)
-    sort_hot = sorting.astype(BF16)
 
     mask_window = lax.dynamic_slice_in_dim(
         jnp.concatenate([jnp.zeros((WINDOW,), jnp.int32), key_mask]), z * rows, rows + WINDOW
@@ -2132,7 +2152,7 @@
     middle, hidden_two, down_all = project_middle(mixed, w_proj, tokens_b, norm2_gain[None], w_down)
     down_all = down_all.reshape(members * units, width)
     middle_grad, branch, sums_two, activated, both_sum, down_in = feed(
-        hidden_two, cotangent_all, middle, cotangent_b, norm2_gain[None], w_both, down_all
+        hidden_two, cotangent_all, middle, w_both, cotangent_b, norm2_gain[None], down_all
     )
     qkv_grad, output_rows, branch_all, both_in, down_whole = attend_back(
         kept,
@@ -2160,16 +2180,27 @@
         both_sum,
         both_in,
     )
-    gate_grad, up_grad = assemble_units(both_whole)
-    down_grad = down_whole.astype(F32).reshape(groups * units, width)
-    query_grad, key_grad, value_grad, proj_grad = assemble_heads(
-        heads_whole.reshape(groups // 2, 2, 4, HEAD_DIM, width // 2)
-    )
-
-    unsort = (((0,), (0,)), ((), ()))
+    (
+        output,
+        input_grad,
+        query_grad,
+        key_grad,
+        value_grad,
+        proj_grad,
+        gate_grad,
+        up_grad,
+        down_grad,
+    ) = assemble(
+        both_whole,
+        down_whole,
+        heads_whole.reshape(groups, 4, HEAD_DIM, width // 2),
+        send_at.astype(F32)[:, None],
+        output_rows,
+        input_rows,
+    )
     return (
-        lax.dot_general(sort_hot, output_rows, unsort, preferred_element_type=F32).astype(BF16),
-        lax.dot_general(sort_hot, input_rows, unsort, preferred_element_type=F32).astype(BF16),
+        output,
+        input_grad,
         gain_sums[0],
         gain_sums[1],
         query_grad.T,

time: 627 us -> 621 us (level)
  matrix products: 6.7 us -> 0 us
    pallas_call x1, Pallas kernels: 65.5 us -> 81.4 us  [project_middle(): pl.pallas_call(middle_kernel, out_shape=(jax.ShapeDtypeStruct((rows, widt...]
    pallas_call x1, Pallas kernels: 139 us -> 128 us  [attend_ahead(): pl.pallas_call(functools.partial(forward_kernel, scale=scale), out_shape=...]
    dot_general x2 -> x0, matrix products: 6.7 us -> none  [the longest x1 3.35 us: swapped(): lax.dot_general(sort_hot, input_rows, unsort, preferred_element_type=F32)]
    pallas_call x2 -> x1, Pallas kernels: 17.5 us -> 21.1 us  [assemble(): pl.pallas_call(assemble_kernel, grid=(groups,), out_shape=(shape((rows, w...]
where the time goes in v8:
time: 621 us; the launch traced here: 617 us
  Pallas kernels  609 us (98%)
    pallas_call x1, Pallas kernels, attend_back(): pl.pallas_call(functools.partial(backward_kernel, scale=scale, groups=gro...  134 us
    pallas_call x1, Pallas kernels, attend_ahead(): pl.pallas_call(functools.partial(forward_kernel, scale=scale), out_shape=...  128 us
    pallas_call x1, Pallas kernels, project_input(): pl.pallas_call(input_kernel, out_shape=(shape((rows, width), BF16), shape...  126 us
    pallas_call x1, Pallas kernels, feed(): pl.pallas_call(feed_kernel, out_shape=(jax.ShapeDtypeStruct((rows, width)...  119 us
    pallas_call x1, Pallas kernels, project_middle(): pl.pallas_call(middle_kernel, out_shape=(jax.ShapeDtypeStruct((rows, widt...  81.4 us
    pallas_call x1, Pallas kernels, assemble(): pl.pallas_call(assemble_kernel, grid=(groups,), out_shape=(shape((rows, w...  21.1 us

profile of v8, /device:TPU:0, one launch (start us, length us, event | category | flops | bytes accessed | tf_op | source)
XLA Modules:
  0.0 617.0 jit_solution(16349535408285317750)
XLA Ops:
  0.6 0.7 add_select_fusion
  1.3 0.2 convert_reduce_fusion
  1.6 0.2 select_reduce_fusion
  1.7 0.1 reshape.47
  1.8 0.1 copy.27
  1.9 0.8 pad_dynamic-slice_fusion
  2.7 1.3 fusion.1.notes
  4.0 0.6 broadcast_in_dim.20.order_row
  4.5 1.3 broadcast_in_dim.21.gain
  5.8 0.0 copy-start.1
  5.8 127.7 %attend_ahead.1 = (bf16[8,384,1792]{2,1,0:T(8,128)(2,1)}, bf16[768,1792]{1,0:T(8,128)(2,1)}, bf16[256,1792]{1,0:T(8,128)(2,1)}, f32[8,56,128]{2,1,0:T(8,128)}, b...) custom-call(bf16[384,1792]{1,0:T(8,128)(2,1)} %tokens.1, ...), custom_call_target="tpu_custom_call" | custom-call | bytes 300000000 | tf_op jit(solution)/shard_map/attend_ahead/pallas_call | solution.py:859
  133.5 0.0 copy-done.1
  133.5 0.6 broadcast_in_dim.38.gain
  134.1 81.4 %project_middle.1 = (f32[384,1792]{1,0:T(8,128)}, bf16[384,1792]{1,0:T(8,128)(2,1)}, bf16[4,128,1792]{2,1,0:T(8,128)(2,1)}) custom-call(bf16[3072,256]{1,0:T(8,128)(2,1)} %bitcast.17, bf16[256,1792]{1,0:T(8,128)(2,1)} %get-tuple-element.50.w_out, bf16[384,1792]{1,0:T(8,128)(2,1)} %get-tuple-element.51.tokens, f32[1,1792]{1,0:T(1,128)} %broadcast_in_dim.38.gain, ...), custom_call_target="tpu_custom_call" | custom-call | bytes 150000000 | tf_op jit(solution)/shard_map/project_middle/pallas_call | solution.py:1582
  215.5 118.6 %feed.1 = (f32[384,1792]{1,0:T(8,128)}, bf16[384,1792]{1,0:T(8,128)(2,1)}, f32[8,1792]{1,0:T(8,128)}, bf16[8,384,512]{2,1,0:T(8,128)(2,1)}, bf16[4,1792,256]{2,1...) custom-call(bf16[384,1792]{1,0:T(8,128)(2,1)} %get-tuple-element.52.hidden_own, ...), custom_call_target="tpu_custom_call" | custom-call | bytes 400000000 | tf_op jit(solution)/shard_map/feed/pallas_call | solution.py:1810
  334.2 134.1 %attend_back.1 = (bf16[8,8,48,768]{3,2,1,0:T(8,128)(2,1)}, bf16[384,1792]{1,0:T(8,128)(2,1)}, bf16[8,384,1792]{2,1,0:T(8,128)(2,1)}, bf16[4,1792,256]{2,1,0:T(8,128)(2,1)}, bf16[8,128,1792]{2,1,0:T(8,128)(2,1)}) custom-call(bf16[8,448,768]{2,1,0:T(8,128)(2,1)} %get-tuple-element.48.kept, bf16[384,1792]{1,0:T(8,128)(2,1)} %get-tuple-element.58.branch, ...), custom_call_target="tpu_custom_call" | custom-call | bytes 300000000 | tf_op jit(solution)/shard_map/attend_back/pallas_call | solution.py:1508
  468.3 126.2 %project_input.1 = (bf16[384,1792]{1,0:T(8,128)(2,1)}, f32[2,1792]{1,0:T(2,128)}, bf16[8,1792,256]{2,1,0:T(8,128)(2,1)}, bf16[8,448,896]{2,1,0:T(8,128)(2,1)}) custom-call(bf16[3072,768]{1,0:T(8,128)(2,1)} %bitcast.19, bf16[768,1792]{1,0:T(8,128)(2,1)} %get-tuple-element.64.w_qkv, bf16[8,384,1792]{2,1,0:T(8,128)(2,1)} %get-tuple-element.65.hidden_all, ...), custom_call_target="tpu_custom_call" | custom-call | bytes 250000000 | tf_op jit(solution)/shard_map/project_input/pallas_call | solution.py:1993
  594.5 0.8 broadcast_in_dim.40.order_column
  595.3 0.0 copy-start
  595.3 21.1 %assemble.1 = (bf16[384,1792]{1,0:T(8,128)(2,1)}, bf16[384,1792]{1,0:T(8,128)(2,1)}, f32[448,1792]{1,0:T(8,128)}, f32[448,1792]{1,0:T(8,128)}, f32[448,1792]{1,0...) custom-call(bf16[8,1792,256]{2,1,0:T(8,128)(2,1)} %get-tuple-element.70.bot, ...), custom_call_target="tpu_custom_call" | custom-call | bytes 58000000 | tf_op jit(solution)/shard_map/assemble/pallas_call | solution.py:2065
  616.4 0.0 copy-done
  616.4 0.6 slice_reduce_fusion
  (2 shorter events, 0.0 us)
Async XLA Ops:
  5.8 127.7 %copy-start.1 = (f32[1792]{0:T(1024)S(1)}, f32[1792]{0:T(1024)}, u32[]{:S(2)}) copy-start(f32[1792]{0:T(1024)} %param.20) | copy-start | bytes 21508
  595.3 21.1 %copy-start = (f32[2,1792]{1,0:T(2,128)S(1)}, f32[2,1792]{1,0:T(2,128)}, u32[]{:S(2)}) copy-start(f32[2,1792]{1,0:T(2,128)} %get-tuple-element.77) | copy-start | bytes 43012

commit v9 on v8

--- a/solution.py
+++ b/solution.py
@@ -373,14 +373,6 @@
     )
 
 
-def greet_plane():
-    _, side, over_x, over_y, _ = plane()
-    barrier = pltpu.get_barrier_semaphore()
-    for other in (side, over_x, over_y):
-        pl.semaphore_signal(barrier, inc=1, device_id={"dp": other}, device_id_type=MESH)
-    return barrier
-
-
 def owner_at(turn):
     me, side, over_x, over_y, _ = plane()
     block = turn // 2
@@ -462,7 +454,8 @@
         self.sent()
 
 
-def greet_all(barrier):
+def greet_all():
+    barrier = pltpu.get_barrier_semaphore()
     me, z = lax.axis_index("dp"), lax.axis_index("mp")
     for step in range(1, 8):
         pl.semaphore_signal(
@@ -477,7 +470,18 @@
                 device_id={"dp": other, "mp": lax.rem(z + step, 4)},
                 device_id_type=MESH,
             )
-    pl.semaphore_wait(barrier, 13)
+    return barrier
+
+
+def start_all(copies):
+    for copy in copies:
+        copy.start()
+    return copies
+
+
+def wait_all(copies):
+    for copy in copies:
+        copy.wait()
 
 
 def swap_all(source, target, send, recv):
@@ -687,25 +691,24 @@
 
 
 def forward_kernel(
-    tokens, cotangent, order_row, gain, notes, query, keys, values, project, gate, upward,
-    hidden_out, w_qkv, w_out, notes_all, w_both, mixed, kept, tokens_b, cotangent_b, cotangent_all,
-    hidden_all, qkv, share, both_own,
+    tokens, cotangent, order_row, gain, notes, query, keys, values, project, gate,
+    hidden_out, w_qkv_out, w_out, notes_all, gate_all, mixed_out, kept_out, tokens_out, cotangent_out,
+    cotangent_all,
+    hidden_all, qkv, share, gate_own, w_qkv, mixed, kept, tokens_b, cotangent_b,
     send, recv, send_a, recv_a, send_g, recv_g, send_w, recv_w, send_n, recv_n, send_c, recv_c,
-    local, out_sem, *, scale,
+    local, out_sem, store_sem, *, scale,
 ):
     groups, rows, width = hidden_all.shape
     me, z = lax.axis_index("dp"), lax.axis_index("mp")
     members = lax.axis_size("mp")
+    barrier = greet_all()
     head = pl.ds(pl.multiple_of(lax.div(me, 2) * HEAD_DIM, 16), HEAD_DIM)
     units = pl.ds(pl.multiple_of(me * LANES, LANES), LANES)
     loads = [
         pltpu.make_async_copy(source.at[head], share.at[piece], local.at[piece])
         for piece, source in enumerate((query, keys, values, project))
     ]
-    loads += [
-        pltpu.make_async_copy(gate.at[:, units], both_own.at[:, pl.ds(0, LANES)], local.at[4]),
-        pltpu.make_async_copy(upward.at[:, units], both_own.at[:, pl.ds(LANES, LANES)], local.at[5]),
-    ]
+    loads.append(pltpu.make_async_copy(gate.at[:, units], gate_own, local.at[4]))
     for copy in loads:
         copy.start()
     none = jnp.zeros((LANES - HEAD_DIM, width), BF16)
@@ -725,7 +728,8 @@
 
     each_chunk(rows, normalise)
     notes_all[me] = notes[...]
-    greet_all(pltpu.get_barrier_semaphore())
+    stores = start_all([pltpu.make_async_copy(tokens_b, tokens_out, store_sem.at[0])])
+    pl.semaphore_wait(barrier, 13)
     gather = Gather(None, hidden_all, send_a, recv_a)
     gather.start()
     swaps = swap_all(notes, notes_all, send_n, recv_n)
@@ -736,17 +740,18 @@
     spread = Spread(share, w_qkv, w_out, send_w, recv_w, local)
     spread.start((0, 1, 2))
     cotangent_b[...] = jnp.dot(sort, cotangent[...], preferred_element_type=F32).astype(BF16)
-    for copy in loads[4:]:
-        copy.wait()
-    column = Column(both_own, w_both, send_c, recv_c, local.at[4])
+    stores += start_all([pltpu.make_async_copy(cotangent_b, cotangent_out, store_sem.at[1])])
+    wait_all(loads[4:])
+    column = Column(gate_own, gate_all, send_c, recv_c, local.at[4])
     second = Gather(cotangent_b, cotangent_all, send_g, recv_g, local.at[5])
+    spread.pass_on((0, 1, 2))
     gather.arrive(0, 1)
     second.start()
-    spread.pass_on((0, 1, 2))
     column.start()
     gather.arrive(2, 3)
     spread.finish((0, 1, 2))
     spread.start((3,))
+    stores += start_all([pltpu.make_async_copy(w_qkv, w_qkv_out, store_sem.at[2])])
     for copy in swaps:
         copy.wait()
 
@@ -778,6 +783,15 @@
             other,
         )
 
+    def store_kept(k):
+        return pltpu.make_async_copy(kept.at[k], kept_out.at[k], store_sem.at[3 + k])
+
+    def store_mixed(k):
+        span = pl.ds(k, 1)
+        return pltpu.make_async_copy(
+            mixed.at[:, span], mixed_out.at[:, span], store_sem.at[3 + groups + k]
+        )
+
     def order(k, carry):
         hot = hot_of(notes_all, k, rows)
         given = qkv[:, pl.ds(k, 1)].reshape(rows, 768)
@@ -803,6 +817,7 @@
         def _():
             halo(k, z).wait_recv()
 
+        store_kept(k).start()
         hot = hot_of(notes_all, k, rows)
         found = []
         for block in range(rows // 128):
@@ -822,6 +837,7 @@
         ordered = jnp.concatenate(found, axis=0)
         back = jnp.dot(hot, ordered, preferred_element_type=F32).astype(BF16)
         mixed[:, pl.ds(k, 1)] = back.reshape(groups, 1, rows // groups, 256)
+        store_mixed(k).start()
         return carry
 
     spread.pass_on((3,))
@@ -834,11 +850,15 @@
     column.finish()
     gather.sent()
 
-    def kept_out(turn, carry):
+    wait_all(stores)
+
+    def stored(turn, carry):
         keep(turn).wait()
+        store_kept(turn).wait()
+        store_mixed(turn).wait()
         return carry
 
-    lax.fori_loop(0, groups, kept_out, 0)
+    lax.fori_loop(0, groups, stored, 0)
 
     @pl.when(z < members - 1)
     def _():
@@ -850,7 +870,7 @@
 
 
 def attend_ahead(
-    tokens, cotangent, order_row, gain, notes, query, keys, values, project, gate, upward, scale
+    tokens, cotangent, order_row, gain, notes, query, keys, values, project, gate, scale
 ):
     rows, width = tokens.shape
     groups, members = lax.axis_size("dp"), lax.axis_size("mp")
@@ -863,24 +883,28 @@
             shape((6 * LANES, width), BF16),
             shape((2 * LANES, width), BF16),
             shape((groups,) + notes.shape, F32),
-            shape((members, width, 2 * LANES), BF16),
+            shape((members, width, LANES), BF16),
             shape((groups, groups, rows // groups, 256), BF16),
             shape((groups, rows + 64, 768), BF16),
             shape((rows, width), BF16),
             shape((rows, width), BF16),
             shape((groups, rows, width), BF16),
         ),
-        in_specs=[on_chip()] * 5 + [anywhere()] * 6,
-        out_specs=(anywhere(),)
-        + (on_chip(),) * 3
-        + (anywhere(),)
-        + (on_chip(),) * 4
-        + (anywhere(),),
+        in_specs=[on_chip()] * 5 + [anywhere()] * 5,
+        out_specs=(
+            anywhere(), anywhere(), on_chip(), on_chip(), anywhere(),
+            anywhere(), anywhere(), anywhere(), anywhere(), anywhere(),
+        ),
         scratch_shapes=[
             pltpu.VMEM((groups, rows, width), BF16),
             pltpu.VMEM((groups, groups, rows // groups, 768), BF16),
             pltpu.VMEM((4, HEAD_DIM, width), BF16),
-            pltpu.VMEM((width, 2 * LANES), BF16),
+            pltpu.VMEM((width, LANES), BF16),
+            pltpu.VMEM((6 * LANES, width), BF16),
+            pltpu.VMEM((groups, groups, rows // groups, 256), BF16),
+            pltpu.VMEM((groups, rows + 64, 768), BF16),
+            pltpu.VMEM((rows, width), BF16),
+            pltpu.VMEM((rows, width), BF16),
             dma((groups,)),
             dma((groups,)),
             dma((13,)),
@@ -895,11 +919,12 @@
             dma((4,)),
             dma((6,)),
             dma((groups,)),
+            dma((3 + 2 * groups,)),
         ],
         compiler_params=remote_params(2, 60 * 1024 * 1024),
         cost_estimate=pl.CostEstimate(flops=0, bytes_accessed=300_000_000, transcendentals=0),
         name="attend_ahead",
-    )(tokens, cotangent, order_row, gain, notes, query, keys, values, project, gate, upward)
+    )(tokens, cotangent, order_row, gain, notes, query, keys, values, project, gate)
 
 
 CHUNK = 32
@@ -1358,23 +1383,33 @@
 
 
 def backward_kernel(
-    kept, branch, w_out, notes_all, activated, w_down, middle, both_sum, down_in,
+    branch, notes_all, kept_in, w_out_in, activated_in, w_down_in, middle_in, both_sum, down_in,
     out, result, branch_all, both_in, down_all,
     totals, query_part, key_value, ending, leaving, arriving, send, recv,
     part, from_side, from_corner, from_near, send_r, recv_r,
     mixed_grad, shard, load_sem, send_g, recv_g,
     both_stage, send_u, recv_u, local, down_found, send_d, recv_d,
+    kept, w_out, activated, w_down, middle, fetch_sem,
     *, scale, groups, rows,
 ):
     z = lax.axis_index("mp")
     members = lax.axis_size("mp")
+    barrier = greet_all()
+    pairs = ((w_down_in, w_down), (activated_in, activated), (w_out_in, w_out))
+    pairs += ((kept_in, kept), (middle_in, middle))
+    fetches = [
+        pltpu.make_async_copy(source, target, fetch_sem.at[number])
+        for number, (source, target) in enumerate(pairs)
+    ]
     load_down = pltpu.make_async_copy(down_in, down_found, load_sem.at[2])
-    load_down.start()
-    greet_all(pltpu.get_barrier_semaphore())
+    pl.semaphore_wait(barrier, 13)
     units = Units(both_sum, both_in, both_stage, send_u, recv_u, local)
     gather = Gather(branch, branch_all, send_g, recv_g, local.at[2])
     gather.start()
     units.start()
+    start_all(fetches)
+    load_down.start()
+    wait_all(fetches[:2])
     reduce = Reduce(activated, w_down, False, part, from_side, from_corner, from_near, send_r, recv_r)
     reduce.products()
     load_down.wait()
@@ -1408,6 +1443,7 @@
         )
         return carry
 
+    fetches[2].wait()
     lax.fori_loop(0, 8, spread_back, 0)
     reduce.launch()
     down.start()
@@ -1455,6 +1491,7 @@
 
         return carry
 
+    wait_all(fetches[3:])
     lax.fori_loop(0, 3, attend, 0)
     reduce.middle()
     lax.fori_loop(3, 7, attend, 0)
@@ -1498,7 +1535,7 @@
 
 
 def attend_back(
-    kept, branch, w_out, notes_all, activated, w_down, middle, both_sum, down_in, scale
+    branch, notes_all, kept, w_out, activated, w_down, middle, both_sum, down_in, scale
 ):
     groups = kept.shape[0]
     rows, width = middle.shape
@@ -1514,7 +1551,7 @@
             shape((members, width, 256), BF16),
             shape((groups, LANES, width), BF16),
         ),
-        in_specs=[on_chip()] * 7 + [anywhere()] * 2,
+        in_specs=[on_chip()] * 2 + [anywhere()] * 7,
         out_specs=(on_chip(),) * 2 + (anywhere(),) * 3,
         scratch_shapes=[
             pltpu.VMEM((rows + 64, 512), F32),
@@ -1540,28 +1577,46 @@
             pltpu.VMEM((members, LANES, width), BF16),
             dma((13,)),
             dma((13,)),
+            pltpu.VMEM(kept.shape, BF16),
+            pltpu.VMEM(w_out.shape, BF16),
+            pltpu.VMEM(activated.shape, BF16),
+            pltpu.VMEM(w_down.shape, BF16),
+            pltpu.VMEM((rows, width), F32),
+            dma((5,)),
         ],
         compiler_params=remote_params(3, 63 * 1024 * 1024),
         cost_estimate=pl.CostEstimate(flops=0, bytes_accessed=300_000_000, transcendentals=0),
         name="attend_back",
-    )(kept, branch, w_out, notes_all, activated, w_down, middle, both_sum, down_in)
+    )(branch, notes_all, kept, w_out, activated, w_down, middle, both_sum, down_in)
 
 
 def middle_kernel(
-    mixed, w_out, tokens, gain, w_down, middle, hidden, down_all,
-    part, from_side, from_corner, from_near, send, recv, down_own, send_c, recv_c, local,
+    mixed, w_out, tokens, gain, w_up, w_down, middle, hidden, up_all, down_all,
+    part, from_side, from_corner, from_near, send, recv, up_own, down_own,
+    send_u, recv_u, send_d, recv_d, local,
 ):
+    barrier = greet_all()
     units = pl.ds(pl.multiple_of(lax.axis_index("dp") * LANES, LANES), LANES)
-    load = pltpu.make_async_copy(w_down.at[units], down_own, local.at[0])
-    load.start()
-    greet_all(pltpu.get_barrier_semaphore())
-    load.wait()
-    column = Column(down_own, down_all, send_c, recv_c, local.at[1])
-    column.start()
+    loads = [
+        pltpu.make_async_copy(w_up.at[:, units], up_own, local.at[0]),
+        pltpu.make_async_copy(w_down.at[units], down_own, local.at[1]),
+    ]
+    for copy in loads:
+        copy.start()
+    pl.semaphore_wait(barrier, 13)
+    for copy in loads:
+        copy.wait()
+    columns = [
+        Column(up_own, up_all, send_u, recv_u, local.at[0]),
+        Column(down_own, down_all, send_d, recv_d, local.at[1]),
+    ]
+    for column in columns:
+        column.start()
     reduce = Reduce(mixed, w_out, False, part, from_side, from_corner, from_near, send, recv)
     reduce.begin()
     reduce.middle()
-    column.pass_on()
+    for column in columns:
+        column.pass_on()
     reduce.end()
 
     def body(span):
@@ -1571,11 +1626,12 @@
         hidden[span, :] = (values * inverse * gain[...]).astype(BF16)
 
     each_chunk(hidden.shape[0], body)
-    column.finish()
+    for column in columns:
+        column.finish()
     reduce.finish()
 
 
-def project_middle(mixed, w_out, tokens, gain, w_down):
+def project_middle(mixed, w_out, tokens, gain, w_up, w_down):
     rows, width = tokens.shape
     dma = pltpu.SemaphoreType.DMA
     members = lax.axis_size("mp")
@@ -1584,16 +1640,25 @@
         out_shape=(
             jax.ShapeDtypeStruct((rows, width), F32),
             jax.ShapeDtypeStruct((rows, width), BF16),
+            jax.ShapeDtypeStruct((members, width, LANES), BF16),
             jax.ShapeDtypeStruct((members, LANES, width), BF16),
         ),
-        in_specs=[on_chip()] * 4 + [anywhere()],
-        out_specs=(on_chip(), on_chip(), anywhere()),
+        in_specs=[on_chip()] * 4 + [anywhere()] * 2,
+        out_specs=(on_chip(), on_chip(), anywhere(), anywhere()),
         scratch_shapes=reduce_scratch(rows, width)
-        + [pltpu.VMEM((LANES, width), BF16), dma((4,)), dma((4,)), dma((2,))],
+        + [
+            pltpu.VMEM((width, LANES), BF16),
+            pltpu.VMEM((LANES, width), BF16),
+            dma((4,)),
+            dma((4,)),
+            dma((4,)),
+            dma((4,)),
+            dma((2,)),
+        ],
         compiler_params=remote_params(4),
         cost_estimate=pl.CostEstimate(flops=0, bytes_accessed=150_000_000, transcendentals=0),
         name="project_middle",
-    )(mixed, w_out, tokens, gain, w_down)
+    )(mixed, w_out, tokens, gain, w_up, w_down)
 
 
 def norm_back_rows(gradient, values, gain, sums, span):
@@ -1609,20 +1674,25 @@
 
 
 def feed_kernel(
-    hidden_own, cotangent_all, middle, w_parts, cotangent, gain, w_down,
-    middle_grad, branch, sums, activated, both_sum, down_in,
+    hidden_own, cotangent_all, middle, gate_all, up_all, cotangent_own, down_all, gain,
+    middle_grad, branch, sums, activated_out, both_sum, down_in,
     hidden_all, both_grad, part, from_side, from_corner, from_near, send_r, recv_r,
-    send_a, recv_a, cot_shard, cot_tile, stage_both, down_sum, w_both, load_sem, local, send_z, recv_z,
+    send_a, recv_a, cot_shard, cot_tile, stage_both, down_sum, w_both, w_down, cotangent, activated,
+    load_sem, local, send_z, recv_z,
 ):
     groups, rows, width = hidden_all.shape
-    members = w_parts.shape[0]
+    members = gate_all.shape[0]
     me = lax.axis_index("dp")
+    barrier = greet_all()
     own = pltpu.make_async_copy(hidden_own, hidden_all.at[me], local.at[0])
     own.start()
     start_middle = pltpu.make_async_copy(middle, middle_grad, local.at[1])
     loads = [
-        pltpu.make_async_copy(w_parts.at[z], w_both.at[:, pl.ds(z * 256, 256)], load_sem.at[6 + z])
+        pltpu.make_async_copy(
+            source.at[z], w_both.at[:, pl.ds(z * 256 + offset, 128)], load_sem.at[6 + 2 * z + number]
+        )
         for z in range(members)
+        for number, (source, offset) in enumerate(((gate_all, 0), (up_all, 128)))
     ]
 
     def slot_of(turn):
@@ -1638,11 +1708,12 @@
             cotangent_all.at[owner_at(turn)], cot_shard.at[turn % 2], load_sem.at[turn % 2]
         )
 
-    for copy in loads:
-        copy.start()
+    loads.append(pltpu.make_async_copy(down_all, w_down, local.at[2]))
+    load_own = pltpu.make_async_copy(cotangent_own, cotangent, local.at[3])
+    start_all(loads)
     load_cotangent(0).start()
-    greet_all(pltpu.get_barrier_semaphore())
     own.wait()
+    pl.semaphore_wait(barrier, 13)
     gather = Gather(None, hidden_all, send_a, recv_a)
     gather.start()
     reduce = Reduce(None, None, False, part, from_side, from_corner, from_near, send_r, recv_r)
@@ -1658,8 +1729,8 @@
     early += [(6, nears)]
     late = [(1, 3), (4, 1), (5, 2), (7, 0)]
     start_middle.start()
-    for copy in loads:
-        copy.wait()
+    load_own.start()
+    wait_all(loads)
 
     def unit(turn, carry):
         for number, action in early:
@@ -1704,6 +1775,8 @@
         return carry
 
     lax.fori_loop(0, 8, unit, 0)
+    store_activated = pltpu.make_async_copy(activated, activated_out, local.at[4])
+    store_activated.start()
 
     def load_tile(t):
         columns = pl.ds(pl.multiple_of(t * 256, 256), 256)
@@ -1741,7 +1814,7 @@
     def down_rows(owner):
         return down_sum.at[pl.ds(pl.multiple_of(owner * LANES, LANES), LANES)]
 
-    keep_down = pltpu.make_async_copy(down_rows(z), down_in.at[z], local.at[2])
+    keep_down = pltpu.make_async_copy(down_rows(z), down_in.at[z], local.at[5])
     pass_down = [
         to_mp(
             down_rows(lax.rem(z + step, members)),
@@ -1784,6 +1857,7 @@
     lax.fori_loop(2, tiles, weight_tile, 0)
     reduce.end()
     start_middle.wait()
+    load_own.wait()
     sums[...] = jnp.zeros_like(sums)
 
     def body(span):
@@ -1798,13 +1872,14 @@
     for t in (tiles - 2, tiles - 1):
         store_both(t).wait()
     keep_down.wait()
+    store_activated.wait()
     for copy in pass_down:
         copy.wait()
 
 
-def feed(hidden_own, cotangent_all, middle, w_both, cotangent, gain, w_down):
+def feed(hidden_own, cotangent_all, middle, gate_all, up_all, cotangent, down_all, gain):
     groups, rows, width = cotangent_all.shape
-    members = w_both.shape[0]
+    members = gate_all.shape[0]
     dma = pltpu.SemaphoreType.DMA
     units = members * 128
     return pl.pallas_call(
@@ -1817,8 +1892,8 @@
             jax.ShapeDtypeStruct((members, width, 256), BF16),
             jax.ShapeDtypeStruct((members, LANES, width), BF16),
         ),
-        in_specs=[anywhere()] * 4 + [on_chip()] * 3,
-        out_specs=(on_chip(),) * 4 + (anywhere(),) * 2,
+        in_specs=[anywhere()] * 7 + [on_chip()],
+        out_specs=(on_chip(),) * 3 + (anywhere(),) * 3,
         scratch_shapes=[
             pltpu.VMEM((groups, rows, width), BF16),
             pltpu.VMEM((groups, rows, 2 * units), BF16),
@@ -1832,26 +1907,31 @@
             pltpu.VMEM((2, members, 256, 256), BF16),
             pltpu.VMEM((units, width), BF16),
             pltpu.VMEM((width, 2 * units), BF16),
-            dma((6 + members,)),
-            dma((3,)),
+            pltpu.VMEM((units, width), BF16),
+            pltpu.VMEM((rows, width), BF16),
+            pltpu.VMEM((groups, rows, units), BF16),
+            dma((6 + 2 * members,)),
+            dma((6,)),
             dma((3,)),
             dma((3,)),
         ],
         compiler_params=remote_params(5, 63 * 1024 * 1024),
         cost_estimate=pl.CostEstimate(flops=0, bytes_accessed=400_000_000, transcendentals=0),
         name="feed",
-    )(hidden_own, cotangent_all, middle, w_both, cotangent, gain, w_down)
+    )(hidden_own, cotangent_all, middle, gate_all, up_all, cotangent, down_all, gain)
 
 
 def input_kernel(
-    qkv_grad, w_qkv, hidden_all, branch_all, mixed, tokens, middle_grad, gain, sums_two,
+    qkv_grad, w_qkv, hidden_all, branch_all, mixed_in, tokens_in, middle_in, gain, sums_two,
     both_sum, both_in,
     result, gains, both_all, heads_all,
     part, from_side, from_corner, from_near, send, recv, sums,
     stage, arrive, send_h, recv_s, recv_h, own, plane_sums, column_sums, send_p, recv_p,
     weight_sum, row_tile, tile_sem, send_b, recv_b, send_t, recv_t, both_found, heads_own, local,
+    mixed, tokens, middle_grad, fetch_sem,
 ):
     me, z = lax.axis_index("dp"), lax.axis_index("mp")
+    barrier = greet_all()
     count = qkv_grad.shape[0]
     tiles = tokens.shape[1] // 256
     outer = (z == 0) | (z == 3)
@@ -1880,8 +1960,49 @@
     def _():
         both_found[3] = jnp.zeros_like(both_found[3])
 
-    load(0, branch_all).start()
-    greet_all(pltpu.get_barrier_semaphore())
+    load(0, hidden_all).start()
+    fetches = start_all(
+        [
+            pltpu.make_async_copy(source, target, fetch_sem.at[number])
+            for number, (source, target) in enumerate(
+                ((mixed_in, mixed), (tokens_in, tokens), (middle_in, middle_grad))
+            )
+        ]
+    )
+    pl.semaphore_wait(barrier, 13)
+    both = Gather(both_found.at[0], both_all, send_b, recv_b, local.at[4])
+
+    def weight_tile(t, carry):
+        @pl.when(t < tiles - 1)
+        def _():
+            load(t + 1, hidden_all).start()
+
+        @pl.when((t >= tiles - 1) & (t < 2 * tiles - 1))
+        def _():
+            load(t + 1, branch_all).start()
+
+        load(t, hidden_all).wait()
+
+        @pl.when(t < tiles)
+        def _():
+            weight_sum[pl.ds(0, 768), columns_of(t)] = lax.dot_general(
+                qkv_grad[...], row_tile[t % 2].reshape(count, 256), TN, preferred_element_type=F32
+            ).astype(BF16)
+
+        @pl.when(t >= tiles)
+        def _():
+            weight_sum[pl.ds(768, 256), columns_of(t)] = lax.dot_general(
+                mixed[...], row_tile[t % 2].reshape(count, 256), TN, preferred_element_type=F32
+            ).astype(BF16)
+
+        return carry
+
+    heads = Heads(weight_sum, stage, arrive, send_h, recv_s, recv_h)
+    reduce = Reduce(qkv_grad, w_qkv, False, part, from_side, from_corner, from_near, send, recv)
+    reduce.begin()
+    lax.fori_loop(0, tiles, weight_tile, 0)
+    heads.start((0, 1, 2))
+    reduce.middle()
     own_part.wait()
     for here, source, place in ways:
         pl.when(here)(came(source, place).wait)
@@ -1892,43 +2013,11 @@
         both_found[0, span, :] = value.astype(BF16)
 
     each_chunk(both_found.shape[1], add)
-    both = Gather(both_found.at[0], both_all, send_b, recv_b, local.at[4])
-
-    def weight_tile(t, carry):
-        @pl.when(t < tiles - 1)
-        def _():
-            load(t + 1, branch_all).start()
-
-        @pl.when((t >= tiles - 1) & (t < 2 * tiles - 1))
-        def _():
-            load(t + 1, hidden_all).start()
-
-        load(t, hidden_all).wait()
-
-        @pl.when(t < tiles)
-        def _():
-            weight_sum[pl.ds(768, 256), columns_of(t)] = lax.dot_general(
-                mixed[...], row_tile[t % 2].reshape(count, 256), TN, preferred_element_type=F32
-            ).astype(BF16)
-
-        @pl.when(t >= tiles)
-        def _():
-            weight_sum[pl.ds(0, 768), columns_of(t)] = lax.dot_general(
-                qkv_grad[...], row_tile[t % 2].reshape(count, 256), TN, preferred_element_type=F32
-            ).astype(BF16)
-
-        return carry
-
-    heads = Heads(weight_sum, stage, arrive, send_h, recv_s, recv_h)
-    reduce = Reduce(qkv_grad, w_qkv, False, part, from_side, from_corner, from_near, send, recv)
-    reduce.begin()
-    lax.fori_loop(0, tiles, weight_tile, 0)
+    both.start()
+    wait_all(fetches)
+    lax.fori_loop(tiles, 2 * tiles, weight_tile, 0)
     heads.start((3,))
-    reduce.middle()
-    both.start()
-    lax.fori_loop(tiles, 2 * tiles, weight_tile, 0)
-    heads.start((0, 1, 2))
-    heads.add((3,))
+    heads.add((0, 1, 2, 3))
     reduce.end()
     sums[...] = jnp.zeros_like(sums)
 
@@ -1949,7 +2038,6 @@
     for copy in swaps:
         copy.start()
     plane_sums[me] = own[...]
-    heads.add((0, 1, 2))
     both.pass_on()
     heads.total(heads_own)
     gather = Gather(heads_own, heads_all, send_t, recv_t, local.at[5])
@@ -1998,7 +2086,7 @@
             shape((groups, width, 256), BF16),
             shape((groups, 4 * HEAD_DIM, width // 2), BF16),
         ),
-        in_specs=[on_chip()] * 2 + [anywhere()] * 2 + [on_chip()] * 5 + [anywhere()] * 2,
+        in_specs=[on_chip()] * 2 + [anywhere()] * 5 + [on_chip()] * 2 + [anywhere()] * 2,
         out_specs=(on_chip(),) * 2 + (anywhere(),) * 2,
         scratch_shapes=reduce_scratch(rows, width)
         + [
@@ -2023,6 +2111,10 @@
             pltpu.VMEM((4, width, 256), BF16),
             pltpu.VMEM((4 * HEAD_DIM, width // 2), BF16),
             dma((6,)),
+            pltpu.VMEM(mixed.shape, BF16),
+            pltpu.VMEM((rows, width), BF16),
+            pltpu.VMEM((rows, width), F32),
+            dma((3,)),
         ],
         compiler_params=remote_params(6, 63 * 1024 * 1024),
         cost_estimate=pl.CostEstimate(flops=0, bytes_accessed=250_000_000, transcendentals=0),
@@ -2128,7 +2220,7 @@
         w_qkv,
         w_proj,
         notes_all,
-        w_both,
+        gate_all,
         mixed,
         kept,
         tokens_b,
@@ -2145,20 +2237,21 @@
         w_value.T,
         w_out,
         w_gate,
-        w_up,
         scale,
     )
     mixed = mixed.reshape(count, 2 * LANES)
-    middle, hidden_two, down_all = project_middle(mixed, w_proj, tokens_b, norm2_gain[None], w_down)
+    middle, hidden_two, up_all, down_all = project_middle(
+        mixed, w_proj, tokens_b, norm2_gain[None], w_up, w_down
+    )
     down_all = down_all.reshape(members * units, width)
     middle_grad, branch, sums_two, activated, both_sum, down_in = feed(
-        hidden_two, cotangent_all, middle, w_both, cotangent_b, norm2_gain[None], down_all
+        hidden_two, cotangent_all, middle, gate_all, up_all, cotangent_b, down_all, norm2_gain[None]
     )
     qkv_grad, output_rows, branch_all, both_in, down_whole = attend_back(
+        branch,
+        notes_all,
         kept,
-        branch,
         w_proj,
-        notes_all,
         activated.reshape(count, units * members),
         down_all,
         middle,

time: 621 us -> 595 us (0.958)
  Pallas kernels: 609 us -> 583 us
    pallas_call x1, Pallas kernels: 128 us -> 114 us  [attend_ahead(): pl.pallas_call(functools.partial(forward_kernel, scale=scale), out_shape=...]
    pallas_call x1, Pallas kernels: 81.4 us -> 73.6 us  [project_middle(): pl.pallas_call(middle_kernel, out_shape=(jax.ShapeDtypeStruct((rows, widt...]
where the time goes in v9:
time: 595 us; the launch traced here: 591 us
  Pallas kernels  583 us (98%)
    pallas_call x1, Pallas kernels, attend_back(): pl.pallas_call(functools.partial(backward_kernel, scale=scale, groups=gro...  130 us
    pallas_call x1, Pallas kernels, project_input(): pl.pallas_call(input_kernel, out_shape=(shape((rows, width), BF16), shape...  126 us
    pallas_call x1, Pallas kernels, feed(): pl.pallas_call(feed_kernel, out_shape=(jax.ShapeDtypeStruct((rows, width)...  117 us
    pallas_call x1, Pallas kernels, attend_ahead(): pl.pallas_call(functools.partial(forward_kernel, scale=scale), out_shape=...  114 us
    pallas_call x1, Pallas kernels, project_middle(): pl.pallas_call(middle_kernel, out_shape=(jax.ShapeDtypeStruct((rows, widt...  73.6 us
    pallas_call x1, Pallas kernels, assemble(): pl.pallas_call(assemble_kernel, grid=(groups,), out_shape=(shape((rows, w...  21.1 us

profile of v9, /device:TPU:0, one launch (start us, length us, event | category | flops | bytes accessed | tf_op | source)
XLA Modules:
  0.0 590.7 jit_solution(11703874413691705596)
XLA Ops:
  0.6 0.7 add_select_fusion
  1.3 0.2 convert_reduce_fusion
  1.6 0.2 select_reduce_fusion
  1.7 0.1 reshape.47
  1.8 0.1 copy.27
  1.9 0.8 pad_dynamic-slice_fusion
  2.7 1.3 fusion.1.notes
  4.0 0.6 broadcast_in_dim.20.order_row
  4.5 1.3 broadcast_in_dim.21.gain
  5.8 0.0 copy-start.1
  5.8 114.5 %attend_ahead.1 = (bf16[8,384,1792]{2,1,0:T(8,128)(2,1)}, bf16[768,1792]{1,0:T(8,128)(2,1)}, bf16[256,1792]{1,0:T(8,128)(2,1)}, f32[8,56,128]{2,1,0:T(8,128)}, b...) custom-call(bf16[384,1792]{1,0:T(8,128)(2,1)} %tokens.1, ...), custom_call_target="tpu_custom_call" | custom-call | bytes 300000000 | tf_op jit(solution)/shard_map/attend_ahead/pallas_call | solution.py:879
  120.3 0.0 copy-done.1
  120.3 0.6 broadcast_in_dim.38.gain
  120.9 73.6 %project_middle.1 = (f32[384,1792]{1,0:T(8,128)}, bf16[384,1792]{1,0:T(8,128)(2,1)}, bf16[4,1792,128]{2,1,0:T(8,128)(2,1)}, bf16[4,128,1792]{2,1,0:T(8,128)(2,1)}) custom-call(bf16[3072,256]{1,0:T(8,128)(2,1)} %bitcast.17, bf16[256,1792]{1,0:T(8,128)(2,1)} %get-tuple-element.50.w_out.w_out_in, bf16[384,1792]{1,0:T(8,128)(2,1)} %get-tuple-element.51.tokens.tokens_in, ...), custom_call_target="tpu_custom_call" | custom-call | bytes 150000000 | tf_op jit(solution)/shard_map/project_middle/pallas_call | solution.py:1638
  194.5 117.3 %feed.1 = (f32[384,1792]{1,0:T(8,128)}, bf16[384,1792]{1,0:T(8,128)(2,1)}, f32[8,1792]{1,0:T(8,128)}, bf16[8,384,512]{2,1,0:T(8,128)(2,1)}, bf16[4,1792,256]{2,1...) custom-call(bf16[384,1792]{1,0:T(8,128)(2,1)} %get-tuple-element.52.hidden_own, ...), custom_call_target="tpu_custom_call" | custom-call | bytes 400000000 | tf_op jit(solution)/shard_map/feed/pallas_call | solution.py:1885
  311.8 130.4 %attend_back.1 = (bf16[8,8,48,768]{3,2,1,0:T(8,128)(2,1)}, bf16[384,1792]{1,0:T(8,128)(2,1)}, bf16[8,384,1792]{2,1,0:T(8,128)(2,1)}, bf16[4,1792,256]{2,1,0:T(8,128)(2,1)}, bf16[8,128,1792]{2,1,0:T(8,128)(2,1)}) custom-call(bf16[384,1792]{1,0:T(8,128)(2,1)} %get-tuple-element.59.branch, f32[8,56,128]{2,1,0:T(8,128)} %get-tuple-element.60.notes_all, ...), custom_call_target="tpu_custom_call" | custom-call | bytes 300000000 | tf_op jit(solution)/shard_map/attend_back/pallas_call | solution.py:1545
  442.2 126.0 %project_input.1 = (bf16[384,1792]{1,0:T(8,128)(2,1)}, f32[2,1792]{1,0:T(2,128)}, bf16[8,1792,256]{2,1,0:T(8,128)(2,1)}, bf16[8,448,896]{2,1,0:T(8,128)(2,1)}) custom-call(bf16[3072,768]{1,0:T(8,128)(2,1)} %bitcast.19, bf16[768,1792]{1,0:T(8,128)(2,1)} %get-tuple-element.66.w_qkv, bf16[8,384,1792]{2,1,0:T(8,128)(2,1)} %get-tuple-element.67.hidden_all, ...), custom_call_target="tpu_custom_call" | custom-call | bytes 250000000 | tf_op jit(solution)/shard_map/project_input/pallas_call | solution.py:2081
  568.2 0.8 broadcast_in_dim.40.order_column
  568.9 0.0 copy-start
  569.0 21.1 %assemble.1 = (bf16[384,1792]{1,0:T(8,128)(2,1)}, bf16[384,1792]{1,0:T(8,128)(2,1)}, f32[448,1792]{1,0:T(8,128)}, f32[448,1792]{1,0:T(8,128)}, f32[448,1792]{1,0...) custom-call(bf16[8,1792,256]{2,1,0:T(8,128)(2,1)} %get-tuple-element.72.bot, ...), custom_call_target="tpu_custom_call" | custom-call | bytes 58000000 | tf_op jit(solution)/shard_map/assemble/pallas_call | solution.py:2157
  590.0 0.0 copy-done
  590.1 0.6 slice_reduce_fusion
  (2 shorter events, 0.0 us)
Async XLA Ops:
  5.8 114.5 %copy-start.1 = (f32[1792]{0:T(1024)S(1)}, f32[1792]{0:T(1024)}, u32[]{:S(2)}) copy-start(f32[1792]{0:T(1024)} %param.20) | copy-start | bytes 21508
  568.9 21.1 %copy-start = (f32[2,1792]{1,0:T(2,128)S(1)}, f32[2,1792]{1,0:T(2,128)}, u32[]{:S(2)}) copy-start(f32[2,1792]{1,0:T(2,128)} %get-tuple-element.79) | copy-start | bytes 43012

commit v10 on v9

--- a/solution.py
+++ b/solution.py
@@ -691,10 +691,10 @@
 
 
 def forward_kernel(
-    tokens, cotangent, order_row, gain, notes, query, keys, values, project, gate,
+    tokens, cotangent, order_row, gain, notes, query, keys, values, project, gate, down,
     hidden_out, w_qkv_out, w_out, notes_all, gate_all, mixed_out, kept_out, tokens_out, cotangent_out,
-    cotangent_all,
-    hidden_all, qkv, share, gate_own, w_qkv, mixed, kept, tokens_b, cotangent_b,
+    cotangent_all, low_all,
+    hidden_all, qkv, share, gate_own, low_own, send_l, recv_l, w_qkv, mixed, kept, tokens_b, cotangent_b,
     send, recv, send_a, recv_a, send_g, recv_g, send_w, recv_w, send_n, recv_n, send_c, recv_c,
     local, out_sem, store_sem, *, scale,
 ):
@@ -708,7 +708,9 @@
         pltpu.make_async_copy(source.at[head], share.at[piece], local.at[piece])
         for piece, source in enumerate((query, keys, values, project))
     ]
+    half_units = pl.ds(pl.multiple_of(me * LANES, LANES // 2), LANES // 2)
     loads.append(pltpu.make_async_copy(gate.at[:, units], gate_own, local.at[4]))
+    loads.append(pltpu.make_async_copy(down.at[half_units], low_own, local.at[6]))
     for copy in loads:
         copy.start()
     none = jnp.zeros((LANES - HEAD_DIM, width), BF16)
@@ -744,6 +746,7 @@
     wait_all(loads[4:])
     column = Column(gate_own, gate_all, send_c, recv_c, local.at[4])
     second = Gather(cotangent_b, cotangent_all, send_g, recv_g, local.at[5])
+    low = Column(low_own, low_all, send_l, recv_l, local.at[6])
     spread.pass_on((0, 1, 2))
     gather.arrive(0, 1)
     second.start()
@@ -841,13 +844,17 @@
         return carry
 
     spread.pass_on((3,))
+    low.start()
     lax.fori_loop(0, groups // 2, attend, 0)
     second.pass_on()
     column.pass_on()
-    lax.fori_loop(groups // 2, groups, attend, 0)
+    lax.fori_loop(groups // 2, groups - 1, attend, 0)
+    low.pass_on()
+    lax.fori_loop(groups - 1, groups, attend, 0)
     spread.finish((3,))
     second.finish()
     column.finish()
+    low.finish()
     gather.sent()
 
     wait_all(stores)
@@ -870,7 +877,7 @@
 
 
 def attend_ahead(
-    tokens, cotangent, order_row, gain, notes, query, keys, values, project, gate, scale
+    tokens, cotangent, order_row, gain, notes, query, keys, values, project, gate, down, scale
 ):
     rows, width = tokens.shape
     groups, members = lax.axis_size("dp"), lax.axis_size("mp")
@@ -889,17 +896,21 @@
             shape((rows, width), BF16),
             shape((rows, width), BF16),
             shape((groups, rows, width), BF16),
+            shape((members, LANES // 2, width), BF16),
         ),
-        in_specs=[on_chip()] * 5 + [anywhere()] * 5,
+        in_specs=[on_chip()] * 5 + [anywhere()] * 6,
         out_specs=(
             anywhere(), anywhere(), on_chip(), on_chip(), anywhere(),
-            anywhere(), anywhere(), anywhere(), anywhere(), anywhere(),
+            anywhere(), anywhere(), anywhere(), anywhere(), anywhere(), anywhere(),
         ),
         scratch_shapes=[
             pltpu.VMEM((groups, rows, width), BF16),
             pltpu.VMEM((groups, groups, rows // groups, 768), BF16),
             pltpu.VMEM((4, HEAD_DIM, width), BF16),
             pltpu.VMEM((width, LANES), BF16),
+            pltpu.VMEM((LANES // 2, width), BF16),
+            dma((4,)),
+            dma((4,)),
             pltpu.VMEM((6 * LANES, width), BF16),
             pltpu.VMEM((groups, groups, rows // groups, 256), BF16),
             pltpu.VMEM((groups, rows + 64, 768), BF16),
@@ -917,14 +928,14 @@
             dma((7,)),
             dma((4,)),
             dma((4,)),
-            dma((6,)),
+            dma((7,)),
             dma((groups,)),
             dma((3 + 2 * groups,)),
         ],
         compiler_params=remote_params(2, 60 * 1024 * 1024),
         cost_estimate=pl.CostEstimate(flops=0, bytes_accessed=300_000_000, transcendentals=0),
         name="attend_ahead",
-    )(tokens, cotangent, order_row, gain, notes, query, keys, values, project, gate)
+    )(tokens, cotangent, order_row, gain, notes, query, keys, values, project, gate, down)
 
 
 CHUNK = 32
@@ -936,6 +947,123 @@
         return carry
 
     lax.fori_loop(0, rows // chunk, step, 0)
+
+
+class Units:
+    def __init__(self, part, came_in, stage, send, recv, local):
+        self.z = lax.axis_index("mp")
+        self.part_of = part
+        self.inputs = (came_in,)
+        self.stages = (stage,)
+        self.send, self.recv, self.local = send, recv, local
+        z = self.z
+        self.outer = (z == 0) | (z == 3)
+        self.far = 3 - z
+        self.near = 1 + lax.div(z, 3)
+        self.second = 3 - self.near
+        self.edge = 3 * (z - 1)
+
+    def part(self, kind, z):
+        return self.part_of(z)
+
+    def straight(self, kind, number, target):
+        return to_mp(
+            self.part(kind, target),
+            self.inputs[kind].at[self.z],
+            self.send.at[number * 2 + kind],
+            self.recv.at[self.z * 2 + kind],
+            target,
+        )
+
+    def staged(self, kind):
+        return to_mp(
+            self.part(kind, self.far),
+            self.stages[kind].at[0],
+            self.send.at[4 + kind],
+            self.recv.at[8 + kind],
+            self.near,
+        )
+
+    def summed(self, kind):
+        return to_mp(
+            self.stages[kind].at[1],
+            self.inputs[kind].at[self.z],
+            self.send.at[4 + kind],
+            self.recv.at[self.z * 2 + kind],
+            3 - self.edge,
+        )
+
+    def mine(self, kind):
+        return pltpu.make_async_copy(
+            self.part(kind, 3 - self.edge), self.stages[kind].at[1], self.local.at[kind]
+        )
+
+    def start(self):
+        @pl.when(self.outer)
+        def _():
+            for kind in range(1):
+                self.staged(kind).start()
+            for kind in range(1):
+                self.straight(kind, 0, self.near).start()
+                self.straight(kind, 1, self.second).start()
+
+        @pl.when(jnp.logical_not(self.outer))
+        def _():
+            for kind in range(1):
+                self.mine(kind).start()
+                self.straight(kind, 0, 3 - self.z).start()
+                self.straight(kind, 1, self.edge).start()
+
+    def add(self):
+        @pl.when(jnp.logical_not(self.outer))
+        def _():
+            for kind in range(1):
+                stage = self.stages[kind]
+                self.mine(kind).wait()
+                to_mp(
+                    self.part(kind, 0),
+                    stage.at[0],
+                    self.send.at[4 + kind],
+                    self.recv.at[8 + kind],
+                    self.edge,
+                ).wait_recv()
+
+                def body(span):
+                    stage[1, span, :] = (
+                        stage[0, span, :].astype(F32) + stage[1, span, :].astype(F32)
+                    ).astype(BF16)
+
+                each_chunk(stage.shape[1], body)
+                self.summed(kind).start()
+
+    def arrived(self, kind, source):
+        to_mp(
+            self.part(kind, 0),
+            self.inputs[kind].at[source],
+            self.send.at[kind],
+            self.recv.at[source * 2 + kind],
+            source,
+        ).wait_recv()
+
+    def finish(self):
+        @pl.when(self.outer)
+        def _():
+            for kind in range(1):
+                self.arrived(kind, 1)
+                self.arrived(kind, 2)
+                self.straight(kind, 0, self.near).wait_send()
+                self.straight(kind, 1, self.second).wait_send()
+                self.staged(kind).wait_send()
+
+        @pl.when(jnp.logical_not(self.outer))
+        def _():
+            for kind in range(1):
+                self.arrived(kind, 0)
+                self.arrived(kind, 3)
+                self.arrived(kind, 3 - self.z)
+                self.straight(kind, 0, 3 - self.z).wait_send()
+                self.straight(kind, 1, self.edge).wait_send()
+                self.summed(kind).wait_send()
 
 
 class Reduce:
@@ -1265,125 +1393,8 @@
     )
 
 
-class Units:
-    def __init__(self, both_sum, both_in, both_stage, send, recv, local):
-        self.z = lax.axis_index("mp")
-        self.sums = (both_sum,)
-        self.inputs = (both_in,)
-        self.stages = (both_stage,)
-        self.send, self.recv, self.local = send, recv, local
-        z = self.z
-        self.outer = (z == 0) | (z == 3)
-        self.far = 3 - z
-        self.near = 1 + lax.div(z, 3)
-        self.second = 3 - self.near
-        self.edge = 3 * (z - 1)
-
-    def part(self, kind, z):
-        return self.sums[kind].at[z]
-
-    def straight(self, kind, number, target):
-        return to_mp(
-            self.part(kind, target),
-            self.inputs[kind].at[self.z],
-            self.send.at[number * 2 + kind],
-            self.recv.at[self.z * 2 + kind],
-            target,
-        )
-
-    def staged(self, kind):
-        return to_mp(
-            self.part(kind, self.far),
-            self.stages[kind].at[0],
-            self.send.at[4 + kind],
-            self.recv.at[8 + kind],
-            self.near,
-        )
-
-    def summed(self, kind):
-        return to_mp(
-            self.stages[kind].at[1],
-            self.inputs[kind].at[self.z],
-            self.send.at[4 + kind],
-            self.recv.at[self.z * 2 + kind],
-            3 - self.edge,
-        )
-
-    def mine(self, kind):
-        return pltpu.make_async_copy(
-            self.part(kind, 3 - self.edge), self.stages[kind].at[1], self.local.at[kind]
-        )
-
-    def start(self):
-        @pl.when(self.outer)
-        def _():
-            for kind in range(1):
-                self.staged(kind).start()
-            for kind in range(1):
-                self.straight(kind, 0, self.near).start()
-                self.straight(kind, 1, self.second).start()
-
-        @pl.when(jnp.logical_not(self.outer))
-        def _():
-            for kind in range(1):
-                self.mine(kind).start()
-                self.straight(kind, 0, 3 - self.z).start()
-                self.straight(kind, 1, self.edge).start()
-
-    def add(self):
-        @pl.when(jnp.logical_not(self.outer))
-        def _():
-            for kind in range(1):
-                stage = self.stages[kind]
-                self.mine(kind).wait()
-                to_mp(
-                    self.part(kind, 0),
-                    stage.at[0],
-                    self.send.at[4 + kind],
-                    self.recv.at[8 + kind],
-                    self.edge,
-                ).wait_recv()
-
-                def body(span):
-                    stage[1, span, :] = (
-                        stage[0, span, :].astype(F32) + stage[1, span, :].astype(F32)
-                    ).astype(BF16)
-
-                each_chunk(stage.shape[1], body)
-                self.summed(kind).start()
-
-    def arrived(self, kind, source):
-        to_mp(
-            self.part(kind, 0),
-            self.inputs[kind].at[source],
-            self.send.at[kind],
-            self.recv.at[source * 2 + kind],
-            source,
-        ).wait_recv()
-
-    def finish(self):
-        @pl.when(self.outer)
-        def _():
-            for kind in range(1):
-                self.arrived(kind, 1)
-                self.arrived(kind, 2)
-                self.straight(kind, 0, self.near).wait_send()
-                self.straight(kind, 1, self.second).wait_send()
-                self.staged(kind).wait_send()
-
-        @pl.when(jnp.logical_not(self.outer))
-        def _():
-            for kind in range(1):
-                self.arrived(kind, 0)
-                self.arrived(kind, 3)
-                self.arrived(kind, 3 - self.z)
-                self.straight(kind, 0, 3 - self.z).wait_send()
-                self.straight(kind, 1, self.edge).wait_send()
-                self.summed(kind).wait_send()
-
-
 def backward_kernel(
-    branch, notes_all, kept_in, w_out_in, activated_in, w_down_in, middle_in, both_sum, down_in,
+    branch, notes_all, kept_in, w_out_in, activated_in, low_all, high_all, middle_in, both_sum, down_in,
     out, result, branch_all, both_in, down_all,
     totals, query_part, key_value, ending, leaving, arriving, send, recv,
     part, from_side, from_corner, from_near, send_r, recv_r,
@@ -1395,24 +1406,28 @@
     z = lax.axis_index("mp")
     members = lax.axis_size("mp")
     barrier = greet_all()
-    pairs = ((w_down_in, w_down), (activated_in, activated), (w_out_in, w_out))
-    pairs += ((kept_in, kept), (middle_in, middle))
+    pairs = ((activated_in, activated), (w_out_in, w_out), (kept_in, kept), (middle_in, middle))
     fetches = [
         pltpu.make_async_copy(source, target, fetch_sem.at[number])
         for number, (source, target) in enumerate(pairs)
     ]
     load_down = pltpu.make_async_copy(down_in, down_found, load_sem.at[2])
     pl.semaphore_wait(barrier, 13)
-    units = Units(both_sum, both_in, both_stage, send_u, recv_u, local)
+    units = Units(lambda owner: both_sum.at[owner], both_in, both_stage, send_u, recv_u, local)
     gather = Gather(branch, branch_all, send_g, recv_g, local.at[2])
     gather.start()
     units.start()
+    halves = start_all(load_halves(low_all, high_all, w_down, fetch_sem, 4))
     start_all(fetches)
     load_down.start()
-    wait_all(fetches[:2])
+    wait_all(halves + fetches[:1])
     reduce = Reduce(activated, w_down, False, part, from_side, from_corner, from_near, send_r, recv_r)
     reduce.products()
     load_down.wait()
+
+    @pl.when((z == 0) | (z == members - 1))
+    def _():
+        down_found[members - 1 - z] = jnp.zeros_like(down_found[0])
 
     def add_down(span):
         value = down_found[0, span, :].astype(F32) + down_found[1, span, :].astype(F32)
@@ -1443,10 +1458,9 @@
         )
         return carry
 
-    fetches[2].wait()
+    fetches[1].wait()
     lax.fori_loop(0, 8, spread_back, 0)
     reduce.launch()
-    down.start()
     units.add()
 
 
@@ -1491,9 +1505,10 @@
 
         return carry
 
-    wait_all(fetches[3:])
+    wait_all(fetches[2:])
     lax.fori_loop(0, 3, attend, 0)
     reduce.middle()
+    down.start()
     lax.fori_loop(3, 7, attend, 0)
     down.pass_on()
     lax.fori_loop(7, groups, attend, 0)
@@ -1535,7 +1550,7 @@
 
 
 def attend_back(
-    branch, notes_all, kept, w_out, activated, w_down, middle, both_sum, down_in, scale
+    branch, notes_all, kept, w_out, activated, low_all, high_all, middle, both_sum, down_in, scale
 ):
     groups = kept.shape[0]
     rows, width = middle.shape
@@ -1551,7 +1566,7 @@
             shape((members, width, 256), BF16),
             shape((groups, LANES, width), BF16),
         ),
-        in_specs=[on_chip()] * 2 + [anywhere()] * 7,
+        in_specs=[on_chip()] * 2 + [anywhere()] * 8,
         out_specs=(on_chip(),) * 2 + (anywhere(),) * 3,
         scratch_shapes=[
             pltpu.VMEM((rows + 64, 512), F32),
@@ -1580,14 +1595,14 @@
             pltpu.VMEM(kept.shape, BF16),
             pltpu.VMEM(w_out.shape, BF16),
             pltpu.VMEM(activated.shape, BF16),
-            pltpu.VMEM(w_down.shape, BF16),
+            pltpu.VMEM((members * LANES, width), BF16),
             pltpu.VMEM((rows, width), F32),
-            dma((5,)),
+            dma((4 + 2 * members,)),
         ],
         compiler_params=remote_params(3, 63 * 1024 * 1024),
         cost_estimate=pl.CostEstimate(flops=0, bytes_accessed=300_000_000, transcendentals=0),
         name="attend_back",
-    )(branch, notes_all, kept, w_out, activated, w_down, middle, both_sum, down_in)
+    )(branch, notes_all, kept, w_out, activated, low_all, high_all, middle, both_sum, down_in)
 
 
 def middle_kernel(
@@ -1597,9 +1612,12 @@
 ):
     barrier = greet_all()
     units = pl.ds(pl.multiple_of(lax.axis_index("dp") * LANES, LANES), LANES)
+    high_units = pl.ds(
+        pl.multiple_of(lax.axis_index("dp") * LANES + LANES // 2, LANES // 2), LANES // 2
+    )
     loads = [
         pltpu.make_async_copy(w_up.at[:, units], up_own, local.at[0]),
-        pltpu.make_async_copy(w_down.at[units], down_own, local.at[1]),
+        pltpu.make_async_copy(w_down.at[high_units], down_own, local.at[1]),
     ]
     for copy in loads:
         copy.start()
@@ -1641,14 +1659,14 @@
             jax.ShapeDtypeStruct((rows, width), F32),
             jax.ShapeDtypeStruct((rows, width), BF16),
             jax.ShapeDtypeStruct((members, width, LANES), BF16),
-            jax.ShapeDtypeStruct((members, LANES, width), BF16),
+            jax.ShapeDtypeStruct((members, LANES // 2, width), BF16),
         ),
         in_specs=[on_chip()] * 4 + [anywhere()] * 2,
         out_specs=(on_chip(), on_chip(), anywhere(), anywhere()),
         scratch_shapes=reduce_scratch(rows, width)
         + [
             pltpu.VMEM((width, LANES), BF16),
-            pltpu.VMEM((LANES, width), BF16),
+            pltpu.VMEM((LANES // 2, width), BF16),
             dma((4,)),
             dma((4,)),
             dma((4,)),
@@ -1673,12 +1691,23 @@
     return inverse * (scaled - normed * mean_rows(scaled * normed))
 
 
+def load_halves(low_all, high_all, weight, sems, first):
+    half = low_all.shape[1]
+    return [
+        pltpu.make_async_copy(
+            source.at[z], weight.at[pl.ds((2 * z + number) * half, half)], sems.at[first + 2 * z + number]
+        )
+        for z in range(low_all.shape[0])
+        for number, source in enumerate((low_all, high_all))
+    ]
+
+
 def feed_kernel(
-    hidden_own, cotangent_all, middle, gate_all, up_all, cotangent_own, down_all, gain,
+    hidden_own, cotangent_all, middle, gate_all, up_all, cotangent_own, low_all, high_all, gain,
     middle_grad, branch, sums, activated_out, both_sum, down_in,
     hidden_all, both_grad, part, from_side, from_corner, from_near, send_r, recv_r,
     send_a, recv_a, cot_shard, cot_tile, stage_both, down_sum, w_both, w_down, cotangent, activated,
-    load_sem, local, send_z, recv_z,
+    load_sem, local, send_z, recv_z, stage_down,
 ):
     groups, rows, width = hidden_all.shape
     members = gate_all.shape[0]
@@ -1708,7 +1737,7 @@
             cotangent_all.at[owner_at(turn)], cot_shard.at[turn % 2], load_sem.at[turn % 2]
         )
 
-    loads.append(pltpu.make_async_copy(down_all, w_down, local.at[2]))
+    loads += load_halves(low_all, high_all, w_down, load_sem, 6 + 2 * members)
     load_own = pltpu.make_async_copy(cotangent_own, cotangent, local.at[3])
     start_all(loads)
     load_cotangent(0).start()
@@ -1815,16 +1844,7 @@
         return down_sum.at[pl.ds(pl.multiple_of(owner * LANES, LANES), LANES)]
 
     keep_down = pltpu.make_async_copy(down_rows(z), down_in.at[z], local.at[5])
-    pass_down = [
-        to_mp(
-            down_rows(lax.rem(z + step, members)),
-            down_in.at[z],
-            send_z.at[step - 1],
-            recv_z.at[step - 1],
-            lax.rem(z + step, members),
-        )
-        for step in range(1, members)
-    ]
+    passing = Units(down_rows, down_in, stage_down, send_z, recv_z, local.at[pl.ds(6, 1)])
 
     def weight_tile(t, carry):
         columns = pl.ds(pl.multiple_of(t * 256, 256), 256)
@@ -1850,10 +1870,10 @@
     reduce.corners[1].start()
     lax.fori_loop(0, tiles, down_tile, 0)
     keep_down.start()
-    for copy in pass_down:
-        copy.start()
+    passing.start()
     lax.fori_loop(0, 2, weight_tile, 0)
     reduce.middle()
+    passing.add()
     lax.fori_loop(2, tiles, weight_tile, 0)
     reduce.end()
     start_middle.wait()
@@ -1873,11 +1893,10 @@
         store_both(t).wait()
     keep_down.wait()
     store_activated.wait()
-    for copy in pass_down:
-        copy.wait()
-
-
-def feed(hidden_own, cotangent_all, middle, gate_all, up_all, cotangent, down_all, gain):
+    passing.finish()
+
+
+def feed(hidden_own, cotangent_all, middle, gate_all, up_all, cotangent, low_all, high_all, gain):
     groups, rows, width = cotangent_all.shape
     members = gate_all.shape[0]
     dma = pltpu.SemaphoreType.DMA
@@ -1892,7 +1911,7 @@
             jax.ShapeDtypeStruct((members, width, 256), BF16),
             jax.ShapeDtypeStruct((members, LANES, width), BF16),
         ),
-        in_specs=[anywhere()] * 7 + [on_chip()],
+        in_specs=[anywhere()] * 8 + [on_chip()],
         out_specs=(on_chip(),) * 3 + (anywhere(),) * 3,
         scratch_shapes=[
             pltpu.VMEM((groups, rows, width), BF16),
@@ -1910,15 +1929,16 @@
             pltpu.VMEM((units, width), BF16),
             pltpu.VMEM((rows, width), BF16),
             pltpu.VMEM((groups, rows, units), BF16),
-            dma((6 + 2 * members,)),
+            dma((6 + 4 * members,)),
+            dma((7,)),
             dma((6,)),
-            dma((3,)),
-            dma((3,)),
+            dma((10,)),
+            pltpu.VMEM((2, LANES, width), BF16),
         ],
         compiler_params=remote_params(5, 63 * 1024 * 1024),
         cost_estimate=pl.CostEstimate(flops=0, bytes_accessed=400_000_000, transcendentals=0),
         name="feed",
-    )(hidden_own, cotangent_all, middle, gate_all, up_all, cotangent, down_all, gain)
+    )(hidden_own, cotangent_all, middle, gate_all, up_all, cotangent, low_all, high_all, gain)
 
 
 def input_kernel(
@@ -1999,10 +2019,6 @@
 
     heads = Heads(weight_sum, stage, arrive, send_h, recv_s, recv_h)
     reduce = Reduce(qkv_grad, w_qkv, False, part, from_side, from_corner, from_near, send, recv)
-    reduce.begin()
-    lax.fori_loop(0, tiles, weight_tile, 0)
-    heads.start((0, 1, 2))
-    reduce.middle()
     own_part.wait()
     for here, source, place in ways:
         pl.when(here)(came(source, place).wait)
@@ -2014,10 +2030,16 @@
 
     each_chunk(both_found.shape[1], add)
     both.start()
+    lax.fori_loop(0, tiles, weight_tile, 0)
+    heads.start((0, 1, 2))
     wait_all(fetches)
     lax.fori_loop(tiles, 2 * tiles, weight_tile, 0)
     heads.start((3,))
-    heads.add((0, 1, 2, 3))
+    both.pass_on()
+    reduce.begin()
+    heads.add((0, 1))
+    reduce.middle()
+    heads.add((2, 3))
     reduce.end()
     sums[...] = jnp.zeros_like(sums)
 
@@ -2038,7 +2060,6 @@
     for copy in swaps:
         copy.start()
     plane_sums[me] = own[...]
-    both.pass_on()
     heads.total(heads_own)
     gather = Gather(heads_own, heads_all, send_t, recv_t, local.at[5])
     gather.start()
@@ -2226,6 +2247,7 @@
         tokens_b,
         cotangent_b,
         cotangent_all,
+        low_all,
     ) = attend_ahead(
         tokens,
         cotangent,
@@ -2237,15 +2259,23 @@
         w_value.T,
         w_out,
         w_gate,
+        w_down,
         scale,
     )
     mixed = mixed.reshape(count, 2 * LANES)
-    middle, hidden_two, up_all, down_all = project_middle(
+    middle, hidden_two, up_all, high_all = project_middle(
         mixed, w_proj, tokens_b, norm2_gain[None], w_up, w_down
     )
-    down_all = down_all.reshape(members * units, width)
     middle_grad, branch, sums_two, activated, both_sum, down_in = feed(
-        hidden_two, cotangent_all, middle, gate_all, up_all, cotangent_b, down_all, norm2_gain[None]
+        hidden_two,
+        cotangent_all,
+        middle,
+        gate_all,
+        up_all,
+        cotangent_b,
+        low_all,
+        high_all,
+        norm2_gain[None],
     )
     qkv_grad, output_rows, branch_all, both_in, down_whole = attend_back(
         branch,
@@ -2253,7 +2283,8 @@
         kept,
         w_proj,
         activated.reshape(count, units * members),
-        down_all,
+        low_all,
+        high_all,
         middle,
         both_sum,
         down_in,

time: 595 us -> 578 us (0.971)
  Pallas kernels: 583 us -> 569 us
    pallas_call x1, Pallas kernels: 126 us -> 117 us  [project_input(): pl.pallas_call(input_kernel, out_shape=(shape((rows, width), BF16), shape...]
where the time goes in v10:
time: 578 us; the launch traced here: 577 us
  Pallas kernels  569 us (98%)
    pallas_call x1, Pallas kernels, attend_back(): pl.pallas_call(functools.partial(backward_kernel, scale=scale, groups=gro...  126 us
    pallas_call x1, Pallas kernels, attend_ahead(): pl.pallas_call(functools.partial(forward_kernel, scale=scale), out_shape=...  118 us
    pallas_call x1, Pallas kernels, project_input(): pl.pallas_call(input_kernel, out_shape=(shape((rows, width), BF16), shape...  117 us
    pallas_call x1, Pallas kernels, feed(): pl.pallas_call(feed_kernel, out_shape=(jax.ShapeDtypeStruct((rows, width)...  117 us
    pallas_call x1, Pallas kernels, project_middle(): pl.pallas_call(middle_kernel, out_shape=(jax.ShapeDtypeStruct((rows, widt...  69.7 us
    pallas_call x1, Pallas kernels, assemble(): pl.pallas_call(assemble_kernel, grid=(groups,), out_shape=(shape((rows, w...  21.1 us

profile of v10, /device:TPU:0, one launch (start us, length us, event | category | flops | bytes accessed | tf_op | source)
XLA Modules:
  0.0 576.5 jit_solution(13347142845431197383)
XLA Ops:
  0.6 0.7 add_select_fusion
  1.3 0.2 convert_reduce_fusion
  1.6 0.2 select_reduce_fusion
  1.7 0.1 reshape.44
  1.8 0.1 copy.27
  1.9 0.8 pad_dynamic-slice_fusion
  2.7 1.3 fusion.1.notes
  4.0 0.6 broadcast_in_dim.20.order_row
  4.5 1.3 broadcast_in_dim.21.gain
  5.8 0.0 copy-start.1
  5.8 117.6 %attend_ahead.1 = (bf16[8,384,1792]{2,1,0:T(8,128)(2,1)}, bf16[768,1792]{1,0:T(8,128)(2,1)}, bf16[256,1792]{1,0:T(8,128)(2,1)}, f32[8,56,128]{2,1,0:T(8,128)}, b...) custom-call(bf16[384,1792]{1,0:T(8,128)(2,1)} %tokens.1, ...), custom_call_target="tpu_custom_call" | custom-call | bytes 300000000 | tf_op jit(solution)/shard_map/attend_ahead/pallas_call | solution.py:886
  123.4 0.0 copy-done.1
  123.5 0.6 broadcast_in_dim.38.gain
  124.1 69.7 %project_middle.1 = (f32[384,1792]{1,0:T(8,128)}, bf16[384,1792]{1,0:T(8,128)(2,1)}, bf16[4,1792,128]{2,1,0:T(8,128)(2,1)}, bf16[4,64,1792]{2,1,0:T(8,128)(2,1)}) custom-call(bf16[3072,256]{1,0:T(8,128)(2,1)} %bitcast.14, bf16[256,1792]{1,0:T(8,128)(2,1)} %get-tuple-element.51.w_out.w_out_in, bf16[384,1792]{1,0:T(8,128)(2,1)} %get-tuple-element.52.tokens.tokens_in, ...), custom_call_target="tpu_custom_call" | custom-call | bytes 150000000 | tf_op jit(solution)/shard_map/project_middle/pallas_call | solution.py:1656
  193.8 117.0 %feed.1 = (f32[384,1792]{1,0:T(8,128)}, bf16[384,1792]{1,0:T(8,128)(2,1)}, f32[8,1792]{1,0:T(8,128)}, bf16[8,384,512]{2,1,0:T(8,128)(2,1)}, bf16[4,1792,256]{2,1...) custom-call(bf16[384,1792]{1,0:T(8,128)(2,1)} %get-tuple-element.53.hidden_own, ...), custom_call_target="tpu_custom_call" | custom-call | bytes 400000000 | tf_op jit(solution)/shard_map/feed/pallas_call | solution.py:1904
  310.8 125.9 %attend_back.1 = (bf16[8,8,48,768]{3,2,1,0:T(8,128)(2,1)}, bf16[384,1792]{1,0:T(8,128)(2,1)}, bf16[8,384,1792]{2,1,0:T(8,128)(2,1)}, bf16[4,1792,256]{2,1,0:T(8,128)(2,1)}, bf16[8,128,1792]{2,1,0:T(8,128)(2,1)}) custom-call(bf16[384,1792]{1,0:T(8,128)(2,1)} %get-tuple-element.61.branch, f32[8,56,128]{2,1,0:T(8,128)} %get-tuple-element.62.notes_all, ...), custom_call_target="tpu_custom_call" | custom-call | bytes 300000000 | tf_op jit(solution)/shard_map/attend_back/pallas_call | solution.py:1560
  436.7 117.3 %project_input.1 = (bf16[384,1792]{1,0:T(8,128)(2,1)}, f32[2,1792]{1,0:T(2,128)}, bf16[8,1792,256]{2,1,0:T(8,128)(2,1)}, bf16[8,448,896]{2,1,0:T(8,128)(2,1)}) custom-call(bf16[3072,768]{1,0:T(8,128)(2,1)} %bitcast.16, bf16[768,1792]{1,0:T(8,128)(2,1)} %get-tuple-element.68.w_qkv, bf16[8,384,1792]{2,1,0:T(8,128)(2,1)} %get-tuple-element.69.hidden_all, ...), custom_call_target="tpu_custom_call" | custom-call | bytes 250000000 | tf_op jit(solution)/shard_map/project_input/pallas_call | solution.py:2102
  554.0 0.8 broadcast_in_dim.40.order_column
  554.8 0.0 copy-start
  554.8 21.1 %assemble.1 = (bf16[384,1792]{1,0:T(8,128)(2,1)}, bf16[384,1792]{1,0:T(8,128)(2,1)}, f32[448,1792]{1,0:T(8,128)}, f32[448,1792]{1,0:T(8,128)}, f32[448,1792]{1,0...) custom-call(bf16[8,1792,256]{2,1,0:T(8,128)(2,1)} %get-tuple-element.74.bot, ...), custom_call_target="tpu_custom_call" | custom-call | bytes 58000000 | tf_op jit(solution)/shard_map/assemble/pallas_call | solution.py:2178
  575.9 0.0 copy-done
  575.9 0.6 slice_reduce_fusion
  (2 shorter events, 0.0 us)
Async XLA Ops:
  5.8 117.6 %copy-start.1 = (f32[1792]{0:T(1024)S(1)}, f32[1792]{0:T(1024)}, u32[]{:S(2)}) copy-start(f32[1792]{0:T(1024)} %param.20) | copy-start | bytes 21508
  554.8 21.1 %copy-start = (f32[2,1792]{1,0:T(2,128)S(1)}, f32[2,1792]{1,0:T(2,128)}, u32[]{:S(2)}) copy-start(f32[2,1792]{1,0:T(2,128)} %get-tuple-element.81) | copy-start | bytes 43012

commit v11 on v10

--- a/solution.py
+++ b/solution.py
@@ -691,10 +691,10 @@
 
 
 def forward_kernel(
-    tokens, cotangent, order_row, gain, notes, query, keys, values, project, gate, down,
+    tokens, cotangent, order_row, gain, notes, query, keys, values, project, gate,
     hidden_out, w_qkv_out, w_out, notes_all, gate_all, mixed_out, kept_out, tokens_out, cotangent_out,
-    cotangent_all, low_all,
-    hidden_all, qkv, share, gate_own, low_own, send_l, recv_l, w_qkv, mixed, kept, tokens_b, cotangent_b,
+    cotangent_all,
+    hidden_all, qkv, share, gate_own, w_qkv, mixed, kept, tokens_b, cotangent_b,
     send, recv, send_a, recv_a, send_g, recv_g, send_w, recv_w, send_n, recv_n, send_c, recv_c,
     local, out_sem, store_sem, *, scale,
 ):
@@ -708,9 +708,7 @@
         pltpu.make_async_copy(source.at[head], share.at[piece], local.at[piece])
         for piece, source in enumerate((query, keys, values, project))
     ]
-    half_units = pl.ds(pl.multiple_of(me * LANES, LANES // 2), LANES // 2)
     loads.append(pltpu.make_async_copy(gate.at[:, units], gate_own, local.at[4]))
-    loads.append(pltpu.make_async_copy(down.at[half_units], low_own, local.at[6]))
     for copy in loads:
         copy.start()
     none = jnp.zeros((LANES - HEAD_DIM, width), BF16)
@@ -746,7 +744,6 @@
     wait_all(loads[4:])
     column = Column(gate_own, gate_all, send_c, recv_c, local.at[4])
     second = Gather(cotangent_b, cotangent_all, send_g, recv_g, local.at[5])
-    low = Column(low_own, low_all, send_l, recv_l, local.at[6])
     spread.pass_on((0, 1, 2))
     gather.arrive(0, 1)
     second.start()
@@ -844,17 +841,13 @@
         return carry
 
     spread.pass_on((3,))
-    low.start()
     lax.fori_loop(0, groups // 2, attend, 0)
     second.pass_on()
     column.pass_on()
-    lax.fori_loop(groups // 2, groups - 1, attend, 0)
-    low.pass_on()
-    lax.fori_loop(groups - 1, groups, attend, 0)
+    lax.fori_loop(groups // 2, groups, attend, 0)
     spread.finish((3,))
     second.finish()
     column.finish()
-    low.finish()
     gather.sent()
 
     wait_all(stores)
@@ -877,7 +870,7 @@
 
 
 def attend_ahead(
-    tokens, cotangent, order_row, gain, notes, query, keys, values, project, gate, down, scale
+    tokens, cotangent, order_row, gain, notes, query, keys, values, project, gate, scale
 ):
     rows, width = tokens.shape
     groups, members = lax.axis_size("dp"), lax.axis_size("mp")
@@ -896,21 +889,17 @@
             shape((rows, width), BF16),
             shape((rows, width), BF16),
             shape((groups, rows, width), BF16),
-            shape((members, LANES // 2, width), BF16),
         ),
-        in_specs=[on_chip()] * 5 + [anywhere()] * 6,
+        in_specs=[on_chip()] * 5 + [anywhere()] * 5,
         out_specs=(
             anywhere(), anywhere(), on_chip(), on_chip(), anywhere(),
-            anywhere(), anywhere(), anywhere(), anywhere(), anywhere(), anywhere(),
+            anywhere(), anywhere(), anywhere(), anywhere(), anywhere(),
         ),
         scratch_shapes=[
             pltpu.VMEM((groups, rows, width), BF16),
             pltpu.VMEM((groups, groups, rows // groups, 768), BF16),
             pltpu.VMEM((4, HEAD_DIM, width), BF16),
             pltpu.VMEM((width, LANES), BF16),
-            pltpu.VMEM((LANES // 2, width), BF16),
-            dma((4,)),
-            dma((4,)),
             pltpu.VMEM((6 * LANES, width), BF16),
             pltpu.VMEM((groups, groups, rows // groups, 256), BF16),
             pltpu.VMEM((groups, rows + 64, 768), BF16),
@@ -928,14 +917,14 @@
             dma((7,)),
             dma((4,)),
             dma((4,)),
-            dma((7,)),
+            dma((6,)),
             dma((groups,)),
             dma((3 + 2 * groups,)),
         ],
         compiler_params=remote_params(2, 60 * 1024 * 1024),
         cost_estimate=pl.CostEstimate(flops=0, bytes_accessed=300_000_000, transcendentals=0),
         name="attend_ahead",
-    )(tokens, cotangent, order_row, gain, notes, query, keys, values, project, gate, down)
+    )(tokens, cotangent, order_row, gain, notes, query, keys, values, project, gate)
 
 
 CHUNK = 32
@@ -1081,7 +1070,11 @@
 
         def tile(t, carry):
             columns = pl.ds(pl.multiple_of(t * 256, 256), 256)
-            if self.across:
+            if callable(self.left):
+                value = jnp.dot(
+                    self.left(owner), self.right[:, columns], preferred_element_type=F32
+                )
+            elif self.across:
                 value = lax.dot_general(
                     self.left[picked, :], self.right[columns, :], NT, preferred_element_type=F32
                 )
@@ -1394,7 +1387,7 @@
 
 
 def backward_kernel(
-    branch, notes_all, kept_in, w_out_in, activated_in, low_all, high_all, middle_in, both_sum, down_in,
+    branch, notes_all, kept_in, w_out_in, activated_in, w_down_in, middle_in, both_sum, down_in,
     out, result, branch_all, both_in, down_all,
     totals, query_part, key_value, ending, leaving, arriving, send, recv,
     part, from_side, from_corner, from_near, send_r, recv_r,
@@ -1407,6 +1400,7 @@
     members = lax.axis_size("mp")
     barrier = greet_all()
     pairs = ((activated_in, activated), (w_out_in, w_out), (kept_in, kept), (middle_in, middle))
+    pairs += ((w_down_in, w_down),)
     fetches = [
         pltpu.make_async_copy(source, target, fetch_sem.at[number])
         for number, (source, target) in enumerate(pairs)
@@ -1417,10 +1411,9 @@
     gather = Gather(branch, branch_all, send_g, recv_g, local.at[2])
     gather.start()
     units.start()
-    halves = start_all(load_halves(low_all, high_all, w_down, fetch_sem, 4))
     start_all(fetches)
     load_down.start()
-    wait_all(halves + fetches[:1])
+    wait_all((fetches[0], fetches[4]))
     reduce = Reduce(activated, w_down, False, part, from_side, from_corner, from_near, send_r, recv_r)
     reduce.products()
     load_down.wait()
@@ -1459,8 +1452,9 @@
         return carry
 
     fetches[1].wait()
-    lax.fori_loop(0, 8, spread_back, 0)
+    lax.fori_loop(0, 4, spread_back, 0)
     reduce.launch()
+    lax.fori_loop(4, 8, spread_back, 0)
     units.add()
 
 
@@ -1505,7 +1499,7 @@
 
         return carry
 
-    wait_all(fetches[2:])
+    wait_all(fetches[2:4])
     lax.fori_loop(0, 3, attend, 0)
     reduce.middle()
     down.start()
@@ -1550,7 +1544,7 @@
 
 
 def attend_back(
-    branch, notes_all, kept, w_out, activated, low_all, high_all, middle, both_sum, down_in, scale
+    branch, notes_all, kept, w_out, activated, w_down, middle, both_sum, down_in, scale
 ):
     groups = kept.shape[0]
     rows, width = middle.shape
@@ -1566,7 +1560,7 @@
             shape((members, width, 256), BF16),
             shape((groups, LANES, width), BF16),
         ),
-        in_specs=[on_chip()] * 2 + [anywhere()] * 8,
+        in_specs=[on_chip()] * 2 + [anywhere()] * 7,
         out_specs=(on_chip(),) * 2 + (anywhere(),) * 3,
         scratch_shapes=[
             pltpu.VMEM((rows + 64, 512), F32),
@@ -1597,86 +1591,12 @@
             pltpu.VMEM(activated.shape, BF16),
             pltpu.VMEM((members * LANES, width), BF16),
             pltpu.VMEM((rows, width), F32),
-            dma((4 + 2 * members,)),
+            dma((5,)),
         ],
         compiler_params=remote_params(3, 63 * 1024 * 1024),
         cost_estimate=pl.CostEstimate(flops=0, bytes_accessed=300_000_000, transcendentals=0),
         name="attend_back",
-    )(branch, notes_all, kept, w_out, activated, low_all, high_all, middle, both_sum, down_in)
-
-
-def middle_kernel(
-    mixed, w_out, tokens, gain, w_up, w_down, middle, hidden, up_all, down_all,
-    part, from_side, from_corner, from_near, send, recv, up_own, down_own,
-    send_u, recv_u, send_d, recv_d, local,
-):
-    barrier = greet_all()
-    units = pl.ds(pl.multiple_of(lax.axis_index("dp") * LANES, LANES), LANES)
-    high_units = pl.ds(
-        pl.multiple_of(lax.axis_index("dp") * LANES + LANES // 2, LANES // 2), LANES // 2
-    )
-    loads = [
-        pltpu.make_async_copy(w_up.at[:, units], up_own, local.at[0]),
-        pltpu.make_async_copy(w_down.at[high_units], down_own, local.at[1]),
-    ]
-    for copy in loads:
-        copy.start()
-    pl.semaphore_wait(barrier, 13)
-    for copy in loads:
-        copy.wait()
-    columns = [
-        Column(up_own, up_all, send_u, recv_u, local.at[0]),
-        Column(down_own, down_all, send_d, recv_d, local.at[1]),
-    ]
-    for column in columns:
-        column.start()
-    reduce = Reduce(mixed, w_out, False, part, from_side, from_corner, from_near, send, recv)
-    reduce.begin()
-    reduce.middle()
-    for column in columns:
-        column.pass_on()
-    reduce.end()
-
-    def body(span):
-        values = tokens[span, :].astype(F32) + reduce.rows_of(span)
-        middle[span, :] = values
-        inverse = lax.rsqrt(mean_rows(values * values) + EPSILON)
-        hidden[span, :] = (values * inverse * gain[...]).astype(BF16)
-
-    each_chunk(hidden.shape[0], body)
-    for column in columns:
-        column.finish()
-    reduce.finish()
-
-
-def project_middle(mixed, w_out, tokens, gain, w_up, w_down):
-    rows, width = tokens.shape
-    dma = pltpu.SemaphoreType.DMA
-    members = lax.axis_size("mp")
-    return pl.pallas_call(
-        middle_kernel,
-        out_shape=(
-            jax.ShapeDtypeStruct((rows, width), F32),
-            jax.ShapeDtypeStruct((rows, width), BF16),
-            jax.ShapeDtypeStruct((members, width, LANES), BF16),
-            jax.ShapeDtypeStruct((members, LANES // 2, width), BF16),
-        ),
-        in_specs=[on_chip()] * 4 + [anywhere()] * 2,
-        out_specs=(on_chip(), on_chip(), anywhere(), anywhere()),
-        scratch_shapes=reduce_scratch(rows, width)
-        + [
-            pltpu.VMEM((width, LANES), BF16),
-            pltpu.VMEM((LANES // 2, width), BF16),
-            dma((4,)),
-            dma((4,)),
-            dma((4,)),
-            dma((4,)),
-            dma((2,)),
-        ],
-        compiler_params=remote_params(4),
-        cost_estimate=pl.CostEstimate(flops=0, bytes_accessed=150_000_000, transcendentals=0),
-        name="project_middle",
-    )(mixed, w_out, tokens, gain, w_up, w_down)
+    )(branch, notes_all, kept, w_out, activated, w_down, middle, both_sum, down_in)
 
 
 def norm_back_rows(gradient, values, gain, sums, span):
@@ -1691,38 +1611,41 @@
     return inverse * (scaled - normed * mean_rows(scaled * normed))
 
 
-def load_halves(low_all, high_all, weight, sems, first):
-    half = low_all.shape[1]
-    return [
-        pltpu.make_async_copy(
-            source.at[z], weight.at[pl.ds((2 * z + number) * half, half)], sems.at[first + 2 * z + number]
-        )
-        for z in range(low_all.shape[0])
-        for number, source in enumerate((low_all, high_all))
-    ]
-
-
 def feed_kernel(
-    hidden_own, cotangent_all, middle, gate_all, up_all, cotangent_own, low_all, high_all, gain,
-    middle_grad, branch, sums, activated_out, both_sum, down_in,
+    mixed, w_out, tokens, cotangent_all, gate_all, w_up, down_weight, cotangent_own, gain,
+    middle, middle_grad, branch, sums, activated_out, both_sum, down_in, up_all, down_all,
     hidden_all, both_grad, part, from_side, from_corner, from_near, send_r, recv_r,
-    send_a, recv_a, cot_shard, cot_tile, stage_both, down_sum, w_both, w_down, cotangent, activated,
-    load_sem, local, send_z, recv_z, stage_down,
+    send_m, recv_m, send_a, recv_a, cot_shard, cot_tile, stage_both, down_sum, w_both, w_down,
+    cotangent, activated, load_sem, local, send_z, recv_z, stage_down,
+    up_own, down_own, send_u, recv_u, send_d, recv_d, first_sem,
 ):
     groups, rows, width = hidden_all.shape
     members = gate_all.shape[0]
     me = lax.axis_index("dp")
     barrier = greet_all()
-    own = pltpu.make_async_copy(hidden_own, hidden_all.at[me], local.at[0])
-    own.start()
-    start_middle = pltpu.make_async_copy(middle, middle_grad, local.at[1])
-    loads = [
-        pltpu.make_async_copy(
-            source.at[z], w_both.at[:, pl.ds(z * 256 + offset, 128)], load_sem.at[6 + 2 * z + number]
-        )
-        for z in range(members)
-        for number, (source, offset) in enumerate(((gate_all, 0), (up_all, 128)))
-    ]
+    units_own = pl.ds(pl.multiple_of(me * LANES, LANES), LANES)
+    first = start_all(
+        [
+            pltpu.make_async_copy(source, target, first_sem.at[number])
+            for number, (source, target) in enumerate(
+                (
+                    (mixed, activated.at[:, :, pl.ds(0, 256)]),
+                    (w_out, down_sum.at[pl.ds(0, 256)]),
+                    (w_up.at[:, units_own], up_own),
+                    (down_weight.at[units_own], down_own),
+                    (tokens, cotangent),
+                )
+            )
+        ]
+    )
+    gates = start_all(
+        [
+            pltpu.make_async_copy(
+                gate_all.at[z], w_both.at[:, pl.ds(z * 256, 128)], load_sem.at[6 + z]
+            )
+            for z in range(members)
+        ]
+    )
 
     def slot_of(turn):
         block = turn // 2
@@ -1737,14 +1660,55 @@
             cotangent_all.at[owner_at(turn)], cot_shard.at[turn % 2], load_sem.at[turn % 2]
         )
 
-    loads += load_halves(low_all, high_all, w_down, load_sem, 6 + 2 * members)
-    load_own = pltpu.make_async_copy(cotangent_own, cotangent, local.at[3])
-    start_all(loads)
     load_cotangent(0).start()
-    own.wait()
+    wait_all(first)
     pl.semaphore_wait(barrier, 13)
+    columns_up = Column(up_own, up_all, send_u, recv_u, local.at[0])
+    columns_down = Column(down_own, down_all, send_d, recv_d, local.at[2])
+    columns_up.start()
+    columns_down.start()
+    project = Reduce(
+        lambda owner: activated[owner, :, 0:256], down_sum.at[pl.ds(0, 256)], False,
+        part, from_side, from_corner, from_near, send_m, recv_m,
+    )
+    project.begin()
+    project.middle()
+    columns_up.pass_on()
+    columns_down.pass_on()
+    project.end()
+
+    def normalise(span):
+        values = cotangent[span, :].astype(F32) + project.rows_of(span)
+        middle_grad[span, :] = values
+        inverse = lax.rsqrt(mean_rows(values * values) + EPSILON)
+        hidden_all[me, span, :] = (values * inverse * gain[...]).astype(BF16)
+
+    each_chunk(rows, normalise)
+    project.finish()
     gather = Gather(None, hidden_all, send_a, recv_a)
     gather.start()
+    store_middle = pltpu.make_async_copy(middle_grad, middle, local.at[1])
+    load_own = pltpu.make_async_copy(cotangent_own, cotangent, local.at[3])
+    store_middle.start()
+    load_own.start()
+    columns_up.finish()
+    columns_down.finish()
+    ups = start_all(
+        [
+            pltpu.make_async_copy(
+                up_all.at[z], w_both.at[:, pl.ds(z * 256 + 128, 128)], load_sem.at[10 + z]
+            )
+            for z in range(members)
+        ]
+    )
+    ups += start_all(
+        [
+            pltpu.make_async_copy(
+                down_all.at[z], w_down.at[pl.ds(z * LANES, LANES)], load_sem.at[14 + z]
+            )
+            for z in range(members)
+        ]
+    )
     reduce = Reduce(None, None, False, part, from_side, from_corner, from_near, send_r, recv_r)
     reduce.prepare()
 
@@ -1757,9 +1721,7 @@
     early = [(turn, functools.partial(gather.arrive, *numbers)) for turn, numbers in ARRIVALS]
     early += [(6, nears)]
     late = [(1, 3), (4, 1), (5, 2), (7, 0)]
-    start_middle.start()
-    load_own.start()
-    wait_all(loads)
+    wait_all(gates + ups)
 
     def unit(turn, carry):
         for number, action in early:
@@ -1876,7 +1838,7 @@
     passing.add()
     lax.fori_loop(2, tiles, weight_tile, 0)
     reduce.end()
-    start_middle.wait()
+    store_middle.wait()
     load_own.wait()
     sums[...] = jnp.zeros_like(sums)
 
@@ -1896,7 +1858,7 @@
     passing.finish()
 
 
-def feed(hidden_own, cotangent_all, middle, gate_all, up_all, cotangent, low_all, high_all, gain):
+def feed(mixed, w_out, tokens, cotangent_all, gate_all, w_up, w_down, cotangent, gain):
     groups, rows, width = cotangent_all.shape
     members = gate_all.shape[0]
     dma = pltpu.SemaphoreType.DMA
@@ -1905,20 +1867,25 @@
         feed_kernel,
         out_shape=(
             jax.ShapeDtypeStruct((rows, width), F32),
+            jax.ShapeDtypeStruct((rows, width), F32),
             jax.ShapeDtypeStruct((rows, width), BF16),
             jax.ShapeDtypeStruct((8, width), F32),
             jax.ShapeDtypeStruct((groups, rows, units), BF16),
             jax.ShapeDtypeStruct((members, width, 256), BF16),
             jax.ShapeDtypeStruct((members, LANES, width), BF16),
+            jax.ShapeDtypeStruct((members, width, LANES), BF16),
+            jax.ShapeDtypeStruct((members, LANES, width), BF16),
         ),
         in_specs=[anywhere()] * 8 + [on_chip()],
-        out_specs=(on_chip(),) * 3 + (anywhere(),) * 3,
+        out_specs=(anywhere(),) + (on_chip(),) * 3 + (anywhere(),) * 5,
         scratch_shapes=[
             pltpu.VMEM((groups, rows, width), BF16),
             pltpu.VMEM((groups, rows, 2 * units), BF16),
         ]
         + reduce_scratch(rows, width)
         + [
+            dma((10,)),
+            dma((10,)),
             dma((13,)),
             dma((13,)),
             pltpu.VMEM((2, rows, width), BF16),
@@ -1934,11 +1901,18 @@
             dma((6,)),
             dma((10,)),
             pltpu.VMEM((2, LANES, width), BF16),
+            pltpu.VMEM((width, LANES), BF16),
+            pltpu.VMEM((LANES, width), BF16),
+            dma((4,)),
+            dma((4,)),
+            dma((4,)),
+            dma((4,)),
+            dma((5,)),
         ],
         compiler_params=remote_params(5, 63 * 1024 * 1024),
         cost_estimate=pl.CostEstimate(flops=0, bytes_accessed=400_000_000, transcendentals=0),
         name="feed",
-    )(hidden_own, cotangent_all, middle, gate_all, up_all, cotangent, low_all, high_all, gain)
+    )(mixed, w_out, tokens, cotangent_all, gate_all, w_up, w_down, cotangent, gain)
 
 
 def input_kernel(
@@ -2247,7 +2221,6 @@
         tokens_b,
         cotangent_b,
         cotangent_all,
-        low_all,
     ) = attend_ahead(
         tokens,
         cotangent,
@@ -2259,22 +2232,18 @@
         w_value.T,
         w_out,
         w_gate,
+        scale,
+    )
+    mixed = mixed.reshape(count, 2 * LANES)
+    middle, middle_grad, branch, sums_two, activated, both_sum, down_in, _, down_all = feed(
+        mixed.reshape(groups, rows, 2 * LANES),
+        w_proj,
+        tokens_b,
+        cotangent_all,
+        gate_all,
+        w_up,
         w_down,
-        scale,
-    )
-    mixed = mixed.reshape(count, 2 * LANES)
-    middle, hidden_two, up_all, high_all = project_middle(
-        mixed, w_proj, tokens_b, norm2_gain[None], w_up, w_down
-    )
-    middle_grad, branch, sums_two, activated, both_sum, down_in = feed(
-        hidden_two,
-        cotangent_all,
-        middle,
-        gate_all,
-        up_all,
         cotangent_b,
-        low_all,
-        high_all,
         norm2_gain[None],
     )
     qkv_grad, output_rows, branch_all, both_in, down_whole = attend_back(
@@ -2283,8 +2252,7 @@
         kept,
         w_proj,
         activated.reshape(count, units * members),
-        low_all,
-        high_all,
+        down_all.reshape(members * units, width),
         middle,
         both_sum,
         down_in,

time: 578 us -> 557 us (0.964)
  Pallas kernels: 569 us -> 548 us
    pallas_call x1 -> x0, Pallas kernels: 69.7 us -> none  [project_middle(): pl.pallas_call(middle_kernel, out_shape=(jax.ShapeDtypeStruct((rows, widt...]
    pallas_call x1, Pallas kernels: 117 us -> 176 us  [feed(): pl.pallas_call(feed_kernel, out_shape=(jax.ShapeDtypeStruct((rows, width)...]
    pallas_call x1, Pallas kernels: 126 us -> 118 us  [attend_back(): pl.pallas_call(functools.partial(backward_kernel, scale=scale, groups=gro...]
where the time goes in v11:
time: 557 us; the launch traced here: 556 us
  Pallas kernels  548 us (98%)
    pallas_call x1, Pallas kernels, feed(): pl.pallas_call(feed_kernel, out_shape=(jax.ShapeDtypeStruct((rows, width)...  176 us
    pallas_call x1, Pallas kernels, project_input(): pl.pallas_call(input_kernel, out_shape=(shape((rows, width), BF16), shape...  118 us
    pallas_call x1, Pallas kernels, attend_back(): pl.pallas_call(functools.partial(backward_kernel, scale=scale, groups=gro...  118 us
    pallas_call x1, Pallas kernels, attend_ahead(): pl.pallas_call(functools.partial(forward_kernel, scale=scale), out_shape=...  114 us
    pallas_call x1, Pallas kernels, assemble(): pl.pallas_call(assemble_kernel, grid=(groups,), out_shape=(shape((rows, w...  21.1 us

profile of v11, /device:TPU:0, one launch (start us, length us, event | category | flops | bytes accessed | tf_op | source)
XLA Modules:
  0.0 555.8 jit_solution(6696605058229764921)
XLA Ops:
  0.6 0.7 add_select_fusion
  1.3 0.2 convert_reduce_fusion
  1.6 0.2 select_reduce_fusion
  1.7 0.1 reshape.47
  1.8 0.1 copy.27
  1.9 0.8 pad_dynamic-slice_fusion
  2.7 1.3 fusion.1.notes
  4.0 0.6 broadcast_in_dim.20.order_row
  4.5 1.3 broadcast_in_dim.34.gain
  5.8 0.0 copy-start.1
  5.8 114.5 %attend_ahead.1 = (bf16[8,384,1792]{2,1,0:T(8,128)(2,1)}, bf16[768,1792]{1,0:T(8,128)(2,1)}, bf16[256,1792]{1,0:T(8,128)(2,1)}, f32[8,56,128]{2,1,0:T(8,128)}, b...) custom-call(bf16[384,1792]{1,0:T(8,128)(2,1)} %tokens.1, ...), custom_call_target="tpu_custom_call" | custom-call | bytes 300000000 | tf_op jit(solution)/shard_map/attend_ahead/pallas_call | solution.py:879
  120.3 0.0 copy-done.1
  120.3 0.6 broadcast_in_dim.37.gain
  120.9 175.9 %feed.1 = (f32[384,1792]{1,0:T(8,128)}, f32[384,1792]{1,0:T(8,128)}, bf16[384,1792]{1,0:T(8,128)(2,1)}, f32[8,1792]{1,0:T(8,128)}, bf16[8,384,512]{2,1,0:T(8,128...) custom-call(bf16[8,384,256]{2,1,0:T(8,128)(2,1)} %bitcast.16, ...), custom_call_target="tpu_custom_call" | custom-call | bytes 400000000 | tf_op jit(solution)/shard_map/feed/pallas_call | solution.py:1866
  296.9 118.1 %attend_back.1 = (bf16[8,8,48,768]{3,2,1,0:T(8,128)(2,1)}, bf16[384,1792]{1,0:T(8,128)(2,1)}, bf16[8,384,1792]{2,1,0:T(8,128)(2,1)}, bf16[4,1792,256]{2,1,0:T(8,128)(2,1)}, bf16[8,128,1792]{2,1,0:T(8,128)(2,1)}) custom-call(bf16[384,1792]{1,0:T(8,128)(2,1)} %get-tuple-element.53.branch, f32[8,56,128]{2,1,0:T(8,128)} %get-tuple-element.54.notes_all, ...), custom_call_target="tpu_custom_call" | custom-call | bytes 300000000 | tf_op jit(solution)/shard_map/attend_back/pallas_call | solution.py:1554
  415.0 118.3 %project_input.1 = (bf16[384,1792]{1,0:T(8,128)(2,1)}, f32[2,1792]{1,0:T(2,128)}, bf16[8,1792,256]{2,1,0:T(8,128)(2,1)}, bf16[8,448,896]{2,1,0:T(8,128)(2,1)}) custom-call(bf16[3072,768]{1,0:T(8,128)(2,1)} %bitcast.18, bf16[768,1792]{1,0:T(8,128)(2,1)} %get-tuple-element.62.w_qkv, bf16[8,384,1792]{2,1,0:T(8,128)(2,1)} %get-tuple-element.63.hidden_all, ...), custom_call_target="tpu_custom_call" | custom-call | bytes 250000000 | tf_op jit(solution)/shard_map/project_input/pallas_call | solution.py:2076
  533.3 0.8 broadcast_in_dim.39.order_column
  534.1 0.0 copy-start
  534.1 21.1 %assemble.1 = (bf16[384,1792]{1,0:T(8,128)(2,1)}, bf16[384,1792]{1,0:T(8,128)(2,1)}, f32[448,1792]{1,0:T(8,128)}, f32[448,1792]{1,0:T(8,128)}, f32[448,1792]{1,0...) custom-call(bf16[8,1792,256]{2,1,0:T(8,128)(2,1)} %get-tuple-element.68.bot, ...), custom_call_target="tpu_custom_call" | custom-call | bytes 58000000 | tf_op jit(solution)/shard_map/assemble/pallas_call | solution.py:2152
  555.2 0.0 copy-done
  555.2 0.6 slice_reduce_fusion
  (2 shorter events, 0.0 us)
Async XLA Ops:
  5.8 114.5 %copy-start.1 = (f32[1792]{0:T(1024)S(1)}, f32[1792]{0:T(1024)}, u32[]{:S(2)}) copy-start(f32[1792]{0:T(1024)} %param.20) | copy-start | bytes 21508
  534.1 21.1 %copy-start = (f32[2,1792]{1,0:T(2,128)S(1)}, f32[2,1792]{1,0:T(2,128)}, u32[]{:S(2)}) copy-start(f32[2,1792]{1,0:T(2,128)} %get-tuple-element.75) | copy-start | bytes 43012

commit v12 on v11

--- a/solution.py
+++ b/solution.py
@@ -819,21 +819,27 @@
 
         store_kept(k).start()
         hot = hot_of(notes_all, k, rows)
-        found = []
-        for block in range(rows // 128):
-            allowed = block_mask(notes_all, k, block, z, rows)
-            heads = []
-            for head in range(2):
-                query = kept[k, pl.ds(64 + block * 128, 128), pl.ds(head * 128, 128)]
-                keys = kept[k, pl.ds(block * 128, 192), pl.ds(256 + head * 128, 128)]
-                values = kept[k, pl.ds(block * 128, 192), pl.ds(512 + head * 128, 128)]
-                scores = lax.dot_general(query, keys, NT, preferred_element_type=F32) * scale
-                scores = jnp.where(allowed, scores, -MASKED)
-                weights = jnp.exp(scores - jnp.max(scores, axis=-1, keepdims=True))
-                total = jnp.sum(weights, axis=-1, keepdims=True)
-                chances = (weights / total).astype(BF16)
-                heads.append(jnp.dot(chances, values, preferred_element_type=F32).astype(BF16))
-            found.append(jnp.concatenate(heads, axis=1))
+        pairs = [(block, head) for block in range(rows // 128) for head in range(2)]
+        masks = [block_mask(notes_all, k, block, z, rows) for block in range(rows // 128)]
+        scores = []
+        for block, head in pairs:
+            query = kept[k, pl.ds(64 + block * 128, 128), pl.ds(head * 128, 128)]
+            keys = kept[k, pl.ds(block * 128, 192), pl.ds(256 + head * 128, 128)]
+            value = lax.dot_general(query, keys, NT, preferred_element_type=F32) * scale
+            scores.append(jnp.where(masks[block], value, -MASKED))
+        chances = []
+        for value in scores:
+            weights = jnp.exp(value - jnp.max(value, axis=-1, keepdims=True))
+            total = jnp.sum(weights, axis=-1, keepdims=True)
+            chances.append((weights / total).astype(BF16))
+        parts = []
+        for (block, head), chance in zip(pairs, chances):
+            values = kept[k, pl.ds(block * 128, 192), pl.ds(512 + head * 128, 128)]
+            parts.append(jnp.dot(chance, values, preferred_element_type=F32).astype(BF16))
+        found = [
+            jnp.concatenate(parts[2 * block : 2 * block + 2], axis=1)
+            for block in range(rows // 128)
+        ]
         ordered = jnp.concatenate(found, axis=0)
         back = jnp.dot(hot, ordered, preferred_element_type=F32).astype(BF16)
         mixed[:, pl.ds(k, 1)] = back.reshape(groups, 1, rows // groups, 256)
@@ -1387,13 +1393,13 @@
 
 
 def backward_kernel(
-    branch, notes_all, kept_in, w_out_in, activated_in, w_down_in, middle_in, both_sum, down_in,
+    branch, notes_all, kept_in, w_out_in, activated_in, w_down_in, middle_in, both_sum, down_sum,
     out, result, branch_all, both_in, down_all,
     totals, query_part, key_value, ending, leaving, arriving, send, recv,
     part, from_side, from_corner, from_near, send_r, recv_r,
     mixed_grad, shard, load_sem, send_g, recv_g,
     both_stage, send_u, recv_u, local, down_found, send_d, recv_d,
-    kept, w_out, activated, w_down, middle, fetch_sem,
+    kept, w_out, activated, w_down, middle, fetch_sem, down_stage, send_v, recv_v, local_v,
     *, scale, groups, rows,
 ):
     z = lax.axis_index("mp")
@@ -1405,29 +1411,24 @@
         pltpu.make_async_copy(source, target, fetch_sem.at[number])
         for number, (source, target) in enumerate(pairs)
     ]
-    load_down = pltpu.make_async_copy(down_in, down_found, load_sem.at[2])
+
+    def down_rows(owner):
+        return down_sum.at[pl.ds(pl.multiple_of(owner * LANES, LANES), LANES)]
+
+    down_units = Units(down_rows, down_found, down_stage, send_v, recv_v, local_v)
+    load_down = pltpu.make_async_copy(down_rows(z), down_found.at[z], load_sem.at[2])
     pl.semaphore_wait(barrier, 13)
     units = Units(lambda owner: both_sum.at[owner], both_in, both_stage, send_u, recv_u, local)
     gather = Gather(branch, branch_all, send_g, recv_g, local.at[2])
     gather.start()
+    down_units.start()
     units.start()
     start_all(fetches)
     load_down.start()
     wait_all((fetches[0], fetches[4]))
     reduce = Reduce(activated, w_down, False, part, from_side, from_corner, from_near, send_r, recv_r)
     reduce.products()
-    load_down.wait()
-
-    @pl.when((z == 0) | (z == members - 1))
-    def _():
-        down_found[members - 1 - z] = jnp.zeros_like(down_found[0])
-
-    def add_down(span):
-        value = down_found[0, span, :].astype(F32) + down_found[1, span, :].astype(F32)
-        value = value + down_found[2, span, :].astype(F32) + down_found[3, span, :].astype(F32)
-        down_found[0, span, :] = value.astype(BF16)
-
-    each_chunk(down_found.shape[1], add_down)
+    down_units.add()
     down = Gather(down_found.at[0], down_all, send_d, recv_d, local.at[1])
 
     def load_shard(turn):
@@ -1466,29 +1467,46 @@
         given = mixed_grad[:, pl.ds(k, 1)].reshape(rows, 256)
         grad_ordered = lax.dot_general(hot, given, TN, preferred_element_type=F32).astype(BF16)
         totals[...] = jnp.zeros_like(totals)
-        for block in range(rows // 128):
-            allowed = block_mask(notes_all, k, block, z, rows)
-            for head in range(2):
-                query = kept[k, pl.ds(64 + block * 128, 128), pl.ds(head * 128, 128)]
-                keys = kept[k, pl.ds(block * 128, 192), pl.ds(256 + head * 128, 128)]
-                values = kept[k, pl.ds(block * 128, 192), pl.ds(512 + head * 128, 128)]
-                grad = grad_ordered[block * 128 : block * 128 + 128, head * 128 : head * 128 + 128]
-                scores = lax.dot_general(query, keys, NT, preferred_element_type=F32) * scale
-                scores = jnp.where(allowed, scores, -MASKED)
-                weights = jnp.exp(scores - jnp.max(scores, axis=-1, keepdims=True))
-                again = weights / jnp.sum(weights, axis=-1, keepdims=True)
-                chance_grad = lax.dot_general(grad, values, NT, preferred_element_type=F32)
-                row_dot = jnp.sum(again * chance_grad, axis=-1, keepdims=True)
-                score_grad = (again * (chance_grad - row_dot)).astype(BF16)
-                query_part[k, pl.ds(block * 128, 128), pl.ds(head * 128, 128)] = (
-                    jnp.dot(score_grad, keys, preferred_element_type=F32) * scale
-                ).astype(BF16)
-                totals[pl.ds(block * 128, 192), pl.ds(head * 128, 128)] += (
-                    lax.dot_general(score_grad, query, TN, preferred_element_type=F32) * scale
-                )
-                totals[pl.ds(block * 128, 192), pl.ds(256 + head * 128, 128)] += lax.dot_general(
-                    again.astype(BF16), grad, TN, preferred_element_type=F32
-                )
+        pairs = [(block, head) for block in range(rows // 128) for head in range(2)]
+        masks = [block_mask(notes_all, k, block, z, rows) for block in range(rows // 128)]
+
+        def query_of(block, head):
+            return kept[k, pl.ds(64 + block * 128, 128), pl.ds(head * 128, 128)]
+
+        def keys_of(block, head):
+            return kept[k, pl.ds(block * 128, 192), pl.ds(256 + head * 128, 128)]
+
+        def grad_of(block, head):
+            return grad_ordered[block * 128 : block * 128 + 128, head * 128 : head * 128 + 128]
+
+        scores, chance_grads = [], []
+        for block, head in pairs:
+            value = lax.dot_general(
+                query_of(block, head), keys_of(block, head), NT, preferred_element_type=F32
+            )
+            scores.append(jnp.where(masks[block], value * scale, -MASKED))
+            values = kept[k, pl.ds(block * 128, 192), pl.ds(512 + head * 128, 128)]
+            chance_grads.append(
+                lax.dot_general(grad_of(block, head), values, NT, preferred_element_type=F32)
+            )
+        agains, score_grads = [], []
+        for value, chance_grad in zip(scores, chance_grads):
+            weights = jnp.exp(value - jnp.max(value, axis=-1, keepdims=True))
+            again = weights / jnp.sum(weights, axis=-1, keepdims=True)
+            row_dot = jnp.sum(again * chance_grad, axis=-1, keepdims=True)
+            agains.append(again.astype(BF16))
+            score_grads.append((again * (chance_grad - row_dot)).astype(BF16))
+        for (block, head), again, score_grad in zip(pairs, agains, score_grads):
+            query_part[k, pl.ds(block * 128, 128), pl.ds(head * 128, 128)] = (
+                jnp.dot(score_grad, keys_of(block, head), preferred_element_type=F32) * scale
+            ).astype(BF16)
+            totals[pl.ds(block * 128, 192), pl.ds(head * 128, 128)] += (
+                lax.dot_general(score_grad, query_of(block, head), TN, preferred_element_type=F32)
+                * scale
+            )
+            totals[pl.ds(block * 128, 192), pl.ds(256 + head * 128, 128)] += lax.dot_general(
+                again, grad_of(block, head), TN, preferred_element_type=F32
+            )
         key_value[k] = totals[pl.ds(64, rows), :].astype(BF16)
         ending[k] = totals[pl.ds(rows, 64), :]
 
@@ -1502,6 +1520,19 @@
     wait_all(fetches[2:4])
     lax.fori_loop(0, 3, attend, 0)
     reduce.middle()
+    load_down.wait()
+    down_units.finish()
+
+    @pl.when((z == 0) | (z == members - 1))
+    def _():
+        down_found[members - 1 - z] = jnp.zeros_like(down_found[0])
+
+    def add_down(span):
+        value = down_found[0, span, :].astype(F32) + down_found[1, span, :].astype(F32)
+        value = value + down_found[2, span, :].astype(F32) + down_found[3, span, :].astype(F32)
+        down_found[0, span, :] = value.astype(BF16)
+
+    each_chunk(down_found.shape[1], add_down)
     down.start()
     lax.fori_loop(3, 7, attend, 0)
     down.pass_on()
@@ -1544,7 +1575,7 @@
 
 
 def attend_back(
-    branch, notes_all, kept, w_out, activated, w_down, middle, both_sum, down_in, scale
+    branch, notes_all, kept, w_out, activated, w_down, middle, both_sum, down_sum, scale
 ):
     groups = kept.shape[0]
     rows, width = middle.shape
@@ -1592,11 +1623,15 @@
             pltpu.VMEM((members * LANES, width), BF16),
             pltpu.VMEM((rows, width), F32),
             dma((5,)),
+            pltpu.VMEM((2, LANES, width), BF16),
+            dma((6,)),
+            dma((10,)),
+            dma((1,)),
         ],
         compiler_params=remote_params(3, 63 * 1024 * 1024),
         cost_estimate=pl.CostEstimate(flops=0, bytes_accessed=300_000_000, transcendentals=0),
         name="attend_back",
-    )(branch, notes_all, kept, w_out, activated, w_down, middle, both_sum, down_in)
+    )(branch, notes_all, kept, w_out, activated, w_down, middle, both_sum, down_sum)
 
 
 def norm_back_rows(gradient, values, gain, sums, span):
@@ -1613,10 +1648,10 @@
 
 def feed_kernel(
     mixed, w_out, tokens, cotangent_all, gate_all, w_up, down_weight, cotangent_own, gain,
-    middle, middle_grad, branch, sums, activated_out, both_sum, down_in, up_all, down_all,
+    middle, middle_grad, branch, sums, activated_out, both_sum, down_out, up_all, down_all,
     hidden_all, both_grad, part, from_side, from_corner, from_near, send_r, recv_r,
     send_m, recv_m, send_a, recv_a, cot_shard, cot_tile, stage_both, down_sum, w_both, w_down,
-    cotangent, activated, load_sem, local, send_z, recv_z, stage_down,
+    cotangent, activated, load_sem, local,
     up_own, down_own, send_u, recv_u, send_d, recv_d, first_sem,
 ):
     groups, rows, width = hidden_all.shape
@@ -1800,13 +1835,7 @@
         ).astype(BF16)
         return carry
 
-    z = lax.axis_index("mp")
-
-    def down_rows(owner):
-        return down_sum.at[pl.ds(pl.multiple_of(owner * LANES, LANES), LANES)]
-
-    keep_down = pltpu.make_async_copy(down_rows(z), down_in.at[z], local.at[5])
-    passing = Units(down_rows, down_in, stage_down, send_z, recv_z, local.at[pl.ds(6, 1)])
+    store_down = pltpu.make_async_copy(down_sum, down_out, local.at[5])
 
     def weight_tile(t, carry):
         columns = pl.ds(pl.multiple_of(t * 256, 256), 256)
@@ -1831,11 +1860,9 @@
     reduce.corners[0].start()
     reduce.corners[1].start()
     lax.fori_loop(0, tiles, down_tile, 0)
-    keep_down.start()
-    passing.start()
+    store_down.start()
     lax.fori_loop(0, 2, weight_tile, 0)
     reduce.middle()
-    passing.add()
     lax.fori_loop(2, tiles, weight_tile, 0)
     reduce.end()
     store_middle.wait()
@@ -1853,9 +1880,8 @@
     reduce.finish()
     for t in (tiles - 2, tiles - 1):
         store_both(t).wait()
-    keep_down.wait()
+    store_down.wait()
     store_activated.wait()
-    passing.finish()
 
 
 def feed(mixed, w_out, tokens, cotangent_all, gate_all, w_up, w_down, cotangent, gain):
@@ -1872,7 +1898,7 @@
             jax.ShapeDtypeStruct((8, width), F32),
             jax.ShapeDtypeStruct((groups, rows, units), BF16),
             jax.ShapeDtypeStruct((members, width, 256), BF16),
-            jax.ShapeDtypeStruct((members, LANES, width), BF16),
+            jax.ShapeDtypeStruct((units, width), BF16),
             jax.ShapeDtypeStruct((members, width, LANES), BF16),
             jax.ShapeDtypeStruct((members, LANES, width), BF16),
         ),
@@ -1897,10 +1923,7 @@
             pltpu.VMEM((rows, width), BF16),
             pltpu.VMEM((groups, rows, units), BF16),
             dma((6 + 4 * members,)),
-            dma((7,)),
             dma((6,)),
-            dma((10,)),
-            pltpu.VMEM((2, LANES, width), BF16),
             pltpu.VMEM((width, LANES), BF16),
             pltpu.VMEM((LANES, width), BF16),
             dma((4,)),
@@ -1916,13 +1939,13 @@
 
 
 def input_kernel(
-    qkv_grad, w_qkv, hidden_all, branch_all, mixed_in, tokens_in, middle_in, gain, sums_two,
+    qkv_in, w_in, hidden_all, branch_all, mixed_in, tokens_in, middle_in, gain, sums_two,
     both_sum, both_in,
     result, gains, both_all, heads_all,
     part, from_side, from_corner, from_near, send, recv, sums,
     stage, arrive, send_h, recv_s, recv_h, own, plane_sums, column_sums, send_p, recv_p,
     weight_sum, row_tile, tile_sem, send_b, recv_b, send_t, recv_t, both_found, heads_own, local,
-    mixed, tokens, middle_grad, fetch_sem,
+    mixed, tokens, middle_grad, fetch_sem, qkv_grad, w_qkv,
 ):
     me, z = lax.axis_index("dp"), lax.axis_index("mp")
     barrier = greet_all()
@@ -1959,7 +1982,13 @@
         [
             pltpu.make_async_copy(source, target, fetch_sem.at[number])
             for number, (source, target) in enumerate(
-                ((mixed_in, mixed), (tokens_in, tokens), (middle_in, middle_grad))
+                (
+                    (qkv_in, qkv_grad),
+                    (w_in, w_qkv),
+                    (mixed_in, mixed),
+                    (tokens_in, tokens),
+                    (middle_in, middle_grad),
+                )
             )
         ]
     )
@@ -2004,9 +2033,10 @@
 
     each_chunk(both_found.shape[1], add)
     both.start()
+    wait_all(fetches[:2])
     lax.fori_loop(0, tiles, weight_tile, 0)
     heads.start((0, 1, 2))
-    wait_all(fetches)
+    wait_all(fetches[2:])
     lax.fori_loop(tiles, 2 * tiles, weight_tile, 0)
     heads.start((3,))
     both.pass_on()
@@ -2081,7 +2111,7 @@
             shape((groups, width, 256), BF16),
             shape((groups, 4 * HEAD_DIM, width // 2), BF16),
         ),
-        in_specs=[on_chip()] * 2 + [anywhere()] * 5 + [on_chip()] * 2 + [anywhere()] * 2,
+        in_specs=[anywhere()] * 7 + [on_chip()] * 2 + [anywhere()] * 2,
         out_specs=(on_chip(),) * 2 + (anywhere(),) * 2,
         scratch_shapes=reduce_scratch(rows, width)
         + [
@@ -2109,7 +2139,9 @@
             pltpu.VMEM(mixed.shape, BF16),
             pltpu.VMEM((rows, width), BF16),
             pltpu.VMEM((rows, width), F32),
-            dma((3,)),
+            dma((5,)),
+            pltpu.VMEM(qkv_grad.shape, BF16),
+            pltpu.VMEM(w_qkv.shape, BF16),
         ],
         compiler_params=remote_params(6, 63 * 1024 * 1024),
         cost_estimate=pl.CostEstimate(flops=0, bytes_accessed=250_000_000, transcendentals=0),
@@ -2235,7 +2267,7 @@
         scale,
     )
     mixed = mixed.reshape(count, 2 * LANES)
-    middle, middle_grad, branch, sums_two, activated, both_sum, down_in, _, down_all = feed(
+    middle, middle_grad, branch, sums_two, activated, both_sum, down_sum, _, down_all = feed(
         mixed.reshape(groups, rows, 2 * LANES),
         w_proj,
         tokens_b,
@@ -2255,7 +2287,7 @@
         down_all.reshape(members * units, width),
         middle,
         both_sum,
-        down_in,
+        down_sum,
         scale,
     )
     qkv_grad = qkv_grad.reshape(count, 6 * LANES)

time: 557 us -> 543 us (0.975)
  Pallas kernels: 548 us -> 534 us
    pallas_call x1, Pallas kernels: 176 us -> 169 us  [feed(): pl.pallas_call(feed_kernel, out_shape=(jax.ShapeDtypeStruct((rows, width)...]
where the time goes in v12:
time: 543 us; the launch traced here: 542 us
  Pallas kernels  534 us (98%)
    pallas_call x1, Pallas kernels, feed(): pl.pallas_call(feed_kernel, out_shape=(jax.ShapeDtypeStruct((rows, width)...  169 us
    pallas_call x1, Pallas kernels, attend_back(): pl.pallas_call(functools.partial(backward_kernel, scale=scale, groups=gro...  118 us
    pallas_call x1, Pallas kernels, project_input(): pl.pallas_call(input_kernel, out_shape=(shape((rows, width), BF16), shape...  117 us
    pallas_call x1, Pallas kernels, attend_ahead(): pl.pallas_call(functools.partial(forward_kernel, scale=scale), out_shape=...  110 us
    pallas_call x1, Pallas kernels, assemble(): pl.pallas_call(assemble_kernel, grid=(groups,), out_shape=(shape((rows, w...  21.1 us

profile of v12, /device:TPU:0, one launch (start us, length us, event | category | flops | bytes accessed | tf_op | source)
XLA Modules:
  0.0 542.2 jit_solution(10429782914668890900)
XLA Ops:
  0.6 0.7 add_select_fusion
  1.3 0.2 convert_reduce_fusion
  1.6 0.2 select_reduce_fusion
  1.7 0.1 reshape.47
  1.8 0.1 copy.27
  1.9 0.8 pad_dynamic-slice_fusion
  2.7 1.3 fusion.1.notes
  4.0 0.6 broadcast_in_dim.20.order_row
  4.5 1.3 broadcast_in_dim.34.gain
  5.8 0.0 copy-start.1
  5.8 109.6 %attend_ahead.1 = (bf16[8,384,1792]{2,1,0:T(8,128)(2,1)}, bf16[768,1792]{1,0:T(8,128)(2,1)}, bf16[256,1792]{1,0:T(8,128)(2,1)}, f32[8,56,128]{2,1,0:T(8,128)}, b...) custom-call(bf16[384,1792]{1,0:T(8,128)(2,1)} %tokens.1, ...), custom_call_target="tpu_custom_call" | custom-call | bytes 300000000 | tf_op jit(solution)/shard_map/attend_ahead/pallas_call | solution.py:885
  115.4 0.0 copy-done.1
  115.4 0.6 broadcast_in_dim.37.gain
  116.0 168.7 %feed.1 = (f32[384,1792]{1,0:T(8,128)}, f32[384,1792]{1,0:T(8,128)}, bf16[384,1792]{1,0:T(8,128)(2,1)}, f32[8,1792]{1,0:T(8,128)}, bf16[8,384,512]{2,1,0:T(8,128...) custom-call(bf16[8,384,256]{2,1,0:T(8,128)(2,1)} %bitcast.16, ...), custom_call_target="tpu_custom_call" | custom-call | bytes 400000000 | tf_op jit(solution)/shard_map/feed/pallas_call | solution.py:1892
  284.8 118.1 %attend_back.1 = (bf16[8,8,48,768]{3,2,1,0:T(8,128)(2,1)}, bf16[384,1792]{1,0:T(8,128)(2,1)}, bf16[8,384,1792]{2,1,0:T(8,128)(2,1)}, bf16[4,1792,256]{2,1,0:T(8,128)(2,1)}, bf16[8,128,1792]{2,1,0:T(8,128)(2,1)}) custom-call(bf16[384,1792]{1,0:T(8,128)(2,1)} %get-tuple-element.53.branch, f32[8,56,128]{2,1,0:T(8,128)} %get-tuple-element.54.notes_all, ...), custom_call_target="tpu_custom_call" | custom-call | bytes 300000000 | tf_op jit(solution)/shard_map/attend_back/pallas_call | solution.py:1585
  402.9 116.8 %project_input.1 = (bf16[384,1792]{1,0:T(8,128)(2,1)}, f32[2,1792]{1,0:T(2,128)}, bf16[8,1792,256]{2,1,0:T(8,128)(2,1)}, bf16[8,448,896]{2,1,0:T(8,128)(2,1)}) custom-call(bf16[3072,768]{1,0:T(8,128)(2,1)} %bitcast.18, bf16[768,1792]{1,0:T(8,128)(2,1)} %get-tuple-element.62.w_in, bf16[8,384,1792]{2,1,0:T(8,128)(2,1)} %get-tuple-element.63.hidden_all, ...), custom_call_target="tpu_custom_call" | custom-call | bytes 250000000 | tf_op jit(solution)/shard_map/project_input/pallas_call | solution.py:2106
  519.7 0.8 broadcast_in_dim.39.order_column
  520.5 0.0 copy-start
  520.5 21.1 %assemble.1 = (bf16[384,1792]{1,0:T(8,128)(2,1)}, bf16[384,1792]{1,0:T(8,128)(2,1)}, f32[448,1792]{1,0:T(8,128)}, f32[448,1792]{1,0:T(8,128)}, f32[448,1792]{1,0...) custom-call(bf16[8,1792,256]{2,1,0:T(8,128)(2,1)} %get-tuple-element.68.bot, ...), custom_call_target="tpu_custom_call" | custom-call | bytes 58000000 | tf_op jit(solution)/shard_map/assemble/pallas_call | solution.py:2184
  541.6 0.0 copy-done
  541.6 0.6 slice_reduce_fusion
  (2 shorter events, 0.0 us)
Async XLA Ops:
  5.8 109.6 %copy-start.1 = (f32[1792]{0:T(1024)S(1)}, f32[1792]{0:T(1024)}, u32[]{:S(2)}) copy-start(f32[1792]{0:T(1024)} %param.20) | copy-start | bytes 21508
  520.5 21.1 %copy-start = (f32[2,1792]{1,0:T(2,128)S(1)}, f32[2,1792]{1,0:T(2,128)}, u32[]{:S(2)}) copy-start(f32[2,1792]{1,0:T(2,128)} %get-tuple-element.75) | copy-start | bytes 43012

commit v13 on v12

--- a/solution.py
+++ b/solution.py
@@ -847,10 +847,10 @@
         return carry
 
     spread.pass_on((3,))
-    lax.fori_loop(0, groups // 2, attend, 0)
+    lax.fori_loop(0, 2, attend, 0)
     second.pass_on()
     column.pass_on()
-    lax.fori_loop(groups // 2, groups, attend, 0)
+    lax.fori_loop(2, groups, attend, 0)
     spread.finish((3,))
     second.finish()
     column.finish()
@@ -1518,7 +1518,7 @@
         return carry
 
     wait_all(fetches[2:4])
-    lax.fori_loop(0, 3, attend, 0)
+    lax.fori_loop(0, 2, attend, 0)
     reduce.middle()
     load_down.wait()
     down_units.finish()
@@ -1534,9 +1534,8 @@
 
     each_chunk(down_found.shape[1], add_down)
     down.start()
-    lax.fori_loop(3, 7, attend, 0)
+    lax.fori_loop(2, groups, attend, 0)
     down.pass_on()
-    lax.fori_loop(7, groups, attend, 0)
 
     def restore(k, carry):
         @pl.when(z < members - 1)
@@ -1650,7 +1649,7 @@
     mixed, w_out, tokens, cotangent_all, gate_all, w_up, down_weight, cotangent_own, gain,
     middle, middle_grad, branch, sums, activated_out, both_sum, down_out, up_all, down_all,
     hidden_all, both_grad, part, from_side, from_corner, from_near, send_r, recv_r,
-    send_m, recv_m, send_a, recv_a, cot_shard, cot_tile, stage_both, down_sum, w_both, w_down,
+    send_m, recv_m, send_n, recv_n, send_a, recv_a, send_b, recv_b, cot_shard, cot_tile, stage_both, down_sum, w_both, w_down,
     cotangent, activated, load_sem, local,
     up_own, down_own, send_u, recv_u, send_d, recv_d, first_sem,
 ):
@@ -1702,26 +1701,43 @@
     columns_down = Column(down_own, down_all, send_d, recv_d, local.at[2])
     columns_up.start()
     columns_down.start()
-    project = Reduce(
-        lambda owner: activated[owner, :, 0:256], down_sum.at[pl.ds(0, 256)], False,
-        part, from_side, from_corner, from_near, send_m, recv_m,
-    )
-    project.begin()
-    project.middle()
+    half_rows = rows // 2
+
+    def half(number, sends, recvs):
+        span = pl.ds(number * half_rows, half_rows)
+        quarter = pl.ds(number * (half_rows // 2), half_rows // 2)
+        return Reduce(
+            lambda owner: activated[owner, span, 0:256], down_sum.at[pl.ds(0, 256)], False,
+            part.at[:, span], from_side.at[:, span], from_corner.at[:, quarter],
+            from_near.at[:, span], sends, recvs,
+        )
+
+    projects = (half(0, send_m, recv_m), half(1, send_n, recv_n))
+    gathers = [
+        Gather(None, hidden_all.at[:, pl.ds(number * half_rows, half_rows)], sends, recvs)
+        for number, (sends, recvs) in enumerate(((send_a, recv_a), (send_b, recv_b)))
+    ]
+    for project in projects:
+        project.begin()
+    for project in projects:
+        project.middle()
     columns_up.pass_on()
     columns_down.pass_on()
-    project.end()
-
-    def normalise(span):
-        values = cotangent[span, :].astype(F32) + project.rows_of(span)
-        middle_grad[span, :] = values
-        inverse = lax.rsqrt(mean_rows(values * values) + EPSILON)
-        hidden_all[me, span, :] = (values * inverse * gain[...]).astype(BF16)
-
-    each_chunk(rows, normalise)
-    project.finish()
-    gather = Gather(None, hidden_all, send_a, recv_a)
-    gather.start()
+    for number, project in enumerate(projects):
+        project.end()
+
+        def normalise(span):
+            own = pl.ds(pl.multiple_of(number * half_rows + span.start, CHUNK), CHUNK)
+            values = cotangent[own, :].astype(F32) + project.rows_of(span)
+            middle_grad[own, :] = values
+            inverse = lax.rsqrt(mean_rows(values * values) + EPSILON)
+            hidden_all[me, own, :] = (values * inverse * gain[...]).astype(BF16)
+
+        each_chunk(half_rows, normalise)
+        gathers[number].start()
+
+    for project in projects:
+        project.finish()
     store_middle = pltpu.make_async_copy(middle_grad, middle, local.at[1])
     load_own = pltpu.make_async_copy(cotangent_own, cotangent, local.at[3])
     store_middle.start()
@@ -1753,7 +1769,11 @@
         reduce.add_side(2)
         reduce.nears[2].start()
 
-    early = [(turn, functools.partial(gather.arrive, *numbers)) for turn, numbers in ARRIVALS]
+    early = [
+        (turn, functools.partial(gather.arrive, *numbers))
+        for turn, numbers in ARRIVALS
+        for gather in gathers
+    ]
     early += [(6, nears)]
     late = [(1, 3), (4, 1), (5, 2), (7, 0)]
     wait_all(gates + ups)
@@ -1876,7 +1896,8 @@
         branch[span, :] = total.astype(BF16)
 
     each_chunk(rows, body)
-    gather.sent()
+    for gather in gathers:
+        gather.sent()
     reduce.finish()
     for t in (tiles - 2, tiles - 1):
         store_both(t).wait()
@@ -1912,6 +1933,10 @@
         + [
             dma((10,)),
             dma((10,)),
+            dma((10,)),
+            dma((10,)),
+            dma((13,)),
+            dma((13,)),
             dma((13,)),
             dma((13,)),
             pltpu.VMEM((2, rows, width), BF16),

time: 543 us -> 537 us (0.989)
  Pallas kernels: 534 us -> 528 us
where the time goes in v13:
time: 537 us; the launch traced here: 536 us
  Pallas kernels  528 us (98%)
    pallas_call x1, Pallas kernels, feed(): pl.pallas_call(feed_kernel, out_shape=(jax.ShapeDtypeStruct((rows, width)...  165 us
    pallas_call x1, Pallas kernels, attend_back(): pl.pallas_call(functools.partial(backward_kernel, scale=scale, groups=gro...  117 us
    pallas_call x1, Pallas kernels, project_input(): pl.pallas_call(input_kernel, out_shape=(shape((rows, width), BF16), shape...  117 us
    pallas_call x1, Pallas kernels, attend_ahead(): pl.pallas_call(functools.partial(forward_kernel, scale=scale), out_shape=...  108 us
    pallas_call x1, Pallas kernels, assemble(): pl.pallas_call(assemble_kernel, grid=(groups,), out_shape=(shape((rows, w...  21.1 us

profile of v13, /device:TPU:0, one launch (start us, length us, event | category | flops | bytes accessed | tf_op | source)
XLA Modules:
  0.0 536.3 jit_solution(8218868650737330887)
XLA Ops:
  0.6 0.7 add_select_fusion
  1.3 0.2 convert_reduce_fusion
  1.6 0.2 select_reduce_fusion
  1.7 0.1 reshape.47
  1.8 0.1 copy.27
  1.9 0.8 pad_dynamic-slice_fusion
  2.7 1.3 fusion.1.notes
  4.0 0.6 broadcast_in_dim.20.order_row
  4.5 1.3 broadcast_in_dim.34.gain
  5.8 0.0 copy-start.1
  5.8 107.5 %attend_ahead.1 = (bf16[8,384,1792]{2,1,0:T(8,128)(2,1)}, bf16[768,1792]{1,0:T(8,128)(2,1)}, bf16[256,1792]{1,0:T(8,128)(2,1)}, f32[8,56,128]{2,1,0:T(8,128)}, b...) custom-call(bf16[384,1792]{1,0:T(8,128)(2,1)} %tokens.1, ...), custom_call_target="tpu_custom_call" | custom-call | bytes 300000000 | tf_op jit(solution)/shard_map/attend_ahead/pallas_call | solution.py:885
  113.4 0.0 copy-done.1
  113.4 0.6 broadcast_in_dim.37.gain
  114.0 165.4 %feed.1 = (f32[384,1792]{1,0:T(8,128)}, f32[384,1792]{1,0:T(8,128)}, bf16[384,1792]{1,0:T(8,128)(2,1)}, f32[8,1792]{1,0:T(8,128)}, bf16[8,384,512]{2,1,0:T(8,128...) custom-call(bf16[8,384,256]{2,1,0:T(8,128)(2,1)} %bitcast.16, ...), custom_call_target="tpu_custom_call" | custom-call | bytes 400000000 | tf_op jit(solution)/shard_map/feed/pallas_call | solution.py:1913
  279.4 117.3 %attend_back.1 = (bf16[8,8,48,768]{3,2,1,0:T(8,128)(2,1)}, bf16[384,1792]{1,0:T(8,128)(2,1)}, bf16[8,384,1792]{2,1,0:T(8,128)(2,1)}, bf16[4,1792,256]{2,1,0:T(8,128)(2,1)}, bf16[8,128,1792]{2,1,0:T(8,128)(2,1)}) custom-call(bf16[384,1792]{1,0:T(8,128)(2,1)} %get-tuple-element.53.branch, f32[8,56,128]{2,1,0:T(8,128)} %get-tuple-element.54.notes_all, ...), custom_call_target="tpu_custom_call" | custom-call | bytes 300000000 | tf_op jit(solution)/shard_map/attend_back/pallas_call | solution.py:1584
  396.7 117.1 %project_input.1 = (bf16[384,1792]{1,0:T(8,128)(2,1)}, f32[2,1792]{1,0:T(2,128)}, bf16[8,1792,256]{2,1,0:T(8,128)(2,1)}, bf16[8,448,896]{2,1,0:T(8,128)(2,1)}) custom-call(bf16[3072,768]{1,0:T(8,128)(2,1)} %bitcast.18, bf16[768,1792]{1,0:T(8,128)(2,1)} %get-tuple-element.62.w_in, bf16[8,384,1792]{2,1,0:T(8,128)(2,1)} %get-tuple-element.63.hidden_all, ...), custom_call_target="tpu_custom_call" | custom-call | bytes 250000000 | tf_op jit(solution)/shard_map/project_input/pallas_call | solution.py:2131
  513.7 0.8 broadcast_in_dim.39.order_column
  514.5 0.0 copy-start
  514.5 21.1 %assemble.1 = (bf16[384,1792]{1,0:T(8,128)(2,1)}, bf16[384,1792]{1,0:T(8,128)(2,1)}, f32[448,1792]{1,0:T(8,128)}, f32[448,1792]{1,0:T(8,128)}, f32[448,1792]{1,0...) custom-call(bf16[8,1792,256]{2,1,0:T(8,128)(2,1)} %get-tuple-element.68.bot, ...), custom_call_target="tpu_custom_call" | custom-call | bytes 58000000 | tf_op jit(solution)/shard_map/assemble/pallas_call | solution.py:2209
  535.6 0.0 copy-done
  535.6 0.6 slice_reduce_fusion
  (2 shorter events, 0.0 us)
Async XLA Ops:
  5.8 107.6 %copy-start.1 = (f32[1792]{0:T(1024)S(1)}, f32[1792]{0:T(1024)}, u32[]{:S(2)}) copy-start(f32[1792]{0:T(1024)} %param.20) | copy-start | bytes 21508
  514.5 21.1 %copy-start = (f32[2,1792]{1,0:T(2,128)S(1)}, f32[2,1792]{1,0:T(2,128)}, u32[]{:S(2)}) copy-start(f32[2,1792]{1,0:T(2,128)} %get-tuple-element.75) | copy-start | bytes 43012

commit v14 on v13

--- a/solution.py
+++ b/solution.py
@@ -724,7 +724,7 @@
     def normalise(span):
         value = tokens_b[span, :].astype(F32)
         inverse = lax.rsqrt(mean_rows(value * value) + EPSILON)
-        hidden_all[me, span, :] = (value * inverse * gain[...]).astype(BF16)
+        hidden_all[me, span, :] = (value * inverse * gain[...].reshape(1, -1)).astype(BF16)
 
     each_chunk(rows, normalise)
     notes_all[me] = notes[...]
@@ -1731,7 +1731,7 @@
             values = cotangent[own, :].astype(F32) + project.rows_of(span)
             middle_grad[own, :] = values
             inverse = lax.rsqrt(mean_rows(values * values) + EPSILON)
-            hidden_all[me, own, :] = (values * inverse * gain[...]).astype(BF16)
+            hidden_all[me, own, :] = (values * inverse * gain[...].reshape(1, -1)).astype(BF16)
 
         each_chunk(half_rows, normalise)
         gathers[number].start()
@@ -1890,7 +1890,7 @@
     sums[...] = jnp.zeros_like(sums)
 
     def body(span):
-        change = norm_back_rows(reduce.rows_of(span), middle_grad[span, :], gain[...], sums, span)
+        change = norm_back_rows(reduce.rows_of(span), middle_grad[span, :], gain[...].reshape(1, -1), sums, span)
         total = cotangent[span, :].astype(F32) + change
         middle_grad[span, :] = total
         branch[span, :] = total.astype(BF16)
@@ -2074,7 +2074,7 @@
 
     def body(span):
         values = tokens[span, :].astype(F32)
-        change = norm_back_rows(reduce.rows_of(span), values, gain[...], sums, span)
+        change = norm_back_rows(reduce.rows_of(span), values, gain[...].reshape(1, -1), sums, span)
         result[span, :] = (middle_grad[span, :] + change).astype(BF16)
 
     each_chunk(result.shape[0], body)
@@ -2178,8 +2178,8 @@
 
 
 def assemble_kernel(
-    both, down, heads, order_column, output_b, input_b,
-    output, inputs, query, keys, values, project, gate, upward, down_out,
+    both, down, heads, order_row, output_b, input_b,
+    output, inputs, query, keys, values, project, gate, upward, down_out, *, tiles,
 ):
     for d in range(both.shape[0]):
         gate[:, d * 128 : d * 128 + 128] = both[d, :, :128].astype(F32)
@@ -2187,27 +2187,33 @@
     down_out[...] = down[0].astype(F32)
     for kind, out in enumerate((query, keys, values, project)):
         out[...] = heads[0, kind].astype(F32)
-    place = lax.broadcasted_iota(jnp.int32, (order_column.shape[0], output_b.shape[0]), 1)
-    unsort = (place.astype(F32) == order_column[...]).astype(BF16)
-    output[...] = jnp.dot(unsort, output_b[...], preferred_element_type=F32).astype(BF16)
-    inputs[...] = jnp.dot(unsort, input_b[...], preferred_element_type=F32).astype(BF16)
-
-
-def assemble(both, down, heads, order_column, output_b, input_b):
+    rows = output_b.shape[0]
+
+    @pl.when(pl.program_id(0) < tiles)
+    def _():
+        place = lax.broadcasted_iota(jnp.int32, (rows, rows), 0).astype(F32)
+        sort = (place == order_row[...]).astype(BF16)
+        for ordered, out in ((output_b, output), (input_b, inputs)):
+            out[...] = lax.dot_general(
+                sort, ordered[...], TN, preferred_element_type=F32
+            ).astype(BF16)
+
+
+def assemble(both, down, heads, order_row, output_b, input_b):
     groups, width, wide = both.shape
     rows = output_b.shape[0]
     units = down.shape[1]
     chips = groups // 2
     columns = heads.shape[3]
-    row_tile, tile = rows // groups, width // groups
+    tile = width // groups
     shape = jax.ShapeDtypeStruct
     head = shape((chips * HEAD_DIM, 2 * columns), F32)
     head_spec = pl.BlockSpec((HEAD_DIM, columns), lambda i: (i // 2, i % 2))
     wide_spec = pl.BlockSpec((tile, groups * units), lambda i: (i, 0))
-    row_spec = pl.BlockSpec((row_tile, width), lambda i: (i, 0))
-    whole_spec = pl.BlockSpec((rows, width), lambda i: (0, 0))
+    tiles = width // 256
+    row_spec = pl.BlockSpec((rows, 256), lambda i: (0, jnp.minimum(i, tiles - 1)))
     return pl.pallas_call(
-        assemble_kernel,
+        functools.partial(assemble_kernel, tiles=tiles),
         grid=(groups,),
         out_shape=(
             shape((rows, width), BF16),
@@ -2224,9 +2230,9 @@
             pl.BlockSpec((groups, tile, wide), lambda i: (0, i, 0)),
             pl.BlockSpec((1, units, width), lambda i: (i, 0, 0)),
             pl.BlockSpec((1, 4, HEAD_DIM, columns), lambda i: (i, 0, 0, 0)),
-            pl.BlockSpec((row_tile, 1), lambda i: (i, 0)),
-            whole_spec,
-            whole_spec,
+            pl.BlockSpec((1, rows), lambda i: (0, 0)),
+            row_spec,
+            row_spec,
         ],
         out_specs=(
             row_spec, row_spec, head_spec, head_spec, head_spec, head_spec, wide_spec, wide_spec,
@@ -2235,7 +2241,7 @@
         compiler_params=pltpu.CompilerParams(vmem_limit_bytes=VMEM_LIMIT),
         cost_estimate=pl.CostEstimate(flops=0, bytes_accessed=58_000_000, transcendentals=0),
         name="assemble",
-    )(both, down, heads, order_column, output_b, input_b)
+    )(both, down, heads, order_row, output_b, input_b)
 
 
 def swapped(
@@ -2267,6 +2273,7 @@
 
     count = groups * rows
     scale = HEAD_DIM ** (-0.5)
+    order_row = send_at.astype(F32)[None]
     (
         hidden_one,
         w_qkv,
@@ -2281,8 +2288,8 @@
     ) = attend_ahead(
         tokens,
         cotangent,
-        send_at.astype(F32)[None],
-        norm1_gain[None],
+        order_row,
+        norm1_gain,
         notes,
         w_query.T,
         w_key.T,
@@ -2301,7 +2308,7 @@
         w_up,
         w_down,
         cotangent_b,
-        norm2_gain[None],
+        norm2_gain,
     )
     qkv_grad, output_rows, branch_all, both_in, down_whole = attend_back(
         branch,
@@ -2324,7 +2331,7 @@
         mixed,
         tokens_b,
         middle_grad,
-        norm1_gain[None],
+        norm1_gain,
         sums_two,
         both_sum,
         both_in,
@@ -2343,7 +2350,7 @@
         both_whole,
         down_whole,
         heads_whole.reshape(groups, 4, HEAD_DIM, width // 2),
-        send_at.astype(F32)[:, None],
+        order_row,
         output_rows,
         input_rows,
     )

time: 537 us -> 536 us (level)
  no operation moved by 1% of the time
where the time goes in v14:
time: 536 us; the launch traced here: 534 us
  Pallas kernels  528 us (99%)
    pallas_call x1, Pallas kernels, feed(): pl.pallas_call(feed_kernel, out_shape=(jax.ShapeDtypeStruct((rows, width)...  166 us
    pallas_call x1, Pallas kernels, project_input(): pl.pallas_call(input_kernel, out_shape=(shape((rows, width), BF16), shape...  117 us
    pallas_call x1, Pallas kernels, attend_back(): pl.pallas_call(functools.partial(backward_kernel, scale=scale, groups=gro...  117 us
    pallas_call x1, Pallas kernels, attend_ahead(): pl.pallas_call(functools.partial(forward_kernel, scale=scale), out_shape=...  108 us
    pallas_call x1, Pallas kernels, assemble(): pl.pallas_call(functools.partial(assemble_kernel, tiles=tiles), grid=(gro...  21 us

profile of v14, /device:TPU:0, one launch (start us, length us, event | category | flops | bytes accessed | tf_op | source)
XLA Modules:
  0.0 534.5 jit_solution(2996255121208117387)
XLA Ops:
  0.6 0.8 pad_dynamic-slice_fusion
  1.4 0.7 add_select_fusion
  2.1 0.2 convert_reduce_fusion
  2.4 0.6 broadcast_in_dim.10.order_row
  3.0 0.1 select_reduce_fusion
  3.1 0.1 reshape.47
  3.2 0.1 copy.26
  3.3 1.3 fusion.1.notes
  4.6 107.5 %attend_ahead.1 = (bf16[8,384,1792]{2,1,0:T(8,128)(2,1)}, bf16[768,1792]{1,0:T(8,128)(2,1)}, bf16[256,1792]{1,0:T(8,128)(2,1)}, f32[8,56,128]{2,1,0:T(8,128)}, b...) custom-call(bf16[384,1792]{1,0:T(8,128)(2,1)} %tokens.1, ...), custom_call_target="tpu_custom_call" | custom-call | bytes 300000000 | tf_op jit(solution)/shard_map/attend_ahead/pallas_call | solution.py:885
  112.1 165.6 %feed.1 = (f32[384,1792]{1,0:T(8,128)}, f32[384,1792]{1,0:T(8,128)}, bf16[384,1792]{1,0:T(8,128)(2,1)}, f32[8,1792]{1,0:T(8,128)}, bf16[8,384,512]{2,1,0:T(8,128...) custom-call(bf16[8,384,256]{2,1,0:T(8,128)(2,1)} %bitcast.16, ...), custom_call_target="tpu_custom_call" | custom-call | bytes 400000000 | tf_op jit(solution)/shard_map/feed/pallas_call | solution.py:1913
  277.7 117.1 %attend_back.1 = (bf16[8,8,48,768]{3,2,1,0:T(8,128)(2,1)}, bf16[384,1792]{1,0:T(8,128)(2,1)}, bf16[8,384,1792]{2,1,0:T(8,128)(2,1)}, bf16[4,1792,256]{2,1,0:T(8,128)(2,1)}, bf16[8,128,1792]{2,1,0:T(8,128)(2,1)}) custom-call(bf16[384,1792]{1,0:T(8,128)(2,1)} %get-tuple-element.53.branch, f32[8,56,128]{2,1,0:T(8,128)} %get-tuple-element.54.notes_all, ...), custom_call_target="tpu_custom_call" | custom-call | bytes 300000000 | tf_op jit(solution)/shard_map/attend_back/pallas_call | solution.py:1584
  394.8 117.1 %project_input.1 = (bf16[384,1792]{1,0:T(8,128)(2,1)}, f32[2,1792]{1,0:T(2,128)}, bf16[8,1792,256]{2,1,0:T(8,128)(2,1)}, bf16[8,448,896]{2,1,0:T(8,128)(2,1)}) custom-call(bf16[3072,768]{1,0:T(8,128)(2,1)} %bitcast.18, bf16[768,1792]{1,0:T(8,128)(2,1)} %get-tuple-element.62.w_in, bf16[8,384,1792]{2,1,0:T(8,128)(2,1)} %get-tuple-element.63.hidden_all, ...), custom_call_target="tpu_custom_call" | custom-call | bytes 250000000 | tf_op jit(solution)/shard_map/project_input/pallas_call | solution.py:2131
  511.9 1.4 slice_reduce_fusion
  513.3 21.0 %assemble.1 = (bf16[384,1792]{1,0:T(8,128)(2,1)}, bf16[384,1792]{1,0:T(8,128)(2,1)}, f32[448,1792]{1,0:T(8,128)}, f32[448,1792]{1,0:T(8,128)}, f32[448,1792]{1,0...) custom-call(bf16[8,1792,256]{2,1,0:T(8,128)(2,1)} %get-tuple-element.68.bot, ...), custom_call_target="tpu_custom_call" | custom-call | bytes 58000000 | tf_op jit(solution)/shard_map/assemble/pallas_call | solution.py:2215
  (2 shorter events, 0.0 us)

commit v15 on v14

--- a/solution.py
+++ b/solution.py
@@ -718,7 +718,7 @@
         w_out[block * LANES + HEAD_DIM : block * LANES + LANES, :] = none
 
     place = lax.broadcasted_iota(jnp.int32, (rows, rows), 0).astype(F32)
-    sort = (place == order_row[...]).astype(BF16)
+    sort = (place == order_row[...].reshape(1, -1)).astype(BF16)
     tokens_b[...] = jnp.dot(sort, tokens[...], preferred_element_type=F32).astype(BF16)
 
     def normalise(span):
@@ -2178,8 +2178,8 @@
 
 
 def assemble_kernel(
-    both, down, heads, order_row, output_b, input_b,
-    output, inputs, query, keys, values, project, gate, upward, down_out, *, tiles,
+    both, down, heads, order_row, output_b, input_b, gains,
+    gain_one, gain_two, output, inputs, query, keys, values, project, gate, upward, down_out, *, tiles,
 ):
     for d in range(both.shape[0]):
         gate[:, d * 128 : d * 128 + 128] = both[d, :, :128].astype(F32)
@@ -2188,18 +2188,20 @@
     for kind, out in enumerate((query, keys, values, project)):
         out[...] = heads[0, kind].astype(F32)
     rows = output_b.shape[0]
+    gain_one[...] = gains[0:1, :].reshape(-1)
+    gain_two[...] = gains[1:2, :].reshape(-1)
 
     @pl.when(pl.program_id(0) < tiles)
     def _():
         place = lax.broadcasted_iota(jnp.int32, (rows, rows), 0).astype(F32)
-        sort = (place == order_row[...]).astype(BF16)
+        sort = (place == order_row[...].reshape(1, -1)).astype(BF16)
         for ordered, out in ((output_b, output), (input_b, inputs)):
             out[...] = lax.dot_general(
                 sort, ordered[...], TN, preferred_element_type=F32
             ).astype(BF16)
 
 
-def assemble(both, down, heads, order_row, output_b, input_b):
+def assemble(both, down, heads, order_row, output_b, input_b, gains):
     groups, width, wide = both.shape
     rows = output_b.shape[0]
     units = down.shape[1]
@@ -2216,6 +2218,8 @@
         functools.partial(assemble_kernel, tiles=tiles),
         grid=(groups,),
         out_shape=(
+            shape((width,), F32),
+            shape((width,), F32),
             shape((rows, width), BF16),
             shape((rows, width), BF16),
             head,
@@ -2230,18 +2234,21 @@
             pl.BlockSpec((groups, tile, wide), lambda i: (0, i, 0)),
             pl.BlockSpec((1, units, width), lambda i: (i, 0, 0)),
             pl.BlockSpec((1, 4, HEAD_DIM, columns), lambda i: (i, 0, 0, 0)),
-            pl.BlockSpec((1, rows), lambda i: (0, 0)),
+            pl.BlockSpec((rows,), lambda i: (0,)),
             row_spec,
             row_spec,
+            pl.BlockSpec((2, width), lambda i: (0, 0)),
         ],
         out_specs=(
+            pl.BlockSpec((width,), lambda i: (0,)),
+            pl.BlockSpec((width,), lambda i: (0,)),
             row_spec, row_spec, head_spec, head_spec, head_spec, head_spec, wide_spec, wide_spec,
             pl.BlockSpec((units, width), lambda i: (i, 0)),
         ),
         compiler_params=pltpu.CompilerParams(vmem_limit_bytes=VMEM_LIMIT),
         cost_estimate=pl.CostEstimate(flops=0, bytes_accessed=58_000_000, transcendentals=0),
         name="assemble",
-    )(both, down, heads, order_row, output_b, input_b)
+    )(both, down, heads, order_row, output_b, input_b, gains)
 
 
 def swapped(
@@ -2273,7 +2280,7 @@
 
     count = groups * rows
     scale = HEAD_DIM ** (-0.5)
-    order_row = send_at.astype(F32)[None]
+    order_row = send_at.astype(F32)
     (
         hidden_one,
         w_qkv,
@@ -2337,6 +2344,8 @@
         both_in,
     )
     (
+        gain_one_grad,
+        gain_two_grad,
         output,
         input_grad,
         query_grad,
@@ -2353,12 +2362,13 @@
         order_row,
         output_rows,
         input_rows,
+        gain_sums,
     )
     return (
         output,
         input_grad,
-        gain_sums[0],
-        gain_sums[1],
+        gain_one_grad,
+        gain_two_grad,
         query_grad.T,
         key_grad.T,
         value_grad.T,

time: 536 us -> 534 us (level)
  no operation moved by 1% of the time
where the time goes in v15:
time: 534 us; the launch traced here: 533 us
  Pallas kernels  528 us (99%)
    pallas_call x1, Pallas kernels, feed(): pl.pallas_call(feed_kernel, out_shape=(jax.ShapeDtypeStruct((rows, width)...  165 us
    pallas_call x1, Pallas kernels, attend_back(): pl.pallas_call(functools.partial(backward_kernel, scale=scale, groups=gro...  117 us
    pallas_call x1, Pallas kernels, project_input(): pl.pallas_call(input_kernel, out_shape=(shape((rows, width), BF16), shape...  117 us
    pallas_call x1, Pallas kernels, attend_ahead(): pl.pallas_call(functools.partial(forward_kernel, scale=scale), out_shape=...  108 us
    pallas_call x1, Pallas kernels, assemble(): pl.pallas_call(functools.partial(assemble_kernel, tiles=tiles), grid=(gro...  20.7 us

profile of v15, /device:TPU:0, one launch (start us, length us, event | category | flops | bytes accessed | tf_op | source)
XLA Modules:
  0.0 532.8 jit_solution(18096978653895655971)
XLA Ops:
  0.6 0.8 pad_dynamic-slice_fusion
  1.4 0.7 add_select_fusion
  2.1 0.2 convert_reduce_fusion
  2.4 0.6 fusion.3
  2.9 0.1 select_reduce_fusion
  3.1 0.1 reshape.47
  3.2 0.1 copy.26
  3.3 1.3 fusion.1.notes
  4.5 107.5 %attend_ahead.1 = (bf16[8,384,1792]{2,1,0:T(8,128)(2,1)}, bf16[768,1792]{1,0:T(8,128)(2,1)}, bf16[256,1792]{1,0:T(8,128)(2,1)}, f32[8,56,128]{2,1,0:T(8,128)}, b...) custom-call(bf16[384,1792]{1,0:T(8,128)(2,1)} %tokens.1, ...), custom_call_target="tpu_custom_call" | custom-call | bytes 300000000 | tf_op jit(solution)/shard_map/attend_ahead/pallas_call | solution.py:885
  112.1 165.3 %feed.1 = (f32[384,1792]{1,0:T(8,128)}, f32[384,1792]{1,0:T(8,128)}, bf16[384,1792]{1,0:T(8,128)(2,1)}, f32[8,1792]{1,0:T(8,128)}, bf16[8,384,512]{2,1,0:T(8,128...) custom-call(bf16[8,384,256]{2,1,0:T(8,128)(2,1)} %bitcast.16, ...), custom_call_target="tpu_custom_call" | custom-call | bytes 400000000 | tf_op jit(solution)/shard_map/feed/pallas_call | solution.py:1913
  277.4 117.4 %attend_back.1 = (bf16[8,8,48,768]{3,2,1,0:T(8,128)(2,1)}, bf16[384,1792]{1,0:T(8,128)(2,1)}, bf16[8,384,1792]{2,1,0:T(8,128)(2,1)}, bf16[4,1792,256]{2,1,0:T(8,128)(2,1)}, bf16[8,128,1792]{2,1,0:T(8,128)(2,1)}) custom-call(bf16[384,1792]{1,0:T(8,128)(2,1)} %get-tuple-element.55.branch, f32[8,56,128]{2,1,0:T(8,128)} %get-tuple-element.56.notes_all, ...), custom_call_target="tpu_custom_call" | custom-call | bytes 300000000 | tf_op jit(solution)/shard_map/attend_back/pallas_call | solution.py:1584
  394.8 117.1 %project_input.1 = (bf16[384,1792]{1,0:T(8,128)(2,1)}, f32[2,1792]{1,0:T(2,128)}, bf16[8,1792,256]{2,1,0:T(8,128)(2,1)}, bf16[8,448,896]{2,1,0:T(8,128)(2,1)}) custom-call(bf16[3072,768]{1,0:T(8,128)(2,1)} %bitcast.18, bf16[768,1792]{1,0:T(8,128)(2,1)} %get-tuple-element.64.w_in, bf16[8,384,1792]{2,1,0:T(8,128)(2,1)} %get-tuple-element.65.hidden_all, ...), custom_call_target="tpu_custom_call" | custom-call | bytes 250000000 | tf_op jit(solution)/shard_map/project_input/pallas_call | solution.py:2131
  511.9 20.7 %assemble.1 = (f32[1792]{0:T(1024)}, f32[1792]{0:T(1024)}, bf16[384,1792]{1,0:T(8,128)(2,1)}, bf16[384,1792]{1,0:T(8,128)(2,1)}, f32[448,1792]{1,0:T(8,128)}, /*...) custom-call(bf16[8,1792,256]{2,1,0:T(8,128)(2,1)} %get-tuple-element, ...), custom_call_target="tpu_custom_call" | custom-call | bytes 58000000 | tf_op jit(solution)/shard_map/assemble/pallas_call | solution.py:2217
  (1 shorter events, 0.0 us)

commit v16 on v15

--- a/solution.py
+++ b/solution.py
@@ -1518,7 +1518,7 @@
         return carry
 
     wait_all(fetches[2:4])
-    lax.fori_loop(0, 2, attend, 0)
+    lax.fori_loop(0, 3, attend, 0)
     reduce.middle()
     load_down.wait()
     down_units.finish()
@@ -1534,7 +1534,7 @@
 
     each_chunk(down_found.shape[1], add_down)
     down.start()
-    lax.fori_loop(2, groups, attend, 0)
+    lax.fori_loop(3, groups, attend, 0)
     down.pass_on()
 
     def restore(k, carry):

time: 534 us -> 534 us (level)
  no operation moved by 1% of the time
where the time goes in v16:
time: 534 us; the launch traced here: 533 us
  Pallas kernels  528 us (99%)
    pallas_call x1, Pallas kernels, feed(): pl.pallas_call(feed_kernel, out_shape=(jax.ShapeDtypeStruct((rows, width)...  165 us
    pallas_call x1, Pallas kernels, attend_back(): pl.pallas_call(functools.partial(backward_kernel, scale=scale, groups=gro...  117 us
    pallas_call x1, Pallas kernels, project_input(): pl.pallas_call(input_kernel, out_shape=(shape((rows, width), BF16), shape...  117 us
    pallas_call x1, Pallas kernels, attend_ahead(): pl.pallas_call(functools.partial(forward_kernel, scale=scale), out_shape=...  108 us
    pallas_call x1, Pallas kernels, assemble(): pl.pallas_call(functools.partial(assemble_kernel, tiles=tiles), grid=(gro...  20.7 us

profile of v16, /device:TPU:0, one launch (start us, length us, event | category | flops | bytes accessed | tf_op | source)
XLA Modules:
  0.0 532.8 jit_solution(14552323360944464344)
XLA Ops:
  0.6 0.8 pad_dynamic-slice_fusion
  1.4 0.7 add_select_fusion
  2.1 0.2 convert_reduce_fusion
  2.4 0.6 fusion.3
  2.9 0.1 select_reduce_fusion
  3.1 0.1 reshape.47
  3.2 0.1 copy.26
  3.3 1.3 fusion.1.notes
  4.5 107.5 %attend_ahead.1 = (bf16[8,384,1792]{2,1,0:T(8,128)(2,1)}, bf16[768,1792]{1,0:T(8,128)(2,1)}, bf16[256,1792]{1,0:T(8,128)(2,1)}, f32[8,56,128]{2,1,0:T(8,128)}, b...) custom-call(bf16[384,1792]{1,0:T(8,128)(2,1)} %tokens.1, ...), custom_call_target="tpu_custom_call" | custom-call | bytes 300000000 | tf_op jit(solution)/shard_map/attend_ahead/pallas_call | solution.py:885
  112.1 165.3 %feed.1 = (f32[384,1792]{1,0:T(8,128)}, f32[384,1792]{1,0:T(8,128)}, bf16[384,1792]{1,0:T(8,128)(2,1)}, f32[8,1792]{1,0:T(8,128)}, bf16[8,384,512]{2,1,0:T(8,128...) custom-call(bf16[8,384,256]{2,1,0:T(8,128)(2,1)} %bitcast.16, ...), custom_call_target="tpu_custom_call" | custom-call | bytes 400000000 | tf_op jit(solution)/shard_map/feed/pallas_call | solution.py:1913
  277.4 117.4 %attend_back.1 = (bf16[8,8,48,768]{3,2,1,0:T(8,128)(2,1)}, bf16[384,1792]{1,0:T(8,128)(2,1)}, bf16[8,384,1792]{2,1,0:T(8,128)(2,1)}, bf16[4,1792,256]{2,1,0:T(8,128)(2,1)}, bf16[8,128,1792]{2,1,0:T(8,128)(2,1)}) custom-call(bf16[384,1792]{1,0:T(8,128)(2,1)} %get-tuple-element.55.branch, f32[8,56,128]{2,1,0:T(8,128)} %get-tuple-element.56.notes_all, ...), custom_call_target="tpu_custom_call" | custom-call | bytes 300000000 | tf_op jit(solution)/shard_map/attend_back/pallas_call | solution.py:1584
  394.8 117.1 %project_input.1 = (bf16[384,1792]{1,0:T(8,128)(2,1)}, f32[2,1792]{1,0:T(2,128)}, bf16[8,1792,256]{2,1,0:T(8,128)(2,1)}, bf16[8,448,896]{2,1,0:T(8,128)(2,1)}) custom-call(bf16[3072,768]{1,0:T(8,128)(2,1)} %bitcast.18, bf16[768,1792]{1,0:T(8,128)(2,1)} %get-tuple-element.64.w_in, bf16[8,384,1792]{2,1,0:T(8,128)(2,1)} %get-tuple-element.65.hidden_all, ...), custom_call_target="tpu_custom_call" | custom-call | bytes 250000000 | tf_op jit(solution)/shard_map/project_input/pallas_call | solution.py:2131
  511.9 20.7 %assemble.1 = (f32[1792]{0:T(1024)}, f32[1792]{0:T(1024)}, bf16[384,1792]{1,0:T(8,128)(2,1)}, bf16[384,1792]{1,0:T(8,128)(2,1)}, f32[448,1792]{1,0:T(8,128)}, /*...) custom-call(bf16[8,1792,256]{2,1,0:T(8,128)(2,1)} %get-tuple-element, ...), custom_call_target="tpu_custom_call" | custom-call | bytes 58000000 | tf_op jit(solution)/shard_map/assemble/pallas_call | solution.py:2217
  (1 shorter events, 0.0 us)
